TPU v7x, 32 devices: a whole 2x2x4 slice. The times are simulated.
32 devices in a mesh: groups: 2 (over y), dap: 4 (over z), chan: 2 (over x), sub: 2 (over core).
Axes of the slice: x: 2, y: 2, z: 4, core: 2. Of those that a mesh axis runs over, the one named last changes fastest.
Arguments:
- pair_input: bfloat16 [768, 384, 128], P(('groups', 'dap'), ('chan', 'sub')), parts along dimension 0, may hold values from -6 to 6
- first_gain: float32 [128], replicated, may hold values from 0.25 to 1.75
- first_project: bfloat16 [128, 512], replicated, may hold values from -0.5 to 0.5
- first_gate: bfloat16 [128, 128], replicated, may hold values from -0.5 to 0.5
- first_norm: float32 [128], replicated, may hold values from 0.25 to 1.75
- first_final: bfloat16 [128, 128], replicated, may hold values from -0.5 to 0.5
- second_gain: float32 [128], replicated, may hold values from 0.25 to 1.75
- second_project: bfloat16 [128, 512], replicated, may hold values from -0.5 to 0.5
- second_gate: bfloat16 [128, 128], replicated, may hold values from -0.5 to 0.5
- second_norm: float32 [128], replicated, may hold values from 0.25 to 1.75
- second_final: bfloat16 [128, 128], replicated, may hold values from -0.5 to 0.5
Outputs:
- pair_output: bfloat16 [768, 384, 128], P(('groups', 'dap'), ('chan', 'sub')), parts along dimension 0
There are 2 independent parts, one for each index of `groups`. A program takes and returns all parts, laid end to end along the dimension named above; an argument that names none is the same for every part. Nothing has to cross between parts.
All inputs are finite; a program needn't handle non-finite values.
Results may differ from a plain program's by a relative error of at most 0.013.
Values may be sent and summed in bfloat16 or wider, within the bound.
No kernel may reach another device: no remote copies, remote signals or barrier semaphores. Data moves between devices by JAX's collectives and lax.ppermute only.
A program may use at most 64 MiB of HBM per device.

v0:
```python
import jax
import jax.numpy as jnp
from jax import lax
from jax.sharding import PartitionSpec as P

epsilon = 1e-05


def layer_norm(values, norm_gain, reduce_axis):
    average = jnp.mean(values, axis=reduce_axis, keepdims=True)
    centred = values - average
    variance = jnp.mean(centred * centred, axis=reduce_axis, keepdims=True)
    return centred * lax.rsqrt(variance + epsilon) * norm_gain


def project_in(pair_state, norm_gain, project, gate_matrix):
    row_count, col_count, features = pair_state.shape
    flattened = pair_state.reshape(row_count * col_count, features).astype(jnp.float32)
    normed = layer_norm(flattened, norm_gain, 1).astype(jnp.bfloat16)
    projected = jnp.einsum("xc,cd->dx", normed, project, preferred_element_type=jnp.float32)
    left_part = jax.nn.sigmoid(projected[:features]) * projected[features : 2 * features]
    right_part = jax.nn.sigmoid(projected[2 * features : 3 * features]) * projected[3 * features :]
    left_part = left_part.astype(jnp.bfloat16).reshape(features, row_count, col_count)
    right_part = right_part.astype(jnp.bfloat16).reshape(features, row_count, col_count)
    gating = jax.nn.sigmoid(jnp.dot(normed, gate_matrix, preferred_element_type=jnp.float32))
    return (left_part, right_part, gating)


def finish(pair_state, mixture, gating, out_gain, final_matrix):
    features = mixture.shape[0]
    flattened = mixture.reshape(features, -1).astype(jnp.float32)
    normed = layer_norm(flattened, out_gain[:, None], 0).astype(jnp.bfloat16)
    update = jnp.einsum("cx,cd->xd", normed, final_matrix, preferred_element_type=jnp.float32)
    result = pair_state.reshape(-1, features).astype(jnp.float32) + gating * update
    return result.astype(jnp.bfloat16).reshape(pair_state.shape)


def shards(
    pair_input,
    first_gain,
    first_project,
    first_gate,
    first_norm,
    first_final,
    second_gain,
    second_project,
    second_gate,
    second_norm,
    second_final,
):
    left_part, right_part, gating = project_in(pair_input, first_gain, first_project, first_gate)
    left_part, right_part = (
        lax.all_to_all(left_part, ("chan", "sub"), split_axis=0, concat_axis=2, tiled=True),
        lax.all_to_all(right_part, ("chan", "sub"), split_axis=0, concat_axis=2, tiled=True),
    )
    mixture = jnp.einsum(
        "cik,cjk->cij",
        left_part,
        lax.all_gather(right_part, "dap", axis=1, tiled=True),
        preferred_element_type=jnp.float32,
    ).astype(jnp.bfloat16)
    mixture = lax.all_to_all(mixture, ("chan", "sub"), split_axis=2, concat_axis=0, tiled=True)
    middle = finish(pair_input, mixture, gating, first_norm, first_final)
    left_part, right_part, gating = project_in(middle, second_gain, second_project, second_gate)
    left_part, right_part = (
        lax.all_to_all(left_part, ("chan", "sub"), split_axis=0, concat_axis=2, tiled=True),
        lax.all_to_all(right_part, ("chan", "sub"), split_axis=0, concat_axis=2, tiled=True),
    )
    turned = lax.all_to_all(left_part, "dap", split_axis=2, concat_axis=1, tiled=True)
    mixture = jnp.einsum(
        "cki,ckj->cij",
        turned,
        lax.all_gather(right_part, "dap", axis=1, tiled=True),
        preferred_element_type=jnp.float32,
    )
    mixture = lax.all_to_all(
        mixture.astype(jnp.bfloat16), ("chan", "sub"), split_axis=2, concat_axis=0, tiled=True
    )
    return finish(middle, mixture, gating, second_norm, second_final)


def solution(mesh):
    placed = (
        P(("groups", "dap"), ("chan", "sub"), None),
        P(),
        P(),
        P(),
        P(),
        P(),
        P(),
        P(),
        P(),
        P(),
        P(),
    )
    return jax.shard_map(
        shards,
        mesh=mesh,
        in_specs=placed,
        out_specs=P(("groups", "dap"), ("chan", "sub"), None),
        check_vma=False,
    )
```

profile of v0, /device:TPU:0, one launch (start us, length us, event | category | flops | bytes accessed | tf_op | source)
XLA Modules:
  0.0 716.9 jit_solution(18188985698345366559)
XLA Ops:
  13.9 4.9 fusion.29
  26.8 4.8 copy.28
  31.6 41.2 %all_to_all.108 = bf16[128,96,96]{2,1,0:T(8,128)(2,1)S(1)} all-to-all(bf16[128,96,96]{2,1,0:T(8,128)(2,1)} %copy.28), channel_id=1, replica_groups=mesh['groups'=2,'dap'=4,'chan'=2,'sub'=2] {'chan','sub'}, dimensions={0} | all-to-all | bytes 4718592 | tf_op jit(solution)/shard_map/all_to_all | solution.py:54
  76.9 5.9 all_to_all.86
  82.9 4.8 copy.26
  87.7 41.0 %all_to_all.109 = bf16[128,96,96]{2,1,0:T(8,128)(2,1)S(1)} all-to-all(bf16[128,96,96]{2,1,0:T(8,128)(2,1)} %copy.26), channel_id=1, replica_groups=mesh['groups'=2,'dap'=4,'chan'=2,'sub'=2] {'chan','sub'}, dimensions={0} | all-to-all | bytes 4718592 | tf_op jit(solution)/shard_map/all_to_all | solution.py:53
  132.7 5.9 all_to_all.82
  138.6 112.3 %all-gather.3.cloned.1.call-done = bf16[32,384,384]{2,1,0:T(8,128)(2,1)} async-done(((bf16[32,96,384]{2,1,0:T(8,128)(2,1)}), bf16[32,384,384]{2,1,0:T(8,128)(2,1)}) %all-gather.3.cloned.1.call-update) | async-done | bytes 9437200 | tf_op jit(solution)/shard_map/all_gather | solution.py:59
  250.9 9.1 %convolution_convert_fusion.1 = bf16[32,96,384]{2,1,0:T(8,128)(2,1)} fusion(bf16[32,96,384]{2,1,0:T(8,128)(2,1)} %all_to_all.82, bf16[32,384,384]{2,1,0:T(8,128)(2,1)} %all-gather.3.cloned.1.call-done), kind=kOutput, calls=%fused_computation.61 | convolution fusion | flops 907149312 | bytes 14155776 | tf_op jit(solution)/shard_map/cik,cjk->cij/dot_general | solution.py:56
  260.0 5.0 copy.30
  265.0 4.7 all-to-all-start.2
  269.7 5.2 fusion.9
  274.9 31.7 %all-to-all-done.2 = bf16[32,96,384]{1,0,2:T(8,128)(2,1)} async-done(((bf16[32,96,384]{1,0,2:T(8,128)(2,1)}), bf16[32,96,384]{1,0,2:T(8,128)(2,1)}, u32[]{:S(2)}, u32[]{:S(2)}) %all-to-all-start.2) | async-done | bytes 2359328 | tf_op jit(solution)/shard_map/all_to_all | solution.py:62
  306.6 6.9 copy.31
  319.3 7.2 %reshape.153 = f32[128,9216]{1,0:T(8,128)} reshape(f32[4,32,96,96]{3,2,1,0:T(8,128)} %bitcast.64) | data formatting | bytes 9437184 | tf_op jit(solution)/shard_map/convert_element_type | solution.py:31
  326.4 5.9 fusion.36
  341.4 4.7 copy.37
  346.1 40.7 %all_to_all.110 = bf16[128,96,96]{2,1,0:T(8,128)(2,1)S(1)} all-to-all(bf16[128,96,96]{2,1,0:T(8,128)(2,1)} %copy.37), channel_id=1, replica_groups=mesh['groups'=2,'dap'=4,'chan'=2,'sub'=2] {'chan','sub'}, dimensions={0} | all-to-all | bytes 4718592 | tf_op jit(solution)/shard_map/all_to_all | solution.py:67
  390.9 5.9 all_to_all.99
  400.1 42.3 %all_to_all.111 = bf16[128,96,96]{2,1,0:T(8,128)(2,1)} all-to-all(bf16[128,96,96]{2,1,0:T(8,128)(2,1)} %copy.32), channel_id=1, replica_groups=mesh['groups'=2,'dap'=4,'chan'=2,'sub'=2] {'chan','sub'}, dimensions={0} | all-to-all | bytes 4718592 | tf_op jit(solution)/shard_map/all_to_all | solution.py:66
  442.4 6.6 copy.41
  449.0 159.6 %all_to_all.112 = bf16[32,96,384]{1,0,2:T(8,128)(2,1)S(1)} all-to-all(bf16[32,96,384]{1,0,2:T(8,128)(2,1)} %bitcast.71), channel_id=1, replica_groups=mesh['groups'=2,'dap'=4,'chan'=2,'sub'=2] {'dap'}, dimensions={2} | all-to-all | bytes 4718592 | tf_op jit(solution)/shard_map/all_to_all | solution.py:69
  612.6 5.0 all_to_all.95
  617.6 10.6 %all-gather.5.cloned.1.call-done = bf16[32,384,384]{2,1,0:T(8,128)(2,1)} async-done(((bf16[32,96,384]{2,1,0:T(8,128)(2,1)}), bf16[32,384,384]{2,1,0:T(8,128)(2,1)}) %all-gather.5.cloned.1.call-update) | async-done | bytes 9437200 | tf_op jit(solution)/shard_map/all_gather | solution.py:73
  628.2 7.0 convolution_convert_fusion
  635.2 5.0 copy.39
  640.2 4.8 all-to-all-start.6
  645.1 6.7 fusion.10
  651.8 30.3 %all-to-all-done.6 = bf16[32,96,384]{1,0,2:T(8,128)(2,1)} async-done(((bf16[32,96,384]{1,0,2:T(8,128)(2,1)}), bf16[32,96,384]{1,0,2:T(8,128)(2,1)}, u32[]{:S(2)}, u32[]{:S(2)}) %all-to-all-start.6) | async-done | bytes 2359328 | tf_op jit(solution)/shard_map/all_to_all | solution.py:76
  682.0 6.9 copy.40
  694.6 7.2 %reshape.154 = f32[128,9216]{1,0:T(8,128)} reshape(f32[4,32,96,96]{3,2,1,0:T(8,128)} %bitcast.65) | data formatting | bytes 9437184 | tf_op jit(solution)/shard_map/convert_element_type | solution.py:31
  701.8 8.0 %fusion.7 = bf16[9216,128]{1,0:T(8,128)(2,1)} fusion(f32[9216,128]{1,0:T(8,128)} %copy-done.4, f32[9216,128]{1,0:T(8,128)} %fusion.10, bf16[128,128]{1,0:T(8,128)(2,1)S(1)} %copy-done.9, f32[128,9216]{1,0:T(8,128)} %reshape.154, f32[128]{0:T(128)S(1)} %copy-done.13, f32[9216]{0:T(1024)S(1)} %rsqrt.47, f32[9216]{0:T(1024)S(1)} %div.63), kind=kOutput, calls=%fused_computation.13 | convolution fusion | flops 310247424 | bytes 16622080 | tf_op jit(solution)/shard_map/cx,cd->xd/dot_general | solution.py:33
  (66 shorter events, 55.0 us)
Async XLA Ops:
  6.5 13.7 %copy-start = (bf16[128,512]{1,0:T(8,128)(2,1)S(1)}, bf16[128,512]{1,0:T(8,128)(2,1)}, u32[]{:S(2)}) copy-start(bf16[128,512]{1,0:T(8,128)(2,1)} %param.13) | copy-start | bytes 393220
  6.5 7.3 %copy-start.5 = (bf16[96,96,128]{2,1,0:T(8,128)(2,1)S(1)}, bf16[96,96,128]{2,1,0:T(8,128)(2,1)}, u32[]{:S(2)}) copy-start(bf16[96,96,128]{2,1,0:T(8,128)(2,1)} %param.11) | copy-start | bytes 7077892
  6.5 7.3 %copy-start.12 = (f32[128]{0:T(128)S(1)}, f32[128]{0:T(128)}, u32[]{:S(2)}) copy-start(f32[128]{0:T(128)} %param.12) | copy-start | bytes 1540
  6.5 244.4 %all-gather.3.cloned.1.call-start = ((), (), s32[]{:S(2)}) async-start(), calls=%async_computation.7 | async-start | bytes 11796480 | tf_op jit(solution)/shard_map/all_gather | solution.py:59
  18.9 1.4 copy-start.6
  260.0 9.7 %copy-start.14 = (bf16[128,128]{1,0:T(8,128)(2,1)S(1)}, bf16[128,128]{1,0:T(8,128)(2,1)}, u32[]{:S(2)}) copy-start(bf16[128,128]{1,0:T(8,128)(2,1)} %param.14) | copy-start | bytes 98308
  265.0 41.6 %all-to-all-start.2 = ((bf16[32,96,384]{1,0,2:T(8,128)(2,1)}), bf16[32,96,384]{1,0,2:T(8,128)(2,1)}, u32[]{:S(2)}, u32[]{:S(2)}) async-start(bf16[32,96,384]{1,0,2:T(8,128)(2,1)} %copy.30), calls=%async_computation.2 | async-start | bytes 6291456 | tf_op jit(solution)/shard_map/all_to_all | solution.py:62
  269.7 358.5 %all-gather.5.cloned.1.call-start = ((), (), s32[]{:S(2)}) async-start(), calls=%async_computation.8 | async-start | bytes 11796480 | tf_op jit(solution)/shard_map/all_gather | solution.py:73
  313.5 4.6 copy-start.2
  319.2 7.2 %copy-start.8 = (bf16[128,128]{1,0:T(8,128)(2,1)S(1)}, bf16[128,128]{1,0:T(8,128)(2,1)}, u32[]{:S(2)}) copy-start(bf16[128,128]{1,0:T(8,128)(2,1)} %param.16) | copy-start | bytes 98308
  319.2 7.2 %copy-start.11 = (f32[128]{0:T(128)S(1)}, f32[128]{0:T(128)}, u32[]{:S(2)}) copy-start(f32[128]{0:T(128)} %param.15) | copy-start | bytes 1540
  332.4 5.5 copy-start.4
  332.4 2.8 copy-start.7
  332.4 2.8 copy-start.10
  635.2 9.9 %copy-start.15 = (bf16[128,128]{1,0:T(8,128)(2,1)S(1)}, bf16[128,128]{1,0:T(8,128)(2,1)}, u32[]{:S(2)}) copy-start(bf16[128,128]{1,0:T(8,128)(2,1)} %param.19) | copy-start | bytes 98308
  640.2 41.8 %all-to-all-start.6 = ((bf16[32,96,384]{1,0,2:T(8,128)(2,1)}), bf16[32,96,384]{1,0,2:T(8,128)(2,1)}, u32[]{:S(2)}, u32[]{:S(2)}) async-start(bf16[32,96,384]{1,0,2:T(8,128)(2,1)} %copy.39), calls=%async_computation.6 | async-start | bytes 6291456 | tf_op jit(solution)/shard_map/all_to_all | solution.py:76
  688.9 4.6 copy-start.3
  694.6 7.2 %copy-start.9 = (bf16[128,128]{1,0:T(8,128)(2,1)S(1)}, bf16[128,128]{1,0:T(8,128)(2,1)}, u32[]{:S(2)}) copy-start(bf16[128,128]{1,0:T(8,128)(2,1)} %param.21) | copy-start | bytes 98308
  694.6 7.2 %copy-start.13 = (f32[128]{0:T(128)S(1)}, f32[128]{0:T(128)}, u32[]{:S(2)}) copy-start(f32[128]{0:T(128)} %param.20) | copy-start | bytes 1540
  694.6 15.2 %copy-start.1 = (bf16[128,512]{1,0:T(8,128)(2,1)S(1)}, bf16[128,512]{1,0:T(8,128)(2,1)}, u32[]{:S(2)}) copy-start(bf16[128,512]{1,0:T(8,128)(2,1)} %param.13) | copy-start | bytes 393220
Sparse Core Ops, SparseCore 0:
  83.0 167.8 all-gather.2
  397.0 231.1 all-gather.4
where the time goes:
time: 727 us; the launch traced here: 717 us
  blocking collectives  325 us (45%)
  waiting for transfers between devices  185 us (25%)
  local copies, waits for them, and re-layouts  106 us (15%)
  matrix products  47 us (6%)
  other arithmetic  30.8 us (4%)
  between operations  13.9 us (2%)
  starting transfers between devices  9.54 us (1%)
    all_to_all x1, blocking collectives, shards(): lax.all_to_all(left_part, 'dap', split_axis=2, concat_axis=1, tiled=True)  160 us
    all_gather x2, waiting for transfers between devices, shards(): lax.all_gather(right_part, 'dap', axis=1, tiled=True)  123 us
    all_to_all x2, blocking collectives, shards(): lax.all_to_all(left_part, ('chan', 'sub'), split_axis=0, concat_axis=2, t...  83.3 us
    all_to_all x2, blocking collectives, shards(): lax.all_to_all(right_part, ('chan', 'sub'), split_axis=0, concat_axis=2,...  82 us
    all_to_all x1, waiting for transfers between devices, shards(): lax.all_to_all(mixture, ('chan', 'sub'), split_axis=2, concat_axis=0, til...  31.7 us
    all_to_all x1, waiting for transfers between devices, shards(): lax.all_to_all(mixture.astype(jnp.bfloat16), ('chan', 'sub'), split_axis=...  30.3 us
    convert_element_type x4, local copies, waits for them, and re-layouts, finish(): flattened = mixture.reshape(features, -1).astype(jnp.float32)  28.1 us
    all_to_all x4, local copies, waits for them, and re-layouts, shards(): lax.all_to_all(right_part, ('chan', 'sub'), split_axis=0, concat_axis=2,...  20 us
  transfers between devices with their start and end apart: 4, of which 4 were waited for; matrix products, arithmetic and copies ran while one was open for 5% of the time, Pallas kernels for 0%

commit v1 on v0

v1 whole, which is shorter than its diff:
```python
import jax
import jax.numpy as jnp
from jax import lax
from jax.sharding import Mesh
from jax.sharding import PartitionSpec as P

epsilon = 1e-05
EVERY = ("near", "chan", "sub")


def layer_norm(values, norm_gain, reduce_axis):
    average = jnp.mean(values, axis=reduce_axis, keepdims=True)
    centred = values - average
    variance = jnp.mean(centred * centred, axis=reduce_axis, keepdims=True)
    return centred * lax.rsqrt(variance + epsilon) * norm_gain


def project_in(pair_state, norm_gain, project, gate_matrix):
    features = pair_state.shape[-1]
    flattened = pair_state.reshape(-1, features).astype(jnp.float32)
    normed = layer_norm(flattened, norm_gain, 1).astype(jnp.bfloat16)
    projected = jnp.einsum("xc,cd->dx", normed, project, preferred_element_type=jnp.float32)
    left_part = jax.nn.sigmoid(projected[:features]) * projected[features : 2 * features]
    right_part = jax.nn.sigmoid(projected[2 * features : 3 * features]) * projected[3 * features :]
    gating = jax.nn.sigmoid(jnp.dot(normed, gate_matrix, preferred_element_type=jnp.float32))
    return left_part.astype(jnp.bfloat16), right_part.astype(jnp.bfloat16), gating


def finish(pair_state, mixture, gating, out_gain, final_matrix):
    features = mixture.shape[0]
    flattened = mixture.astype(jnp.float32)
    normed = layer_norm(flattened, out_gain[:, None], 0).astype(jnp.bfloat16)
    update = jnp.einsum("cx,cd->xd", normed, final_matrix, preferred_element_type=jnp.float32)
    result = pair_state.reshape(-1, features).astype(jnp.float32) + gating * update
    return result.astype(jnp.bfloat16).reshape(pair_state.shape)


def update(incoming, sizes, pair_state, norm_gain, project, gate_matrix, out_gain, final_matrix):
    far, near, col_parts = sizes
    row_count, col_count, features = pair_state.shape
    parts = near * col_parts
    width = features // parts
    left_part, right_part, gating = project_in(pair_state, norm_gain, project, gate_matrix)
    both = jnp.stack([left_part.reshape(parts, width, -1), right_part.reshape(parts, width, -1)], axis=1)
    both = lax.all_to_all(both, EVERY, split_axis=0, concat_axis=0, tiled=True)
    both = both.reshape(near, col_parts, 2, width, row_count, col_count)
    both = both.transpose(2, 3, 0, 4, 1, 5).reshape(2, width, near * row_count, col_parts * col_count)
    left_part, right_part = both[0], both[1]
    if incoming:
        mixture = jnp.einsum("cki,ckj->cij", left_part, right_part, preferred_element_type=jnp.float32)
        if far > 1:
            mixture = lax.psum_scatter(mixture, "far", scatter_dimension=1, tiled=True)
    else:
        if far > 1:
            right_part = lax.all_gather(right_part, "far", axis=1, tiled=True)
        mixture = jnp.einsum("cik,cjk->cij", left_part, right_part, preferred_element_type=jnp.float32)
    mixture = mixture.astype(jnp.bfloat16).reshape(width, near, row_count, col_parts, col_count)
    mixture = mixture.transpose(1, 3, 0, 2, 4).reshape(parts, width, row_count * col_count)
    mixture = lax.all_to_all(mixture, EVERY, split_axis=0, concat_axis=0, tiled=True)
    return finish(pair_state, mixture.reshape(features, -1), gating, out_gain, final_matrix)


def split_rows(row_parts, col_parts, features, least):
    near = row_parts
    while near > 1 and (row_parts % near or features % (near * col_parts) or features < least * near * col_parts):
        near -= 1
    return row_parts // near, near


def solution(mesh):
    row_parts, col_parts = mesh.shape["dap"], mesh.shape["chan"] * mesh.shape["sub"]

    def whole(pair_input, *weights):
        far, near = split_rows(row_parts, col_parts, pair_input.shape[-1], 8)
        sizes = (far, near, col_parts)
        finer = Mesh(
            mesh.devices.reshape(mesh.shape["groups"], far, near, mesh.shape["chan"], mesh.shape["sub"]),
            ("groups", "far", "near", "chan", "sub"),
        )

        def shards(pair_input, *weights):
            middle = update(False, sizes, pair_input, *weights[:5])
            return update(True, sizes, middle, *weights[5:])

        pair_spec = P(("groups", "far", "near"), ("chan", "sub"), None)
        return jax.shard_map(
            shards,
            mesh=finer,
            in_specs=(pair_spec,) + (P(),) * 10,
            out_specs=pair_spec,
            check_vma=False,
        )(pair_input, *weights)

    return whole
```

time: 727 us -> 497 us (0.68)
  the two profiles are of different devices: /device:TPU:0 before, /device:TPU:11 now
where the time goes in v1:
time: 497 us; the launch traced here: 490 us
  blocking collectives  218 us (44%)
  local copies, waits for them, and re-layouts  101 us (20%)
  waiting for transfers between devices  94.3 us (19%)
  matrix products  38.3 us (8%)
  other arithmetic  26.6 us (5%)
  starting transfers between devices  10.5 us (2%)
    all_to_all x2, blocking collectives, update(): both = lax.all_to_all(both, EVERY, split_axis=0, concat_axis=0, tiled=True)  218 us
    all_to_all x2, waiting for transfers between devices, update(): lax.all_to_all(mixture, EVERY, split_axis=0, concat_axis=0, tiled=True)  94.3 us
    reshape x4, local copies, waits for them, and re-layouts, update(): both = both.reshape(near, col_parts, 2, width, row_count, col_count)  41.7 us
    squeeze x4, local copies, waits for them, and re-layouts, update(): left_part, right_part = (both[0], both[1])  19.3 us
    reshape x4, local copies, waits for them, and re-layouts, update(): mixture.astype(jnp.bfloat16)  16 us
    reshape x2, local copies, waits for them, and re-layouts, update(): mixture.transpose(1, 3, 0, 2, 4)  13.4 us
    dot_general x2, matrix products, project_in(): jnp.dot(normed, gate_matrix, preferred_element_type=jnp.float32)  11.8 us
    all_to_all x2, starting transfers between devices, update(): lax.all_to_all(mixture, EVERY, split_axis=0, concat_axis=0, tiled=True)  10.5 us
  transfers between devices with their start and end apart: 2, of which 2 were waited for; matrix products, arithmetic and copies ran while one was open for 2% of the time, Pallas kernels for 0%

profile of v1, /device:TPU:11, one launch (start us, length us, event | category | flops | bytes accessed | tf_op | source)
XLA Modules:
  0.0 489.8 jit_solution(4026803121116600913)
XLA Ops:
  0.0 2.7 convert_reduce_fusion.2
  2.8 4.4 multiply_reduce_fusion.1
  7.4 4.9 %fusion.41 = bf16[9216,128]{1,0:T(8,128)(2,1)S(1)} fusion(bf16[96,96,128]{2,1,0:T(8,128)(2,1)S(1)} %copy-done.3, f32[128]{0:T(128)S(1)} %copy-done.13, f32[9216]{0:T(1024)S(1)} %rsqrt.36, f32[9216]{0:T(1024)S(1)} %div.45), kind=kLoop, calls=%fused_computation.66 | loop fusion | flops 5898240 | bytes 4792832 | tf_op jit(solution)/shard_map/convert_element_type | solution.py:21
  18.0 110.1 %all_to_all.20 = bf16[16,2,8,9216]{3,2,1,0:T(8,128)(2,1)} all-to-all(bf16[16,2,8,9216]{3,2,1,0:T(8,128)(2,1)S(1)} %pad_maximum_fusion), channel_id=1, replica_groups=mesh['groups'=2,'dap'=4,'chan'=2,'sub'=2] {'dap','chan','sub'}, dimensions={0} | all-to-all | bytes 9437184 | tf_op jit(solution)/shard_map/all_to_all | solution.py:45
  128.0 10.0 %reshape.123 = bf16[4,4,2,8,96,96]{5,4,3,2,1,0:T(8,128)(2,1)} reshape(bf16[16,2,8,9216]{3,2,1,0:T(8,128)(2,1)} %all_to_all.20) | data formatting | bytes 9437184 | tf_op jit(solution)/shard_map/reshape | solution.py:46
  138.0 10.9 %copy.35 = bf16[4,4,2,8,96,96]{5,1,4,0,3,2:T(4,128)(2,1)S(1)} copy(bf16[4,4,2,8,96,96]{5,4,3,2,1,0:T(8,128)(2,1)} %reshape.123) | data formatting | bytes 9437184 | tf_op jit(solution)/shard_map/reshape | solution.py:46
  148.9 4.4 fusion.55
  153.3 6.1 %squeeze.12 = bf16[8,384,384]{2,1,0:T(8,128)(2,1)} reshape(bf16[1,8,4,96,4,96]{5,4,3,2,1,0:T(4,128)(2,1)} %get-tuple-element.12) | data formatting | bytes 4718592 | tf_op jit(solution)/shard_map/squeeze | solution.py:48
  159.5 3.6 squeeze.13
  163.1 5.5 %convolution_convert_fusion.1 = bf16[8,384,384]{2,1,0:T(8,128)(2,1)} fusion(bf16[8,384,384]{2,1,0:T(8,128)(2,1)} %squeeze.12, bf16[8,384,384]{2,1,0:T(8,128)(2,1)} %squeeze.13), kind=kOutput, calls=%fused_computation.84 | convolution fusion | flops 907149312 | bytes 7077888 | tf_op jit(solution)/shard_map/cik,cjk->cij/dot_general | solution.py:56
  168.6 5.8 %reshape.124 = bf16[8,4,96,4,96]{4,3,2,1,0:T(4,128)(2,1)S(1)} reshape(bf16[8,384,384]{2,1,0:T(8,128)(2,1)} %convolution_convert_fusion.1) | data formatting | bytes 4718592 | tf_op jit(solution)/shard_map/reshape | solution.py:57
  176.6 6.7 %reshape.125 = bf16[16,8,9216]{2,1,0:T(8,128)(2,1)} reshape(bf16[4,4,8,96,96]{4,3,2,1,0:T(8,128)(2,1)} %bitcast.89) | data formatting | bytes 4718592 | tf_op jit(solution)/shard_map/reshape | solution.py:58
  183.3 5.2 %all-to-all-start.1 = ((bf16[16,8,9216]{2,1,0:T(8,128)(2,1)}), bf16[16,8,9216]{2,1,0:T(8,128)(2,1)S(1)}, u32[]{:S(2)}, u32[]{:S(2)}) async-start(bf16[16,8,9216]{2,1,0:T(8,128)(2,1)} %reshape.125), calls=%async_computation.1 | async-start | bytes 4718592 | tf_op jit(solution)/shard_map/all_to_all | solution.py:59
  188.5 5.2 %fusion.9 = f32[9216,128]{1,0:T(8,128)} fusion(bf16[9216,128]{1,0:T(8,128)(2,1)} %copy-done.7, bf16[128,128]{1,0:T(8,128)(2,1)S(1)} %copy-done.16), kind=kOutput, calls=%fused_computation.15 | convolution fusion | flops 305528832 | bytes 7110656 | tf_op jit(solution)/shard_map/dot_general | solution.py:25
  193.7 47.9 %all-to-all-done.1 = bf16[16,8,9216]{2,1,0:T(8,128)(2,1)S(1)} async-done(((bf16[16,8,9216]{2,1,0:T(8,128)(2,1)}), bf16[16,8,9216]{2,1,0:T(8,128)(2,1)S(1)}, u32[]{:S(2)}, u32[]{:S(2)}) %all-to-all-start.1) | async-done | bytes 2359328 | tf_op jit(solution)/shard_map/all_to_all | solution.py:59
  243.2 4.7 fusion.56
  250.7 2.8 convolution_bitcast_fusion
  253.6 3.9 fusion.52
  257.5 2.8 pad_maximum_fusion.1
  260.3 108.3 %all_to_all.21 = bf16[16,2,8,9216]{3,2,1,0:T(8,128)(2,1)} all-to-all(bf16[16,2,8,9216]{3,2,1,0:T(8,128)(2,1)S(1)} %pad_maximum_fusion.1), channel_id=1, replica_groups=mesh['groups'=2,'dap'=4,'chan'=2,'sub'=2] {'dap','chan','sub'}, dimensions={0} | all-to-all | bytes 9437184 | tf_op jit(solution)/shard_map/all_to_all | solution.py:45
  368.6 10.0 %reshape.126 = bf16[4,4,2,8,96,96]{5,4,3,2,1,0:T(8,128)(2,1)} reshape(bf16[16,2,8,9216]{3,2,1,0:T(8,128)(2,1)} %all_to_all.21) | data formatting | bytes 9437184 | tf_op jit(solution)/shard_map/reshape | solution.py:46
  378.6 10.9 %copy.34 = bf16[4,4,2,8,96,96]{5,1,4,0,3,2:T(4,128)(2,1)S(1)} copy(bf16[4,4,2,8,96,96]{5,4,3,2,1,0:T(8,128)(2,1)} %reshape.126) | data formatting | bytes 9437184 | tf_op jit(solution)/shard_map/reshape | solution.py:46
  389.5 4.4 fusion.54
  393.9 6.1 %reshape.133 = bf16[8,384,384]{2,1,0:T(8,128)(2,1)} reshape(bf16[1,8,4,96,4,96]{5,4,3,2,1,0:T(4,128)(2,1)} %get-tuple-element.10) | data formatting | bytes 4718592 | tf_op jit(solution)/shard_map/squeeze | solution.py:48
  400.0 3.4 squeeze.15
  403.4 5.4 %convolution_convert_fusion = bf16[8,384,384]{2,1,0:T(8,128)(2,1)} fusion(bf16[8,384,384]{2,1,0:T(8,128)(2,1)} %reshape.133, bf16[8,384,384]{2,1,0:T(8,128)(2,1)} %squeeze.15), kind=kOutput, calls=%fused_computation.83 | convolution fusion | flops 907149312 | bytes 7077888 | tf_op jit(solution)/shard_map/cki,ckj->cij/dot_general | solution.py:50
  408.9 5.8 %reshape.127 = bf16[8,4,96,4,96]{4,3,2,1,0:T(4,128)(2,1)S(1)} reshape(bf16[8,384,384]{2,1,0:T(8,128)(2,1)} %convolution_convert_fusion) | data formatting | bytes 4718592 | tf_op jit(solution)/shard_map/reshape | solution.py:57
  416.9 6.7 %reshape.128 = bf16[16,8,9216]{2,1,0:T(8,128)(2,1)} reshape(bf16[4,4,8,96,96]{4,3,2,1,0:T(8,128)(2,1)} %bitcast.90) | data formatting | bytes 4718592 | tf_op jit(solution)/shard_map/reshape | solution.py:58
  423.6 5.2 %all-to-all-start.3 = ((bf16[16,8,9216]{2,1,0:T(8,128)(2,1)}), bf16[16,8,9216]{2,1,0:T(8,128)(2,1)S(1)}, u32[]{:S(2)}, u32[]{:S(2)}) async-start(bf16[16,8,9216]{2,1,0:T(8,128)(2,1)} %reshape.128), calls=%async_computation.3 | async-start | bytes 4718592 | tf_op jit(solution)/shard_map/all_to_all | solution.py:59
  428.8 6.6 %fusion.10 = f32[9216,128]{1,0:T(8,128)} fusion(bf16[128,128]{1,0:T(8,128)(2,1)S(1)} %copy-done.17, f32[9216,128]{1,0:T(8,128)} %copy-done.2, f32[128]{0:T(128)S(1)} %copy-done.12, f32[9216]{0:T(1024)S(1)} %add_rsqrt_fusion.2, f32[9216]{0:T(1024)S(1)} %broadcast_multiply_fusion.2), kind=kOutput, calls=%fused_computation.16 | convolution fusion | flops 310247424 | bytes 9544192 | tf_op jit(solution)/shard_map/dot_general | solution.py:25
  435.4 46.4 %all-to-all-done.3 = bf16[16,8,9216]{2,1,0:T(8,128)(2,1)S(1)} async-done(((bf16[16,8,9216]{2,1,0:T(8,128)(2,1)}), bf16[16,8,9216]{2,1,0:T(8,128)(2,1)S(1)}, u32[]{:S(2)}, u32[]{:S(2)}) %all-to-all-start.3) | async-done | bytes 2359328 | tf_op jit(solution)/shard_map/all_to_all | solution.py:59
  484.2 5.4 %fusion.7 = bf16[9216,128]{1,0:T(8,128)(2,1)} fusion(f32[9216,128]{1,0:T(8,128)} %copy-done.2, f32[9216,128]{1,0:T(8,128)S(1)} %copy-done.8, bf16[128,128]{1,0:T(8,128)(2,1)S(1)} %copy-done.11, bf16[16,8,9216]{2,1,0:T(8,128)(2,1)S(1)} %all-to-all-done.3, f32[128]{0:T(128)S(1)} %copy-done.15, f32[9216]{0:T(1024)S(1)} %add_rsqrt_fusion.1, ...), kind=kOutput, calls=%fused_computation.13 | convolution fusion | flops 311427072 | bytes 14262784 | tf_op jit(solution)/shard_map/cx,cd->xd/dot_general | solution.py:33
  (56 shorter events, 16.9 us)
Async XLA Ops:
  0.0 12.3 %copy-start = (bf16[128,512]{1,0:T(8,128)(2,1)S(1)}, bf16[128,512]{1,0:T(8,128)(2,1)}, u32[]{:S(2)}) copy-start(bf16[128,512]{1,0:T(8,128)(2,1)} %param.13) | copy-start | bytes 393220
  0.0 7.3 %copy-start.3 = (bf16[96,96,128]{2,1,0:T(8,128)(2,1)S(1)}, bf16[96,96,128]{2,1,0:T(8,128)(2,1)}, u32[]{:S(2)}) copy-start(bf16[96,96,128]{2,1,0:T(8,128)(2,1)} %param.11) | copy-start | bytes 7077892
  0.0 7.3 %copy-start.13 = (f32[128]{0:T(128)S(1)}, f32[128]{0:T(128)}, u32[]{:S(2)}) copy-start(f32[128]{0:T(128)} %param.12) | copy-start | bytes 1540
  12.3 2.7 copy-start.7
  153.3 6.2 %copy-start.5 = (bf16[1,8,4,96,4,96]{5,4,3,2,1,0:T(4,128)(2,1)S(1)}, bf16[1,8,4,96,4,96]{5,4,3,2,1,0:T(4,128)(2,1)}, u32[]{:S(2)}) copy-start(bf16[1,8,4,96,4,96]{5,4,3,2,1,0:T(4,128)(2,1)} %get-tuple-element.11) | copy-start | bytes 7077892
  176.6 11.9 %copy-start.16 = (bf16[128,128]{1,0:T(8,128)(2,1)S(1)}, bf16[128,128]{1,0:T(8,128)(2,1)}, u32[]{:S(2)}) copy-start(bf16[128,128]{1,0:T(8,128)(2,1)} %param.14) | copy-start | bytes 98308
  183.3 58.3 %all-to-all-start.1 = ((bf16[16,8,9216]{2,1,0:T(8,128)(2,1)}), bf16[16,8,9216]{2,1,0:T(8,128)(2,1)S(1)}, u32[]{:S(2)}, u32[]{:S(2)}) async-start(bf16[16,8,9216]{2,1,0:T(8,128)(2,1)} %reshape.125), calls=%async_computation.1 | async-start | bytes 4718592 | tf_op jit(solution)/shard_map/all_to_all | solution.py:59
  193.7 49.0 %copy-start.10 = (bf16[128,128]{1,0:T(8,128)(2,1)S(1)}, bf16[128,128]{1,0:T(8,128)(2,1)}, u32[]{:S(2)}) copy-start(bf16[128,128]{1,0:T(8,128)(2,1)} %param.16) | copy-start | bytes 98308
  193.7 49.0 %copy-start.14 = (f32[128]{0:T(128)S(1)}, f32[128]{0:T(128)}, u32[]{:S(2)}) copy-start(f32[128]{0:T(128)} %param.15) | copy-start | bytes 1540
  241.5 1.7 copy-start.4
  247.9 5.7 %copy-start.2 = (f32[9216,128]{1,0:T(8,128)}, f32[9216,128]{1,0:T(8,128)S(1)}, u32[]{:S(2)}) copy-start(f32[9216,128]{1,0:T(8,128)S(1)} %get-tuple-element.14) | copy-start | bytes 14155780
  247.9 2.8 copy-start.9
  247.9 2.8 copy-start.12
  393.9 6.1 %copy-start.6 = (bf16[1,8,4,96,4,96]{5,4,3,2,1,0:T(4,128)(2,1)S(1)}, bf16[1,8,4,96,4,96]{5,4,3,2,1,0:T(4,128)(2,1)}, u32[]{:S(2)}) copy-start(bf16[1,8,4,96,4,96]{5,4,3,2,1,0:T(4,128)(2,1)} %get-tuple-element.9) | copy-start | bytes 7077892
  416.9 11.9 %copy-start.17 = (bf16[128,128]{1,0:T(8,128)(2,1)S(1)}, bf16[128,128]{1,0:T(8,128)(2,1)}, u32[]{:S(2)}) copy-start(bf16[128,128]{1,0:T(8,128)(2,1)} %param.19) | copy-start | bytes 98308
  423.6 58.3 %all-to-all-start.3 = ((bf16[16,8,9216]{2,1,0:T(8,128)(2,1)}), bf16[16,8,9216]{2,1,0:T(8,128)(2,1)S(1)}, u32[]{:S(2)}, u32[]{:S(2)}) async-start(bf16[16,8,9216]{2,1,0:T(8,128)(2,1)} %reshape.128), calls=%async_computation.3 | async-start | bytes 4718592 | tf_op jit(solution)/shard_map/all_to_all | solution.py:59
  435.4 47.6 %copy-start.11 = (bf16[128,128]{1,0:T(8,128)(2,1)S(1)}, bf16[128,128]{1,0:T(8,128)(2,1)}, u32[]{:S(2)}) copy-start(bf16[128,128]{1,0:T(8,128)(2,1)} %param.21) | copy-start | bytes 98308
  435.4 47.6 %copy-start.15 = (f32[128]{0:T(128)S(1)}, f32[128]{0:T(128)}, u32[]{:S(2)}) copy-start(f32[128]{0:T(128)} %param.20) | copy-start | bytes 1540
  481.8 2.3 copy-start.8
  482.9 6.7 %copy-start.1 = (bf16[128,512]{1,0:T(8,128)(2,1)S(1)}, bf16[128,512]{1,0:T(8,128)(2,1)}, u32[]{:S(2)}) copy-start(bf16[128,512]{1,0:T(8,128)(2,1)} %param.13) | copy-start | bytes 393220

commit v2 on v1

--- a/solution.py
+++ b/solution.py
@@ -1,11 +1,17 @@
+import functools
+
 import jax
 import jax.numpy as jnp
 from jax import lax
+from jax.experimental import pallas as pl
+from jax.experimental.pallas import tpu as pltpu
 from jax.sharding import Mesh
 from jax.sharding import PartitionSpec as P
 
 epsilon = 1e-05
 EVERY = ("near", "chan", "sub")
+LANES = 128
+BUDGET = 56 << 20
 
 
 def layer_norm(values, norm_gain, reduce_axis):
@@ -13,6 +19,10 @@
     centred = values - average
     variance = jnp.mean(centred * centred, axis=reduce_axis, keepdims=True)
     return centred * lax.rsqrt(variance + epsilon) * norm_gain
+
+
+def sigmoid(values):
+    return 0.5 * jnp.tanh(0.5 * values) + 0.5
 
 
 def project_in(pair_state, norm_gain, project, gate_matrix):
@@ -67,11 +77,375 @@
     return row_parts // near, near
 
 
+def emit_projections(normed, gate_rows, value_rows, out_refs):
+    at = 0
+    for ref in out_refs:
+        rows = ref.shape[0]
+        gates = lax.dot_general(
+            gate_rows[at : at + rows, :], normed, (((1,), (1,)), ((), ())), preferred_element_type=jnp.float32
+        )
+        values = lax.dot_general(
+            value_rows[at : at + rows, :], normed, (((1,), (1,)), ((), ())), preferred_element_type=jnp.float32
+        )
+        ref[...] = (sigmoid(gates) * values).astype(ref.dtype)
+        at += rows
+
+
+def project_kernel(state_ref, gain_ref, gate_rows, value_rows, *out_refs):
+    normed = layer_norm(state_ref[...].astype(jnp.float32), gain_ref[...], 1).astype(jnp.bfloat16)
+    emit_projections(normed, gate_rows, value_rows, out_refs)
+
+
+def finish_kernel(pieces, onward, *refs):
+    mix_refs, refs = refs[:pieces], refs[pieces:]
+    state_ref, gain_ref, gate_ref, out_gain_ref, final_ref = refs[:5]
+    state = state_ref[...].astype(jnp.float32)
+    normed = layer_norm(state, gain_ref[...], 1).astype(jnp.bfloat16)
+    gating = sigmoid(jnp.dot(normed, gate_ref[...], preferred_element_type=jnp.float32))
+    mixed = jnp.concatenate([ref[...].astype(jnp.float32) for ref in mix_refs], axis=0)
+    mixed = layer_norm(mixed, out_gain_ref[...], 0).astype(jnp.bfloat16)
+    change = lax.dot_general(
+        mixed, final_ref[...], (((0,), (0,)), ((), ())), preferred_element_type=jnp.float32
+    )
+    result = (state + gating * change).astype(jnp.bfloat16)
+    if onward:
+        next_gain, gate_rows, value_rows, middle_ref = refs[5:9]
+        middle_ref[...] = result
+        normed = layer_norm(result.astype(jnp.float32), next_gain[...], 1).astype(jnp.bfloat16)
+        emit_projections(normed, gate_rows, value_rows, refs[9:])
+    else:
+        refs[5][...] = result
+
+
+def whole_spec(array):
+    return pl.BlockSpec(array.shape, lambda step: (0,) * array.ndim)
+
+
+def row_step(positions):
+    step = positions
+    for candidate in range(LANES, 1152 + 1, LANES):
+        if positions % candidate == 0:
+            step = candidate
+    return step
+
+
+def run_projections(state, gain, gate_rows, value_rows, out_rows):
+    positions, features = state.shape
+    step = row_step(positions)
+    weights = (gain[None, :], gate_rows, value_rows)
+    return pl.pallas_call(
+        project_kernel,
+        grid=(positions // step,),
+        in_specs=[pl.BlockSpec((step, features), lambda i: (i, 0))] + [whole_spec(w) for w in weights],
+        out_specs=[pl.BlockSpec((rows, step), lambda i: (0, i)) for rows in out_rows],
+        out_shape=[jax.ShapeDtypeStruct((rows, positions), jnp.bfloat16) for rows in out_rows],
+        compiler_params=pltpu.CompilerParams(vmem_limit_bytes=BUDGET),
+        name="project",
+    )(state, *weights)
+
+
+def run_finish(mixes, state, gain, gate_matrix, out_gain, final_matrix, onward=None):
+    positions, features = state.shape
+    step = row_step(positions)
+    weights = (gain[None, :], gate_matrix, out_gain[:, None], final_matrix)
+    out_shape = [jax.ShapeDtypeStruct((positions, features), jnp.bfloat16)]
+    out_specs = [pl.BlockSpec((step, features), lambda i: (i, 0))]
+    if onward is not None:
+        next_gain, gate_rows, value_rows, out_rows = onward
+        weights += (next_gain[None, :], gate_rows, value_rows)
+        out_shape += [jax.ShapeDtypeStruct((rows, positions), jnp.bfloat16) for rows in out_rows]
+        out_specs += [pl.BlockSpec((rows, step), lambda i: (0, i)) for rows in out_rows]
+    return pl.pallas_call(
+        functools.partial(finish_kernel, len(mixes), onward is not None),
+        grid=(positions // step,),
+        in_specs=[pl.BlockSpec((m.shape[0], step), lambda i: (0, i)) for m in mixes]
+        + [pl.BlockSpec((step, features), lambda i: (i, 0))]
+        + [whole_spec(w) for w in weights],
+        out_specs=out_specs,
+        out_shape=out_shape,
+        compiler_params=pltpu.CompilerParams(vmem_limit_bytes=BUDGET),
+        name="finish",
+    )(*mixes, state, *weights)
+
+
+class Folds:
+    def __init__(self, row_count, col_count):
+        turn = 1
+        while (turn * col_count) % LANES:
+            turn *= 2
+        self.turn, self.tiles = turn, turn * col_count // LANES
+        self.cols, self.rows = col_count, row_count
+        self.groups = row_count // turn
+        self.lane_rows = row_count * col_count // LANES
+
+    def fits(self):
+        return self.cols <= LANES and self.rows % self.turn == 0 and self.groups % 8 == 0
+
+    def split(self, lane_rows):
+        lane = lax.broadcasted_iota(jnp.int32, lane_rows[0].shape, 1)
+        out = []
+        for phase in range(self.turn):
+            first, offset = divmod(phase * self.cols, LANES)
+            value = lane_rows[first]
+            if offset + self.cols > LANES:
+                value = jnp.where(lane >= offset, value, lane_rows[first + 1])
+            if offset:
+                value = pltpu.roll(value, LANES - offset, 1)
+            out.append(jnp.where(lane < self.cols, value, 0.0))
+        return out
+
+    def join(self, block_rows):
+        lane = lax.broadcasted_iota(jnp.int32, block_rows[0].shape, 1)
+        rolled = []
+        for phase, value in enumerate(block_rows):
+            offset = (phase * self.cols) % LANES
+            rolled.append(pltpu.roll(value, offset, 1) if offset else value)
+        out = []
+        for tile in range(self.tiles):
+            value = None
+            for phase in range(self.turn):
+                begin, end = phase * self.cols - tile * LANES, (phase + 1) * self.cols - tile * LANES
+                if end <= 0 or begin >= LANES:
+                    continue
+                value = rolled[phase] if value is None else jnp.where(lane >= begin, rolled[phase], value)
+            out.append(value)
+        return out
+
+
+def stage(source_ref, staged):
+    rows = source_ref.shape[0]
+    for tile in range(source_ref.shape[1] // LANES):
+        staged[tile * rows : (tile + 1) * rows, :] = source_ref[:, tile * LANES : (tile + 1) * LANES].astype(
+            jnp.float32
+        )
+
+
+def unstage(staged, target_ref):
+    rows = target_ref.shape[0]
+    for tile in range(target_ref.shape[1] // LANES):
+        target_ref[:, tile * LANES : (tile + 1) * LANES] = staged[tile * rows : (tile + 1) * rows, :].astype(
+            target_ref.dtype
+        )
+
+
+def lane_rows_of(folds, rows, row):
+    return [pl.ds(row + tile * rows, folds.groups, stride=folds.tiles * rows) for tile in range(folds.tiles)]
+
+
+def mix_out_kernel(folds, near, cols, width, half_ref, left_ref, here_ref, there_ref, mix_ref, staged, left, right):
+    parts = near * cols
+    rows = parts * width
+    block = folds.rows
+    far = cols // near
+
+    stage(left_ref, staged)
+
+    @pl.loop(0, rows)
+    def _(row):
+        pieces = folds.split([staged[at, :] for at in lane_rows_of(folds, rows, row)])
+        source, channel = row // width, row % width
+        at = (channel * cols + source % cols) * near * block + (source // cols) * block
+        left[pl.ds(pl.multiple_of(at, block), block), :] = jnp.concatenate(pieces, axis=0).astype(jnp.bfloat16)
+
+    for which, ref in ((0, here_ref), (1, there_ref)):
+        stage(ref, staged)
+        half = half_ref[which]
+
+        @pl.loop(0, rows)
+        def _(row):
+            pieces = folds.split([staged[at, :] for at in lane_rows_of(folds, rows, row)])
+            source, channel = row // width, row % width
+            at = ((channel * cols + source % cols) * far + half) * near * block + (source // cols) * block
+            for phase, piece in enumerate(pieces):
+                right[pl.ds(at + phase, folds.groups, stride=folds.turn), :] = piece
+
+    @pl.loop(0, width)
+    def _(channel):
+        for target in range(cols):
+            total = None
+            for col in range(cols):
+                lhs = left[pl.ds(pl.multiple_of((channel * cols + col) * near * block, block), near * block), :]
+                at = ((channel * cols + col) * far * near + target) * block
+                rhs = right[pl.ds(pl.multiple_of(at, block), block), :].astype(jnp.bfloat16)
+                part = lax.dot_general(lhs, rhs, (((1,), (1,)), ((), ())), preferred_element_type=jnp.float32)
+                total = part if total is None else total + part
+            total = jnp.concatenate([total, jnp.zeros((near * block, LANES - block), jnp.float32)], axis=1)
+            for piece in range(near):
+                groups = folds.groups
+                base = piece * block
+                lane_rows = folds.join(
+                    [total[base + phase * groups : base + (phase + 1) * groups, :] for phase in range(folds.turn)]
+                )
+                out_row = (piece * cols + target) * width + channel
+                for at, value in zip(lane_rows_of(folds, rows, out_row), lane_rows):
+                    staged[at, :] = value
+
+    unstage(staged, mix_ref)
+
+
+def mix_in_kernel(folds, near, cols, width, half_ref, both_ref, keep_ref, send_ref, staged, left, right, turned, mixed):
+    parts = near * cols
+    rows = 2 * parts * width
+    block = folds.rows
+
+    stage(both_ref, staged)
+
+    for target, shift in ((left, 0), (right, width)):
+
+        @pl.loop(0, parts * width)
+        def _(step):
+            source, channel = step // width, step % width
+            row = source * 2 * width + shift + channel
+            pieces = folds.split([staged[at, :] for at in lane_rows_of(folds, rows, row)])
+            at = (channel * cols + source % cols) * near * block + (source // cols) * block
+            target[pl.ds(pl.multiple_of(at, block), block), :] = jnp.concatenate(pieces, axis=0).astype(jnp.bfloat16)
+
+    out_rows = parts * width
+    tall = near * block
+
+    @pl.loop(0, width)
+    def _(channel):
+        for upper in range(cols):
+            lhs = left[pl.ds(pl.multiple_of((channel * cols + upper) * tall, block), tall), :]
+            for target in range(cols):
+                rhs = right[pl.ds(pl.multiple_of((channel * cols + target) * tall, block), tall), :]
+                turned[target] = lax.dot_general(lhs, rhs, (((0,), (0,)), ((), ())), preferred_element_type=jnp.float32)
+                lane_rows = folds.join(
+                    [turned[target, pl.ds(phase, folds.groups, stride=folds.turn), :] for phase in range(folds.turn)]
+                )
+                half, piece = divmod(upper, near)
+                out_row = (piece * cols + target) * width + channel
+                for at, value in zip(lane_rows_of(folds, out_rows, out_row), lane_rows):
+                    mixed[half, at, :] = value
+
+    unstage(mixed.at[half_ref[0]], keep_ref)
+    unstage(mixed.at[half_ref[1]], send_ref)
+
+
+SMEM_SPEC = pl.BlockSpec(memory_space=pltpu.SMEM)
+VMEM_SPEC = pl.BlockSpec(memory_space=pltpu.VMEM)
+
+
+def run_mix_out(folds, near, cols, halves, left, here, there):
+    rows, positions = left.shape
+    width = rows // (near * cols)
+    block = folds.rows
+    return pl.pallas_call(
+        functools.partial(mix_out_kernel, folds, near, cols, width),
+        in_specs=[SMEM_SPEC, VMEM_SPEC, VMEM_SPEC, VMEM_SPEC],
+        out_specs=VMEM_SPEC,
+        out_shape=jax.ShapeDtypeStruct((rows, positions), jnp.bfloat16),
+        scratch_shapes=[
+            pltpu.VMEM((rows * folds.lane_rows, LANES), jnp.float32),
+            pltpu.VMEM((width * cols * near * block, LANES), jnp.bfloat16),
+            pltpu.VMEM((width * cols * cols * block, LANES), jnp.float32),
+        ],
+        compiler_params=pltpu.CompilerParams(vmem_limit_bytes=BUDGET),
+        name="mix_out",
+    )(halves, left, here, there)
+
+
+def run_mix_in(folds, near, cols, halves, both):
+    rows, positions = both.shape
+    width = rows // (2 * near * cols)
+    block = folds.rows
+    return pl.pallas_call(
+        functools.partial(mix_in_kernel, folds, near, cols, width),
+        in_specs=[SMEM_SPEC, VMEM_SPEC],
+        out_specs=[VMEM_SPEC, VMEM_SPEC],
+        out_shape=[
+            jax.ShapeDtypeStruct((rows // 2, positions), jnp.float32),
+            jax.ShapeDtypeStruct((rows // 2, positions), jnp.bfloat16),
+        ],
+        scratch_shapes=[
+            pltpu.VMEM((rows * folds.lane_rows, LANES), jnp.float32),
+            pltpu.VMEM((width * cols * near * block, LANES), jnp.bfloat16),
+            pltpu.VMEM((width * cols * near * block, LANES), jnp.bfloat16),
+            pltpu.VMEM((cols, LANES, LANES), jnp.float32),
+            pltpu.VMEM((2, rows // 2 * folds.lane_rows, LANES), jnp.float32),
+        ],
+        compiler_params=pltpu.CompilerParams(vmem_limit_bytes=BUDGET),
+        name="mix_in",
+    )(halves, both)
+
+
+PIECES = 2
+
+
+def exchange(array):
+    return lax.all_to_all(array, EVERY, split_axis=0, concat_axis=0, tiled=True)
+
+
+def across(array):
+    return lax.ppermute(array, "far", ((0, 1), (1, 0)))
+
+
+def in_halves(sizes, pair_input, weights):
+    far, near, cols = sizes
+    row_count, col_count, features = pair_input.shape
+    parts = near * cols
+    width = features // parts
+    pieces = PIECES
+    folds = Folds(row_count, col_count)
+    half = lax.axis_index("far")
+    halves = jnp.stack([half, 1 - half]).astype(jnp.int32)
+
+    def by_piece(rows):
+        return rows.reshape(parts, pieces, width // pieces, -1).transpose(1, 0, 2, 3)
+
+    def rows_of(project, order):
+        ga, va, gb, vb = (by_piece(rows) for rows in jnp.split(project.T, 4, axis=0))
+        return order(ga, gb).reshape(-1, features), order(va, vb).reshape(-1, features)
+
+    def right_then_left(left, right):
+        return jnp.concatenate([right, left], axis=0)
+
+    def side_by_side(left, right):
+        return jnp.concatenate([left, right], axis=2)
+
+    def unordered(array):
+        return by_piece(array.reshape(features, -1)).reshape(array.shape)
+
+    gain_1, project_1, gate_1, norm_1, final_1, gain_2, project_2, gate_2, norm_2, final_2 = weights
+    state = pair_input.reshape(-1, features)
+    piece_rows = features // pieces
+
+    out = run_projections(state, gain_1, *rows_of(project_1, right_then_left), (piece_rows,) * (2 * pieces))
+    here = [exchange(x) for x in out[:pieces]]
+    there = [across(x) for x in here]
+    left = [exchange(x) for x in out[pieces:]]
+    mixes = [exchange(run_mix_out(folds, near, cols, halves, *x)) for x in zip(left, here, there)]
+    onward = (gain_2, *rows_of(project_2, side_by_side), (2 * piece_rows,) * pieces)
+    out = run_finish(mixes, state, gain_1, gate_1, unordered(norm_1), unordered(final_1), onward)
+    middle, both = out[0], [exchange(x) for x in out[1:]]
+    parted = [run_mix_in(folds, near, cols, halves, x) for x in both]
+    arrived = [across(sent) for _, sent in parted]
+    mixes = [
+        exchange((kept + got.astype(jnp.float32)).astype(jnp.bfloat16)) for (kept, _), got in zip(parted, arrived)
+    ]
+    result = run_finish(mixes, middle, gain_2, gate_2, unordered(norm_2), unordered(final_2))[0]
+    return result.reshape(pair_input.shape)
+
+
 def solution(mesh):
     row_parts, col_parts = mesh.shape["dap"], mesh.shape["chan"] * mesh.shape["sub"]
 
     def whole(pair_input, *weights):
-        far, near = split_rows(row_parts, col_parts, pair_input.shape[-1], 8)
+        features = pair_input.shape[-1]
+        block_rows = pair_input.shape[0] // (mesh.shape["groups"] * row_parts)
+        block_cols = pair_input.shape[1] // col_parts
+        halved = (
+            row_parts % 2 == 0
+            and row_parts == col_parts
+            and block_rows == block_cols
+            and Folds(block_rows, block_cols).fits()
+            and features == LANES
+            and features % (row_parts // 2 * col_parts * 8 * PIECES) == 0
+        )
+        if halved:
+            far, near = 2, row_parts // 2
+        else:
+            far, near = split_rows(row_parts, col_parts, features, 8)
         sizes = (far, near, col_parts)
         finer = Mesh(
             mesh.devices.reshape(mesh.shape["groups"], far, near, mesh.shape["chan"], mesh.shape["sub"]),
@@ -79,6 +453,8 @@
         )
 
         def shards(pair_input, *weights):
+            if halved:
+                return in_halves(sizes, pair_input, weights)
             middle = update(False, sizes, pair_input, *weights[:5])
             return update(True, sizes, middle, *weights[5:])
 

time: 497 us -> 501 us (level)
  the two profiles are of different devices: /device:TPU:11 before, /device:TPU:0 now
where the time goes in v2:
time: 501 us; the launch traced here: 500 us
  waiting for transfers between devices  208 us (42%)
  Pallas kernels  146 us (29%)
  blocking collectives  94 us (19%)
  starting transfers between devices  33 us (7%)
  local copies, waits for them, and re-layouts  14 us (3%)
    ppermute x4, waiting for transfers between devices, across(): return lax.ppermute(array, 'far', ((0, 1), (1, 0)))  171 us
    all_to_all x4, blocking collectives, exchange(): return lax.all_to_all(array, EVERY, split_axis=0, concat_axis=0, tiled=True)  94 us
    pallas_call x2, Pallas kernels, run_mix_out(): pl.pallas_call(functools.partial(mix_out_kernel, folds, near, cols, width...  60.1 us
    pallas_call x2, Pallas kernels, run_mix_in(): pl.pallas_call(functools.partial(mix_in_kernel, folds, near, cols, width)...  51.2 us
    all_to_all x6, waiting for transfers between devices, exchange(): return lax.all_to_all(array, EVERY, split_axis=0, concat_axis=0, tiled=True)  37.3 us
    pallas_call x2, Pallas kernels, run_finish(): pl.pallas_call(functools.partial(finish_kernel, len(mixes), onward is not...  23.6 us
    all_to_all x6, starting transfers between devices, exchange(): return lax.all_to_all(array, EVERY, split_axis=0, concat_axis=0, tiled=True)  21.6 us
    ppermute x4, starting transfers between devices, across(): return lax.ppermute(array, 'far', ((0, 1), (1, 0)))  11.5 us
  transfers between devices with their start and end apart: 10, of which 7 were waited for; matrix products, arithmetic and copies ran while one was open for 2% of the time, Pallas kernels for 22%

profile of v2, /device:TPU:0, one launch (start us, length us, event | category | flops | bytes accessed | tf_op | source)
XLA Modules:
  0.0 500.1 jit_solution(6059163577474827554)
XLA Ops:
  2.3 11.1 %project.1 = (bf16[64,9216]{1,0:T(8,128)(2,1)}, bf16[64,9216]{1,0:T(8,128)(2,1)}, bf16[64,9216]{1,0:T(8,128)(2,1)}, bf16[64,9216]{1,0:T(8,128)(2,1)}) custom-call(bf16[9216,128]{1,0:T(8,128)(2,1)} %bitcast.78, f32[1,128]{1,0:T(1,128)} %bitcast.120, bf16[256,128]{1,0:T(8,128)(2,1)} %bitcast.103, bf16[256,128]{1,0:T(8,128)(2,1)} %bitcast.102), custom_call_target="tpu_custom_call" | custom-call | tf_op jit(solution)/shard_map/project/pallas_call | solution.py:136
  13.5 21.9 %all_to_all.110 = bf16[8,8,9216]{2,1,0:T(8,128)(2,1)S(1)} all-to-all(bf16[8,8,9216]{2,1,0:T(8,128)(2,1)} %bitcast.97), channel_id=1, replica_groups=mesh['groups'=2,'far'=2,'near'=2,'chan'=2,'sub'=2] {'near','chan','sub'}, dimensions={0} | all-to-all | bytes 2359296 | tf_op jit(solution)/shard_map/all_to_all | solution.py:376
  35.4 19.9 %all_to_all.111 = bf16[8,8,9216]{2,1,0:T(8,128)(2,1)} all-to-all(bf16[8,8,9216]{2,1,0:T(8,128)(2,1)S(1)} %bitcast.96), channel_id=1, replica_groups=mesh['groups'=2,'far'=2,'near'=2,'chan'=2,'sub'=2] {'near','chan','sub'}, dimensions={0} | all-to-all | bytes 2359296 | tf_op jit(solution)/shard_map/all_to_all | solution.py:376
  55.3 18.9 %all_to_all.112 = bf16[8,8,9216]{2,1,0:T(8,128)(2,1)S(1)} all-to-all(bf16[8,8,9216]{2,1,0:T(8,128)(2,1)S(1)} %bitcast.95), channel_id=1, replica_groups=mesh['groups'=2,'far'=2,'near'=2,'chan'=2,'sub'=2] {'near','chan','sub'}, dimensions={0} | all-to-all | bytes 2359296 | tf_op jit(solution)/shard_map/all_to_all | solution.py:376
  74.3 3.6 all-to-all-start
  77.9 2.7 collective-permute-start.1
  81.1 51.3 %collective-permute-done.1.there_ref = bf16[64,9216]{1,0:T(8,128)(2,1)} collective-permute-done((bf16[64,9216]{1,0:T(8,128)(2,1)S(1)}, bf16[64,9216]{1,0:T(8,128)(2,1)}, u32[]{:S(2)}, u32[]{:S(2)}) %collective-permute-start.1) | collective-permute-done | bytes 1179680 | tf_op jit(solution)/shard_map/ppermute | solution.py:380
  132.5 30.0 %mix_out.3 = bf16[64,9216]{1,0:T(8,128)(2,1)} custom-call(s32[2]{0:T(128)} %pad_add_fusion.half_ref, bf16[64,9216]{1,0:T(8,128)(2,1)} %bitcast.87, bf16[64,9216]{1,0:T(8,128)(2,1)} %bitcast.86, bf16[64,9216]{1,0:T(8,128)(2,1)} %collective-permute-done.1.there_ref), custom_call_target="tpu_custom_call" | custom-call | tf_op jit(solution)/shard_map/mix_out/pallas_call | solution.py:333
  163.5 3.6 all-to-all-start.5
  167.1 2.9 collective-permute-start
  170.0 51.9 %collective-permute-done.there_ref = bf16[64,9216]{1,0:T(8,128)(2,1)S(1)} collective-permute-done((bf16[64,9216]{1,0:T(8,128)(2,1)S(1)}, bf16[64,9216]{1,0:T(8,128)(2,1)S(1)}, u32[]{:S(2)}, u32[]{:S(2)}) %collective-permute-start) | collective-permute-done | bytes 1179680 | tf_op jit(solution)/shard_map/ppermute | solution.py:380
  223.0 30.1 %mix_out.2 = bf16[64,9216]{1,0:T(8,128)(2,1)} custom-call(s32[2]{0:T(128)} %pad_add_fusion.half_ref, bf16[64,9216]{1,0:T(8,128)(2,1)} %bitcast.82, bf16[64,9216]{1,0:T(8,128)(2,1)} %bitcast.81, bf16[64,9216]{1,0:T(8,128)(2,1)} %copy-done.10), custom_call_target="tpu_custom_call" | custom-call | tf_op jit(solution)/shard_map/mix_out/pallas_call | solution.py:333
  253.1 1.0 copy-done.6
  254.1 3.6 all-to-all-start.2
  260.5 13.0 %all-to-all-done.2 = bf16[8,8,9216]{2,1,0:T(8,128)(2,1)S(1)} async-done(((bf16[8,8,9216]{2,1,0:T(8,128)(2,1)}), bf16[8,8,9216]{2,1,0:T(8,128)(2,1)S(1)}, u32[]{:S(2)}, u32[]{:S(2)}) %all-to-all-start.2) | async-done | bytes 1179680 | tf_op jit(solution)/shard_map/all_to_all | solution.py:376
  274.5 14.1 %finish.2 = (bf16[9216,128]{1,0:T(8,128)(2,1)}, bf16[128,9216]{1,0:T(8,128)(2,1)}, bf16[128,9216]{1,0:T(8,128)(2,1)}) custom-call(bf16[64,9216]{1,0:T(8,128)(2,1)} %bitcast.91, bf16[64,9216]{1,0:T(8,128)(2,1)} %bitcast.90, bf16[9216,128]{1,0:T(8,128)(2,1)} %bitcast.79, f32[1,128]{1,0:T(1,128)} %bitcast.121, bf16[128,128]{1,0:T(8,128)(2,1)} %refs_4_.2, ...), custom_call_target="tpu_custom_call" | custom-call | tf_op jit(solution)/shard_map/finish/pallas_call | solution.py:158
  288.6 33.2 %all_to_all.113 = bf16[8,16,9216]{2,1,0:T(8,128)(2,1)} all-to-all(bf16[8,16,9216]{2,1,0:T(8,128)(2,1)} %bitcast.93), channel_id=1, replica_groups=mesh['groups'=2,'far'=2,'near'=2,'chan'=2,'sub'=2] {'near','chan','sub'}, dimensions={0} | all-to-all | bytes 4718592 | tf_op jit(solution)/shard_map/all_to_all | solution.py:376
  321.8 3.6 all-to-all-start.6
  325.4 25.5 %mix_in.3 = (f32[64,9216]{1,0:T(8,128)}, bf16[64,9216]{1,0:T(8,128)(2,1)}) custom-call(s32[2]{0:T(128)} %pad_add_fusion.half_ref, bf16[128,9216]{1,0:T(8,128)(2,1)} %bitcast.77), custom_call_target="tpu_custom_call" | custom-call | tf_op jit(solution)/shard_map/mix_in/pallas_call | solution.py:352
  350.9 3.0 collective-permute-start.3
  353.9 1.4 copy-done
  355.3 25.7 %mix_in.2 = (f32[64,9216]{1,0:T(8,128)}, bf16[64,9216]{1,0:T(8,128)(2,1)}) custom-call(s32[2]{0:T(128)} %pad_add_fusion.half_ref, bf16[128,9216]{1,0:T(8,128)(2,1)} %bitcast.76), custom_call_target="tpu_custom_call" | custom-call | tf_op jit(solution)/shard_map/mix_in/pallas_call | solution.py:352
  381.0 2.9 collective-permute-start.2
  383.9 47.6 %collective-permute-done.3 = bf16[64,9216]{1,0:T(8,128)(2,1)S(1)} collective-permute-done((bf16[64,9216]{1,0:T(8,128)(2,1)}, bf16[64,9216]{1,0:T(8,128)(2,1)S(1)}, u32[]{:S(2)}, u32[]{:S(2)}) %collective-permute-start.3) | collective-permute-done | bytes 1179680 | tf_op jit(solution)/shard_map/ppermute | solution.py:380
  431.5 1.3 fusion.1
  432.7 3.7 all-to-all-start.9
  436.4 20.2 %collective-permute-done.2 = bf16[64,9216]{1,0:T(8,128)(2,1)} collective-permute-done((bf16[64,9216]{1,0:T(8,128)(2,1)}, bf16[64,9216]{1,0:T(8,128)(2,1)}, u32[]{:S(2)}, u32[]{:S(2)}) %collective-permute-start.2) | collective-permute-done | bytes 1179680 | tf_op jit(solution)/shard_map/ppermute | solution.py:380
  456.7 2.5 fusion
  459.1 9.9 %all-to-all-done.9 = bf16[8,8,9216]{2,1,0:T(8,128)(2,1)S(1)} async-done(((bf16[8,8,9216]{2,1,0:T(8,128)(2,1)}), bf16[8,8,9216]{2,1,0:T(8,128)(2,1)S(1)}, u32[]{:S(2)}, u32[]{:S(2)}) %all-to-all-start.9) | async-done | bytes 1179680 | tf_op jit(solution)/shard_map/all_to_all | solution.py:376
  470.1 3.6 all-to-all-start.7
  475.1 14.4 %all-to-all-done.7 = bf16[8,8,9216]{2,1,0:T(8,128)(2,1)S(1)} async-done(((bf16[8,8,9216]{2,1,0:T(8,128)(2,1)}), bf16[8,8,9216]{2,1,0:T(8,128)(2,1)S(1)}, u32[]{:S(2)}, u32[]{:S(2)}) %all-to-all-start.7) | async-done | bytes 1179680 | tf_op jit(solution)/shard_map/all_to_all | solution.py:376
  490.5 9.6 %finish.3 = bf16[9216,128]{1,0:T(8,128)(2,1)} custom-call(bf16[64,9216]{1,0:T(8,128)(2,1)} %bitcast.89, bf16[64,9216]{1,0:T(8,128)(2,1)} %bitcast.84, bf16[9216,128]{1,0:T(8,128)(2,1)} %get-tuple-element.26.refs_2_, f32[1,128]{1,0:T(1,128)} %bitcast.119, bf16[128,128]{1,0:T(8,128)(2,1)} %refs_4_.3, f32[128,1]{1,0:T(8,128)} %broadcast_in_dim_reshape.9.refs_5_, ...), custom_call_target="tpu_custom_call" | custom-call | tf_op jit(solution)/shard_map/finish/pallas_call | solution.py:158
  (58 shorter events, 12.3 us)
Async XLA Ops:
  13.5 21.9 %copy-start.12 = (bf16[64,9216]{1,0:T(8,128)(2,1)S(1)}, bf16[64,9216]{1,0:T(8,128)(2,1)}, u32[]{:S(2)}) copy-start(bf16[64,9216]{1,0:T(8,128)(2,1)} %get-tuple-element.18) | copy-start | bytes 3538948
  35.4 42.5 %copy-start.4 = (bf16[8,8,9216]{2,1,0:T(8,128)(2,1)}, bf16[8,8,9216]{2,1,0:T(8,128)(2,1)S(1)}, u32[]{:S(2)}) copy-start(bf16[8,8,9216]{2,1,0:T(8,128)(2,1)S(1)} %all_to_all.110) | copy-start | bytes 3538948
  35.4 19.9 %copy-start.11 = (bf16[64,9216]{1,0:T(8,128)(2,1)S(1)}, bf16[64,9216]{1,0:T(8,128)(2,1)}, u32[]{:S(2)}) copy-start(bf16[64,9216]{1,0:T(8,128)(2,1)} %get-tuple-element.17) | copy-start | bytes 3538948
  74.3 92.8 %copy-start.1 = (bf16[8,8,9216]{2,1,0:T(8,128)(2,1)}, bf16[8,8,9216]{2,1,0:T(8,128)(2,1)S(1)}, u32[]{:S(2)}) copy-start(bf16[8,8,9216]{2,1,0:T(8,128)(2,1)S(1)} %all_to_all.112) | copy-start | bytes 3538948
  74.3 88.2 %all-to-all-start = ((bf16[8,8,9216]{2,1,0:T(8,128)(2,1)}), bf16[8,8,9216]{2,1,0:T(8,128)(2,1)S(1)}, u32[]{:S(2)}, u32[]{:S(2)}) async-start(bf16[8,8,9216]{2,1,0:T(8,128)(2,1)} %bitcast.94), calls=%async_computation | async-start | bytes 2359296 | tf_op jit(solution)/shard_map/all_to_all | solution.py:376
  77.9 54.6 %collective-permute-start.1 = (bf16[64,9216]{1,0:T(8,128)(2,1)S(1)}, bf16[64,9216]{1,0:T(8,128)(2,1)}, u32[]{:S(2)}, u32[]{:S(2)}) collective-permute-start(bf16[64,9216]{1,0:T(8,128)(2,1)S(1)} %bitcast.85), channel_id=1, source_target_pairs={{0,8},{8,0},{1,9},{9,1},{2,10},{10,2},{3,11},{11,3},{4,12},{12,4},... | collective-permute-start | bytes 3538952 | tf_op jit(solution)/shard_map/ppermute | solution.py:380
  162.5 1.0 copy-start.2
  163.5 89.5 %all-to-all-start.5 = ((bf16[8,8,9216]{2,1,0:T(8,128)(2,1)}), bf16[8,8,9216]{2,1,0:T(8,128)(2,1)S(1)}, u32[]{:S(2)}, u32[]{:S(2)}) async-start(bf16[8,8,9216]{2,1,0:T(8,128)(2,1)} %bitcast.88), calls=%async_computation.5 | async-start | bytes 2359296 | tf_op jit(solution)/shard_map/all_to_all | solution.py:376
  167.1 54.8 %collective-permute-start = (bf16[64,9216]{1,0:T(8,128)(2,1)S(1)}, bf16[64,9216]{1,0:T(8,128)(2,1)S(1)}, u32[]{:S(2)}, u32[]{:S(2)}) collective-permute-start(bf16[64,9216]{1,0:T(8,128)(2,1)S(1)} %bitcast.80), channel_id=1, source_target_pairs={{0,8},{8,0},{1,9},{9,1},{2,10},{10,2},{3,11},{11,3},{4,12},{12,4},... | collective-permute-start | bytes 3538952 | tf_op jit(solution)/shard_map/ppermute | solution.py:380
  221.9 1.0 copy-start.10
  253.0 1.1 copy-start.6
  253.0 4.6 copy-start.13
  253.1 6.1 %copy-start.16 = (f32[128]{0:T(128)S(1)}, f32[128]{0:T(128)}, u32[]{:S(2)}) copy-start(f32[128]{0:T(128)} %param.15) | copy-start | bytes 1540
  253.1 6.9 %copy-start.14 = (bf16[128,128]{1,0:T(8,128)(2,1)S(1)}, bf16[128,128]{1,0:T(8,128)(2,1)}, u32[]{:S(2)}) copy-start(bf16[128,128]{1,0:T(8,128)(2,1)} %param.16) | copy-start | bytes 98308
  254.1 19.4 %all-to-all-start.2 = ((bf16[8,8,9216]{2,1,0:T(8,128)(2,1)}), bf16[8,8,9216]{2,1,0:T(8,128)(2,1)S(1)}, u32[]{:S(2)}, u32[]{:S(2)}) async-start(bf16[8,8,9216]{2,1,0:T(8,128)(2,1)} %bitcast.83), calls=%async_computation.2 | async-start | bytes 2359296 | tf_op jit(solution)/shard_map/all_to_all | solution.py:376
  273.5 1.0 copy-start.7
  321.8 32.1 %all-to-all-start.6 = ((bf16[8,16,9216]{2,1,0:T(8,128)(2,1)}), bf16[8,16,9216]{2,1,0:T(8,128)(2,1)S(1)}, u32[]{:S(2)}, u32[]{:S(2)}) async-start(bf16[8,16,9216]{2,1,0:T(8,128)(2,1)} %bitcast.92), calls=%async_computation.6 | async-start | bytes 4718592 | tf_op jit(solution)/shard_map/all_to_all | solution.py:376
  350.9 80.6 %collective-permute-start.3 = (bf16[64,9216]{1,0:T(8,128)(2,1)}, bf16[64,9216]{1,0:T(8,128)(2,1)S(1)}, u32[]{:S(2)}, u32[]{:S(2)}) collective-permute-start(bf16[64,9216]{1,0:T(8,128)(2,1)} %get-tuple-element.25), channel_id=1, source_target_pairs={{0,8},{8,0},{1,9},{9,1},{2,10},{10,2},{3,11},{11,3},{4,12},{12,4},... | collective-permute-start | bytes 3538952 | tf_op jit(solution)/shard_map/ppermute | solution.py:380
  353.9 1.4 copy-start
  355.3 76.2 %copy-start.8 = (f32[64,9216]{1,0:T(8,128)S(1)}, f32[64,9216]{1,0:T(8,128)}, u32[]{:S(2)}) copy-start(f32[64,9216]{1,0:T(8,128)} %get-tuple-element.24) | copy-start | bytes 7077892
  381.0 75.7 %collective-permute-start.2 = (bf16[64,9216]{1,0:T(8,128)(2,1)}, bf16[64,9216]{1,0:T(8,128)(2,1)}, u32[]{:S(2)}, u32[]{:S(2)}) collective-permute-start(bf16[64,9216]{1,0:T(8,128)(2,1)} %get-tuple-element.22), channel_id=1, source_target_pairs={{0,8},{8,0},{1,9},{9,1},{2,10},{10,2},{3,11},{11,3},{4,12},{12,4},... | collective-permute-start | bytes 3538952 | tf_op jit(solution)/shard_map/ppermute | solution.py:380
  432.7 23.9 %copy-start.9 = (f32[64,9216]{1,0:T(8,128)S(1)}, f32[64,9216]{1,0:T(8,128)}, u32[]{:S(2)}) copy-start(f32[64,9216]{1,0:T(8,128)} %get-tuple-element.21) | copy-start | bytes 7077892
  432.7 36.4 %all-to-all-start.9 = ((bf16[8,8,9216]{2,1,0:T(8,128)(2,1)}), bf16[8,8,9216]{2,1,0:T(8,128)(2,1)S(1)}, u32[]{:S(2)}, u32[]{:S(2)}) async-start(bf16[8,8,9216]{2,1,0:T(8,128)(2,1)} %fusion.1), calls=%async_computation.9 | async-start | bytes 2359296 | tf_op jit(solution)/shard_map/all_to_all | solution.py:376
  459.1 14.5 %copy-start.17 = (f32[128]{0:T(128)S(1)}, f32[128]{0:T(128)}, u32[]{:S(2)}) copy-start(f32[128]{0:T(128)} %param.20) | copy-start | bytes 1540
  459.1 15.4 %copy-start.15 = (bf16[128,128]{1,0:T(8,128)(2,1)S(1)}, bf16[128,128]{1,0:T(8,128)(2,1)}, u32[]{:S(2)}) copy-start(bf16[128,128]{1,0:T(8,128)(2,1)} %param.21) | copy-start | bytes 98308
  469.1 1.0 copy-start.3
  470.1 19.4 %all-to-all-start.7 = ((bf16[8,8,9216]{2,1,0:T(8,128)(2,1)}), bf16[8,8,9216]{2,1,0:T(8,128)(2,1)S(1)}, u32[]{:S(2)}, u32[]{:S(2)}) async-start(bf16[8,8,9216]{2,1,0:T(8,128)(2,1)} %fusion), calls=%async_computation.7 | async-start | bytes 2359296 | tf_op jit(solution)/shard_map/all_to_all | solution.py:376
  489.5 1.0 copy-start.5

commit v3 on v2

--- a/solution.py
+++ b/solution.py
@@ -7,6 +7,7 @@
 from jax.experimental.pallas import tpu as pltpu
 from jax.sharding import Mesh
 from jax.sharding import PartitionSpec as P
+
 
 epsilon = 1e-05
 EVERY = ("near", "chan", "sub")
@@ -240,7 +241,7 @@
 
     stage(left_ref, staged)
 
-    @pl.loop(0, rows)
+    @pl.loop(0, rows, unroll=8)
     def _(row):
         pieces = folds.split([staged[at, :] for at in lane_rows_of(folds, rows, row)])
         source, channel = row // width, row % width
@@ -251,7 +252,7 @@
         stage(ref, staged)
         half = half_ref[which]
 
-        @pl.loop(0, rows)
+        @pl.loop(0, rows, unroll=8)
         def _(row):
             pieces = folds.split([staged[at, :] for at in lane_rows_of(folds, rows, row)])
             source, channel = row // width, row % width
@@ -259,7 +260,7 @@
             for phase, piece in enumerate(pieces):
                 right[pl.ds(at + phase, folds.groups, stride=folds.turn), :] = piece
 
-    @pl.loop(0, width)
+    @pl.loop(0, width, unroll=2)
     def _(channel):
         for target in range(cols):
             total = None
@@ -292,7 +293,7 @@
 
     for target, shift in ((left, 0), (right, width)):
 
-        @pl.loop(0, parts * width)
+        @pl.loop(0, parts * width, unroll=8)
         def _(step):
             source, channel = step // width, step % width
             row = source * 2 * width + shift + channel
@@ -303,7 +304,7 @@
     out_rows = parts * width
     tall = near * block
 
-    @pl.loop(0, width)
+    @pl.loop(0, width, unroll=2)
     def _(channel):
         for upper in range(cols):
             lhs = left[pl.ds(pl.multiple_of((channel * cols + upper) * tall, block), tall), :]
@@ -381,7 +382,7 @@
 
 
 def in_halves(sizes, pair_input, weights):
-    far, near, cols = sizes
+    _, near, cols = sizes
     row_count, col_count, features = pair_input.shape
     parts = near * cols
     width = features // parts
@@ -410,19 +411,29 @@
     state = pair_input.reshape(-1, features)
     piece_rows = features // pieces
 
-    out = run_projections(state, gain_1, *rows_of(project_1, right_then_left), (piece_rows,) * (2 * pieces))
-    here = [exchange(x) for x in out[:pieces]]
-    there = [across(x) for x in here]
-    left = [exchange(x) for x in out[pieces:]]
-    mixes = [exchange(run_mix_out(folds, near, cols, halves, *x)) for x in zip(left, here, there)]
+    gates, values = rows_of(project_1, right_then_left)
+    here, there, left, mixes = [], [], [], []
+    right_out = run_projections(state, gain_1, gates[:features], values[:features], (piece_rows,) * pieces)
+    for piece in range(pieces):
+        here.append(exchange(right_out[piece]))
+        there.append(across(here[piece]))
+    left_out = run_projections(state, gain_1, gates[features:], values[features:], (piece_rows,) * pieces)
+    for piece in range(pieces):
+        left.append(exchange(left_out[piece]))
+    for piece in range(pieces):
+        mixed = run_mix_out(folds, near, cols, halves, left[piece], here[piece], there[piece])
+        mixes.append(exchange(mixed))
     onward = (gain_2, *rows_of(project_2, side_by_side), (2 * piece_rows,) * pieces)
     out = run_finish(mixes, state, gain_1, gate_1, unordered(norm_1), unordered(final_1), onward)
-    middle, both = out[0], [exchange(x) for x in out[1:]]
-    parted = [run_mix_in(folds, near, cols, halves, x) for x in both]
-    arrived = [across(sent) for _, sent in parted]
-    mixes = [
-        exchange((kept + got.astype(jnp.float32)).astype(jnp.bfloat16)) for (kept, _), got in zip(parted, arrived)
-    ]
+    middle, both, parted, mixes = out[0], [], [], []
+    for piece in range(pieces):
+        both.append(exchange(out[1 + piece]))
+    for piece in range(pieces):
+        kept, sent = run_mix_in(folds, near, cols, halves, both[piece])
+        parted.append((kept, across(sent)))
+    for kept, got in parted:
+        mixed = (kept + got.astype(jnp.float32)).astype(jnp.bfloat16)
+        mixes.append(exchange(mixed))
     result = run_finish(mixes, middle, gain_2, gate_2, unordered(norm_2), unordered(final_2))[0]
     return result.reshape(pair_input.shape)
 
@@ -459,12 +470,13 @@
             return update(True, sizes, middle, *weights[5:])
 
         pair_spec = P(("groups", "far", "near"), ("chan", "sub"), None)
-        return jax.shard_map(
+        mapped = jax.shard_map(
             shards,
             mesh=finer,
             in_specs=(pair_spec,) + (P(),) * 10,
             out_specs=pair_spec,
             check_vma=False,
-        )(pair_input, *weights)
+        )
+        return mapped(pair_input, *weights)
 
     return whole

time: 501 us -> 458 us (0.914)
  Pallas kernels: 146 us -> 102 us
  blocking collectives: 94 us -> 73.2 us
  waiting for transfers between devices: 208 us -> 226 us
    pallas_call x2, Pallas kernels: 60.1 us -> 28.3 us  [run_mix_out(): pl.pallas_call(functools.partial(mix_out_kernel, folds, near, cols, width...]
    all_to_all x6 -> x7, waiting for transfers between devices: 37.3 us -> 62.4 us  [exchange(): return lax.all_to_all(array, EVERY, split_axis=0, concat_axis=0, tiled=True)]
    all_to_all x4 -> x3, blocking collectives: 94 us -> 73.2 us  [exchange(): return lax.all_to_all(array, EVERY, split_axis=0, concat_axis=0, tiled=True)]
    pallas_call x2, Pallas kernels: 51.2 us -> 32.6 us  [run_mix_in(): pl.pallas_call(functools.partial(mix_in_kernel, folds, near, cols, width)...]
    ppermute x4, waiting for transfers between devices: 171 us -> 164 us  [across(): return lax.ppermute(array, 'far', ((0, 1), (1, 0)))]
    pallas_call x1 -> x2, Pallas kernels: 11.1 us -> 17.7 us  [run_projections(): pl.pallas_call(project_kernel, grid=(positions // step,), in_specs=[pl.Bl...]
    all_to_all x6 -> x7, starting transfers between devices: 21.6 us -> 27 us  [exchange(): return lax.all_to_all(array, EVERY, split_axis=0, concat_axis=0, tiled=True)]
  transfers between devices with their start and end apart: 10 -> 11, of which waited for: 7 -> 9; matrix products, arithmetic and copies ran while one was open for 2% -> 2% of each run, Pallas kernels for 22% -> 15%
where the time goes in v3:
time: 458 us; the launch traced here: 457 us
  waiting for transfers between devices  226 us (49%)
  Pallas kernels  102 us (22%)
  blocking collectives  73.2 us (16%)
  starting transfers between devices  35.6 us (8%)
  local copies, waits for them, and re-layouts  15.2 us (3%)
    ppermute x4, waiting for transfers between devices, across(): return lax.ppermute(array, 'far', ((0, 1), (1, 0)))  164 us
    all_to_all x3, blocking collectives, exchange(): return lax.all_to_all(array, EVERY, split_axis=0, concat_axis=0, tiled=True)  73.2 us
    all_to_all x7, waiting for transfers between devices, exchange(): return lax.all_to_all(array, EVERY, split_axis=0, concat_axis=0, tiled=True)  62.4 us
    pallas_call x2, Pallas kernels, run_mix_in(): pl.pallas_call(functools.partial(mix_in_kernel, folds, near, cols, width)...  32.6 us
    pallas_call x2, Pallas kernels, run_mix_out(): pl.pallas_call(functools.partial(mix_out_kernel, folds, near, cols, width...  28.3 us
    all_to_all x7, starting transfers between devices, exchange(): return lax.all_to_all(array, EVERY, split_axis=0, concat_axis=0, tiled=True)  27 us
    pallas_call x2, Pallas kernels, run_finish(): pl.pallas_call(functools.partial(finish_kernel, len(mixes), onward is not...  23.6 us
    pallas_call x2, Pallas kernels, run_projections(): pl.pallas_call(project_kernel, grid=(positions // step,), in_specs=[pl.Bl...  17.7 us
  transfers between devices with their start and end apart: 11, of which 9 were waited for; matrix products, arithmetic and copies ran while one was open for 2% of the time, Pallas kernels for 15%

profile of v3, /device:TPU:0, one launch (start us, length us, event | category | flops | bytes accessed | tf_op | source)
XLA Modules:
  0.0 457.0 jit_solution(15201687745610548726)
XLA Ops:
  2.3 8.9 %project.3 = (bf16[64,9216]{1,0:T(8,128)(2,1)}, bf16[64,9216]{1,0:T(8,128)(2,1)}) custom-call(bf16[9216,128]{1,0:T(8,128)(2,1)} %bitcast.78, f32[1,128]{1,0:T(1,128)} %bitcast.123, bf16[128,128]{1,0:T(8,128)(2,1)} %bitcast.108, bf16[128,128]{1,0:T(8,128)(2,1)} %bitcast.109), custom_call_target="tpu_custom_call" | custom-call | tf_op jit(solution)/shard_map/project/pallas_call | solution.py:137
  11.1 5.3 %all-to-all-start.4 = ((bf16[8,8,9216]{2,1,0:T(8,128)(2,1)}), bf16[8,8,9216]{2,1,0:T(8,128)(2,1)S(1)}, u32[]{:S(2)}, u32[]{:S(2)}) async-start(bf16[8,8,9216]{2,1,0:T(8,128)(2,1)} %bitcast.99), calls=%async_computation.4 | async-start | bytes 2359296 | tf_op jit(solution)/shard_map/all_to_all | solution.py:377
  17.6 8.9 %project.2 = (bf16[64,9216]{1,0:T(8,128)(2,1)}, bf16[64,9216]{1,0:T(8,128)(2,1)}) custom-call(bf16[9216,128]{1,0:T(8,128)(2,1)} %bitcast.79, f32[1,128]{1,0:T(1,128)} %bitcast.124, bf16[128,128]{1,0:T(8,128)(2,1)} %bitcast.110, bf16[128,128]{1,0:T(8,128)(2,1)} %bitcast.107), custom_call_target="tpu_custom_call" | custom-call | tf_op jit(solution)/shard_map/project/pallas_call | solution.py:137
  26.5 5.8 %all-to-all-done.4 = bf16[8,8,9216]{2,1,0:T(8,128)(2,1)S(1)} async-done(((bf16[8,8,9216]{2,1,0:T(8,128)(2,1)}), bf16[8,8,9216]{2,1,0:T(8,128)(2,1)S(1)}, u32[]{:S(2)}, u32[]{:S(2)}) %all-to-all-start.4) | async-done | bytes 1179680 | tf_op jit(solution)/shard_map/all_to_all | solution.py:377
  32.3 21.1 %all_to_all.110 = bf16[8,8,9216]{2,1,0:T(8,128)(2,1)} all-to-all(bf16[8,8,9216]{2,1,0:T(8,128)(2,1)} %bitcast.100), channel_id=1, replica_groups=mesh['groups'=2,'far'=2,'near'=2,'chan'=2,'sub'=2] {'near','chan','sub'}, dimensions={0} | all-to-all | bytes 2359296 | tf_op jit(solution)/shard_map/all_to_all | solution.py:377
  53.3 18.9 %all_to_all.111 = bf16[8,8,9216]{2,1,0:T(8,128)(2,1)S(1)} all-to-all(bf16[8,8,9216]{2,1,0:T(8,128)(2,1)S(1)} %bitcast.98), channel_id=1, replica_groups=mesh['groups'=2,'far'=2,'near'=2,'chan'=2,'sub'=2] {'near','chan','sub'}, dimensions={0} | all-to-all | bytes 2359296 | tf_op jit(solution)/shard_map/all_to_all | solution.py:377
  72.3 3.6 all-to-all-start
  75.9 2.7 collective-permute-start.1
  79.1 51.4 %collective-permute-done.1.there_ref = bf16[64,9216]{1,0:T(8,128)(2,1)} collective-permute-done((bf16[64,9216]{1,0:T(8,128)(2,1)S(1)}, bf16[64,9216]{1,0:T(8,128)(2,1)}, u32[]{:S(2)}, u32[]{:S(2)}) %collective-permute-start.1) | collective-permute-done | bytes 1179680 | tf_op jit(solution)/shard_map/ppermute | solution.py:381
  130.5 14.2 %mix_out.3 = bf16[64,9216]{1,0:T(8,128)(2,1)} custom-call(s32[2]{0:T(128)} %pad_add_fusion.half_ref, bf16[64,9216]{1,0:T(8,128)(2,1)} %bitcast.90, bf16[64,9216]{1,0:T(8,128)(2,1)} %bitcast.84, bf16[64,9216]{1,0:T(8,128)(2,1)} %collective-permute-done.1.there_ref), custom_call_target="tpu_custom_call" | custom-call | tf_op jit(solution)/shard_map/mix_out/pallas_call | solution.py:334
  145.7 3.6 all-to-all-start.5
  149.2 2.9 collective-permute-start
  152.2 51.9 %collective-permute-done.there_ref = bf16[64,9216]{1,0:T(8,128)(2,1)S(1)} collective-permute-done((bf16[64,9216]{1,0:T(8,128)(2,1)S(1)}, bf16[64,9216]{1,0:T(8,128)(2,1)S(1)}, u32[]{:S(2)}, u32[]{:S(2)}) %collective-permute-start) | collective-permute-done | bytes 1179680 | tf_op jit(solution)/shard_map/ppermute | solution.py:381
  205.1 14.1 %mix_out.2 = bf16[64,9216]{1,0:T(8,128)(2,1)} custom-call(s32[2]{0:T(128)} %pad_add_fusion.half_ref, bf16[64,9216]{1,0:T(8,128)(2,1)} %bitcast.87, bf16[64,9216]{1,0:T(8,128)(2,1)} %bitcast.86, bf16[64,9216]{1,0:T(8,128)(2,1)} %copy-done.10), custom_call_target="tpu_custom_call" | custom-call | tf_op jit(solution)/shard_map/mix_out/pallas_call | solution.py:334
  220.2 3.6 all-to-all-start.2
  226.7 12.9 %all-to-all-done.2 = bf16[8,8,9216]{2,1,0:T(8,128)(2,1)S(1)} async-done(((bf16[8,8,9216]{2,1,0:T(8,128)(2,1)}), bf16[8,8,9216]{2,1,0:T(8,128)(2,1)S(1)}, u32[]{:S(2)}, u32[]{:S(2)}) %all-to-all-start.2) | async-done | bytes 1179680 | tf_op jit(solution)/shard_map/all_to_all | solution.py:377
  240.6 14.1 %finish.2 = (bf16[9216,128]{1,0:T(8,128)(2,1)}, bf16[128,9216]{1,0:T(8,128)(2,1)}, bf16[128,9216]{1,0:T(8,128)(2,1)}) custom-call(bf16[64,9216]{1,0:T(8,128)(2,1)} %bitcast.94, bf16[64,9216]{1,0:T(8,128)(2,1)} %bitcast.93, bf16[9216,128]{1,0:T(8,128)(2,1)} %bitcast.80, f32[1,128]{1,0:T(1,128)} %bitcast.125, bf16[128,128]{1,0:T(8,128)(2,1)} %refs_4_.2, ...), custom_call_target="tpu_custom_call" | custom-call | tf_op jit(solution)/shard_map/finish/pallas_call | solution.py:159
  254.7 33.2 %all_to_all.112 = bf16[8,16,9216]{2,1,0:T(8,128)(2,1)} all-to-all(bf16[8,16,9216]{2,1,0:T(8,128)(2,1)} %bitcast.96), channel_id=1, replica_groups=mesh['groups'=2,'far'=2,'near'=2,'chan'=2,'sub'=2] {'near','chan','sub'}, dimensions={0} | all-to-all | bytes 4718592 | tf_op jit(solution)/shard_map/all_to_all | solution.py:377
  287.9 3.8 all-to-all-start.6
  291.7 16.2 %mix_in.3 = (f32[64,9216]{1,0:T(8,128)}, bf16[64,9216]{1,0:T(8,128)(2,1)}) custom-call(s32[2]{0:T(128)} %pad_add_fusion.half_ref, bf16[128,9216]{1,0:T(8,128)(2,1)} %bitcast.82), custom_call_target="tpu_custom_call" | custom-call | tf_op jit(solution)/shard_map/mix_in/pallas_call | solution.py:353
  307.9 3.0 collective-permute-start.3
  310.9 19.4 %all-to-all-done.6 = bf16[8,16,9216]{2,1,0:T(8,128)(2,1)S(1)} async-done(((bf16[8,16,9216]{2,1,0:T(8,128)(2,1)}), bf16[8,16,9216]{2,1,0:T(8,128)(2,1)S(1)}, u32[]{:S(2)}, u32[]{:S(2)}) %all-to-all-start.6) | async-done | bytes 2359328 | tf_op jit(solution)/shard_map/all_to_all | solution.py:377
  330.3 1.4 copy-done
  331.7 16.4 %mix_in.2 = (f32[64,9216]{1,0:T(8,128)}, bf16[64,9216]{1,0:T(8,128)(2,1)}) custom-call(s32[2]{0:T(128)} %pad_add_fusion.half_ref, bf16[128,9216]{1,0:T(8,128)(2,1)} %bitcast.81), custom_call_target="tpu_custom_call" | custom-call | tf_op jit(solution)/shard_map/mix_in/pallas_call | solution.py:353
  348.1 40.4 %collective-permute-done.3 = bf16[64,9216]{1,0:T(8,128)(2,1)S(1)} collective-permute-done((bf16[64,9216]{1,0:T(8,128)(2,1)}, bf16[64,9216]{1,0:T(8,128)(2,1)S(1)}, u32[]{:S(2)}, u32[]{:S(2)}) %collective-permute-start.3) | collective-permute-done | bytes 1179680 | tf_op jit(solution)/shard_map/ppermute | solution.py:381
  389.8 3.7 all-to-all-start.9
  393.5 20.0 %collective-permute-done.2 = bf16[64,9216]{1,0:T(8,128)(2,1)} collective-permute-done((bf16[64,9216]{1,0:T(8,128)(2,1)}, bf16[64,9216]{1,0:T(8,128)(2,1)}, u32[]{:S(2)}, u32[]{:S(2)}) %collective-permute-start.2) | collective-permute-done | bytes 1179680 | tf_op jit(solution)/shard_map/ppermute | solution.py:381
  413.5 2.5 fusion
  416.0 9.9 %all-to-all-done.9 = bf16[8,8,9216]{2,1,0:T(8,128)(2,1)S(1)} async-done(((bf16[8,8,9216]{2,1,0:T(8,128)(2,1)}), bf16[8,8,9216]{2,1,0:T(8,128)(2,1)S(1)}, u32[]{:S(2)}, u32[]{:S(2)}) %all-to-all-start.9) | async-done | bytes 1179680 | tf_op jit(solution)/shard_map/all_to_all | solution.py:377
  427.0 3.6 all-to-all-start.7
  432.0 14.4 %all-to-all-done.7 = bf16[8,8,9216]{2,1,0:T(8,128)(2,1)S(1)} async-done(((bf16[8,8,9216]{2,1,0:T(8,128)(2,1)}), bf16[8,8,9216]{2,1,0:T(8,128)(2,1)S(1)}, u32[]{:S(2)}, u32[]{:S(2)}) %all-to-all-start.7) | async-done | bytes 1179680 | tf_op jit(solution)/shard_map/all_to_all | solution.py:377
  447.4 9.6 %finish.3 = bf16[9216,128]{1,0:T(8,128)(2,1)} custom-call(bf16[64,9216]{1,0:T(8,128)(2,1)} %bitcast.92, bf16[64,9216]{1,0:T(8,128)(2,1)} %bitcast.89, bf16[9216,128]{1,0:T(8,128)(2,1)} %get-tuple-element.26.refs_2_, f32[1,128]{1,0:T(1,128)} %bitcast.127, bf16[128,128]{1,0:T(8,128)(2,1)} %refs_4_.3, f32[128,1]{1,0:T(8,128)} %broadcast_in_dim_reshape.9.refs_5_, ...), custom_call_target="tpu_custom_call" | custom-call | tf_op jit(solution)/shard_map/finish/pallas_call | solution.py:159
  (58 shorter events, 15.7 us)
Async XLA Ops:
  11.1 21.1 %all-to-all-start.4 = ((bf16[8,8,9216]{2,1,0:T(8,128)(2,1)}), bf16[8,8,9216]{2,1,0:T(8,128)(2,1)S(1)}, u32[]{:S(2)}, u32[]{:S(2)}) async-start(bf16[8,8,9216]{2,1,0:T(8,128)(2,1)} %bitcast.99), calls=%async_computation.4 | async-start | bytes 2359296 | tf_op jit(solution)/shard_map/all_to_all | solution.py:377
  32.3 43.6 %copy-start.1 = (bf16[8,8,9216]{2,1,0:T(8,128)(2,1)}, bf16[8,8,9216]{2,1,0:T(8,128)(2,1)S(1)}, u32[]{:S(2)}) copy-start(bf16[8,8,9216]{2,1,0:T(8,128)(2,1)S(1)} %all-to-all-done.4) | copy-start | bytes 3538948
  32.3 21.1 %copy-start.11 = (bf16[64,9216]{1,0:T(8,128)(2,1)S(1)}, bf16[64,9216]{1,0:T(8,128)(2,1)}, u32[]{:S(2)}) copy-start(bf16[64,9216]{1,0:T(8,128)(2,1)} %get-tuple-element.17) | copy-start | bytes 3538948
  72.3 76.9 %copy-start.2 = (bf16[8,8,9216]{2,1,0:T(8,128)(2,1)}, bf16[8,8,9216]{2,1,0:T(8,128)(2,1)S(1)}, u32[]{:S(2)}) copy-start(bf16[8,8,9216]{2,1,0:T(8,128)(2,1)S(1)} %all_to_all.111) | copy-start | bytes 3538948
  72.3 72.3 %all-to-all-start = ((bf16[8,8,9216]{2,1,0:T(8,128)(2,1)}), bf16[8,8,9216]{2,1,0:T(8,128)(2,1)S(1)}, u32[]{:S(2)}, u32[]{:S(2)}) async-start(bf16[8,8,9216]{2,1,0:T(8,128)(2,1)} %bitcast.97), calls=%async_computation | async-start | bytes 2359296 | tf_op jit(solution)/shard_map/all_to_all | solution.py:377
  75.9 54.6 %collective-permute-start.1 = (bf16[64,9216]{1,0:T(8,128)(2,1)S(1)}, bf16[64,9216]{1,0:T(8,128)(2,1)}, u32[]{:S(2)}, u32[]{:S(2)}) collective-permute-start(bf16[64,9216]{1,0:T(8,128)(2,1)S(1)} %bitcast.83), channel_id=1, source_target_pairs={{0,8},{8,0},{1,9},{9,1},{2,10},{10,2},{3,11},{11,3},{4,12},{12,4},... | collective-permute-start | bytes 3538952 | tf_op jit(solution)/shard_map/ppermute | solution.py:381
  144.6 1.0 copy-start.3
  145.7 73.5 %all-to-all-start.5 = ((bf16[8,8,9216]{2,1,0:T(8,128)(2,1)}), bf16[8,8,9216]{2,1,0:T(8,128)(2,1)S(1)}, u32[]{:S(2)}, u32[]{:S(2)}) async-start(bf16[8,8,9216]{2,1,0:T(8,128)(2,1)} %bitcast.91), calls=%async_computation.5 | async-start | bytes 2359296 | tf_op jit(solution)/shard_map/all_to_all | solution.py:377
  149.2 54.8 %collective-permute-start = (bf16[64,9216]{1,0:T(8,128)(2,1)S(1)}, bf16[64,9216]{1,0:T(8,128)(2,1)S(1)}, u32[]{:S(2)}, u32[]{:S(2)}) collective-permute-start(bf16[64,9216]{1,0:T(8,128)(2,1)S(1)} %bitcast.85), channel_id=1, source_target_pairs={{0,8},{8,0},{1,9},{9,1},{2,10},{10,2},{3,11},{11,3},{4,12},{12,4},... | collective-permute-start | bytes 3538952 | tf_op jit(solution)/shard_map/ppermute | solution.py:381
  204.1 1.0 copy-start.10
  219.2 1.1 copy-start.6
  219.2 4.6 %copy-start.12 = (bf16[128,512]{1,0:T(8,128)(2,1)S(1)}, bf16[128,512]{1,0:T(8,128)(2,1)}, u32[]{:S(2)}) copy-start(bf16[128,512]{1,0:T(8,128)(2,1)} %param.18) | copy-start | bytes 393220
  219.2 6.1 %copy-start.15 = (f32[128]{0:T(128)S(1)}, f32[128]{0:T(128)}, u32[]{:S(2)}) copy-start(f32[128]{0:T(128)} %param.15) | copy-start | bytes 1540
  219.2 6.9 %copy-start.13 = (bf16[128,128]{1,0:T(8,128)(2,1)S(1)}, bf16[128,128]{1,0:T(8,128)(2,1)}, u32[]{:S(2)}) copy-start(bf16[128,128]{1,0:T(8,128)(2,1)} %param.16) | copy-start | bytes 98308
  220.2 19.4 %all-to-all-start.2 = ((bf16[8,8,9216]{2,1,0:T(8,128)(2,1)}), bf16[8,8,9216]{2,1,0:T(8,128)(2,1)S(1)}, u32[]{:S(2)}, u32[]{:S(2)}) async-start(bf16[8,8,9216]{2,1,0:T(8,128)(2,1)} %bitcast.88), calls=%async_computation.2 | async-start | bytes 2359296 | tf_op jit(solution)/shard_map/all_to_all | solution.py:377
  239.6 1.0 copy-start.7
  287.9 42.3 %all-to-all-start.6 = ((bf16[8,16,9216]{2,1,0:T(8,128)(2,1)}), bf16[8,16,9216]{2,1,0:T(8,128)(2,1)S(1)}, u32[]{:S(2)}, u32[]{:S(2)}) async-start(bf16[8,16,9216]{2,1,0:T(8,128)(2,1)} %bitcast.95), calls=%async_computation.6 | async-start | bytes 4718592 | tf_op jit(solution)/shard_map/all_to_all | solution.py:377
  307.9 80.6 %collective-permute-start.3 = (bf16[64,9216]{1,0:T(8,128)(2,1)}, bf16[64,9216]{1,0:T(8,128)(2,1)S(1)}, u32[]{:S(2)}, u32[]{:S(2)}) collective-permute-start(bf16[64,9216]{1,0:T(8,128)(2,1)} %get-tuple-element.25), channel_id=1, source_target_pairs={{0,8},{8,0},{1,9},{9,1},{2,10},{10,2},{3,11},{11,3},{4,12},{12,4},... | collective-permute-start | bytes 3538952 | tf_op jit(solution)/shard_map/ppermute | solution.py:381
  330.3 1.4 copy-start
  331.7 56.9 %copy-start.8 = (f32[64,9216]{1,0:T(8,128)S(1)}, f32[64,9216]{1,0:T(8,128)}, u32[]{:S(2)}) copy-start(f32[64,9216]{1,0:T(8,128)} %get-tuple-element.24) | copy-start | bytes 7077892
  348.1 65.5 %collective-permute-start.2 = (bf16[64,9216]{1,0:T(8,128)(2,1)}, bf16[64,9216]{1,0:T(8,128)(2,1)}, u32[]{:S(2)}, u32[]{:S(2)}) collective-permute-start(bf16[64,9216]{1,0:T(8,128)(2,1)} %get-tuple-element.22), channel_id=1, source_target_pairs={{0,8},{8,0},{1,9},{9,1},{2,10},{10,2},{3,11},{11,3},{4,12},{12,4},... | collective-permute-start | bytes 3538952 | tf_op jit(solution)/shard_map/ppermute | solution.py:381
  389.8 23.8 %copy-start.9 = (f32[64,9216]{1,0:T(8,128)S(1)}, f32[64,9216]{1,0:T(8,128)}, u32[]{:S(2)}) copy-start(f32[64,9216]{1,0:T(8,128)} %get-tuple-element.21) | copy-start | bytes 7077892
  389.8 36.2 %all-to-all-start.9 = ((bf16[8,8,9216]{2,1,0:T(8,128)(2,1)}), bf16[8,8,9216]{2,1,0:T(8,128)(2,1)S(1)}, u32[]{:S(2)}, u32[]{:S(2)}) async-start(bf16[8,8,9216]{2,1,0:T(8,128)(2,1)} %fusion.1), calls=%async_computation.9 | async-start | bytes 2359296 | tf_op jit(solution)/shard_map/all_to_all | solution.py:377
  416.0 14.5 %copy-start.16 = (f32[128]{0:T(128)S(1)}, f32[128]{0:T(128)}, u32[]{:S(2)}) copy-start(f32[128]{0:T(128)} %param.20) | copy-start | bytes 1540
  416.0 15.3 %copy-start.14 = (bf16[128,128]{1,0:T(8,128)(2,1)S(1)}, bf16[128,128]{1,0:T(8,128)(2,1)}, u32[]{:S(2)}) copy-start(bf16[128,128]{1,0:T(8,128)(2,1)} %param.21) | copy-start | bytes 98308
  426.0 1.0 copy-start.4
  427.0 19.4 %all-to-all-start.7 = ((bf16[8,8,9216]{2,1,0:T(8,128)(2,1)}), bf16[8,8,9216]{2,1,0:T(8,128)(2,1)S(1)}, u32[]{:S(2)}, u32[]{:S(2)}) async-start(bf16[8,8,9216]{2,1,0:T(8,128)(2,1)} %fusion), calls=%async_computation.7 | async-start | bytes 2359296 | tf_op jit(solution)/shard_map/all_to_all | solution.py:377
  446.4 1.0 copy-start.5

commit v4 on v3

--- a/solution.py
+++ b/solution.py
@@ -81,14 +81,17 @@
 def emit_projections(normed, gate_rows, value_rows, out_refs):
     at = 0
     for ref in out_refs:
-        rows = ref.shape[0]
+        parts, width, _ = ref.shape
+        rows = parts * width
         gates = lax.dot_general(
             gate_rows[at : at + rows, :], normed, (((1,), (1,)), ((), ())), preferred_element_type=jnp.float32
         )
         values = lax.dot_general(
             value_rows[at : at + rows, :], normed, (((1,), (1,)), ((), ())), preferred_element_type=jnp.float32
         )
-        ref[...] = (sigmoid(gates) * values).astype(ref.dtype)
+        gated = sigmoid(gates) * values
+        for part in range(parts):
+            ref[part] = gated[part * width : (part + 1) * width, :].astype(ref.dtype)
         at += rows
 
 
@@ -103,7 +106,9 @@
     state = state_ref[...].astype(jnp.float32)
     normed = layer_norm(state, gain_ref[...], 1).astype(jnp.bfloat16)
     gating = sigmoid(jnp.dot(normed, gate_ref[...], preferred_element_type=jnp.float32))
-    mixed = jnp.concatenate([ref[...].astype(jnp.float32) for ref in mix_refs], axis=0)
+    mixed = jnp.concatenate(
+        [ref[part].astype(jnp.float32) for ref in mix_refs for part in range(ref.shape[0])], axis=0
+    )
     mixed = layer_norm(mixed, out_gain_ref[...], 0).astype(jnp.bfloat16)
     change = lax.dot_general(
         mixed, final_ref[...], (((0,), (0,)), ((), ())), preferred_element_type=jnp.float32
@@ -130,7 +135,7 @@
     return step
 
 
-def run_projections(state, gain, gate_rows, value_rows, out_rows):
+def run_projections(state, gain, gate_rows, value_rows, out_shapes):
     positions, features = state.shape
     step = row_step(positions)
     weights = (gain[None, :], gate_rows, value_rows)
@@ -138,8 +143,8 @@
         project_kernel,
         grid=(positions // step,),
         in_specs=[pl.BlockSpec((step, features), lambda i: (i, 0))] + [whole_spec(w) for w in weights],
-        out_specs=[pl.BlockSpec((rows, step), lambda i: (0, i)) for rows in out_rows],
-        out_shape=[jax.ShapeDtypeStruct((rows, positions), jnp.bfloat16) for rows in out_rows],
+        out_specs=[pl.BlockSpec((*shape, step), lambda i: (0, 0, i)) for shape in out_shapes],
+        out_shape=[jax.ShapeDtypeStruct((*shape, positions), jnp.bfloat16) for shape in out_shapes],
         compiler_params=pltpu.CompilerParams(vmem_limit_bytes=BUDGET),
         name="project",
     )(state, *weights)
@@ -152,14 +157,14 @@
     out_shape = [jax.ShapeDtypeStruct((positions, features), jnp.bfloat16)]
     out_specs = [pl.BlockSpec((step, features), lambda i: (i, 0))]
     if onward is not None:
-        next_gain, gate_rows, value_rows, out_rows = onward
+        next_gain, gate_rows, value_rows, out_shapes = onward
         weights += (next_gain[None, :], gate_rows, value_rows)
-        out_shape += [jax.ShapeDtypeStruct((rows, positions), jnp.bfloat16) for rows in out_rows]
-        out_specs += [pl.BlockSpec((rows, step), lambda i: (0, i)) for rows in out_rows]
+        out_shape += [jax.ShapeDtypeStruct((*shape, positions), jnp.bfloat16) for shape in out_shapes]
+        out_specs += [pl.BlockSpec((*shape, step), lambda i: (0, 0, i)) for shape in out_shapes]
     return pl.pallas_call(
         functools.partial(finish_kernel, len(mixes), onward is not None),
         grid=(positions // step,),
-        in_specs=[pl.BlockSpec((m.shape[0], step), lambda i: (0, i)) for m in mixes]
+        in_specs=[pl.BlockSpec((*m.shape[:2], step), lambda i: (0, 0, i)) for m in mixes]
         + [pl.BlockSpec((step, features), lambda i: (i, 0))]
         + [whole_spec(w) for w in weights],
         out_specs=out_specs,
@@ -213,33 +218,39 @@
         return out
 
 
-def stage(source_ref, staged):
-    rows = source_ref.shape[0]
-    for tile in range(source_ref.shape[1] // LANES):
-        staged[tile * rows : (tile + 1) * rows, :] = source_ref[:, tile * LANES : (tile + 1) * LANES].astype(
-            jnp.float32
-        )
+def stage(source_ref, staged, shift=0, width=None):
+    parts, held, positions = source_ref.shape
+    width = width or held
+    rows = parts * width
+    for part in range(parts):
+        values = source_ref[part].astype(jnp.float32)[shift : shift + width, :]
+        for tile in range(positions // LANES):
+            at = tile * rows + part * width
+            staged[at : at + width, :] = values[:, tile * LANES : (tile + 1) * LANES]
 
 
 def unstage(staged, target_ref):
-    rows = target_ref.shape[0]
-    for tile in range(target_ref.shape[1] // LANES):
-        target_ref[:, tile * LANES : (tile + 1) * LANES] = staged[tile * rows : (tile + 1) * rows, :].astype(
-            target_ref.dtype
-        )
+    parts, width, positions = target_ref.shape
+    rows = parts * width
+    for tile in range(positions // LANES):
+        for part in range(parts):
+            at = tile * rows + part * width
+            target_ref[part, :, tile * LANES : (tile + 1) * LANES] = staged[at : at + width, :].astype(
+                target_ref.dtype
+            )
 
 
 def lane_rows_of(folds, rows, row):
     return [pl.ds(row + tile * rows, folds.groups, stride=folds.tiles * rows) for tile in range(folds.tiles)]
 
 
-def mix_out_kernel(folds, near, cols, width, half_ref, left_ref, here_ref, there_ref, mix_ref, staged, left, right):
+def mix_out_kernel(folds, near, cols, width, shift, half_ref, left_ref, here_ref, there_ref, mix_ref, staged, left, right):
     parts = near * cols
     rows = parts * width
     block = folds.rows
     far = cols // near
 
-    stage(left_ref, staged)
+    stage(left_ref, staged, shift * width, width)
 
     @pl.loop(0, rows, unroll=8)
     def _(row):
@@ -327,15 +338,15 @@
 VMEM_SPEC = pl.BlockSpec(memory_space=pltpu.VMEM)
 
 
-def run_mix_out(folds, near, cols, halves, left, here, there):
-    rows, positions = left.shape
-    width = rows // (near * cols)
+def run_mix_out(folds, near, cols, halves, left, here, there, shift):
+    parts, width, _ = here.shape
+    rows = parts * width
     block = folds.rows
     return pl.pallas_call(
-        functools.partial(mix_out_kernel, folds, near, cols, width),
+        functools.partial(mix_out_kernel, folds, near, cols, width, shift),
         in_specs=[SMEM_SPEC, VMEM_SPEC, VMEM_SPEC, VMEM_SPEC],
         out_specs=VMEM_SPEC,
-        out_shape=jax.ShapeDtypeStruct((rows, positions), jnp.bfloat16),
+        out_shape=jax.ShapeDtypeStruct(here.shape, jnp.bfloat16),
         scratch_shapes=[
             pltpu.VMEM((rows * folds.lane_rows, LANES), jnp.float32),
             pltpu.VMEM((width * cols * near * block, LANES), jnp.bfloat16),
@@ -347,16 +358,16 @@
 
 
 def run_mix_in(folds, near, cols, halves, both):
-    rows, positions = both.shape
-    width = rows // (2 * near * cols)
+    parts, width, positions = both.shape
+    rows, width = parts * width, width // 2
     block = folds.rows
     return pl.pallas_call(
         functools.partial(mix_in_kernel, folds, near, cols, width),
         in_specs=[SMEM_SPEC, VMEM_SPEC],
         out_specs=[VMEM_SPEC, VMEM_SPEC],
         out_shape=[
-            jax.ShapeDtypeStruct((rows // 2, positions), jnp.float32),
-            jax.ShapeDtypeStruct((rows // 2, positions), jnp.bfloat16),
+            jax.ShapeDtypeStruct((parts, width, positions), jnp.float32),
+            jax.ShapeDtypeStruct((parts, width, positions), jnp.bfloat16),
         ],
         scratch_shapes=[
             pltpu.VMEM((rows * folds.lane_rows, LANES), jnp.float32),
@@ -370,7 +381,7 @@
     )(halves, both)
 
 
-PIECES = 2
+PIECES = 4
 
 
 def exchange(array):
@@ -399,7 +410,8 @@
         return order(ga, gb).reshape(-1, features), order(va, vb).reshape(-1, features)
 
     def right_then_left(left, right):
-        return jnp.concatenate([right, left], axis=0)
+        paired = left.reshape(pieces // 2, 2, *left.shape[1:]).transpose(0, 2, 1, 3, 4)
+        return jnp.concatenate([right.reshape(-1, features), paired.reshape(-1, features)], axis=0)
 
     def side_by_side(left, right):
         return jnp.concatenate([left, right], axis=2)
@@ -409,21 +421,22 @@
 
     gain_1, project_1, gate_1, norm_1, final_1, gain_2, project_2, gate_2, norm_2, final_2 = weights
     state = pair_input.reshape(-1, features)
-    piece_rows = features // pieces
+    piece_width = width // pieces
 
     gates, values = rows_of(project_1, right_then_left)
     here, there, left, mixes = [], [], [], []
-    right_out = run_projections(state, gain_1, gates[:features], values[:features], (piece_rows,) * pieces)
+    out = run_projections(
+        state, gain_1, gates, values, ((parts, piece_width),) * pieces + ((parts, 2 * piece_width),) * (pieces // 2)
+    )
     for piece in range(pieces):
-        here.append(exchange(right_out[piece]))
+        here.append(exchange(out[piece]))
         there.append(across(here[piece]))
-    left_out = run_projections(state, gain_1, gates[features:], values[features:], (piece_rows,) * pieces)
+    for pair in range(pieces // 2):
+        left.append(exchange(out[pieces + pair]))
     for piece in range(pieces):
-        left.append(exchange(left_out[piece]))
-    for piece in range(pieces):
-        mixed = run_mix_out(folds, near, cols, halves, left[piece], here[piece], there[piece])
+        mixed = run_mix_out(folds, near, cols, halves, left[piece // 2], here[piece], there[piece], piece % 2)
         mixes.append(exchange(mixed))
-    onward = (gain_2, *rows_of(project_2, side_by_side), (2 * piece_rows,) * pieces)
+    onward = (gain_2, *rows_of(project_2, side_by_side), ((parts, 2 * piece_width),) * pieces)
     out = run_finish(mixes, state, gain_1, gate_1, unordered(norm_1), unordered(final_1), onward)
     middle, both, parted, mixes = out[0], [], [], []
     for piece in range(pieces):
@@ -451,7 +464,7 @@
             and block_rows == block_cols
             and Folds(block_rows, block_cols).fits()
             and features == LANES
-            and features % (row_parts // 2 * col_parts * 8 * PIECES) == 0
+            and features % (row_parts // 2 * col_parts * PIECES) == 0
         )
         if halved:
             far, near = 2, row_parts // 2

time: 458 us -> 527 us (1.15)
  blocking collectives: 73.2 us -> 134 us
  waiting for transfers between devices: 226 us -> 203 us
  starting transfers between devices: 35.6 us -> 56 us
  Pallas kernels: 102 us -> 112 us
    all_to_all x3 -> x8, blocking collectives: 73.2 us -> 134 us  [exchange(): return lax.all_to_all(array, EVERY, split_axis=0, concat_axis=0, tiled=True)]
    ppermute x4 -> x8, waiting for transfers between devices: 164 us -> 143 us  [across(): return lax.ppermute(array, 'far', ((0, 1), (1, 0)))]
    all_to_all x7 -> x10, starting transfers between devices: 27 us -> 39.3 us  [exchange(): return lax.all_to_all(array, EVERY, split_axis=0, concat_axis=0, tiled=True)]
    ppermute x4 -> x8, starting transfers between devices: 8.54 us -> 16.6 us  [across(): return lax.ppermute(array, 'far', ((0, 1), (1, 0)))]
    convert_element_type x0 -> x4, other arithmetic: none -> 6.62 us  [in_halves(): mixed = (kept + got.astype(jnp.float32)).astype(jnp.bfloat16)]
    pallas_call x2 -> x4, Pallas kernels: 28.3 us -> 34.9 us  [run_mix_out(): pl.pallas_call(functools.partial(mix_out_kernel, folds, near, cols, width...]
    pallas_call x2 -> x4, Pallas kernels: 32.6 us -> 37.2 us  [run_mix_in(): pl.pallas_call(functools.partial(mix_in_kernel, folds, near, cols, width)...]
    pallas_call x2 -> x1, Pallas kernels: 17.7 us -> 13.8 us  [run_projections(): pl.pallas_call(project_kernel, grid=(positions // step,), in_specs=[pl.Bl...]
  transfers between devices with their start and end apart: 11 -> 18, of which waited for: 9 -> 11; matrix products, arithmetic and copies ran while one was open for 2% -> 2% of each run, Pallas kernels for 15% -> 14%
where the time goes in v4:
time: 527 us; the launch traced here: 525 us
  waiting for transfers between devices  203 us (39%)
  blocking collectives  134 us (25%)
  Pallas kernels  112 us (21%)
  starting transfers between devices  56 us (11%)
  local copies, waits for them, and re-layouts  10.7 us (2%)
  other arithmetic  8.01 us (2%)
    ppermute x8, waiting for transfers between devices, across(): return lax.ppermute(array, 'far', ((0, 1), (1, 0)))  143 us
    all_to_all x8, blocking collectives, exchange(): return lax.all_to_all(array, EVERY, split_axis=0, concat_axis=0, tiled=True)  134 us
    all_to_all x10, waiting for transfers between devices, exchange(): return lax.all_to_all(array, EVERY, split_axis=0, concat_axis=0, tiled=True)  60.1 us
    all_to_all x10, starting transfers between devices, exchange(): return lax.all_to_all(array, EVERY, split_axis=0, concat_axis=0, tiled=True)  39.3 us
    pallas_call x4, Pallas kernels, run_mix_in(): pl.pallas_call(functools.partial(mix_in_kernel, folds, near, cols, width)...  37.2 us
    pallas_call x4, Pallas kernels, run_mix_out(): pl.pallas_call(functools.partial(mix_out_kernel, folds, near, cols, width...  34.9 us
    pallas_call x2, Pallas kernels, run_finish(): pl.pallas_call(functools.partial(finish_kernel, len(mixes), onward is not...  26.4 us
    ppermute x8, starting transfers between devices, across(): return lax.ppermute(array, 'far', ((0, 1), (1, 0)))  16.6 us
  transfers between devices with their start and end apart: 18, of which 11 were waited for; matrix products, arithmetic and copies ran while one was open for 2% of the time, Pallas kernels for 14%

profile of v4, /device:TPU:0, one launch (start us, length us, event | category | flops | bytes accessed | tf_op | source)
XLA Modules:
  0.0 524.6 jit_solution(15636744792275587980)
XLA Ops:
  1.8 13.8 %project.1 = (bf16[8,4,9216]{2,1,0:T(4,128)(2,1)}, bf16[8,4,9216]{2,1,0:T(4,128)(2,1)}, bf16[8,4,9216]{2,1,0:T(4,128)(2,1)}, bf16[8,4,9216]{2,1,0:T(4,128)(2,1)}...) custom-call(bf16[9216,128]{1,0:T(8,128)(2,1)} %bitcast.62, f32[1,128]{1,0:T(1,128)} %bitcast.90, ...), custom_call_target="tpu_custom_call" | custom-call | tf_op jit(solution)/shard_map/project/pallas_call | solution.py:142
  15.6 15.7 %all_to_all.90.here_ref = bf16[8,4,9216]{2,1,0:T(4,128)(2,1)S(1)} all-to-all(bf16[8,4,9216]{2,1,0:T(4,128)(2,1)} %get-tuple-element.29), channel_id=1, replica_groups=mesh['groups'=2,'far'=2,'near'=2,'chan'=2,'sub'=2] {'near','chan','sub'}, dimensions={0} | all-to-all | bytes 1179648 | tf_op jit(solution)/shard_map/all_to_all | solution.py:388
  31.4 12.8 %all_to_all.91.here_ref = bf16[8,4,9216]{2,1,0:T(4,128)(2,1)S(1)} all-to-all(bf16[8,4,9216]{2,1,0:T(4,128)(2,1)S(1)} %copy-done.23), channel_id=1, replica_groups=mesh['groups'=2,'far'=2,'near'=2,'chan'=2,'sub'=2] {'near','chan','sub'}, dimensions={0} | all-to-all | bytes 1179648 | tf_op jit(solution)/shard_map/all_to_all | solution.py:388
  44.2 12.8 %all_to_all.92.here_ref = bf16[8,4,9216]{2,1,0:T(4,128)(2,1)S(1)} all-to-all(bf16[8,4,9216]{2,1,0:T(4,128)(2,1)S(1)} %copy-done.22), channel_id=1, replica_groups=mesh['groups'=2,'far'=2,'near'=2,'chan'=2,'sub'=2] {'near','chan','sub'}, dimensions={0} | all-to-all | bytes 1179648 | tf_op jit(solution)/shard_map/all_to_all | solution.py:388
  57.0 12.7 %all_to_all.93.here_ref = bf16[8,4,9216]{2,1,0:T(4,128)(2,1)S(1)} all-to-all(bf16[8,4,9216]{2,1,0:T(4,128)(2,1)S(1)} %copy-done.21), channel_id=1, replica_groups=mesh['groups'=2,'far'=2,'near'=2,'chan'=2,'sub'=2] {'near','chan','sub'}, dimensions={0} | all-to-all | bytes 1179648 | tf_op jit(solution)/shard_map/all_to_all | solution.py:388
  69.7 19.6 %all_to_all.94.left_ref = bf16[8,8,9216]{2,1,0:T(8,128)(2,1)} all-to-all(bf16[8,8,9216]{2,1,0:T(8,128)(2,1)S(1)} %copy-done.20), channel_id=1, replica_groups=mesh['groups'=2,'far'=2,'near'=2,'chan'=2,'sub'=2] {'near','chan','sub'}, dimensions={0} | all-to-all | bytes 2359296 | tf_op jit(solution)/shard_map/all_to_all | solution.py:388
  96.3 23.1 %collective-permute-done.3.there_ref = bf16[8,4,9216]{2,1,0:T(4,128)(2,1)} collective-permute-done((bf16[8,4,9216]{2,1,0:T(4,128)(2,1)S(1)}, bf16[8,4,9216]{2,1,0:T(4,128)(2,1)}, u32[]{:S(2)}, u32[]{:S(2)}) %collective-permute-start.3) | collective-permute-done | bytes 589856 | tf_op jit(solution)/shard_map/ppermute | solution.py:392
  119.3 8.7 %mix_out.7 = bf16[8,4,9216]{2,1,0:T(4,128)(2,1)} custom-call(s32[2]{0:T(128)} %pad_add_fusion.half_ref, bf16[8,8,9216]{2,1,0:T(8,128)(2,1)} %all_to_all.94.left_ref, bf16[8,4,9216]{2,1,0:T(4,128)(2,1)} %copy-done.13, bf16[8,4,9216]{2,1,0:T(4,128)(2,1)} %collective-permute-done.3.there_ref), custom_call_target="tpu_custom_call" | custom-call | tf_op jit(solution)/shard_map/mix_out/pallas_call | solution.py:345
  128.1 7.0 %all-to-all-start.9 = ((bf16[8,4,9216]{2,1,0:T(4,128)(2,1)}), bf16[8,4,9216]{2,1,0:T(4,128)(2,1)S(1)}, u32[]{:S(2)}, u32[]{:S(2)}) async-start(bf16[8,4,9216]{2,1,0:T(4,128)(2,1)} %mix_out.7), calls=%async_computation.9 | async-start | bytes 1179648 | tf_op jit(solution)/shard_map/all_to_all | solution.py:388
  137.5 26.8 %collective-permute-done.2.there_ref = bf16[8,4,9216]{2,1,0:T(4,128)(2,1)S(1)} collective-permute-done((bf16[8,4,9216]{2,1,0:T(4,128)(2,1)S(1)}, bf16[8,4,9216]{2,1,0:T(4,128)(2,1)S(1)}, u32[]{:S(2)}, u32[]{:S(2)}) %collective-permute-start.2) | collective-permute-done | bytes 589856 | tf_op jit(solution)/shard_map/ppermute | solution.py:392
  165.2 8.7 %mix_out.6 = bf16[8,4,9216]{2,1,0:T(4,128)(2,1)} custom-call(s32[2]{0:T(128)} %pad_add_fusion.half_ref, bf16[8,8,9216]{2,1,0:T(8,128)(2,1)} %all_to_all.94.left_ref, bf16[8,4,9216]{2,1,0:T(4,128)(2,1)} %copy-done.11, bf16[8,4,9216]{2,1,0:T(4,128)(2,1)} %copy-done.24), custom_call_target="tpu_custom_call" | custom-call | tf_op jit(solution)/shard_map/mix_out/pallas_call | solution.py:345
  180.2 26.6 %collective-permute-done.1.there_ref = bf16[8,4,9216]{2,1,0:T(4,128)(2,1)S(1)} collective-permute-done((bf16[8,4,9216]{2,1,0:T(4,128)(2,1)S(1)}, bf16[8,4,9216]{2,1,0:T(4,128)(2,1)S(1)}, u32[]{:S(2)}, u32[]{:S(2)}) %collective-permute-start.1) | collective-permute-done | bytes 589856 | tf_op jit(solution)/shard_map/ppermute | solution.py:392
  207.7 8.7 %mix_out.5 = bf16[8,4,9216]{2,1,0:T(4,128)(2,1)} custom-call(s32[2]{0:T(128)} %pad_add_fusion.half_ref, bf16[8,8,9216]{2,1,0:T(8,128)(2,1)} %copy-done, bf16[8,4,9216]{2,1,0:T(4,128)(2,1)} %copy-done.9, bf16[8,4,9216]{2,1,0:T(4,128)(2,1)} %copy-done.26), custom_call_target="tpu_custom_call" | custom-call | tf_op jit(solution)/shard_map/mix_out/pallas_call | solution.py:345
  216.4 3.7 all-to-all-start.4
  222.9 26.6 %collective-permute-done.there_ref = bf16[8,4,9216]{2,1,0:T(4,128)(2,1)S(1)} collective-permute-done((bf16[8,4,9216]{2,1,0:T(4,128)(2,1)S(1)}, bf16[8,4,9216]{2,1,0:T(4,128)(2,1)S(1)}, u32[]{:S(2)}, u32[]{:S(2)}) %collective-permute-start) | collective-permute-done | bytes 589856 | tf_op jit(solution)/shard_map/ppermute | solution.py:392
  250.4 8.7 %mix_out.4 = bf16[8,4,9216]{2,1,0:T(4,128)(2,1)} custom-call(s32[2]{0:T(128)} %pad_add_fusion.half_ref, bf16[8,8,9216]{2,1,0:T(8,128)(2,1)} %copy-done, bf16[8,4,9216]{2,1,0:T(4,128)(2,1)} %copy-done.7, bf16[8,4,9216]{2,1,0:T(4,128)(2,1)} %copy-done.25), custom_call_target="tpu_custom_call" | custom-call | tf_op jit(solution)/shard_map/mix_out/pallas_call | solution.py:345
  265.8 6.5 %all-to-all-done.2.refs_0_ = bf16[8,4,9216]{2,1,0:T(4,128)(2,1)S(1)} async-done(((bf16[8,4,9216]{2,1,0:T(4,128)(2,1)}), bf16[8,4,9216]{2,1,0:T(4,128)(2,1)S(1)}, u32[]{:S(2)}, u32[]{:S(2)}) %all-to-all-start.2) | async-done | bytes 589856 | tf_op jit(solution)/shard_map/all_to_all | solution.py:388
  273.2 16.8 %finish.2 = (bf16[9216,128]{1,0:T(8,128)(2,1)}, bf16[8,8,9216]{2,1,0:T(8,128)(2,1)}, bf16[8,8,9216]{2,1,0:T(8,128)(2,1)}, bf16[8,8,9216]{2,1,0:T(8,128)(2,1)}, bf16[8,8,9216]{2,1,0:T(8,128)(2,1)}) custom-call(bf16[8,4,9216]{2,1,0:T(4,128)(2,1)} %copy-done.12, bf16[8,4,9216]{2,1,0:T(4,128)(2,1)} %copy-done.10, bf16[8,4,9216]{2,1,0:T(4,128)(2,1)} %copy-done.8, ...), custom_call_target="tpu_custom_call" | custom-call | tf_op jit(solution)/shard_map/finish/pallas_call | solution.py:164
  290.0 20.9 %all_to_all.95.both_ref = bf16[8,8,9216]{2,1,0:T(8,128)(2,1)} all-to-all(bf16[8,8,9216]{2,1,0:T(8,128)(2,1)} %get-tuple-element.39), channel_id=1, replica_groups=mesh['groups'=2,'far'=2,'near'=2,'chan'=2,'sub'=2] {'near','chan','sub'}, dimensions={0} | all-to-all | bytes 2359296 | tf_op jit(solution)/shard_map/all_to_all | solution.py:388
  310.9 19.8 %all_to_all.96.both_ref = bf16[8,8,9216]{2,1,0:T(8,128)(2,1)} all-to-all(bf16[8,8,9216]{2,1,0:T(8,128)(2,1)S(1)} %copy-done.19), channel_id=1, replica_groups=mesh['groups'=2,'far'=2,'near'=2,'chan'=2,'sub'=2] {'near','chan','sub'}, dimensions={0} | all-to-all | bytes 2359296 | tf_op jit(solution)/shard_map/all_to_all | solution.py:388
  330.7 19.7 %all_to_all.97.both_ref = bf16[8,8,9216]{2,1,0:T(8,128)(2,1)} all-to-all(bf16[8,8,9216]{2,1,0:T(8,128)(2,1)S(1)} %copy-done.18), channel_id=1, replica_groups=mesh['groups'=2,'far'=2,'near'=2,'chan'=2,'sub'=2] {'near','chan','sub'}, dimensions={0} | all-to-all | bytes 2359296 | tf_op jit(solution)/shard_map/all_to_all | solution.py:388
  353.9 9.2 %mix_in.7 = (f32[8,4,9216]{2,1,0:T(4,128)}, bf16[8,4,9216]{2,1,0:T(4,128)(2,1)}) custom-call(s32[2]{0:T(128)} %pad_add_fusion.half_ref, bf16[8,8,9216]{2,1,0:T(8,128)(2,1)} %all_to_all.95.both_ref), custom_call_target="tpu_custom_call" | custom-call | tf_op jit(solution)/shard_map/mix_in/pallas_call | solution.py:364
  366.1 9.3 %mix_in.6 = (f32[8,4,9216]{2,1,0:T(4,128)}, bf16[8,4,9216]{2,1,0:T(4,128)(2,1)}) custom-call(s32[2]{0:T(128)} %pad_add_fusion.half_ref, bf16[8,8,9216]{2,1,0:T(8,128)(2,1)} %all_to_all.96.both_ref), custom_call_target="tpu_custom_call" | custom-call | tf_op jit(solution)/shard_map/mix_in/pallas_call | solution.py:364
  375.4 9.5 %mix_in.5 = (f32[8,4,9216]{2,1,0:T(4,128)}, bf16[8,4,9216]{2,1,0:T(4,128)(2,1)}) custom-call(s32[2]{0:T(128)} %pad_add_fusion.half_ref, bf16[8,8,9216]{2,1,0:T(8,128)(2,1)} %all_to_all.97.both_ref), custom_call_target="tpu_custom_call" | custom-call | tf_op jit(solution)/shard_map/mix_in/pallas_call | solution.py:364
  388.7 9.3 %mix_in.4 = (f32[8,4,9216]{2,1,0:T(4,128)}, bf16[8,4,9216]{2,1,0:T(4,128)(2,1)}) custom-call(s32[2]{0:T(128)} %pad_add_fusion.half_ref, bf16[8,8,9216]{2,1,0:T(8,128)(2,1)} %copy-done.1), custom_call_target="tpu_custom_call" | custom-call | tf_op jit(solution)/shard_map/mix_in/pallas_call | solution.py:364
  398.1 33.1 %collective-permute-done.7 = bf16[8,4,9216]{2,1,0:T(4,128)(2,1)} collective-permute-done((bf16[8,4,9216]{2,1,0:T(4,128)(2,1)}, bf16[8,4,9216]{2,1,0:T(4,128)(2,1)}, u32[]{:S(2)}, u32[]{:S(2)}) %collective-permute-start.7) | collective-permute-done | bytes 589856 | tf_op jit(solution)/shard_map/ppermute | solution.py:392
  437.1 6.9 %collective-permute-done.6 = bf16[8,4,9216]{2,1,0:T(4,128)(2,1)} collective-permute-done((bf16[8,4,9216]{2,1,0:T(4,128)(2,1)}, bf16[8,4,9216]{2,1,0:T(4,128)(2,1)}, u32[]{:S(2)}, u32[]{:S(2)}) %collective-permute-start.6) | collective-permute-done | bytes 589856 | tf_op jit(solution)/shard_map/ppermute | solution.py:392
  446.2 28.9 %all-to-all-done.17.refs_3_ = bf16[8,4,9216]{2,1,0:T(4,128)(2,1)S(1)} async-done(((bf16[8,4,9216]{2,1,0:T(4,128)(2,1)}), bf16[8,4,9216]{2,1,0:T(4,128)(2,1)S(1)}, u32[]{:S(2)}, u32[]{:S(2)}) %all-to-all-start.17) | async-done | bytes 589856 | tf_op jit(solution)/shard_map/all_to_all | solution.py:388
  479.8 8.3 %all-to-all-done.15.refs_2_ = bf16[8,4,9216]{2,1,0:T(4,128)(2,1)S(1)} async-done(((bf16[8,4,9216]{2,1,0:T(4,128)(2,1)}), bf16[8,4,9216]{2,1,0:T(4,128)(2,1)S(1)}, u32[]{:S(2)}, u32[]{:S(2)}) %all-to-all-start.15) | async-done | bytes 589856 | tf_op jit(solution)/shard_map/all_to_all | solution.py:388
  492.8 8.3 %all-to-all-done.13.refs_1_ = bf16[8,4,9216]{2,1,0:T(4,128)(2,1)S(1)} async-done(((bf16[8,4,9216]{2,1,0:T(4,128)(2,1)}), bf16[8,4,9216]{2,1,0:T(4,128)(2,1)S(1)}, u32[]{:S(2)}, u32[]{:S(2)}) %all-to-all-start.13) | async-done | bytes 589856 | tf_op jit(solution)/shard_map/all_to_all | solution.py:388
  506.2 8.0 %all-to-all-done.11.refs_0_ = bf16[8,4,9216]{2,1,0:T(4,128)(2,1)S(1)} async-done(((bf16[8,4,9216]{2,1,0:T(4,128)(2,1)}), bf16[8,4,9216]{2,1,0:T(4,128)(2,1)S(1)}, u32[]{:S(2)}, u32[]{:S(2)}) %all-to-all-start.11) | async-done | bytes 589856 | tf_op jit(solution)/shard_map/all_to_all | solution.py:388
  515.0 9.6 %finish.3 = bf16[9216,128]{1,0:T(8,128)(2,1)} custom-call(bf16[8,4,9216]{2,1,0:T(4,128)(2,1)} %copy-done.5, bf16[8,4,9216]{2,1,0:T(4,128)(2,1)} %copy-done.4, bf16[8,4,9216]{2,1,0:T(4,128)(2,1)} %copy-done.3, bf16[8,4,9216]{2,1,0:T(4,128)(2,1)} %copy-done.2, bf16[9216,128]{1,0:T(8,128)(2,1)} %get-tuple-element.42.refs_4_, f32[1,128]{1,0:T(1,128)} %bitcast.89, ...), custom_call_target="tpu_custom_call" | custom-call | tf_op jit(solution)/shard_map/finish/pallas_call | solution.py:164
  (115 shorter events, 64.0 us)
Async XLA Ops:
  15.6 28.6 %copy-start.22 = (bf16[8,4,9216]{2,1,0:T(4,128)(2,1)S(1)}, bf16[8,4,9216]{2,1,0:T(4,128)(2,1)}, u32[]{:S(2)}) copy-start(bf16[8,4,9216]{2,1,0:T(4,128)(2,1)} %get-tuple-element.26) | copy-start | bytes 1769476
  31.4 61.6 %copy-start.13 = (bf16[8,4,9216]{2,1,0:T(4,128)(2,1)}, bf16[8,4,9216]{2,1,0:T(4,128)(2,1)S(1)}, u32[]{:S(2)}) copy-start(bf16[8,4,9216]{2,1,0:T(4,128)(2,1)S(1)} %all_to_all.90.here_ref) | copy-start | bytes 1769476
  31.4 25.7 %copy-start.21 = (bf16[8,4,9216]{2,1,0:T(4,128)(2,1)S(1)}, bf16[8,4,9216]{2,1,0:T(4,128)(2,1)}, u32[]{:S(2)}) copy-start(bf16[8,4,9216]{2,1,0:T(4,128)(2,1)} %get-tuple-element.25) | copy-start | bytes 1769476
  44.2 90.8 %copy-start.11 = (bf16[8,4,9216]{2,1,0:T(4,128)(2,1)}, bf16[8,4,9216]{2,1,0:T(4,128)(2,1)S(1)}, u32[]{:S(2)}) copy-start(bf16[8,4,9216]{2,1,0:T(4,128)(2,1)S(1)} %all_to_all.91.here_ref) | copy-start | bytes 1769476
  44.2 25.5 %copy-start.20 = (bf16[8,8,9216]{2,1,0:T(8,128)(2,1)S(1)}, bf16[8,8,9216]{2,1,0:T(8,128)(2,1)}, u32[]{:S(2)}) copy-start(bf16[8,8,9216]{2,1,0:T(8,128)(2,1)} %get-tuple-element.27) | copy-start | bytes 3538948
  57.0 120.4 %copy-start.9 = (bf16[8,4,9216]{2,1,0:T(4,128)(2,1)}, bf16[8,4,9216]{2,1,0:T(4,128)(2,1)S(1)}, u32[]{:S(2)}) copy-start(bf16[8,4,9216]{2,1,0:T(4,128)(2,1)S(1)} %all_to_all.92.here_ref) | copy-start | bytes 1769476
  69.7 150.4 %copy-start.7 = (bf16[8,4,9216]{2,1,0:T(4,128)(2,1)}, bf16[8,4,9216]{2,1,0:T(4,128)(2,1)S(1)}, u32[]{:S(2)}) copy-start(bf16[8,4,9216]{2,1,0:T(4,128)(2,1)S(1)} %all_to_all.93.here_ref) | copy-start | bytes 1769476
  89.4 38.7 %all-to-all-start = ((bf16[8,8,9216]{2,1,0:T(8,128)(2,1)}), bf16[8,8,9216]{2,1,0:T(8,128)(2,1)S(1)}, u32[]{:S(2)}, u32[]{:S(2)}) async-start(bf16[8,8,9216]{2,1,0:T(8,128)(2,1)} %get-tuple-element.24), calls=%async_computation | async-start | bytes 2359296 | tf_op jit(solution)/shard_map/all_to_all | solution.py:388
  93.0 26.4 %collective-permute-start.3 = (bf16[8,4,9216]{2,1,0:T(4,128)(2,1)S(1)}, bf16[8,4,9216]{2,1,0:T(4,128)(2,1)}, u32[]{:S(2)}, u32[]{:S(2)}) collective-permute-start(bf16[8,4,9216]{2,1,0:T(4,128)(2,1)S(1)} %all_to_all.90.here_ref), channel_id=1, source_target_pairs={{0,8},{8,0},{1,9},{9,1},{2,10},{10,2},{3,11},{11,3},{4,12},{12,4},... | collective-permute-start | bytes 1769480 | tf_op jit(solution)/shard_map/ppermute | solution.py:392
  128.1 45.8 %copy-start = (bf16[8,8,9216]{2,1,0:T(8,128)(2,1)}, bf16[8,8,9216]{2,1,0:T(8,128)(2,1)S(1)}, u32[]{:S(2)}) copy-start(bf16[8,8,9216]{2,1,0:T(8,128)(2,1)S(1)} %all-to-all-done.left_ref) | copy-start | bytes 3538948
  128.1 45.8 %all-to-all-start.9 = ((bf16[8,4,9216]{2,1,0:T(4,128)(2,1)}), bf16[8,4,9216]{2,1,0:T(4,128)(2,1)S(1)}, u32[]{:S(2)}, u32[]{:S(2)}) async-start(bf16[8,4,9216]{2,1,0:T(4,128)(2,1)} %mix_out.7), calls=%async_computation.9 | async-start | bytes 1179648 | tf_op jit(solution)/shard_map/all_to_all | solution.py:388
  135.0 29.3 %collective-permute-start.2 = (bf16[8,4,9216]{2,1,0:T(4,128)(2,1)S(1)}, bf16[8,4,9216]{2,1,0:T(4,128)(2,1)S(1)}, u32[]{:S(2)}, u32[]{:S(2)}) collective-permute-start(bf16[8,4,9216]{2,1,0:T(4,128)(2,1)S(1)} %all_to_all.91.here_ref), channel_id=1, source_target_pairs={{0,8},{8,0},{1,9},{9,1},{2,10},{10,2},{3,11},{11,3},{4,12},{12,4},... | collective-permute-start | bytes 1769480 | tf_op jit(solution)/shard_map/ppermute | solution.py:392
  173.9 42.5 %copy-start.6 = (bf16[8,4,9216]{2,1,0:T(4,128)(2,1)}, bf16[8,4,9216]{2,1,0:T(4,128)(2,1)S(1)}, u32[]{:S(2)}) copy-start(bf16[8,4,9216]{2,1,0:T(4,128)(2,1)S(1)} %all-to-all-done.9.refs_3_) | copy-start | bytes 1769476
  173.9 42.5 %all-to-all-start.7 = ((bf16[8,4,9216]{2,1,0:T(4,128)(2,1)}), bf16[8,4,9216]{2,1,0:T(4,128)(2,1)S(1)}, u32[]{:S(2)}, u32[]{:S(2)}) async-start(bf16[8,4,9216]{2,1,0:T(4,128)(2,1)} %mix_out.6), calls=%async_computation.7 | async-start | bytes 1179648 | tf_op jit(solution)/shard_map/all_to_all | solution.py:388
  177.5 29.4 %collective-permute-start.1 = (bf16[8,4,9216]{2,1,0:T(4,128)(2,1)S(1)}, bf16[8,4,9216]{2,1,0:T(4,128)(2,1)S(1)}, u32[]{:S(2)}, u32[]{:S(2)}) collective-permute-start(bf16[8,4,9216]{2,1,0:T(4,128)(2,1)S(1)} %all_to_all.92.here_ref), channel_id=1, source_target_pairs={{0,8},{8,0},{1,9},{9,1},{2,10},{10,2},{3,11},{11,3},{4,12},{12,4},... | collective-permute-start | bytes 1769480 | tf_op jit(solution)/shard_map/ppermute | solution.py:392
  216.4 42.7 %copy-start.8 = (bf16[8,4,9216]{2,1,0:T(4,128)(2,1)}, bf16[8,4,9216]{2,1,0:T(4,128)(2,1)S(1)}, u32[]{:S(2)}) copy-start(bf16[8,4,9216]{2,1,0:T(4,128)(2,1)S(1)} %all-to-all-done.7.refs_2_) | copy-start | bytes 1769476
  216.4 42.7 %all-to-all-start.4 = ((bf16[8,4,9216]{2,1,0:T(4,128)(2,1)}), bf16[8,4,9216]{2,1,0:T(4,128)(2,1)S(1)}, u32[]{:S(2)}, u32[]{:S(2)}) async-start(bf16[8,4,9216]{2,1,0:T(4,128)(2,1)} %mix_out.5), calls=%async_computation.4 | async-start | bytes 1179648 | tf_op jit(solution)/shard_map/all_to_all | solution.py:388
  220.2 29.4 %collective-permute-start = (bf16[8,4,9216]{2,1,0:T(4,128)(2,1)S(1)}, bf16[8,4,9216]{2,1,0:T(4,128)(2,1)S(1)}, u32[]{:S(2)}, u32[]{:S(2)}) collective-permute-start(bf16[8,4,9216]{2,1,0:T(4,128)(2,1)S(1)} %all_to_all.93.here_ref), channel_id=1, source_target_pairs={{0,8},{8,0},{1,9},{9,1},{2,10},{10,2},{3,11},{11,3},{4,12},{12,4},... | collective-permute-start | bytes 1769480 | tf_op jit(solution)/shard_map/ppermute | solution.py:392
  259.1 13.2 %all-to-all-start.2 = ((bf16[8,4,9216]{2,1,0:T(4,128)(2,1)}), bf16[8,4,9216]{2,1,0:T(4,128)(2,1)S(1)}, u32[]{:S(2)}, u32[]{:S(2)}) async-start(bf16[8,4,9216]{2,1,0:T(4,128)(2,1)} %mix_out.4), calls=%async_computation.2 | async-start | bytes 1179648 | tf_op jit(solution)/shard_map/all_to_all | solution.py:388
  290.0 21.0 %copy-start.19 = (bf16[8,8,9216]{2,1,0:T(8,128)(2,1)S(1)}, bf16[8,8,9216]{2,1,0:T(8,128)(2,1)}, u32[]{:S(2)}) copy-start(bf16[8,8,9216]{2,1,0:T(8,128)(2,1)} %get-tuple-element.36) | copy-start | bytes 3538948
  310.9 19.8 %copy-start.18 = (bf16[8,8,9216]{2,1,0:T(8,128)(2,1)S(1)}, bf16[8,8,9216]{2,1,0:T(8,128)(2,1)}, u32[]{:S(2)}) copy-start(bf16[8,8,9216]{2,1,0:T(8,128)(2,1)} %get-tuple-element.33) | copy-start | bytes 3538948
  350.4 37.3 %all-to-all-start.10 = ((bf16[8,8,9216]{2,1,0:T(8,128)(2,1)}), bf16[8,8,9216]{2,1,0:T(8,128)(2,1)S(1)}, u32[]{:S(2)}, u32[]{:S(2)}) async-start(bf16[8,8,9216]{2,1,0:T(8,128)(2,1)} %get-tuple-element.30), calls=%async_computation.10 | async-start | bytes 2359296 | tf_op jit(solution)/shard_map/all_to_all | solution.py:388
  363.2 68.1 %collective-permute-start.7 = (bf16[8,4,9216]{2,1,0:T(4,128)(2,1)}, bf16[8,4,9216]{2,1,0:T(4,128)(2,1)}, u32[]{:S(2)}, u32[]{:S(2)}) collective-permute-start(bf16[8,4,9216]{2,1,0:T(4,128)(2,1)} %get-tuple-element.41), channel_id=1, source_target_pairs={{0,8},{8,0},{1,9},{9,1},{2,10},{10,2},{3,11},{11,3},{4,12},{12,4},... | collective-permute-start | bytes 1769480 | tf_op jit(solution)/shard_map/ppermute | solution.py:392
  375.4 55.8 %copy-start.17 = (f32[8,4,9216]{2,1,0:T(4,128)S(1)}, f32[8,4,9216]{2,1,0:T(4,128)}, u32[]{:S(2)}) copy-start(f32[8,4,9216]{2,1,0:T(4,128)} %get-tuple-element.40) | copy-start | bytes 3538948
  375.4 68.6 %collective-permute-start.6 = (bf16[8,4,9216]{2,1,0:T(4,128)(2,1)}, bf16[8,4,9216]{2,1,0:T(4,128)(2,1)}, u32[]{:S(2)}, u32[]{:S(2)}) collective-permute-start(bf16[8,4,9216]{2,1,0:T(4,128)(2,1)} %get-tuple-element.38), channel_id=1, source_target_pairs={{0,8},{8,0},{1,9},{9,1},{2,10},{10,2},{3,11},{11,3},{4,12},{12,4},... | collective-permute-start | bytes 1769480 | tf_op jit(solution)/shard_map/ppermute | solution.py:392
  384.9 93.8 %collective-permute-start.5 = (bf16[8,4,9216]{2,1,0:T(4,128)(2,1)}, bf16[8,4,9216]{2,1,0:T(4,128)(2,1)S(1)}, u32[]{:S(2)}, u32[]{:S(2)}) collective-permute-start(bf16[8,4,9216]{2,1,0:T(4,128)(2,1)} %get-tuple-element.35), channel_id=1, source_target_pairs={{0,8},{8,0},{1,9},{9,1},{2,10},{10,2},{3,11},{11,3},{4,12},{12,4},... | collective-permute-start | bytes 1769480 | tf_op jit(solution)/shard_map/ppermute | solution.py:392
  398.0 93.7 %collective-permute-start.4 = (bf16[8,4,9216]{2,1,0:T(4,128)(2,1)}, bf16[8,4,9216]{2,1,0:T(4,128)(2,1)S(1)}, u32[]{:S(2)}, u32[]{:S(2)}) collective-permute-start(bf16[8,4,9216]{2,1,0:T(4,128)(2,1)} %get-tuple-element.32), channel_id=1, source_target_pairs={{0,8},{8,0},{1,9},{9,1},{2,10},{10,2},{3,11},{11,3},{4,12},{12,4},... | collective-permute-start | bytes 1769480 | tf_op jit(solution)/shard_map/ppermute | solution.py:392
  433.4 41.7 %all-to-all-start.17 = ((bf16[8,4,9216]{2,1,0:T(4,128)(2,1)}), bf16[8,4,9216]{2,1,0:T(4,128)(2,1)S(1)}, u32[]{:S(2)}, u32[]{:S(2)}) async-start(bf16[8,4,9216]{2,1,0:T(4,128)(2,1)} %add_convert_fusion), calls=%async_computation.17 | async-start | bytes 1179648 | tf_op jit(solution)/shard_map/all_to_all | solution.py:388
  446.2 32.5 %copy-start.15 = (f32[8,4,9216]{2,1,0:T(4,128)S(1)}, f32[8,4,9216]{2,1,0:T(4,128)}, u32[]{:S(2)}) copy-start(f32[8,4,9216]{2,1,0:T(4,128)} %get-tuple-element.34) | copy-start | bytes 3538948
  475.1 13.0 %all-to-all-start.15 = ((bf16[8,4,9216]{2,1,0:T(4,128)(2,1)}), bf16[8,4,9216]{2,1,0:T(4,128)(2,1)S(1)}, u32[]{:S(2)}, u32[]{:S(2)}) async-start(bf16[8,4,9216]{2,1,0:T(4,128)(2,1)} %add_convert_fusion.1), calls=%async_computation.15 | async-start | bytes 1179648 | tf_op jit(solution)/shard_map/all_to_all | solution.py:388
  488.1 13.0 %all-to-all-start.13 = ((bf16[8,4,9216]{2,1,0:T(4,128)(2,1)}), bf16[8,4,9216]{2,1,0:T(4,128)(2,1)S(1)}, u32[]{:S(2)}, u32[]{:S(2)}) async-start(bf16[8,4,9216]{2,1,0:T(4,128)(2,1)} %add_convert_fusion.2), calls=%async_computation.13 | async-start | bytes 1179648 | tf_op jit(solution)/shard_map/all_to_all | solution.py:388
  501.2 13.0 %all-to-all-start.11 = ((bf16[8,4,9216]{2,1,0:T(4,128)(2,1)}), bf16[8,4,9216]{2,1,0:T(4,128)(2,1)S(1)}, u32[]{:S(2)}, u32[]{:S(2)}) async-start(bf16[8,4,9216]{2,1,0:T(4,128)(2,1)} %add_convert_fusion.3), calls=%async_computation.11 | async-start | bytes 1179648 | tf_op jit(solution)/shard_map/all_to_all | solution.py:388
  (18 other events, 111.6 us)

commit v5 on v4

--- a/solution.py
+++ b/solution.py
@@ -78,26 +78,26 @@
     return row_parts // near, near
 
 
-def emit_projections(normed, gate_rows, value_rows, out_refs):
-    at = 0
-    for ref in out_refs:
-        parts, width, _ = ref.shape
-        rows = parts * width
-        gates = lax.dot_general(
-            gate_rows[at : at + rows, :], normed, (((1,), (1,)), ((), ())), preferred_element_type=jnp.float32
-        )
-        values = lax.dot_general(
-            value_rows[at : at + rows, :], normed, (((1,), (1,)), ((), ())), preferred_element_type=jnp.float32
-        )
-        gated = sigmoid(gates) * values
-        for part in range(parts):
-            ref[part] = gated[part * width : (part + 1) * width, :].astype(ref.dtype)
-        at += rows
-
-
-def project_kernel(state_ref, gain_ref, gate_rows, value_rows, *out_refs):
+def emit_projections(normed, rows_ref, out_refs):
+    step = normed.shape[0]
+    half = rows_ref.shape[0] // 2
+    group = 256 if step % 256 == 0 else LANES
+    for begin in range(0, step, group):
+        projected = lax.dot_general(
+            rows_ref[...], normed[begin : begin + group, :], (((1,), (1,)), ((), ())), preferred_element_type=jnp.float32
+        )
+        gated = sigmoid(projected[:half, :]) * projected[half:, :]
+        at = 0
+        for ref in out_refs:
+            parts, width, _ = ref.shape
+            for part in range(parts):
+                ref[part, :, begin : begin + group] = gated[at : at + width, :].astype(ref.dtype)
+                at += width
+
+
+def project_kernel(state_ref, gain_ref, rows_ref, *out_refs):
     normed = layer_norm(state_ref[...].astype(jnp.float32), gain_ref[...], 1).astype(jnp.bfloat16)
-    emit_projections(normed, gate_rows, value_rows, out_refs)
+    emit_projections(normed, rows_ref, out_refs)
 
 
 def finish_kernel(pieces, onward, *refs):
@@ -115,10 +115,10 @@
     )
     result = (state + gating * change).astype(jnp.bfloat16)
     if onward:
-        next_gain, gate_rows, value_rows, middle_ref = refs[5:9]
+        next_gain, rows_ref, middle_ref = refs[5:8]
         middle_ref[...] = result
         normed = layer_norm(result.astype(jnp.float32), next_gain[...], 1).astype(jnp.bfloat16)
-        emit_projections(normed, gate_rows, value_rows, refs[9:])
+        emit_projections(normed, rows_ref, refs[8:])
     else:
         refs[5][...] = result
 
@@ -129,16 +129,16 @@
 
 def row_step(positions):
     step = positions
-    for candidate in range(LANES, 1152 + 1, LANES):
+    for candidate in range(LANES, 2304 + 1, LANES):
         if positions % candidate == 0:
             step = candidate
     return step
 
 
-def run_projections(state, gain, gate_rows, value_rows, out_shapes):
+def run_projections(state, gain, rows, out_shapes):
     positions, features = state.shape
     step = row_step(positions)
-    weights = (gain[None, :], gate_rows, value_rows)
+    weights = (gain[None, :], rows)
     return pl.pallas_call(
         project_kernel,
         grid=(positions // step,),
@@ -157,8 +157,8 @@
     out_shape = [jax.ShapeDtypeStruct((positions, features), jnp.bfloat16)]
     out_specs = [pl.BlockSpec((step, features), lambda i: (i, 0))]
     if onward is not None:
-        next_gain, gate_rows, value_rows, out_shapes = onward
-        weights += (next_gain[None, :], gate_rows, value_rows)
+        next_gain, rows, out_shapes = onward
+        weights += (next_gain[None, :], rows)
         out_shape += [jax.ShapeDtypeStruct((*shape, positions), jnp.bfloat16) for shape in out_shapes]
         out_specs += [pl.BlockSpec((*shape, step), lambda i: (0, 0, i)) for shape in out_shapes]
     return pl.pallas_call(
@@ -187,7 +187,7 @@
     def fits(self):
         return self.cols <= LANES and self.rows % self.turn == 0 and self.groups % 8 == 0
 
-    def split(self, lane_rows):
+    def split(self, lane_rows, clear=False):
         lane = lax.broadcasted_iota(jnp.int32, lane_rows[0].shape, 1)
         out = []
         for phase in range(self.turn):
@@ -197,7 +197,7 @@
                 value = jnp.where(lane >= offset, value, lane_rows[first + 1])
             if offset:
                 value = pltpu.roll(value, LANES - offset, 1)
-            out.append(jnp.where(lane < self.cols, value, 0.0))
+            out.append(jnp.where(lane < self.cols, value, 0.0) if clear else value)
         return out
 
     def join(self, block_rows):
@@ -244,23 +244,23 @@
     return [pl.ds(row + tile * rows, folds.groups, stride=folds.tiles * rows) for tile in range(folds.tiles)]
 
 
-def mix_out_kernel(folds, near, cols, width, shift, half_ref, left_ref, here_ref, there_ref, mix_ref, staged, left, right):
+def mix_out_kernel(folds, near, cols, width, half_ref, both_ref, there_ref, mix_ref, staged, left, right):
     parts = near * cols
     rows = parts * width
     block = folds.rows
     far = cols // near
 
-    stage(left_ref, staged, shift * width, width)
+    stage(both_ref, staged, 0, width)
 
     @pl.loop(0, rows, unroll=8)
     def _(row):
-        pieces = folds.split([staged[at, :] for at in lane_rows_of(folds, rows, row)])
+        pieces = folds.split([staged[at, :] for at in lane_rows_of(folds, rows, row)], clear=True)
         source, channel = row // width, row % width
         at = (channel * cols + source % cols) * near * block + (source // cols) * block
         left[pl.ds(pl.multiple_of(at, block), block), :] = jnp.concatenate(pieces, axis=0).astype(jnp.bfloat16)
 
-    for which, ref in ((0, here_ref), (1, there_ref)):
-        stage(ref, staged)
+    for which, ref, shift in ((0, both_ref, width), (1, there_ref, 0)):
+        stage(ref, staged, shift, width)
         half = half_ref[which]
 
         @pl.loop(0, rows, unroll=8)
@@ -271,16 +271,18 @@
             for phase, piece in enumerate(pieces):
                 right[pl.ds(at + phase, folds.groups, stride=folds.turn), :] = piece
 
-    @pl.loop(0, width, unroll=2)
+    @pl.loop(0, width, unroll=1)
     def _(channel):
+        tall = near * block
+        lhs = jnp.concatenate(
+            [left[pl.ds(pl.multiple_of((channel * cols + col) * tall, block), tall), :] for col in range(cols)], axis=1
+        )
         for target in range(cols):
-            total = None
-            for col in range(cols):
-                lhs = left[pl.ds(pl.multiple_of((channel * cols + col) * near * block, block), near * block), :]
-                at = ((channel * cols + col) * far * near + target) * block
-                rhs = right[pl.ds(pl.multiple_of(at, block), block), :].astype(jnp.bfloat16)
-                part = lax.dot_general(lhs, rhs, (((1,), (1,)), ((), ())), preferred_element_type=jnp.float32)
-                total = part if total is None else total + part
+            starts = [((channel * cols + col) * far * near + target) * block for col in range(cols)]
+            rhs = jnp.concatenate([right[pl.ds(pl.multiple_of(at, block), block), :] for at in starts], axis=1)
+            total = lax.dot_general(
+                lhs, rhs.astype(jnp.bfloat16), (((1,), (1,)), ((), ())), preferred_element_type=jnp.float32
+            )
             total = jnp.concatenate([total, jnp.zeros((near * block, LANES - block), jnp.float32)], axis=1)
             for piece in range(near):
                 groups = folds.groups
@@ -315,17 +317,20 @@
     out_rows = parts * width
     tall = near * block
 
-    @pl.loop(0, width, unroll=2)
+    @pl.loop(0, width, unroll=1)
     def _(channel):
+        rhs = jnp.concatenate(
+            [right[pl.ds(pl.multiple_of((channel * cols + col) * tall, block), tall), :] for col in range(cols)], axis=1
+        )
         for upper in range(cols):
             lhs = left[pl.ds(pl.multiple_of((channel * cols + upper) * tall, block), tall), :]
+            summed = lax.dot_general(lhs, rhs, (((0,), (0,)), ((), ())), preferred_element_type=jnp.float32)
+            half, piece = divmod(upper, near)
             for target in range(cols):
-                rhs = right[pl.ds(pl.multiple_of((channel * cols + target) * tall, block), tall), :]
-                turned[target] = lax.dot_general(lhs, rhs, (((0,), (0,)), ((), ())), preferred_element_type=jnp.float32)
+                turned[upper, target] = summed[:, target * LANES : (target + 1) * LANES]
                 lane_rows = folds.join(
-                    [turned[target, pl.ds(phase, folds.groups, stride=folds.turn), :] for phase in range(folds.turn)]
+                    [turned[upper, target, pl.ds(phase, folds.groups, stride=folds.turn), :] for phase in range(folds.turn)]
                 )
-                half, piece = divmod(upper, near)
                 out_row = (piece * cols + target) * width + channel
                 for at, value in zip(lane_rows_of(folds, out_rows, out_row), lane_rows):
                     mixed[half, at, :] = value
@@ -338,15 +343,15 @@
 VMEM_SPEC = pl.BlockSpec(memory_space=pltpu.VMEM)
 
 
-def run_mix_out(folds, near, cols, halves, left, here, there, shift):
-    parts, width, _ = here.shape
+def run_mix_out(folds, near, cols, halves, both, there):
+    parts, width, _ = there.shape
     rows = parts * width
     block = folds.rows
     return pl.pallas_call(
-        functools.partial(mix_out_kernel, folds, near, cols, width, shift),
-        in_specs=[SMEM_SPEC, VMEM_SPEC, VMEM_SPEC, VMEM_SPEC],
+        functools.partial(mix_out_kernel, folds, near, cols, width),
+        in_specs=[SMEM_SPEC, VMEM_SPEC, VMEM_SPEC],
         out_specs=VMEM_SPEC,
-        out_shape=jax.ShapeDtypeStruct(here.shape, jnp.bfloat16),
+        out_shape=jax.ShapeDtypeStruct(there.shape, jnp.bfloat16),
         scratch_shapes=[
             pltpu.VMEM((rows * folds.lane_rows, LANES), jnp.float32),
             pltpu.VMEM((width * cols * near * block, LANES), jnp.bfloat16),
@@ -354,7 +359,7 @@
         ],
         compiler_params=pltpu.CompilerParams(vmem_limit_bytes=BUDGET),
         name="mix_out",
-    )(halves, left, here, there)
+    )(halves, both, there)
 
 
 def run_mix_in(folds, near, cols, halves, both):
@@ -373,7 +378,7 @@
             pltpu.VMEM((rows * folds.lane_rows, LANES), jnp.float32),
             pltpu.VMEM((width * cols * near * block, LANES), jnp.bfloat16),
             pltpu.VMEM((width * cols * near * block, LANES), jnp.bfloat16),
-            pltpu.VMEM((cols, LANES, LANES), jnp.float32),
+            pltpu.VMEM((cols, cols, LANES, LANES), jnp.float32),
             pltpu.VMEM((2, rows // 2 * folds.lane_rows, LANES), jnp.float32),
         ],
         compiler_params=pltpu.CompilerParams(vmem_limit_bytes=BUDGET),
@@ -407,11 +412,7 @@
 
     def rows_of(project, order):
         ga, va, gb, vb = (by_piece(rows) for rows in jnp.split(project.T, 4, axis=0))
-        return order(ga, gb).reshape(-1, features), order(va, vb).reshape(-1, features)
-
-    def right_then_left(left, right):
-        paired = left.reshape(pieces // 2, 2, *left.shape[1:]).transpose(0, 2, 1, 3, 4)
-        return jnp.concatenate([right.reshape(-1, features), paired.reshape(-1, features)], axis=0)
+        return jnp.concatenate([order(ga, gb).reshape(-1, features), order(va, vb).reshape(-1, features)])
 
     def side_by_side(left, right):
         return jnp.concatenate([left, right], axis=2)
@@ -423,20 +424,16 @@
     state = pair_input.reshape(-1, features)
     piece_width = width // pieces
 
-    gates, values = rows_of(project_1, right_then_left)
-    here, there, left, mixes = [], [], [], []
-    out = run_projections(
-        state, gain_1, gates, values, ((parts, piece_width),) * pieces + ((parts, 2 * piece_width),) * (pieces // 2)
-    )
+    shapes = ((parts, 2 * piece_width),) * pieces
+    both, mixes = [], []
+    out = run_projections(state, gain_1, rows_of(project_1, side_by_side), shapes)
     for piece in range(pieces):
-        here.append(exchange(out[piece]))
-        there.append(across(here[piece]))
-    for pair in range(pieces // 2):
-        left.append(exchange(out[pieces + pair]))
+        both.append(exchange(out[piece]))
     for piece in range(pieces):
-        mixed = run_mix_out(folds, near, cols, halves, left[piece // 2], here[piece], there[piece], piece % 2)
+        there = across(both[piece][:, piece_width:, :])
+        mixed = run_mix_out(folds, near, cols, halves, both[piece], there)
         mixes.append(exchange(mixed))
-    onward = (gain_2, *rows_of(project_2, side_by_side), ((parts, 2 * piece_width),) * pieces)
+    onward = (gain_2, rows_of(project_2, side_by_side), shapes)
     out = run_finish(mixes, state, gain_1, gate_1, unordered(norm_1), unordered(final_1), onward)
     middle, both, parted, mixes = out[0], [], [], []
     for piece in range(pieces):

time: 527 us -> 506 us (0.960)
  blocking collectives: 134 us -> 120 us
  Pallas kernels: 112 us -> 102 us
    all_to_all x8 -> x6, blocking collectives: 134 us -> 120 us  [exchange(): return lax.all_to_all(array, EVERY, split_axis=0, concat_axis=0, tiled=True)]
    pallas_call x1, Pallas kernels: 13.8 us -> 7.32 us  [run_projections(): pl.pallas_call(project_kernel, grid=(positions // step,), in_specs=[pl.Bl...]
    pallas_call x2, Pallas kernels: 26.4 us -> 21 us  [run_finish(): pl.pallas_call(functools.partial(finish_kernel, len(mixes), onward is not...]
  transfers between devices with their start and end apart: 18 -> 18, of which waited for: 11 -> 11; matrix products, arithmetic and copies ran while one was open for 2% -> 3% of each run, Pallas kernels for 14% -> 15%
where the time goes in v5:
time: 506 us; the launch traced here: 504 us
  waiting for transfers between devices  206 us (41%)
  blocking collectives  120 us (24%)
  Pallas kernels  102 us (20%)
  starting transfers between devices  53.7 us (11%)
  local copies, waits for them, and re-layouts  12.7 us (3%)
  other arithmetic  8.75 us (2%)
    ppermute x8, waiting for transfers between devices, across(): return lax.ppermute(array, 'far', ((0, 1), (1, 0)))  145 us
    all_to_all x6, blocking collectives, exchange(): return lax.all_to_all(array, EVERY, split_axis=0, concat_axis=0, tiled=True)  120 us
    all_to_all x10, waiting for transfers between devices, exchange(): return lax.all_to_all(array, EVERY, split_axis=0, concat_axis=0, tiled=True)  60.6 us
    pallas_call x4, Pallas kernels, run_mix_in(): pl.pallas_call(functools.partial(mix_in_kernel, folds, near, cols, width)...  38.4 us
    all_to_all x10, starting transfers between devices, exchange(): return lax.all_to_all(array, EVERY, split_axis=0, concat_axis=0, tiled=True)  36.8 us
    pallas_call x4, Pallas kernels, run_mix_out(): pl.pallas_call(functools.partial(mix_out_kernel, folds, near, cols, width...  35.3 us
    pallas_call x2, Pallas kernels, run_finish(): pl.pallas_call(functools.partial(finish_kernel, len(mixes), onward is not...  21 us
    ppermute x8, starting transfers between devices, across(): return lax.ppermute(array, 'far', ((0, 1), (1, 0)))  16.9 us
  transfers between devices with their start and end apart: 18, of which 11 were waited for; matrix products, arithmetic and copies ran while one was open for 3% of the time, Pallas kernels for 15%

profile of v5, /device:TPU:0, one launch (start us, length us, event | category | flops | bytes accessed | tf_op | source)
XLA Modules:
  0.0 504.1 jit_solution(3953136667235547518)
XLA Ops:
  1.9 7.3 %project.1 = (bf16[8,8,9216]{2,1,0:T(8,128)(2,1)}, bf16[8,8,9216]{2,1,0:T(8,128)(2,1)}, bf16[8,8,9216]{2,1,0:T(8,128)(2,1)}, bf16[8,8,9216]{2,1,0:T(8,128)(2,1)}) custom-call(bf16[9216,128]{1,0:T(8,128)(2,1)} %bitcast.54, f32[1,128]{1,0:T(1,128)} %bitcast.78, bf16[512,128]{1,0:T(8,128)(2,1)} %pad_maximum_fusion.rows_ref), custom_call_target="tpu_custom_call" | custom-call | tf_op jit(solution)/shard_map/project/pallas_call | solution.py:142
  9.2 22.0 %all_to_all.80.both_ref = bf16[8,8,9216]{2,1,0:T(8,128)(2,1)} all-to-all(bf16[8,8,9216]{2,1,0:T(8,128)(2,1)} %get-tuple-element.25), channel_id=1, replica_groups=mesh['groups'=2,'far'=2,'near'=2,'chan'=2,'sub'=2] {'near','chan','sub'}, dimensions={0} | all-to-all | bytes 2359296 | tf_op jit(solution)/shard_map/all_to_all | solution.py:393
  31.2 19.1 %all_to_all.81.both_ref = bf16[8,8,9216]{2,1,0:T(8,128)(2,1)S(1)} all-to-all(bf16[8,8,9216]{2,1,0:T(8,128)(2,1)S(1)} %copy-done.18), channel_id=1, replica_groups=mesh['groups'=2,'far'=2,'near'=2,'chan'=2,'sub'=2] {'near','chan','sub'}, dimensions={0} | all-to-all | bytes 2359296 | tf_op jit(solution)/shard_map/all_to_all | solution.py:393
  50.3 18.9 %all_to_all.82.both_ref = bf16[8,8,9216]{2,1,0:T(8,128)(2,1)S(1)} all-to-all(bf16[8,8,9216]{2,1,0:T(8,128)(2,1)S(1)} %copy-done.17), channel_id=1, replica_groups=mesh['groups'=2,'far'=2,'near'=2,'chan'=2,'sub'=2] {'near','chan','sub'}, dimensions={0} | all-to-all | bytes 2359296 | tf_op jit(solution)/shard_map/all_to_all | solution.py:393
  69.3 3.6 all-to-all-start
  78.8 26.3 %collective-permute-done.3.there_ref = bf16[8,4,9216]{2,1,0:T(4,128)(2,1)} collective-permute-done((bf16[8,4,9216]{2,1,0:T(4,128)(2,1)}, bf16[8,4,9216]{2,1,0:T(4,128)(2,1)}, u32[]{:S(2)}, u32[]{:S(2)}) %collective-permute-start.3) | collective-permute-done | bytes 589856 | tf_op jit(solution)/shard_map/ppermute | solution.py:397
  105.1 8.8 %mix_out.7 = bf16[8,4,9216]{2,1,0:T(4,128)(2,1)} custom-call(s32[2]{0:T(128)} %pad_add_fusion.half_ref, bf16[8,8,9216]{2,1,0:T(8,128)(2,1)} %all_to_all.80.both_ref, bf16[8,4,9216]{2,1,0:T(4,128)(2,1)} %collective-permute-done.3.there_ref), custom_call_target="tpu_custom_call" | custom-call | tf_op jit(solution)/shard_map/mix_out/pallas_call | solution.py:350
  113.9 4.2 all-to-all-start.7
  120.8 26.9 %collective-permute-done.2.there_ref = bf16[8,4,9216]{2,1,0:T(4,128)(2,1)S(1)} collective-permute-done((bf16[8,4,9216]{2,1,0:T(4,128)(2,1)S(1)}, bf16[8,4,9216]{2,1,0:T(4,128)(2,1)S(1)}, u32[]{:S(2)}, u32[]{:S(2)}) %collective-permute-start.2) | collective-permute-done | bytes 589856 | tf_op jit(solution)/shard_map/ppermute | solution.py:397
  148.5 8.8 %mix_out.6 = bf16[8,4,9216]{2,1,0:T(4,128)(2,1)} custom-call(s32[2]{0:T(128)} %pad_add_fusion.half_ref, bf16[8,8,9216]{2,1,0:T(8,128)(2,1)} %copy-done.2, bf16[8,4,9216]{2,1,0:T(4,128)(2,1)} %copy-done.19), custom_call_target="tpu_custom_call" | custom-call | tf_op jit(solution)/shard_map/mix_out/pallas_call | solution.py:350
  164.0 26.7 %collective-permute-done.1.there_ref = bf16[8,4,9216]{2,1,0:T(4,128)(2,1)S(1)} collective-permute-done((bf16[8,4,9216]{2,1,0:T(4,128)(2,1)S(1)}, bf16[8,4,9216]{2,1,0:T(4,128)(2,1)S(1)}, u32[]{:S(2)}, u32[]{:S(2)}) %collective-permute-start.1) | collective-permute-done | bytes 589856 | tf_op jit(solution)/shard_map/ppermute | solution.py:397
  191.5 8.8 %mix_out.5 = bf16[8,4,9216]{2,1,0:T(4,128)(2,1)} custom-call(s32[2]{0:T(128)} %pad_add_fusion.half_ref, bf16[8,8,9216]{2,1,0:T(8,128)(2,1)} %copy-done.1, bf16[8,4,9216]{2,1,0:T(4,128)(2,1)} %copy-done.20), custom_call_target="tpu_custom_call" | custom-call | tf_op jit(solution)/shard_map/mix_out/pallas_call | solution.py:350
  207.1 26.7 %collective-permute-done.there_ref = bf16[8,4,9216]{2,1,0:T(4,128)(2,1)S(1)} collective-permute-done((bf16[8,4,9216]{2,1,0:T(4,128)(2,1)S(1)}, bf16[8,4,9216]{2,1,0:T(4,128)(2,1)S(1)}, u32[]{:S(2)}, u32[]{:S(2)}) %collective-permute-start) | collective-permute-done | bytes 589856 | tf_op jit(solution)/shard_map/ppermute | solution.py:397
  234.6 8.8 %mix_out.4 = bf16[8,4,9216]{2,1,0:T(4,128)(2,1)} custom-call(s32[2]{0:T(128)} %pad_add_fusion.half_ref, bf16[8,8,9216]{2,1,0:T(8,128)(2,1)} %copy-done, bf16[8,4,9216]{2,1,0:T(4,128)(2,1)} %copy-done.21), custom_call_target="tpu_custom_call" | custom-call | tf_op jit(solution)/shard_map/mix_out/pallas_call | solution.py:350
  243.5 3.9 all-to-all-start.1
  249.8 7.1 %all-to-all-done.1.refs_0_ = bf16[8,4,9216]{2,1,0:T(4,128)(2,1)S(1)} async-done(((bf16[8,4,9216]{2,1,0:T(4,128)(2,1)}), bf16[8,4,9216]{2,1,0:T(4,128)(2,1)S(1)}, u32[]{:S(2)}, u32[]{:S(2)}) %all-to-all-start.1) | async-done | bytes 589856 | tf_op jit(solution)/shard_map/all_to_all | solution.py:393
  257.7 12.7 %finish.2 = (bf16[9216,128]{1,0:T(8,128)(2,1)}, bf16[8,8,9216]{2,1,0:T(8,128)(2,1)}, bf16[8,8,9216]{2,1,0:T(8,128)(2,1)}, bf16[8,8,9216]{2,1,0:T(8,128)(2,1)}, bf16[8,8,9216]{2,1,0:T(8,128)(2,1)}) custom-call(bf16[8,4,9216]{2,1,0:T(4,128)(2,1)} %copy-done.10, bf16[8,4,9216]{2,1,0:T(4,128)(2,1)} %copy-done.9, bf16[8,4,9216]{2,1,0:T(4,128)(2,1)} %copy-done.8, ...), custom_call_target="tpu_custom_call" | custom-call | tf_op jit(solution)/shard_map/finish/pallas_call | solution.py:164
  270.4 20.9 %all_to_all.83.both_ref = bf16[8,8,9216]{2,1,0:T(8,128)(2,1)} all-to-all(bf16[8,8,9216]{2,1,0:T(8,128)(2,1)} %get-tuple-element.35), channel_id=1, replica_groups=mesh['groups'=2,'far'=2,'near'=2,'chan'=2,'sub'=2] {'near','chan','sub'}, dimensions={0} | all-to-all | bytes 2359296 | tf_op jit(solution)/shard_map/all_to_all | solution.py:393
  291.4 19.8 %all_to_all.84.both_ref = bf16[8,8,9216]{2,1,0:T(8,128)(2,1)} all-to-all(bf16[8,8,9216]{2,1,0:T(8,128)(2,1)S(1)} %copy-done.16), channel_id=1, replica_groups=mesh['groups'=2,'far'=2,'near'=2,'chan'=2,'sub'=2] {'near','chan','sub'}, dimensions={0} | all-to-all | bytes 2359296 | tf_op jit(solution)/shard_map/all_to_all | solution.py:393
  311.2 19.7 %all_to_all.85.both_ref = bf16[8,8,9216]{2,1,0:T(8,128)(2,1)} all-to-all(bf16[8,8,9216]{2,1,0:T(8,128)(2,1)S(1)} %copy-done.15), channel_id=1, replica_groups=mesh['groups'=2,'far'=2,'near'=2,'chan'=2,'sub'=2] {'near','chan','sub'}, dimensions={0} | all-to-all | bytes 2359296 | tf_op jit(solution)/shard_map/all_to_all | solution.py:393
  334.4 9.5 %mix_in.7 = (f32[8,4,9216]{2,1,0:T(4,128)}, bf16[8,4,9216]{2,1,0:T(4,128)(2,1)}) custom-call(s32[2]{0:T(128)} %pad_add_fusion.half_ref, bf16[8,8,9216]{2,1,0:T(8,128)(2,1)} %all_to_all.83.both_ref), custom_call_target="tpu_custom_call" | custom-call | tf_op jit(solution)/shard_map/mix_in/pallas_call | solution.py:369
  346.9 9.5 %mix_in.6 = (f32[8,4,9216]{2,1,0:T(4,128)}, bf16[8,4,9216]{2,1,0:T(4,128)(2,1)}) custom-call(s32[2]{0:T(128)} %pad_add_fusion.half_ref, bf16[8,8,9216]{2,1,0:T(8,128)(2,1)} %all_to_all.84.both_ref), custom_call_target="tpu_custom_call" | custom-call | tf_op jit(solution)/shard_map/mix_in/pallas_call | solution.py:369
  356.5 9.7 %mix_in.5 = (f32[8,4,9216]{2,1,0:T(4,128)}, bf16[8,4,9216]{2,1,0:T(4,128)(2,1)}) custom-call(s32[2]{0:T(128)} %pad_add_fusion.half_ref, bf16[8,8,9216]{2,1,0:T(8,128)(2,1)} %all_to_all.85.both_ref), custom_call_target="tpu_custom_call" | custom-call | tf_op jit(solution)/shard_map/mix_in/pallas_call | solution.py:369
  370.0 9.6 %mix_in.4 = (f32[8,4,9216]{2,1,0:T(4,128)}, bf16[8,4,9216]{2,1,0:T(4,128)(2,1)}) custom-call(s32[2]{0:T(128)} %pad_add_fusion.half_ref, bf16[8,8,9216]{2,1,0:T(8,128)(2,1)} %copy-done.3), custom_call_target="tpu_custom_call" | custom-call | tf_op jit(solution)/shard_map/mix_in/pallas_call | solution.py:369
  379.7 32.3 %collective-permute-done.7 = bf16[8,4,9216]{2,1,0:T(4,128)(2,1)} collective-permute-done((bf16[8,4,9216]{2,1,0:T(4,128)(2,1)}, bf16[8,4,9216]{2,1,0:T(4,128)(2,1)}, u32[]{:S(2)}, u32[]{:S(2)}) %collective-permute-start.7) | collective-permute-done | bytes 589856 | tf_op jit(solution)/shard_map/ppermute | solution.py:397
  414.2 3.9 all-to-all-start.15
  418.1 6.6 %collective-permute-done.6 = bf16[8,4,9216]{2,1,0:T(4,128)(2,1)} collective-permute-done((bf16[8,4,9216]{2,1,0:T(4,128)(2,1)}, bf16[8,4,9216]{2,1,0:T(4,128)(2,1)}, u32[]{:S(2)}, u32[]{:S(2)}) %collective-permute-start.6) | collective-permute-done | bytes 589856 | tf_op jit(solution)/shard_map/ppermute | solution.py:397
  426.9 28.9 %all-to-all-done.15.refs_3_ = bf16[8,4,9216]{2,1,0:T(4,128)(2,1)S(1)} async-done(((bf16[8,4,9216]{2,1,0:T(4,128)(2,1)}), bf16[8,4,9216]{2,1,0:T(4,128)(2,1)S(1)}, u32[]{:S(2)}, u32[]{:S(2)}) %all-to-all-start.15) | async-done | bytes 589856 | tf_op jit(solution)/shard_map/all_to_all | solution.py:393
  460.6 8.3 %all-to-all-done.13.refs_2_ = bf16[8,4,9216]{2,1,0:T(4,128)(2,1)S(1)} async-done(((bf16[8,4,9216]{2,1,0:T(4,128)(2,1)}), bf16[8,4,9216]{2,1,0:T(4,128)(2,1)S(1)}, u32[]{:S(2)}, u32[]{:S(2)}) %all-to-all-start.13) | async-done | bytes 589856 | tf_op jit(solution)/shard_map/all_to_all | solution.py:393
  473.6 8.3 %all-to-all-done.11.refs_1_ = bf16[8,4,9216]{2,1,0:T(4,128)(2,1)S(1)} async-done(((bf16[8,4,9216]{2,1,0:T(4,128)(2,1)}), bf16[8,4,9216]{2,1,0:T(4,128)(2,1)S(1)}, u32[]{:S(2)}, u32[]{:S(2)}) %all-to-all-start.11) | async-done | bytes 589856 | tf_op jit(solution)/shard_map/all_to_all | solution.py:393
  486.9 8.0 %all-to-all-done.9.refs_0_ = bf16[8,4,9216]{2,1,0:T(4,128)(2,1)S(1)} async-done(((bf16[8,4,9216]{2,1,0:T(4,128)(2,1)}), bf16[8,4,9216]{2,1,0:T(4,128)(2,1)S(1)}, u32[]{:S(2)}, u32[]{:S(2)}) %all-to-all-start.9) | async-done | bytes 589856 | tf_op jit(solution)/shard_map/all_to_all | solution.py:393
  495.8 8.3 %finish.3 = bf16[9216,128]{1,0:T(8,128)(2,1)} custom-call(bf16[8,4,9216]{2,1,0:T(4,128)(2,1)} %copy-done.7, bf16[8,4,9216]{2,1,0:T(4,128)(2,1)} %copy-done.6, bf16[8,4,9216]{2,1,0:T(4,128)(2,1)} %copy-done.5, bf16[8,4,9216]{2,1,0:T(4,128)(2,1)} %copy-done.4, bf16[9216,128]{1,0:T(8,128)(2,1)} %get-tuple-element.38.refs_4_, f32[1,128]{1,0:T(1,128)} %bitcast.77, ...), custom_call_target="tpu_custom_call" | custom-call | tf_op jit(solution)/shard_map/finish/pallas_call | solution.py:164
  (106 shorter events, 59.7 us)
Async XLA Ops:
  9.2 22.0 %copy-start.18 = (bf16[8,8,9216]{2,1,0:T(8,128)(2,1)S(1)}, bf16[8,8,9216]{2,1,0:T(8,128)(2,1)}, u32[]{:S(2)}) copy-start(bf16[8,8,9216]{2,1,0:T(8,128)(2,1)} %get-tuple-element.24) | copy-start | bytes 3538948
  31.2 19.1 %copy-start.17 = (bf16[8,8,9216]{2,1,0:T(8,128)(2,1)S(1)}, bf16[8,8,9216]{2,1,0:T(8,128)(2,1)}, u32[]{:S(2)}) copy-start(bf16[8,8,9216]{2,1,0:T(8,128)(2,1)} %get-tuple-element.23) | copy-start | bytes 3538948
  50.3 67.8 %copy-start.2 = (bf16[8,8,9216]{2,1,0:T(8,128)(2,1)}, bf16[8,8,9216]{2,1,0:T(8,128)(2,1)S(1)}, u32[]{:S(2)}) copy-start(bf16[8,8,9216]{2,1,0:T(8,128)(2,1)S(1)} %all_to_all.81.both_ref) | copy-start | bytes 3538948
  69.2 91.6 %copy-start.1 = (bf16[8,8,9216]{2,1,0:T(8,128)(2,1)}, bf16[8,8,9216]{2,1,0:T(8,128)(2,1)S(1)}, u32[]{:S(2)}) copy-start(bf16[8,8,9216]{2,1,0:T(8,128)(2,1)S(1)} %all_to_all.82.both_ref) | copy-start | bytes 3538948
  69.3 44.7 %all-to-all-start = ((bf16[8,8,9216]{2,1,0:T(8,128)(2,1)}), bf16[8,8,9216]{2,1,0:T(8,128)(2,1)S(1)}, u32[]{:S(2)}, u32[]{:S(2)}) async-start(bf16[8,8,9216]{2,1,0:T(8,128)(2,1)} %get-tuple-element.22), calls=%async_computation | async-start | bytes 2359296 | tf_op jit(solution)/shard_map/all_to_all | solution.py:393
  75.2 29.8 %collective-permute-start.3 = (bf16[8,4,9216]{2,1,0:T(4,128)(2,1)}, bf16[8,4,9216]{2,1,0:T(4,128)(2,1)}, u32[]{:S(2)}, u32[]{:S(2)}) collective-permute-start(bf16[8,4,9216]{2,1,0:T(4,128)(2,1)} %slice.19), channel_id=1, source_target_pairs={{0,8},{8,0},{1,9},{9,1},{2,10},{10,2},{3,11},{11,3},{4,12},{12,4},... | collective-permute-start | bytes 1769480 | tf_op jit(solution)/shard_map/ppermute | solution.py:397
  113.9 89.9 %copy-start = (bf16[8,8,9216]{2,1,0:T(8,128)(2,1)}, bf16[8,8,9216]{2,1,0:T(8,128)(2,1)S(1)}, u32[]{:S(2)}) copy-start(bf16[8,8,9216]{2,1,0:T(8,128)(2,1)S(1)} %all-to-all-done.both_ref) | copy-start | bytes 3538948
  113.9 43.4 %all-to-all-start.7 = ((bf16[8,4,9216]{2,1,0:T(4,128)(2,1)}), bf16[8,4,9216]{2,1,0:T(4,128)(2,1)}, u32[]{:S(2)}, u32[]{:S(2)}) async-start(bf16[8,4,9216]{2,1,0:T(4,128)(2,1)} %mix_out.7), calls=%async_computation.7 | async-start | bytes 1179648 | tf_op jit(solution)/shard_map/all_to_all | solution.py:393
  118.5 29.3 %collective-permute-start.2 = (bf16[8,4,9216]{2,1,0:T(4,128)(2,1)S(1)}, bf16[8,4,9216]{2,1,0:T(4,128)(2,1)S(1)}, u32[]{:S(2)}, u32[]{:S(2)}) collective-permute-start(bf16[8,4,9216]{2,1,0:T(4,128)(2,1)S(1)} %slice.18), channel_id=1, source_target_pairs={{0,8},{8,0},{1,9},{9,1},{2,10},{10,2},{3,11},{11,3},{4,12},{12,4},... | collective-permute-start | bytes 1769480 | tf_op jit(solution)/shard_map/ppermute | solution.py:397
  157.3 42.9 %all-to-all-start.5 = ((bf16[8,4,9216]{2,1,0:T(4,128)(2,1)}), bf16[8,4,9216]{2,1,0:T(4,128)(2,1)S(1)}, u32[]{:S(2)}, u32[]{:S(2)}) async-start(bf16[8,4,9216]{2,1,0:T(4,128)(2,1)} %mix_out.6), calls=%async_computation.5 | async-start | bytes 1179648 | tf_op jit(solution)/shard_map/all_to_all | solution.py:393
  161.2 29.4 %collective-permute-start.1 = (bf16[8,4,9216]{2,1,0:T(4,128)(2,1)S(1)}, bf16[8,4,9216]{2,1,0:T(4,128)(2,1)S(1)}, u32[]{:S(2)}, u32[]{:S(2)}) collective-permute-start(bf16[8,4,9216]{2,1,0:T(4,128)(2,1)S(1)} %slice.17), channel_id=1, source_target_pairs={{0,8},{8,0},{1,9},{9,1},{2,10},{10,2},{3,11},{11,3},{4,12},{12,4},... | collective-permute-start | bytes 1769480 | tf_op jit(solution)/shard_map/ppermute | solution.py:397
  200.3 43.2 %all-to-all-start.3 = ((bf16[8,4,9216]{2,1,0:T(4,128)(2,1)}), bf16[8,4,9216]{2,1,0:T(4,128)(2,1)S(1)}, u32[]{:S(2)}, u32[]{:S(2)}) async-start(bf16[8,4,9216]{2,1,0:T(4,128)(2,1)} %mix_out.5), calls=%async_computation.3 | async-start | bytes 1179648 | tf_op jit(solution)/shard_map/all_to_all | solution.py:393
  204.2 29.6 %collective-permute-start = (bf16[8,4,9216]{2,1,0:T(4,128)(2,1)S(1)}, bf16[8,4,9216]{2,1,0:T(4,128)(2,1)S(1)}, u32[]{:S(2)}, u32[]{:S(2)}) collective-permute-start(bf16[8,4,9216]{2,1,0:T(4,128)(2,1)S(1)} %slice.16), channel_id=1, source_target_pairs={{0,8},{8,0},{1,9},{9,1},{2,10},{10,2},{3,11},{11,3},{4,12},{12,4},... | collective-permute-start | bytes 1769480 | tf_op jit(solution)/shard_map/ppermute | solution.py:397
  243.5 13.4 %all-to-all-start.1 = ((bf16[8,4,9216]{2,1,0:T(4,128)(2,1)}), bf16[8,4,9216]{2,1,0:T(4,128)(2,1)S(1)}, u32[]{:S(2)}, u32[]{:S(2)}) async-start(bf16[8,4,9216]{2,1,0:T(4,128)(2,1)} %mix_out.4), calls=%async_computation.1 | async-start | bytes 1179648 | tf_op jit(solution)/shard_map/all_to_all | solution.py:393
  270.4 20.9 %copy-start.16 = (bf16[8,8,9216]{2,1,0:T(8,128)(2,1)S(1)}, bf16[8,8,9216]{2,1,0:T(8,128)(2,1)}, u32[]{:S(2)}) copy-start(bf16[8,8,9216]{2,1,0:T(8,128)(2,1)} %get-tuple-element.32) | copy-start | bytes 3538948
  291.4 19.8 %copy-start.15 = (bf16[8,8,9216]{2,1,0:T(8,128)(2,1)S(1)}, bf16[8,8,9216]{2,1,0:T(8,128)(2,1)}, u32[]{:S(2)}) copy-start(bf16[8,8,9216]{2,1,0:T(8,128)(2,1)} %get-tuple-element.29) | copy-start | bytes 3538948
  330.8 38.2 %all-to-all-start.8 = ((bf16[8,8,9216]{2,1,0:T(8,128)(2,1)}), bf16[8,8,9216]{2,1,0:T(8,128)(2,1)S(1)}, u32[]{:S(2)}, u32[]{:S(2)}) async-start(bf16[8,8,9216]{2,1,0:T(8,128)(2,1)} %get-tuple-element.26), calls=%async_computation.8 | async-start | bytes 2359296 | tf_op jit(solution)/shard_map/all_to_all | solution.py:393
  343.9 68.1 %collective-permute-start.7 = (bf16[8,4,9216]{2,1,0:T(4,128)(2,1)}, bf16[8,4,9216]{2,1,0:T(4,128)(2,1)}, u32[]{:S(2)}, u32[]{:S(2)}) collective-permute-start(bf16[8,4,9216]{2,1,0:T(4,128)(2,1)} %get-tuple-element.37), channel_id=1, source_target_pairs={{0,8},{8,0},{1,9},{9,1},{2,10},{10,2},{3,11},{11,3},{4,12},{12,4},... | collective-permute-start | bytes 1769480 | tf_op jit(solution)/shard_map/ppermute | solution.py:397
  356.4 55.5 %copy-start.14 = (f32[8,4,9216]{2,1,0:T(4,128)S(1)}, f32[8,4,9216]{2,1,0:T(4,128)}, u32[]{:S(2)}) copy-start(f32[8,4,9216]{2,1,0:T(4,128)} %get-tuple-element.36) | copy-start | bytes 3538948
  356.4 68.3 %collective-permute-start.6 = (bf16[8,4,9216]{2,1,0:T(4,128)(2,1)}, bf16[8,4,9216]{2,1,0:T(4,128)(2,1)}, u32[]{:S(2)}, u32[]{:S(2)}) collective-permute-start(bf16[8,4,9216]{2,1,0:T(4,128)(2,1)} %get-tuple-element.34), channel_id=1, source_target_pairs={{0,8},{8,0},{1,9},{9,1},{2,10},{10,2},{3,11},{11,3},{4,12},{12,4},... | collective-permute-start | bytes 1769480 | tf_op jit(solution)/shard_map/ppermute | solution.py:397
  366.2 93.2 %collective-permute-start.5 = (bf16[8,4,9216]{2,1,0:T(4,128)(2,1)}, bf16[8,4,9216]{2,1,0:T(4,128)(2,1)S(1)}, u32[]{:S(2)}, u32[]{:S(2)}) collective-permute-start(bf16[8,4,9216]{2,1,0:T(4,128)(2,1)} %get-tuple-element.31), channel_id=1, source_target_pairs={{0,8},{8,0},{1,9},{9,1},{2,10},{10,2},{3,11},{11,3},{4,12},{12,4},... | collective-permute-start | bytes 1769480 | tf_op jit(solution)/shard_map/ppermute | solution.py:397
  379.6 92.8 %collective-permute-start.4 = (bf16[8,4,9216]{2,1,0:T(4,128)(2,1)}, bf16[8,4,9216]{2,1,0:T(4,128)(2,1)S(1)}, u32[]{:S(2)}, u32[]{:S(2)}) collective-permute-start(bf16[8,4,9216]{2,1,0:T(4,128)(2,1)} %get-tuple-element.28), channel_id=1, source_target_pairs={{0,8},{8,0},{1,9},{9,1},{2,10},{10,2},{3,11},{11,3},{4,12},{12,4},... | collective-permute-start | bytes 1769480 | tf_op jit(solution)/shard_map/ppermute | solution.py:397
  414.2 10.6 %copy-start.13 = (f32[8,4,9216]{2,1,0:T(4,128)S(1)}, f32[8,4,9216]{2,1,0:T(4,128)}, u32[]{:S(2)}) copy-start(f32[8,4,9216]{2,1,0:T(4,128)} %get-tuple-element.33) | copy-start | bytes 3538948
  414.2 41.6 %all-to-all-start.15 = ((bf16[8,4,9216]{2,1,0:T(4,128)(2,1)}), bf16[8,4,9216]{2,1,0:T(4,128)(2,1)S(1)}, u32[]{:S(2)}, u32[]{:S(2)}) async-start(bf16[8,4,9216]{2,1,0:T(4,128)(2,1)} %add_convert_fusion), calls=%async_computation.15 | async-start | bytes 1179648 | tf_op jit(solution)/shard_map/all_to_all | solution.py:393
  426.9 32.5 %copy-start.12 = (f32[8,4,9216]{2,1,0:T(4,128)S(1)}, f32[8,4,9216]{2,1,0:T(4,128)}, u32[]{:S(2)}) copy-start(f32[8,4,9216]{2,1,0:T(4,128)} %get-tuple-element.30) | copy-start | bytes 3538948
  455.8 13.0 %all-to-all-start.13 = ((bf16[8,4,9216]{2,1,0:T(4,128)(2,1)}), bf16[8,4,9216]{2,1,0:T(4,128)(2,1)S(1)}, u32[]{:S(2)}, u32[]{:S(2)}) async-start(bf16[8,4,9216]{2,1,0:T(4,128)(2,1)} %add_convert_fusion.1), calls=%async_computation.13 | async-start | bytes 1179648 | tf_op jit(solution)/shard_map/all_to_all | solution.py:393
  460.6 11.9 %copy-start.11 = (f32[8,4,9216]{2,1,0:T(4,128)S(1)}, f32[8,4,9216]{2,1,0:T(4,128)}, u32[]{:S(2)}) copy-start(f32[8,4,9216]{2,1,0:T(4,128)} %get-tuple-element.27) | copy-start | bytes 3538948
  468.9 13.0 %all-to-all-start.11 = ((bf16[8,4,9216]{2,1,0:T(4,128)(2,1)}), bf16[8,4,9216]{2,1,0:T(4,128)(2,1)S(1)}, u32[]{:S(2)}, u32[]{:S(2)}) async-start(bf16[8,4,9216]{2,1,0:T(4,128)(2,1)} %add_convert_fusion.2), calls=%async_computation.11 | async-start | bytes 1179648 | tf_op jit(solution)/shard_map/all_to_all | solution.py:393
  473.6 11.9 %copy-start.26 = (f32[128]{0:T(128)S(1)}, f32[128]{0:T(128)}, u32[]{:S(2)}) copy-start(f32[128]{0:T(128)} %param.20) | copy-start | bytes 1540
  473.6 12.7 %copy-start.24 = (bf16[128,128]{1,0:T(8,128)(2,1)S(1)}, bf16[128,128]{1,0:T(8,128)(2,1)}, u32[]{:S(2)}) copy-start(bf16[128,128]{1,0:T(8,128)(2,1)} %param.21) | copy-start | bytes 98308
  481.9 13.0 %copy-start.6 = (bf16[8,4,9216]{2,1,0:T(4,128)(2,1)}, bf16[8,4,9216]{2,1,0:T(4,128)(2,1)S(1)}, u32[]{:S(2)}) copy-start(bf16[8,4,9216]{2,1,0:T(4,128)(2,1)S(1)} %all-to-all-done.11.refs_1_) | copy-start | bytes 1769476
  481.9 13.0 %all-to-all-start.9 = ((bf16[8,4,9216]{2,1,0:T(4,128)(2,1)}), bf16[8,4,9216]{2,1,0:T(4,128)(2,1)S(1)}, u32[]{:S(2)}, u32[]{:S(2)}) async-start(bf16[8,4,9216]{2,1,0:T(4,128)(2,1)} %add_convert_fusion.3), calls=%async_computation.9 | async-start | bytes 1179648 | tf_op jit(solution)/shard_map/all_to_all | solution.py:393
  (13 other events, 36.6 us)

commit v6 on v5

--- a/solution.py
+++ b/solution.py
@@ -229,47 +229,54 @@
             staged[at : at + width, :] = values[:, tile * LANES : (tile + 1) * LANES]
 
 
-def unstage(staged, target_ref):
-    parts, width, positions = target_ref.shape
+def unstage(staged, target_ref, earlier_ref=None):
+    parts, height, positions = target_ref.shape
+    width = height if earlier_ref is None else height // 2
     rows = parts * width
     for tile in range(positions // LANES):
+        lanes = slice(tile * LANES, (tile + 1) * LANES)
         for part in range(parts):
             at = tile * rows + part * width
-            target_ref[part, :, tile * LANES : (tile + 1) * LANES] = staged[at : at + width, :].astype(
-                target_ref.dtype
-            )
+            values = staged[at : at + width, :]
+            if earlier_ref is not None:
+                values = jnp.concatenate([earlier_ref[part, :, lanes].astype(jnp.float32), values], axis=0)
+            target_ref[part, :, lanes] = values.astype(target_ref.dtype)
 
 
 def lane_rows_of(folds, rows, row):
     return [pl.ds(row + tile * rows, folds.groups, stride=folds.tiles * rows) for tile in range(folds.tiles)]
 
 
-def mix_out_kernel(folds, near, cols, width, half_ref, both_ref, there_ref, mix_ref, staged, left, right):
+def mix_out_kernel(folds, near, cols, width, half_ref, both_ref, there_ref, *refs):
+    earlier_ref, (mix_ref, staged, left, right) = (refs[0] if len(refs) == 5 else None), refs[-4:]
     parts = near * cols
     rows = parts * width
     block = folds.rows
     far = cols // near
 
-    stage(both_ref, staged, 0, width)
+    stage(both_ref, staged)
 
     @pl.loop(0, rows, unroll=8)
-    def _(row):
-        pieces = folds.split([staged[at, :] for at in lane_rows_of(folds, rows, row)], clear=True)
-        source, channel = row // width, row % width
+    def _(step):
+        source, channel = step // width, step % width
+        row = source * 2 * width + channel
+        pieces = folds.split([staged[at, :] for at in lane_rows_of(folds, 2 * rows, row)], clear=True)
         at = (channel * cols + source % cols) * near * block + (source // cols) * block
         left[pl.ds(pl.multiple_of(at, block), block), :] = jnp.concatenate(pieces, axis=0).astype(jnp.bfloat16)
 
-    for which, ref, shift in ((0, both_ref, width), (1, there_ref, 0)):
-        stage(ref, staged, shift, width)
-        half = half_ref[which]
-
+    def place(half, total, shift, height):
         @pl.loop(0, rows, unroll=8)
-        def _(row):
-            pieces = folds.split([staged[at, :] for at in lane_rows_of(folds, rows, row)])
-            source, channel = row // width, row % width
+        def _(step):
+            source, channel = step // width, step % width
+            row = source * height + shift + channel
+            pieces = folds.split([staged[at, :] for at in lane_rows_of(folds, total, row)])
             at = ((channel * cols + source % cols) * far + half) * near * block + (source // cols) * block
             for phase, piece in enumerate(pieces):
                 right[pl.ds(at + phase, folds.groups, stride=folds.turn), :] = piece
+
+    place(half_ref[0], 2 * rows, width, 2 * width)
+    stage(there_ref, staged)
+    place(half_ref[1], rows, 0, width)
 
     @pl.loop(0, width, unroll=1)
     def _(channel):
@@ -294,7 +301,10 @@
                 for at, value in zip(lane_rows_of(folds, rows, out_row), lane_rows):
                     staged[at, :] = value
 
-    unstage(staged, mix_ref)
+    if earlier_ref is None:
+        unstage(staged, mix_ref)
+    else:
+        unstage(staged, mix_ref, earlier_ref)
 
 
 def mix_in_kernel(folds, near, cols, width, half_ref, both_ref, keep_ref, send_ref, staged, left, right, turned, mixed):
@@ -343,23 +353,46 @@
 VMEM_SPEC = pl.BlockSpec(memory_space=pltpu.VMEM)
 
 
-def run_mix_out(folds, near, cols, halves, both, there):
-    parts, width, _ = there.shape
+def run_mix_out(folds, near, cols, halves, both, there, earlier=()):
+    parts, width, positions = there.shape
     rows = parts * width
     block = folds.rows
     return pl.pallas_call(
         functools.partial(mix_out_kernel, folds, near, cols, width),
-        in_specs=[SMEM_SPEC, VMEM_SPEC, VMEM_SPEC],
+        in_specs=[SMEM_SPEC] + [VMEM_SPEC] * (2 + len(earlier)),
         out_specs=VMEM_SPEC,
-        out_shape=jax.ShapeDtypeStruct(there.shape, jnp.bfloat16),
+        out_shape=jax.ShapeDtypeStruct((parts, width * (1 + len(earlier)), positions), jnp.bfloat16),
         scratch_shapes=[
-            pltpu.VMEM((rows * folds.lane_rows, LANES), jnp.float32),
+            pltpu.VMEM((2 * rows * folds.lane_rows, LANES), jnp.float32),
             pltpu.VMEM((width * cols * near * block, LANES), jnp.bfloat16),
             pltpu.VMEM((width * cols * cols * block, LANES), jnp.float32),
         ],
         compiler_params=pltpu.CompilerParams(vmem_limit_bytes=BUDGET),
         name="mix_out",
-    )(halves, both, there)
+    )(halves, both, there, *earlier)
+
+
+def add_kernel(*refs):
+    target_ref = refs[-1]
+    parts = target_ref.shape[0]
+    for part in range(parts):
+        sums = [kept[part] + got[part].astype(jnp.float32) for kept, got in zip(refs[:-1:2], refs[1:-1:2])]
+        target_ref[part] = jnp.concatenate(sums, axis=0).astype(target_ref.dtype)
+
+
+def run_add(*arrays):
+    parts, width, positions = arrays[0].shape
+    step = row_step(positions)
+    height = width * len(arrays) // 2
+    return pl.pallas_call(
+        add_kernel,
+        grid=(positions // step,),
+        in_specs=[pl.BlockSpec((parts, width, step), lambda i: (0, 0, i))] * len(arrays),
+        out_specs=pl.BlockSpec((parts, height, step), lambda i: (0, 0, i)),
+        out_shape=jax.ShapeDtypeStruct((parts, height, positions), jnp.bfloat16),
+        compiler_params=pltpu.CompilerParams(vmem_limit_bytes=BUDGET),
+        name="add",
+    )(*arrays)
 
 
 def run_mix_in(folds, near, cols, halves, both):
@@ -403,6 +436,7 @@
     parts = near * cols
     width = features // parts
     pieces = PIECES
+    piece_width = width // pieces
     folds = Folds(row_count, col_count)
     half = lax.axis_index("far")
     halves = jnp.stack([half, 1 - half]).astype(jnp.int32)
@@ -418,11 +452,11 @@
         return jnp.concatenate([left, right], axis=2)
 
     def unordered(array):
-        return by_piece(array.reshape(features, -1)).reshape(array.shape)
+        rows = array.reshape(parts, pieces // 2, 2 * piece_width, -1)
+        return rows.transpose(1, 0, 2, 3).reshape(array.shape)
 
     gain_1, project_1, gate_1, norm_1, final_1, gain_2, project_2, gate_2, norm_2, final_2 = weights
     state = pair_input.reshape(-1, features)
-    piece_width = width // pieces
 
     shapes = ((parts, 2 * piece_width),) * pieces
     both, mixes = [], []
@@ -431,8 +465,9 @@
         both.append(exchange(out[piece]))
     for piece in range(pieces):
         there = across(both[piece][:, piece_width:, :])
-        mixed = run_mix_out(folds, near, cols, halves, both[piece], there)
-        mixes.append(exchange(mixed))
+        mixed = run_mix_out(folds, near, cols, halves, both[piece], there, (mixed,) if piece % 2 else ())
+        if piece % 2:
+            mixes.append(exchange(mixed))
     onward = (gain_2, rows_of(project_2, side_by_side), shapes)
     out = run_finish(mixes, state, gain_1, gate_1, unordered(norm_1), unordered(final_1), onward)
     middle, both, parted, mixes = out[0], [], [], []
@@ -441,8 +476,8 @@
     for piece in range(pieces):
         kept, sent = run_mix_in(folds, near, cols, halves, both[piece])
         parted.append((kept, across(sent)))
-    for kept, got in parted:
-        mixed = (kept + got.astype(jnp.float32)).astype(jnp.bfloat16)
+    for pair in range(pieces // 2):
+        mixed = run_add(*parted[2 * pair], *parted[2 * pair + 1])
         mixes.append(exchange(mixed))
     result = run_finish(mixes, middle, gain_2, gate_2, unordered(norm_2), unordered(final_2))[0]
     return result.reshape(pair_input.shape)

time: 506 us -> 482 us (0.953)
  starting transfers between devices: 53.7 us -> 33.7 us
  Pallas kernels: 102 us -> 114 us
  waiting for transfers between devices: 206 us -> 194 us
  other arithmetic: 8.75 us -> 2.08 us
    all_to_all x10 -> x6, waiting for transfers between devices: 60.6 us -> 27.7 us  [exchange(): return lax.all_to_all(array, EVERY, split_axis=0, concat_axis=0, tiled=True)]
    ppermute x8, waiting for transfers between devices: 145 us -> 166 us  [across(): return lax.ppermute(array, 'far', ((0, 1), (1, 0)))]
    all_to_all x10 -> x6, starting transfers between devices: 36.8 us -> 21.8 us  [exchange(): return lax.all_to_all(array, EVERY, split_axis=0, concat_axis=0, tiled=True)]
    pallas_call x0 -> x2, Pallas kernels: none -> 7.97 us  [run_add(): pl.pallas_call(add_kernel, grid=(positions // step,), in_specs=[pl.BlockS...]
    convert_element_type x4 -> x0, other arithmetic: 6.64 us -> none  [in_halves(): mixed = (kept + got.astype(jnp.float32)).astype(jnp.bfloat16)]
    unnamed x56 -> x52, local copies, waits for them, and re-layouts: 6.42 us -> 10.4 us
  transfers between devices with their start and end apart: 18 -> 14, of which waited for: 11 -> 10; matrix products, arithmetic and copies ran while one was open for 3% -> 1% of each run, Pallas kernels for 15% -> 18%
where the time goes in v6:
time: 482 us; the launch traced here: 480 us
  waiting for transfers between devices  194 us (40%)
  blocking collectives  121 us (25%)
  Pallas kernels  114 us (24%)
  starting transfers between devices  33.7 us (7%)
  local copies, waits for them, and re-layouts  15.4 us (3%)
    ppermute x8, waiting for transfers between devices, across(): return lax.ppermute(array, 'far', ((0, 1), (1, 0)))  166 us
    all_to_all x6, blocking collectives, exchange(): return lax.all_to_all(array, EVERY, split_axis=0, concat_axis=0, tiled=True)  121 us
    pallas_call x4, Pallas kernels, run_mix_out(): pl.pallas_call(functools.partial(mix_out_kernel, folds, near, cols, width...  40.1 us
    pallas_call x4, Pallas kernels, run_mix_in(): pl.pallas_call(functools.partial(mix_in_kernel, folds, near, cols, width)...  38.2 us
    all_to_all x6, waiting for transfers between devices, exchange(): return lax.all_to_all(array, EVERY, split_axis=0, concat_axis=0, tiled=True)  27.7 us
    all_to_all x6, starting transfers between devices, exchange(): return lax.all_to_all(array, EVERY, split_axis=0, concat_axis=0, tiled=True)  21.8 us
    pallas_call x2, Pallas kernels, run_finish(): pl.pallas_call(functools.partial(finish_kernel, len(mixes), onward is not...  20.5 us
    ppermute x8, starting transfers between devices, across(): return lax.ppermute(array, 'far', ((0, 1), (1, 0)))  11.9 us
  transfers between devices with their start and end apart: 14, of which 10 were waited for; matrix products, arithmetic and copies ran while one was open for 1% of the time, Pallas kernels for 18%

profile of v6, /device:TPU:0, one launch (start us, length us, event | category | flops | bytes accessed | tf_op | source)
XLA Modules:
  0.0 480.4 jit_solution(2268691294737218572)
XLA Ops:
  1.8 7.3 %project.1 = (bf16[8,8,9216]{2,1,0:T(8,128)(2,1)}, bf16[8,8,9216]{2,1,0:T(8,128)(2,1)}, bf16[8,8,9216]{2,1,0:T(8,128)(2,1)}, bf16[8,8,9216]{2,1,0:T(8,128)(2,1)}) custom-call(bf16[9216,128]{1,0:T(8,128)(2,1)} %bitcast.54, f32[1,128]{1,0:T(1,128)} %bitcast.78, bf16[512,128]{1,0:T(8,128)(2,1)} %pad_maximum_fusion.rows_ref), custom_call_target="tpu_custom_call" | custom-call | tf_op jit(solution)/shard_map/project/pallas_call | solution.py:142
  9.2 21.9 %all_to_all.60.both_ref = bf16[8,8,9216]{2,1,0:T(8,128)(2,1)S(1)} all-to-all(bf16[8,8,9216]{2,1,0:T(8,128)(2,1)} %get-tuple-element.25), channel_id=1, replica_groups=mesh['groups'=2,'far'=2,'near'=2,'chan'=2,'sub'=2] {'near','chan','sub'}, dimensions={0} | all-to-all | bytes 2359296 | tf_op jit(solution)/shard_map/all_to_all | solution.py:426
  31.1 19.9 %all_to_all.61.both_ref = bf16[8,8,9216]{2,1,0:T(8,128)(2,1)} all-to-all(bf16[8,8,9216]{2,1,0:T(8,128)(2,1)S(1)} %copy-done.12), channel_id=1, replica_groups=mesh['groups'=2,'far'=2,'near'=2,'chan'=2,'sub'=2] {'near','chan','sub'}, dimensions={0} | all-to-all | bytes 2359296 | tf_op jit(solution)/shard_map/all_to_all | solution.py:426
  51.0 18.9 %all_to_all.62.both_ref = bf16[8,8,9216]{2,1,0:T(8,128)(2,1)S(1)} all-to-all(bf16[8,8,9216]{2,1,0:T(8,128)(2,1)S(1)} %copy-done.11), channel_id=1, replica_groups=mesh['groups'=2,'far'=2,'near'=2,'chan'=2,'sub'=2] {'near','chan','sub'}, dimensions={0} | all-to-all | bytes 2359296 | tf_op jit(solution)/shard_map/all_to_all | solution.py:426
  70.0 3.6 all-to-all-start
  78.6 38.7 %collective-permute-done.3.there_ref = bf16[8,4,9216]{2,1,0:T(4,128)(2,1)S(1)} collective-permute-done((bf16[8,4,9216]{2,1,0:T(4,128)(2,1)}, bf16[8,4,9216]{2,1,0:T(4,128)(2,1)S(1)}, u32[]{:S(2)}, u32[]{:S(2)}) %collective-permute-start.3) | collective-permute-done | bytes 589856 | tf_op jit(solution)/shard_map/ppermute | solution.py:430
  118.2 9.7 %mix_out.6.refs_0_ = bf16[8,4,9216]{2,1,0:T(4,128)(2,1)} custom-call(s32[2]{0:T(128)} %pad_add_fusion.half_ref, bf16[8,8,9216]{2,1,0:T(8,128)(2,1)} %copy-done.1, bf16[8,4,9216]{2,1,0:T(4,128)(2,1)} %copy-done.17), custom_call_target="tpu_custom_call" | custom-call | tf_op jit(solution)/shard_map/mix_out/pallas_call | solution.py:360
  129.5 10.3 %mix_out.7 = bf16[8,8,9216]{2,1,0:T(8,128)(2,1)} custom-call(s32[2]{0:T(128)} %pad_add_fusion.half_ref, bf16[8,8,9216]{2,1,0:T(8,128)(2,1)} %all_to_all.61.both_ref, bf16[8,4,9216]{2,1,0:T(4,128)(2,1)} %collective-permute-done.2.there_ref, bf16[8,4,9216]{2,1,0:T(4,128)(2,1)} %mix_out.6.refs_0_), custom_call_target="tpu_custom_call" | custom-call | tf_op jit(solution)/shard_map/mix_out/pallas_call | solution.py:360
  139.8 3.7 all-to-all-start.5
  147.3 22.9 %collective-permute-done.1.there_ref = bf16[8,4,9216]{2,1,0:T(4,128)(2,1)S(1)} collective-permute-done((bf16[8,4,9216]{2,1,0:T(4,128)(2,1)S(1)}, bf16[8,4,9216]{2,1,0:T(4,128)(2,1)S(1)}, u32[]{:S(2)}, u32[]{:S(2)}) %collective-permute-start.1) | collective-permute-done | bytes 589856 | tf_op jit(solution)/shard_map/ppermute | solution.py:430
  171.0 9.7 %mix_out.4.refs_0_ = bf16[8,4,9216]{2,1,0:T(4,128)(2,1)} custom-call(s32[2]{0:T(128)} %pad_add_fusion.half_ref, bf16[8,8,9216]{2,1,0:T(8,128)(2,1)} %copy-done, bf16[8,4,9216]{2,1,0:T(4,128)(2,1)} %copy-done.18), custom_call_target="tpu_custom_call" | custom-call | tf_op jit(solution)/shard_map/mix_out/pallas_call | solution.py:360
  180.8 17.9 %collective-permute-done.there_ref = bf16[8,4,9216]{2,1,0:T(4,128)(2,1)S(1)} collective-permute-done((bf16[8,4,9216]{2,1,0:T(4,128)(2,1)S(1)}, bf16[8,4,9216]{2,1,0:T(4,128)(2,1)S(1)}, u32[]{:S(2)}, u32[]{:S(2)}) %collective-permute-start) | collective-permute-done | bytes 589856 | tf_op jit(solution)/shard_map/ppermute | solution.py:430
  199.4 10.3 %mix_out.5 = bf16[8,8,9216]{2,1,0:T(8,128)(2,1)} custom-call(s32[2]{0:T(128)} %pad_add_fusion.half_ref, bf16[8,8,9216]{2,1,0:T(8,128)(2,1)} %copy-done.2, bf16[8,4,9216]{2,1,0:T(4,128)(2,1)} %copy-done.19, bf16[8,4,9216]{2,1,0:T(4,128)(2,1)} %mix_out.4.refs_0_), custom_call_target="tpu_custom_call" | custom-call | tf_op jit(solution)/shard_map/mix_out/pallas_call | solution.py:360
  216.8 13.4 %all-to-all-done.2.refs_0_ = bf16[8,8,9216]{2,1,0:T(8,128)(2,1)S(1)} async-done(((bf16[8,8,9216]{2,1,0:T(8,128)(2,1)}), bf16[8,8,9216]{2,1,0:T(8,128)(2,1)S(1)}, u32[]{:S(2)}, u32[]{:S(2)}) %all-to-all-start.2) | async-done | bytes 1179680 | tf_op jit(solution)/shard_map/all_to_all | solution.py:426
  231.2 12.6 %finish.2 = (bf16[9216,128]{1,0:T(8,128)(2,1)}, bf16[8,8,9216]{2,1,0:T(8,128)(2,1)}, bf16[8,8,9216]{2,1,0:T(8,128)(2,1)}, bf16[8,8,9216]{2,1,0:T(8,128)(2,1)}, bf16[8,8,9216]{2,1,0:T(8,128)(2,1)}) custom-call(bf16[8,8,9216]{2,1,0:T(8,128)(2,1)} %copy-done.8, bf16[8,8,9216]{2,1,0:T(8,128)(2,1)} %copy-done.7, bf16[9216,128]{1,0:T(8,128)(2,1)} %bitcast.55, ...), custom_call_target="tpu_custom_call" | custom-call | tf_op jit(solution)/shard_map/finish/pallas_call | solution.py:164
  243.8 20.9 %all_to_all.63.both_ref = bf16[8,8,9216]{2,1,0:T(8,128)(2,1)} all-to-all(bf16[8,8,9216]{2,1,0:T(8,128)(2,1)} %get-tuple-element.32), channel_id=1, replica_groups=mesh['groups'=2,'far'=2,'near'=2,'chan'=2,'sub'=2] {'near','chan','sub'}, dimensions={0} | all-to-all | bytes 2359296 | tf_op jit(solution)/shard_map/all_to_all | solution.py:426
  264.7 19.8 %all_to_all.64.both_ref = bf16[8,8,9216]{2,1,0:T(8,128)(2,1)} all-to-all(bf16[8,8,9216]{2,1,0:T(8,128)(2,1)S(1)} %copy-done.10), channel_id=1, replica_groups=mesh['groups'=2,'far'=2,'near'=2,'chan'=2,'sub'=2] {'near','chan','sub'}, dimensions={0} | all-to-all | bytes 2359296 | tf_op jit(solution)/shard_map/all_to_all | solution.py:426
  284.5 19.7 %all_to_all.65.both_ref = bf16[8,8,9216]{2,1,0:T(8,128)(2,1)} all-to-all(bf16[8,8,9216]{2,1,0:T(8,128)(2,1)S(1)} %copy-done.9), channel_id=1, replica_groups=mesh['groups'=2,'far'=2,'near'=2,'chan'=2,'sub'=2] {'near','chan','sub'}, dimensions={0} | all-to-all | bytes 2359296 | tf_op jit(solution)/shard_map/all_to_all | solution.py:426
  304.2 3.8 all-to-all-start.6
  307.9 9.5 %mix_in.6 = (f32[8,4,9216]{2,1,0:T(4,128)}, bf16[8,4,9216]{2,1,0:T(4,128)(2,1)}) custom-call(s32[2]{0:T(128)} %pad_add_fusion.half_ref, bf16[8,8,9216]{2,1,0:T(8,128)(2,1)} %all_to_all.63.both_ref), custom_call_target="tpu_custom_call" | custom-call | tf_op jit(solution)/shard_map/mix_in/pallas_call | solution.py:402
  320.4 9.6 %mix_in.7 = (f32[8,4,9216]{2,1,0:T(4,128)}, bf16[8,4,9216]{2,1,0:T(4,128)(2,1)}) custom-call(s32[2]{0:T(128)} %pad_add_fusion.half_ref, bf16[8,8,9216]{2,1,0:T(8,128)(2,1)} %all_to_all.64.both_ref), custom_call_target="tpu_custom_call" | custom-call | tf_op jit(solution)/shard_map/mix_in/pallas_call | solution.py:402
  330.0 30.1 %collective-permute-done.6.refs_1_ = bf16[8,4,9216]{2,1,0:T(4,128)(2,1)S(1)} collective-permute-done((bf16[8,4,9216]{2,1,0:T(4,128)(2,1)}, bf16[8,4,9216]{2,1,0:T(4,128)(2,1)S(1)}, u32[]{:S(2)}, u32[]{:S(2)}) %collective-permute-start.6) | collective-permute-done | bytes 589856 | tf_op jit(solution)/shard_map/ppermute | solution.py:430
  360.1 12.1 %collective-permute-done.7.refs_3_ = bf16[8,4,9216]{2,1,0:T(4,128)(2,1)S(1)} collective-permute-done((bf16[8,4,9216]{2,1,0:T(4,128)(2,1)}, bf16[8,4,9216]{2,1,0:T(4,128)(2,1)S(1)}, u32[]{:S(2)}, u32[]{:S(2)}) %collective-permute-start.7) | collective-permute-done | bytes 589856 | tf_op jit(solution)/shard_map/ppermute | solution.py:430
  373.1 4.0 add.5
  381.7 9.5 %mix_in.5 = (f32[8,4,9216]{2,1,0:T(4,128)}, bf16[8,4,9216]{2,1,0:T(4,128)(2,1)}) custom-call(s32[2]{0:T(128)} %pad_add_fusion.half_ref, bf16[8,8,9216]{2,1,0:T(8,128)(2,1)} %all_to_all.65.both_ref), custom_call_target="tpu_custom_call" | custom-call | tf_op jit(solution)/shard_map/mix_in/pallas_call | solution.py:402
  394.1 9.6 %mix_in.4 = (f32[8,4,9216]{2,1,0:T(4,128)}, bf16[8,4,9216]{2,1,0:T(4,128)(2,1)}) custom-call(s32[2]{0:T(128)} %pad_add_fusion.half_ref, bf16[8,8,9216]{2,1,0:T(8,128)(2,1)} %copy-done.6), custom_call_target="tpu_custom_call" | custom-call | tf_op jit(solution)/shard_map/mix_in/pallas_call | solution.py:402
  403.7 30.2 %collective-permute-done.5.refs_3_ = bf16[8,4,9216]{2,1,0:T(4,128)(2,1)S(1)} collective-permute-done((bf16[8,4,9216]{2,1,0:T(4,128)(2,1)}, bf16[8,4,9216]{2,1,0:T(4,128)(2,1)S(1)}, u32[]{:S(2)}, u32[]{:S(2)}) %collective-permute-start.5) | collective-permute-done | bytes 589856 | tf_op jit(solution)/shard_map/ppermute | solution.py:430
  433.9 12.4 %collective-permute-done.4.refs_1_ = bf16[8,4,9216]{2,1,0:T(4,128)(2,1)S(1)} collective-permute-done((bf16[8,4,9216]{2,1,0:T(4,128)(2,1)}, bf16[8,4,9216]{2,1,0:T(4,128)(2,1)S(1)}, u32[]{:S(2)}, u32[]{:S(2)}) %collective-permute-start.4) | collective-permute-done | bytes 589856 | tf_op jit(solution)/shard_map/ppermute | solution.py:430
  447.1 4.0 add.4
  452.1 3.6 all-to-all-start.8
  457.1 14.3 %all-to-all-done.8.refs_0_ = bf16[8,8,9216]{2,1,0:T(8,128)(2,1)S(1)} async-done(((bf16[8,8,9216]{2,1,0:T(8,128)(2,1)}), bf16[8,8,9216]{2,1,0:T(8,128)(2,1)S(1)}, u32[]{:S(2)}, u32[]{:S(2)}) %all-to-all-start.8) | async-done | bytes 1179680 | tf_op jit(solution)/shard_map/all_to_all | solution.py:426
  472.5 7.9 %finish.3 = bf16[9216,128]{1,0:T(8,128)(2,1)} custom-call(bf16[8,8,9216]{2,1,0:T(8,128)(2,1)} %copy-done.5, bf16[8,8,9216]{2,1,0:T(8,128)(2,1)} %copy-done.4, bf16[9216,128]{1,0:T(8,128)(2,1)} %get-tuple-element.38.refs_2_, f32[1,128]{1,0:T(1,128)} %bitcast.77, bf16[128,128]{1,0:T(8,128)(2,1)} %refs_4_.3, f32[128,1]{1,0:T(8,128)} %broadcast_in_dim_reshape.9.refs_5_, ...), custom_call_target="tpu_custom_call" | custom-call | tf_op jit(solution)/shard_map/finish/pallas_call | solution.py:164
  (92 shorter events, 38.1 us)
Async XLA Ops:
  9.2 21.9 %copy-start.12 = (bf16[8,8,9216]{2,1,0:T(8,128)(2,1)S(1)}, bf16[8,8,9216]{2,1,0:T(8,128)(2,1)}, u32[]{:S(2)}) copy-start(bf16[8,8,9216]{2,1,0:T(8,128)(2,1)} %get-tuple-element.24) | copy-start | bytes 3538948
  31.1 42.4 %copy-start.1 = (bf16[8,8,9216]{2,1,0:T(8,128)(2,1)}, bf16[8,8,9216]{2,1,0:T(8,128)(2,1)S(1)}, u32[]{:S(2)}) copy-start(bf16[8,8,9216]{2,1,0:T(8,128)(2,1)S(1)} %all_to_all.60.both_ref) | copy-start | bytes 3538948
  31.1 19.9 %copy-start.11 = (bf16[8,8,9216]{2,1,0:T(8,128)(2,1)S(1)}, bf16[8,8,9216]{2,1,0:T(8,128)(2,1)}, u32[]{:S(2)}) copy-start(bf16[8,8,9216]{2,1,0:T(8,128)(2,1)} %get-tuple-element.23) | copy-start | bytes 3538948
  70.0 73.6 %copy-start = (bf16[8,8,9216]{2,1,0:T(8,128)(2,1)}, bf16[8,8,9216]{2,1,0:T(8,128)(2,1)S(1)}, u32[]{:S(2)}) copy-start(bf16[8,8,9216]{2,1,0:T(8,128)(2,1)S(1)} %all_to_all.62.both_ref) | copy-start | bytes 3538948
  70.0 69.8 %all-to-all-start = ((bf16[8,8,9216]{2,1,0:T(8,128)(2,1)}), bf16[8,8,9216]{2,1,0:T(8,128)(2,1)S(1)}, u32[]{:S(2)}, u32[]{:S(2)}) async-start(bf16[8,8,9216]{2,1,0:T(8,128)(2,1)} %get-tuple-element.22), calls=%async_computation | async-start | bytes 2359296 | tf_op jit(solution)/shard_map/all_to_all | solution.py:426
  73.6 3.7 copy-start.3
  74.7 42.6 %collective-permute-start.3 = (bf16[8,4,9216]{2,1,0:T(4,128)(2,1)}, bf16[8,4,9216]{2,1,0:T(4,128)(2,1)S(1)}, u32[]{:S(2)}, u32[]{:S(2)}) collective-permute-start(bf16[8,4,9216]{2,1,0:T(4,128)(2,1)} %slice.19), channel_id=1, source_target_pairs={{0,8},{8,0},{1,9},{9,1},{2,10},{10,2},{3,11},{11,3},{4,12},{12,4},... | collective-permute-start | bytes 1769480 | tf_op jit(solution)/shard_map/ppermute | solution.py:430
  77.6 51.9 %collective-permute-start.2 = (bf16[8,4,9216]{2,1,0:T(4,128)(2,1)S(1)}, bf16[8,4,9216]{2,1,0:T(4,128)(2,1)}, u32[]{:S(2)}, u32[]{:S(2)}) collective-permute-start(bf16[8,4,9216]{2,1,0:T(4,128)(2,1)S(1)} %slice.18), channel_id=1, source_target_pairs={{0,8},{8,0},{1,9},{9,1},{2,10},{10,2},{3,11},{11,3},{4,12},{12,4},... | collective-permute-start | bytes 1769480 | tf_op jit(solution)/shard_map/ppermute | solution.py:430
  139.8 6.8 %copy-start.2 = (bf16[8,8,9216]{2,1,0:T(8,128)(2,1)}, bf16[8,8,9216]{2,1,0:T(8,128)(2,1)S(1)}, u32[]{:S(2)}) copy-start(bf16[8,8,9216]{2,1,0:T(8,128)(2,1)S(1)} %all-to-all-done.both_ref) | copy-start | bytes 3538948
  139.8 69.9 %all-to-all-start.5 = ((bf16[8,8,9216]{2,1,0:T(8,128)(2,1)}), bf16[8,8,9216]{2,1,0:T(8,128)(2,1)S(1)}, u32[]{:S(2)}, u32[]{:S(2)}) async-start(bf16[8,8,9216]{2,1,0:T(8,128)(2,1)} %mix_out.7), calls=%async_computation.5 | async-start | bytes 2359296 | tf_op jit(solution)/shard_map/all_to_all | solution.py:426
  143.9 26.3 %collective-permute-start.1 = (bf16[8,4,9216]{2,1,0:T(4,128)(2,1)S(1)}, bf16[8,4,9216]{2,1,0:T(4,128)(2,1)S(1)}, u32[]{:S(2)}, u32[]{:S(2)}) collective-permute-start(bf16[8,4,9216]{2,1,0:T(4,128)(2,1)S(1)} %slice.17), channel_id=1, source_target_pairs={{0,8},{8,0},{1,9},{9,1},{2,10},{10,2},{3,11},{11,3},{4,12},{12,4},... | collective-permute-start | bytes 1769480 | tf_op jit(solution)/shard_map/ppermute | solution.py:430
  147.0 51.6 %collective-permute-start = (bf16[8,4,9216]{2,1,0:T(4,128)(2,1)S(1)}, bf16[8,4,9216]{2,1,0:T(4,128)(2,1)S(1)}, u32[]{:S(2)}, u32[]{:S(2)}) collective-permute-start(bf16[8,4,9216]{2,1,0:T(4,128)(2,1)S(1)} %slice.16), channel_id=1, source_target_pairs={{0,8},{8,0},{1,9},{9,1},{2,10},{10,2},{3,11},{11,3},{4,12},{12,4},... | collective-permute-start | bytes 1769480 | tf_op jit(solution)/shard_map/ppermute | solution.py:430
  209.7 4.6 copy-start.20
  209.7 4.9 %copy-start.23 = (f32[128]{0:T(128)S(1)}, f32[128]{0:T(128)}, u32[]{:S(2)}) copy-start(f32[128]{0:T(128)} %param.15) | copy-start | bytes 1540
  209.7 5.7 %copy-start.21 = (bf16[128,128]{1,0:T(8,128)(2,1)S(1)}, bf16[128,128]{1,0:T(8,128)(2,1)}, u32[]{:S(2)}) copy-start(bf16[128,128]{1,0:T(8,128)(2,1)} %param.16) | copy-start | bytes 98308
  209.7 1.0 copy-start.7
  210.8 19.4 %all-to-all-start.2 = ((bf16[8,8,9216]{2,1,0:T(8,128)(2,1)}), bf16[8,8,9216]{2,1,0:T(8,128)(2,1)S(1)}, u32[]{:S(2)}, u32[]{:S(2)}) async-start(bf16[8,8,9216]{2,1,0:T(8,128)(2,1)} %mix_out.5), calls=%async_computation.2 | async-start | bytes 2359296 | tf_op jit(solution)/shard_map/all_to_all | solution.py:426
  243.7 20.9 %copy-start.10 = (bf16[8,8,9216]{2,1,0:T(8,128)(2,1)S(1)}, bf16[8,8,9216]{2,1,0:T(8,128)(2,1)}, u32[]{:S(2)}) copy-start(bf16[8,8,9216]{2,1,0:T(8,128)(2,1)} %get-tuple-element.35) | copy-start | bytes 3538948
  264.7 19.8 %copy-start.9 = (bf16[8,8,9216]{2,1,0:T(8,128)(2,1)S(1)}, bf16[8,8,9216]{2,1,0:T(8,128)(2,1)}, u32[]{:S(2)}) copy-start(bf16[8,8,9216]{2,1,0:T(8,128)(2,1)} %get-tuple-element.29) | copy-start | bytes 3538948
  304.2 72.9 %all-to-all-start.6 = ((bf16[8,8,9216]{2,1,0:T(8,128)(2,1)}), bf16[8,8,9216]{2,1,0:T(8,128)(2,1)S(1)}, u32[]{:S(2)}, u32[]{:S(2)}) async-start(bf16[8,8,9216]{2,1,0:T(8,128)(2,1)} %get-tuple-element.26), calls=%async_computation.6 | async-start | bytes 2359296 | tf_op jit(solution)/shard_map/all_to_all | solution.py:426
  317.5 42.7 %collective-permute-start.6 = (bf16[8,4,9216]{2,1,0:T(4,128)(2,1)}, bf16[8,4,9216]{2,1,0:T(4,128)(2,1)S(1)}, u32[]{:S(2)}, u32[]{:S(2)}) collective-permute-start(bf16[8,4,9216]{2,1,0:T(4,128)(2,1)} %get-tuple-element.34), channel_id=1, source_target_pairs={{0,8},{8,0},{1,9},{9,1},{2,10},{10,2},{3,11},{11,3},{4,12},{12,4},... | collective-permute-start | bytes 1769480 | tf_op jit(solution)/shard_map/ppermute | solution.py:430
  330.0 42.2 %collective-permute-start.7 = (bf16[8,4,9216]{2,1,0:T(4,128)(2,1)}, bf16[8,4,9216]{2,1,0:T(4,128)(2,1)S(1)}, u32[]{:S(2)}, u32[]{:S(2)}) collective-permute-start(bf16[8,4,9216]{2,1,0:T(4,128)(2,1)} %get-tuple-element.37), channel_id=1, source_target_pairs={{0,8},{8,0},{1,9},{9,1},{2,10},{10,2},{3,11},{11,3},{4,12},{12,4},... | collective-permute-start | bytes 1769480 | tf_op jit(solution)/shard_map/ppermute | solution.py:430
  360.1 12.1 %copy-start.14 = (bf16[8,4,9216]{2,1,0:T(4,128)(2,1)}, bf16[8,4,9216]{2,1,0:T(4,128)(2,1)S(1)}, u32[]{:S(2)}) copy-start(bf16[8,4,9216]{2,1,0:T(4,128)(2,1)S(1)} %collective-permute-done.6.refs_1_) | copy-start | bytes 1769476
  378.1 72.9 %all-to-all-start.11 = ((bf16[8,8,9216]{2,1,0:T(8,128)(2,1)}), bf16[8,8,9216]{2,1,0:T(8,128)(2,1)S(1)}, u32[]{:S(2)}, u32[]{:S(2)}) async-start(bf16[8,8,9216]{2,1,0:T(8,128)(2,1)} %add.5), calls=%async_computation.11 | async-start | bytes 2359296 | tf_op jit(solution)/shard_map/all_to_all | solution.py:426
  391.2 42.6 %collective-permute-start.5 = (bf16[8,4,9216]{2,1,0:T(4,128)(2,1)}, bf16[8,4,9216]{2,1,0:T(4,128)(2,1)S(1)}, u32[]{:S(2)}, u32[]{:S(2)}) collective-permute-start(bf16[8,4,9216]{2,1,0:T(4,128)(2,1)} %get-tuple-element.31), channel_id=1, source_target_pairs={{0,8},{8,0},{1,9},{9,1},{2,10},{10,2},{3,11},{11,3},{4,12},{12,4},... | collective-permute-start | bytes 1769480 | tf_op jit(solution)/shard_map/ppermute | solution.py:430
  403.6 42.6 %collective-permute-start.4 = (bf16[8,4,9216]{2,1,0:T(4,128)(2,1)}, bf16[8,4,9216]{2,1,0:T(4,128)(2,1)S(1)}, u32[]{:S(2)}, u32[]{:S(2)}) collective-permute-start(bf16[8,4,9216]{2,1,0:T(4,128)(2,1)} %get-tuple-element.28), channel_id=1, source_target_pairs={{0,8},{8,0},{1,9},{9,1},{2,10},{10,2},{3,11},{11,3},{4,12},{12,4},... | collective-permute-start | bytes 1769480 | tf_op jit(solution)/shard_map/ppermute | solution.py:430
  433.9 12.4 %copy-start.13 = (bf16[8,4,9216]{2,1,0:T(4,128)(2,1)}, bf16[8,4,9216]{2,1,0:T(4,128)(2,1)S(1)}, u32[]{:S(2)}) copy-start(bf16[8,4,9216]{2,1,0:T(4,128)(2,1)S(1)} %collective-permute-done.5.refs_3_) | copy-start | bytes 1769476
  451.0 4.6 copy-start.24
  451.0 5.5 %copy-start.22 = (bf16[128,128]{1,0:T(8,128)(2,1)S(1)}, bf16[128,128]{1,0:T(8,128)(2,1)}, u32[]{:S(2)}) copy-start(bf16[128,128]{1,0:T(8,128)(2,1)} %param.21) | copy-start | bytes 98308
  451.0 1.0 copy-start.4
  452.1 19.4 %all-to-all-start.8 = ((bf16[8,8,9216]{2,1,0:T(8,128)(2,1)}), bf16[8,8,9216]{2,1,0:T(8,128)(2,1)S(1)}, u32[]{:S(2)}, u32[]{:S(2)}) async-start(bf16[8,8,9216]{2,1,0:T(8,128)(2,1)} %add.4), calls=%async_computation.8 | async-start | bytes 2359296 | tf_op jit(solution)/shard_map/all_to_all | solution.py:426
  471.4 1.0 copy-start.5
  (7 other events, 6.1 us)

commit v7 on v6

--- a/solution.py
+++ b/solution.py
@@ -78,6 +78,20 @@
     return row_parts // near, near
 
 
+def lane_mean(values):
+    lanes = values.shape[1]
+    return jnp.dot(values, jnp.full((lanes, lanes), 1 / lanes, jnp.bfloat16), preferred_element_type=jnp.float32)
+
+
+def lane_norm(values, norm_gain):
+    centred = values.astype(jnp.float32) - lane_mean(values)
+    squares = centred * centred
+    high = squares.astype(jnp.bfloat16)
+    low = (squares - high.astype(jnp.float32)).astype(jnp.bfloat16)
+    variance = lane_mean(high) + lane_mean(low)
+    return centred * lax.rsqrt(variance + epsilon) * norm_gain
+
+
 def emit_projections(normed, rows_ref, out_refs):
     step = normed.shape[0]
     half = rows_ref.shape[0] // 2
@@ -96,7 +110,7 @@
 
 
 def project_kernel(state_ref, gain_ref, rows_ref, *out_refs):
-    normed = layer_norm(state_ref[...].astype(jnp.float32), gain_ref[...], 1).astype(jnp.bfloat16)
+    normed = lane_norm(state_ref[...], gain_ref[...]).astype(jnp.bfloat16)
     emit_projections(normed, rows_ref, out_refs)
 
 
@@ -104,7 +118,7 @@
     mix_refs, refs = refs[:pieces], refs[pieces:]
     state_ref, gain_ref, gate_ref, out_gain_ref, final_ref = refs[:5]
     state = state_ref[...].astype(jnp.float32)
-    normed = layer_norm(state, gain_ref[...], 1).astype(jnp.bfloat16)
+    normed = lane_norm(state_ref[...], gain_ref[...]).astype(jnp.bfloat16)
     gating = sigmoid(jnp.dot(normed, gate_ref[...], preferred_element_type=jnp.float32))
     mixed = jnp.concatenate(
         [ref[part].astype(jnp.float32) for ref in mix_refs for part in range(ref.shape[0])], axis=0
@@ -117,7 +131,7 @@
     if onward:
         next_gain, rows_ref, middle_ref = refs[5:8]
         middle_ref[...] = result
-        normed = layer_norm(result.astype(jnp.float32), next_gain[...], 1).astype(jnp.bfloat16)
+        normed = lane_norm(result, next_gain[...]).astype(jnp.bfloat16)
         emit_projections(normed, rows_ref, refs[8:])
     else:
         refs[5][...] = result
@@ -171,7 +185,7 @@
         out_shape=out_shape,
         compiler_params=pltpu.CompilerParams(vmem_limit_bytes=BUDGET),
         name="finish",
-    )(*mixes, state, *weights)
+    )(*(pltpu.with_memory_space_constraint(m, pltpu.HBM) for m in mixes), state, *weights)
 
 
 class Folds:
@@ -420,6 +434,12 @@
 
 
 PIECES = 4
+OUT_GROUPS = ((0, 2), (2, 1), (3, 1))
+IN_GROUPS = ((0, 2), (2, 2))
+
+
+def group_of(groups, piece):
+    return next((begin, count, at) for at, (begin, count) in enumerate(groups) if begin <= piece < begin + count)
 
 
 def exchange(array):
@@ -444,42 +464,47 @@
     def by_piece(rows):
         return rows.reshape(parts, pieces, width // pieces, -1).transpose(1, 0, 2, 3)
 
-    def rows_of(project, order):
-        ga, va, gb, vb = (by_piece(rows) for rows in jnp.split(project.T, 4, axis=0))
-        return jnp.concatenate([order(ga, gb).reshape(-1, features), order(va, vb).reshape(-1, features)])
-
-    def side_by_side(left, right):
-        return jnp.concatenate([left, right], axis=2)
-
-    def unordered(array):
-        rows = array.reshape(parts, pieces // 2, 2 * piece_width, -1)
-        return rows.transpose(1, 0, 2, 3).reshape(array.shape)
+    def rows_of(project, begin, end):
+        ga, va, gb, vb = (by_piece(rows)[begin:end] for rows in jnp.split(project.T, 4, axis=0))
+        gates, values = jnp.concatenate([ga, gb], axis=2), jnp.concatenate([va, vb], axis=2)
+        return jnp.concatenate([gates.reshape(-1, features), values.reshape(-1, features)])
+
+    def in_groups(array, groups):
+        rows = by_piece(array.reshape(features, -1))
+        ordered = [rows[begin : begin + count].transpose(1, 0, 2, 3).reshape(-1, rows.shape[-1]) for begin, count in groups]
+        return jnp.concatenate(ordered).reshape(array.shape)
 
     gain_1, project_1, gate_1, norm_1, final_1, gain_2, project_2, gate_2, norm_2, final_2 = weights
     state = pair_input.reshape(-1, features)
 
     shapes = ((parts, 2 * piece_width),) * pieces
-    both, mixes = [], []
-    out = run_projections(state, gain_1, rows_of(project_1, side_by_side), shapes)
+    mixed, both, mixes = None, [], []
+    out = run_projections(state, gain_1, rows_of(project_1, 0, 1), shapes[:1])
+    out += run_projections(state, gain_1, rows_of(project_1, 1, pieces), shapes[1:])
     for piece in range(pieces):
         both.append(exchange(out[piece]))
     for piece in range(pieces):
+        begin, count, _ = group_of(OUT_GROUPS, piece)
         there = across(both[piece][:, piece_width:, :])
-        mixed = run_mix_out(folds, near, cols, halves, both[piece], there, (mixed,) if piece % 2 else ())
-        if piece % 2:
+        mixed = run_mix_out(folds, near, cols, halves, both[piece], there, (mixed,) if piece > begin else ())
+        if piece == begin + count - 1:
             mixes.append(exchange(mixed))
-    onward = (gain_2, rows_of(project_2, side_by_side), shapes)
-    out = run_finish(mixes, state, gain_1, gate_1, unordered(norm_1), unordered(final_1), onward)
-    middle, both, parted, mixes = out[0], [], [], []
+    onward = (gain_2, rows_of(project_2, 0, 1), shapes[:1])
+    norm, final = in_groups(norm_1, OUT_GROUPS), in_groups(final_1, OUT_GROUPS)
+    middle, *out = run_finish(mixes, state, gain_1, gate_1, norm, final, onward)
+    out += run_projections(middle, gain_2, rows_of(project_2, 1, pieces), shapes[1:])
+    both, parted, mixes = [], [], []
     for piece in range(pieces):
-        both.append(exchange(out[1 + piece]))
+        both.append(exchange(out[piece]))
     for piece in range(pieces):
         kept, sent = run_mix_in(folds, near, cols, halves, both[piece])
         parted.append((kept, across(sent)))
-    for pair in range(pieces // 2):
-        mixed = run_add(*parted[2 * pair], *parted[2 * pair + 1])
+    for begin, count in IN_GROUPS:
+        last = begin + count - 1
+        mixed = run_add(*(array for pair in parted[begin : last + 1] for array in pair))
         mixes.append(exchange(mixed))
-    result = run_finish(mixes, middle, gain_2, gate_2, unordered(norm_2), unordered(final_2))[0]
+    norm, final = in_groups(norm_2, IN_GROUPS), in_groups(final_2, IN_GROUPS)
+    result = run_finish(mixes, middle, gain_2, gate_2, norm, final)[0]
     return result.reshape(pair_input.shape)
 
 

time: 482 us -> 501 us (1.039)
  blocking collectives: 121 us -> 79.7 us
  waiting for transfers between devices: 194 us -> 216 us
  starting transfers between devices: 33.7 us -> 53.5 us
  Pallas kernels: 114 us -> 128 us
    all_to_all x6 -> x4, blocking collectives: 121 us -> 79.7 us  [exchange(): return lax.all_to_all(array, EVERY, split_axis=0, concat_axis=0, tiled=True)]
    all_to_all x6 -> x9, starting transfers between devices: 21.8 us -> 38.2 us  [exchange(): return lax.all_to_all(array, EVERY, split_axis=0, concat_axis=0, tiled=True)]
    all_to_all x6 -> x9, waiting for transfers between devices: 27.7 us -> 43.6 us  [exchange(): return lax.all_to_all(array, EVERY, split_axis=0, concat_axis=0, tiled=True)]
    pallas_call x1 -> x3, Pallas kernels: 7.33 us -> 21.2 us  [run_projections(): pl.pallas_call(project_kernel, grid=(positions // step,), in_specs=[pl.Bl...]
    ppermute x8, waiting for transfers between devices: 166 us -> 173 us  [across(): return lax.ppermute(array, 'far', ((0, 1), (1, 0)))]
  transfers between devices with their start and end apart: 14 -> 17, of which waited for: 10 -> 12; matrix products, arithmetic and copies ran while one was open for 1% -> 2% of each run, Pallas kernels for 18% -> 20%
where the time goes in v7:
time: 501 us; the launch traced here: 500 us
  waiting for transfers between devices  216 us (43%)
  Pallas kernels  128 us (26%)
  blocking collectives  79.7 us (16%)
  starting transfers between devices  53.5 us (11%)
  local copies, waits for them, and re-layouts  16.9 us (3%)
    ppermute x8, waiting for transfers between devices, across(): return lax.ppermute(array, 'far', ((0, 1), (1, 0)))  173 us
    all_to_all x4, blocking collectives, exchange(): return lax.all_to_all(array, EVERY, split_axis=0, concat_axis=0, tiled=True)  79.7 us
    all_to_all x9, waiting for transfers between devices, exchange(): return lax.all_to_all(array, EVERY, split_axis=0, concat_axis=0, tiled=True)  43.6 us
    pallas_call x4, Pallas kernels, run_mix_out(): pl.pallas_call(functools.partial(mix_out_kernel, folds, near, cols, width...  39.5 us
    pallas_call x4, Pallas kernels, run_mix_in(): pl.pallas_call(functools.partial(mix_in_kernel, folds, near, cols, width)...  38.3 us
    all_to_all x9, starting transfers between devices, exchange(): return lax.all_to_all(array, EVERY, split_axis=0, concat_axis=0, tiled=True)  38.2 us
    pallas_call x2, Pallas kernels, run_finish(): pl.pallas_call(functools.partial(finish_kernel, len(mixes), onward is not...  21.4 us
    pallas_call x3, Pallas kernels, run_projections(): pl.pallas_call(project_kernel, grid=(positions // step,), in_specs=[pl.Bl...  21.2 us
  transfers between devices with their start and end apart: 17, of which 12 were waited for; matrix products, arithmetic and copies ran while one was open for 2% of the time, Pallas kernels for 20%

profile of v7, /device:TPU:0, one launch (start us, length us, event | category | flops | bytes accessed | tf_op | source)
XLA Modules:
  0.0 499.9 jit_solution(3151975376513354047)
XLA Ops:
  1.9 7.5 %project.3 = (bf16[8,8,9216]{2,1,0:T(8,128)(2,1)}, bf16[8,8,9216]{2,1,0:T(8,128)(2,1)}, bf16[8,8,9216]{2,1,0:T(8,128)(2,1)}) custom-call(bf16[9216,128]{1,0:T(8,128)(2,1)} %bitcast.76, f32[1,128]{1,0:T(1,128)} %bitcast.116, bf16[384,128]{1,0:T(8,128)(2,1)} %pad_maximum_fusion.rows_ref), custom_call_target="tpu_custom_call" | custom-call | tf_op jit(solution)/shard_map/project/pallas_call | solution.py:156
  9.4 5.3 %all-to-all-start = ((bf16[8,8,9216]{2,1,0:T(8,128)(2,1)}), bf16[8,8,9216]{2,1,0:T(8,128)(2,1)}, u32[]{:S(2)}, u32[]{:S(2)}) async-start(bf16[8,8,9216]{2,1,0:T(8,128)(2,1)} %get-tuple-element.21), calls=%async_computation | async-start | bytes 2359296 | tf_op jit(solution)/shard_map/all_to_all | solution.py:446
  15.3 6.2 %project.4 = bf16[8,8,9216]{2,1,0:T(8,128)(2,1)} custom-call(bf16[9216,128]{1,0:T(8,128)(2,1)} %bitcast.77, f32[1,128]{1,0:T(1,128)} %bitcast.117, bf16[128,128]{1,0:T(8,128)(2,1)} %pad_maximum_fusion.6.rows_ref), custom_call_target="tpu_custom_call" | custom-call | tf_op jit(solution)/shard_map/project/pallas_call | solution.py:156
  21.5 9.1 %all-to-all-done.both_ref = bf16[8,8,9216]{2,1,0:T(8,128)(2,1)} async-done(((bf16[8,8,9216]{2,1,0:T(8,128)(2,1)}), bf16[8,8,9216]{2,1,0:T(8,128)(2,1)}, u32[]{:S(2)}, u32[]{:S(2)}) %all-to-all-start) | async-done | bytes 1179680 | tf_op jit(solution)/shard_map/all_to_all | solution.py:446
  30.6 20.0 %all_to_all.65.both_ref = bf16[8,8,9216]{2,1,0:T(8,128)(2,1)S(1)} all-to-all(bf16[8,8,9216]{2,1,0:T(8,128)(2,1)} %project.4), channel_id=1, replica_groups=mesh['groups'=2,'far'=2,'near'=2,'chan'=2,'sub'=2] {'near','chan','sub'}, dimensions={0} | all-to-all | bytes 2359296 | tf_op jit(solution)/shard_map/all_to_all | solution.py:446
  50.6 18.9 %all_to_all.66.both_ref = bf16[8,8,9216]{2,1,0:T(8,128)(2,1)S(1)} all-to-all(bf16[8,8,9216]{2,1,0:T(8,128)(2,1)S(1)} %copy-done.10), channel_id=1, replica_groups=mesh['groups'=2,'far'=2,'near'=2,'chan'=2,'sub'=2] {'near','chan','sub'}, dimensions={0} | all-to-all | bytes 2359296 | tf_op jit(solution)/shard_map/all_to_all | solution.py:446
  77.9 21.8 %collective-permute-done.2.there_ref = bf16[8,4,9216]{2,1,0:T(4,128)(2,1)S(1)} collective-permute-done((bf16[8,4,9216]{2,1,0:T(4,128)(2,1)}, bf16[8,4,9216]{2,1,0:T(4,128)(2,1)S(1)}, u32[]{:S(2)}, u32[]{:S(2)}) %collective-permute-start.2) | collective-permute-done | bytes 589856 | tf_op jit(solution)/shard_map/ppermute | solution.py:450
  100.5 9.7 %mix_out.6 = bf16[8,4,9216]{2,1,0:T(4,128)(2,1)} custom-call(s32[2]{0:T(128)} %pad_add_fusion.half_ref, bf16[8,8,9216]{2,1,0:T(8,128)(2,1)} %copy-done.2, bf16[8,4,9216]{2,1,0:T(4,128)(2,1)} %copy-done.16), custom_call_target="tpu_custom_call" | custom-call | tf_op jit(solution)/shard_map/mix_out/pallas_call | solution.py:374
  110.2 7.6 %all-to-all-start.4 = ((bf16[8,4,9216]{2,1,0:T(4,128)(2,1)}), bf16[8,4,9216]{2,1,0:T(4,128)(2,1)S(1)}, u32[]{:S(2)}, u32[]{:S(2)}) async-start(bf16[8,4,9216]{2,1,0:T(4,128)(2,1)} %mix_out.6), calls=%async_computation.4 | async-start | bytes 1179648 | tf_op jit(solution)/shard_map/all_to_all | solution.py:446
  121.5 26.7 %collective-permute-done.3.there_ref = bf16[8,4,9216]{2,1,0:T(4,128)(2,1)S(1)} collective-permute-done((bf16[8,4,9216]{2,1,0:T(4,128)(2,1)S(1)}, bf16[8,4,9216]{2,1,0:T(4,128)(2,1)S(1)}, u32[]{:S(2)}, u32[]{:S(2)}) %collective-permute-start.3) | collective-permute-done | bytes 589856 | tf_op jit(solution)/shard_map/ppermute | solution.py:450
  149.0 9.7 %mix_out.7 = bf16[8,4,9216]{2,1,0:T(4,128)(2,1)} custom-call(s32[2]{0:T(128)} %pad_add_fusion.half_ref, bf16[8,8,9216]{2,1,0:T(8,128)(2,1)} %copy-done.1, bf16[8,4,9216]{2,1,0:T(4,128)(2,1)} %copy-done.18), custom_call_target="tpu_custom_call" | custom-call | tf_op jit(solution)/shard_map/mix_out/pallas_call | solution.py:374
  167.4 37.9 %collective-permute-done.1.there_ref = bf16[8,4,9216]{2,1,0:T(4,128)(2,1)S(1)} collective-permute-done((bf16[8,4,9216]{2,1,0:T(4,128)(2,1)S(1)}, bf16[8,4,9216]{2,1,0:T(4,128)(2,1)S(1)}, u32[]{:S(2)}, u32[]{:S(2)}) %collective-permute-start.1) | collective-permute-done | bytes 589856 | tf_op jit(solution)/shard_map/ppermute | solution.py:450
  206.1 9.7 %mix_out.4.refs_0_ = bf16[8,4,9216]{2,1,0:T(4,128)(2,1)} custom-call(s32[2]{0:T(128)} %pad_add_fusion.half_ref, bf16[8,8,9216]{2,1,0:T(8,128)(2,1)} %copy-done, bf16[8,4,9216]{2,1,0:T(4,128)(2,1)} %copy-done.17), custom_call_target="tpu_custom_call" | custom-call | tf_op jit(solution)/shard_map/mix_out/pallas_call | solution.py:374
  218.4 10.3 %mix_out.5 = bf16[8,8,9216]{2,1,0:T(8,128)(2,1)} custom-call(s32[2]{0:T(128)} %pad_add_fusion.half_ref, bf16[8,8,9216]{2,1,0:T(8,128)(2,1)} %all-to-all-done.both_ref, bf16[8,4,9216]{2,1,0:T(4,128)(2,1)} %copy-done.19, bf16[8,4,9216]{2,1,0:T(4,128)(2,1)} %mix_out.4.refs_0_), custom_call_target="tpu_custom_call" | custom-call | tf_op jit(solution)/shard_map/mix_out/pallas_call | solution.py:374
  235.9 13.0 %all-to-all-done.2.refs_0_ = bf16[8,8,9216]{2,1,0:T(8,128)(2,1)S(1)} async-done(((bf16[8,8,9216]{2,1,0:T(8,128)(2,1)}), bf16[8,8,9216]{2,1,0:T(8,128)(2,1)S(1)}, u32[]{:S(2)}, u32[]{:S(2)}) %all-to-all-start.2) | async-done | bytes 1179680 | tf_op jit(solution)/shard_map/all_to_all | solution.py:446
  249.9 12.4 %finish.2 = (bf16[9216,128]{1,0:T(8,128)(2,1)}, bf16[8,8,9216]{2,1,0:T(8,128)(2,1)}) custom-call(bf16[8,8,9216]{2,1,0:T(8,128)(2,1)} %copy-done.7, bf16[8,4,9216]{2,1,0:T(4,128)(2,1)} %copy-done.8, bf16[8,4,9216]{2,1,0:T(4,128)(2,1)} %copy-done.9, bf16[9216,128]{1,0:T(8,128)(2,1)} %bitcast.78, f32[1,128]{1,0:T(1,128)} %bitcast.118, ...), custom_call_target="tpu_custom_call" | custom-call | tf_op jit(solution)/shard_map/finish/pallas_call | solution.py:178
  266.7 7.5 %project.5 = (bf16[8,8,9216]{2,1,0:T(8,128)(2,1)}, bf16[8,8,9216]{2,1,0:T(8,128)(2,1)}, bf16[8,8,9216]{2,1,0:T(8,128)(2,1)}) custom-call(bf16[9216,128]{1,0:T(8,128)(2,1)} %get-tuple-element.27.state_ref.refs_2_, f32[1,128]{1,0:T(1,128)} %bitcast.114, bf16[384,128]{1,0:T(8,128)(2,1)} %pad_maximum_fusion.1.rows_ref), custom_call_target="tpu_custom_call" | custom-call | tf_op jit(solution)/shard_map/project/pallas_call | solution.py:156
  274.2 7.5 %all-to-all-done.7.both_ref = bf16[8,8,9216]{2,1,0:T(8,128)(2,1)S(1)} async-done(((bf16[8,8,9216]{2,1,0:T(8,128)(2,1)}), bf16[8,8,9216]{2,1,0:T(8,128)(2,1)S(1)}, u32[]{:S(2)}, u32[]{:S(2)}) %all-to-all-start.7) | async-done | bytes 1179680 | tf_op jit(solution)/shard_map/all_to_all | solution.py:446
  281.7 21.0 %all_to_all.67.both_ref = bf16[8,8,9216]{2,1,0:T(8,128)(2,1)} all-to-all(bf16[8,8,9216]{2,1,0:T(8,128)(2,1)} %get-tuple-element.28), channel_id=1, replica_groups=mesh['groups'=2,'far'=2,'near'=2,'chan'=2,'sub'=2] {'near','chan','sub'}, dimensions={0} | all-to-all | bytes 2359296 | tf_op jit(solution)/shard_map/all_to_all | solution.py:446
  302.8 19.7 %all_to_all.68.both_ref = bf16[8,8,9216]{2,1,0:T(8,128)(2,1)} all-to-all(bf16[8,8,9216]{2,1,0:T(8,128)(2,1)S(1)} %copy-done.11), channel_id=1, replica_groups=mesh['groups'=2,'far'=2,'near'=2,'chan'=2,'sub'=2] {'near','chan','sub'}, dimensions={0} | all-to-all | bytes 2359296 | tf_op jit(solution)/shard_map/all_to_all | solution.py:446
  326.2 9.6 %mix_in.4 = (f32[8,4,9216]{2,1,0:T(4,128)}, bf16[8,4,9216]{2,1,0:T(4,128)(2,1)}) custom-call(s32[2]{0:T(128)} %pad_add_fusion.half_ref, bf16[8,8,9216]{2,1,0:T(8,128)(2,1)} %copy-done.6), custom_call_target="tpu_custom_call" | custom-call | tf_op jit(solution)/shard_map/mix_in/pallas_call | solution.py:416
  338.7 9.6 %mix_in.5 = (f32[8,4,9216]{2,1,0:T(4,128)}, bf16[8,4,9216]{2,1,0:T(4,128)(2,1)}) custom-call(s32[2]{0:T(128)} %pad_add_fusion.half_ref, bf16[8,8,9216]{2,1,0:T(8,128)(2,1)} %all_to_all.67.both_ref), custom_call_target="tpu_custom_call" | custom-call | tf_op jit(solution)/shard_map/mix_in/pallas_call | solution.py:416
  348.3 30.1 %collective-permute-done.4.refs_1_ = bf16[8,4,9216]{2,1,0:T(4,128)(2,1)S(1)} collective-permute-done((bf16[8,4,9216]{2,1,0:T(4,128)(2,1)}, bf16[8,4,9216]{2,1,0:T(4,128)(2,1)S(1)}, u32[]{:S(2)}, u32[]{:S(2)}) %collective-permute-start.4) | collective-permute-done | bytes 589856 | tf_op jit(solution)/shard_map/ppermute | solution.py:450
  378.4 12.1 %collective-permute-done.5.refs_3_ = bf16[8,4,9216]{2,1,0:T(4,128)(2,1)S(1)} collective-permute-done((bf16[8,4,9216]{2,1,0:T(4,128)(2,1)}, bf16[8,4,9216]{2,1,0:T(4,128)(2,1)S(1)}, u32[]{:S(2)}, u32[]{:S(2)}) %collective-permute-start.5) | collective-permute-done | bytes 589856 | tf_op jit(solution)/shard_map/ppermute | solution.py:450
  391.4 4.0 add.10
  400.0 9.6 %mix_in.6 = (f32[8,4,9216]{2,1,0:T(4,128)}, bf16[8,4,9216]{2,1,0:T(4,128)(2,1)}) custom-call(s32[2]{0:T(128)} %pad_add_fusion.half_ref, bf16[8,8,9216]{2,1,0:T(8,128)(2,1)} %all_to_all.68.both_ref), custom_call_target="tpu_custom_call" | custom-call | tf_op jit(solution)/shard_map/mix_in/pallas_call | solution.py:416
  412.5 9.6 %mix_in.7 = (f32[8,4,9216]{2,1,0:T(4,128)}, bf16[8,4,9216]{2,1,0:T(4,128)(2,1)}) custom-call(s32[2]{0:T(128)} %pad_add_fusion.half_ref, bf16[8,8,9216]{2,1,0:T(8,128)(2,1)} %copy-done.5), custom_call_target="tpu_custom_call" | custom-call | tf_op jit(solution)/shard_map/mix_in/pallas_call | solution.py:416
  422.1 30.2 %collective-permute-done.6.refs_1_ = bf16[8,4,9216]{2,1,0:T(4,128)(2,1)S(1)} collective-permute-done((bf16[8,4,9216]{2,1,0:T(4,128)(2,1)}, bf16[8,4,9216]{2,1,0:T(4,128)(2,1)S(1)}, u32[]{:S(2)}, u32[]{:S(2)}) %collective-permute-start.6) | collective-permute-done | bytes 589856 | tf_op jit(solution)/shard_map/ppermute | solution.py:450
  452.3 12.4 %collective-permute-done.7.refs_3_ = bf16[8,4,9216]{2,1,0:T(4,128)(2,1)S(1)} collective-permute-done((bf16[8,4,9216]{2,1,0:T(4,128)(2,1)}, bf16[8,4,9216]{2,1,0:T(4,128)(2,1)S(1)}, u32[]{:S(2)}, u32[]{:S(2)}) %collective-permute-start.7) | collective-permute-done | bytes 589856 | tf_op jit(solution)/shard_map/ppermute | solution.py:450
  465.5 4.0 add.11
  475.9 14.0 %all-to-all-done.12.refs_1_ = bf16[8,8,9216]{2,1,0:T(8,128)(2,1)S(1)} async-done(((bf16[8,8,9216]{2,1,0:T(8,128)(2,1)}), bf16[8,8,9216]{2,1,0:T(8,128)(2,1)S(1)}, u32[]{:S(2)}, u32[]{:S(2)}) %all-to-all-start.12) | async-done | bytes 1179680 | tf_op jit(solution)/shard_map/all_to_all | solution.py:446
  490.9 9.0 %finish.3 = bf16[9216,128]{1,0:T(8,128)(2,1)} custom-call(bf16[8,8,9216]{2,1,0:T(8,128)(2,1)} %copy-done.3, bf16[8,8,9216]{2,1,0:T(8,128)(2,1)} %copy-done.4, bf16[9216,128]{1,0:T(8,128)(2,1)} %get-tuple-element.27.state_ref.refs_2_, f32[1,128]{1,0:T(1,128)} %bitcast.115, bf16[128,128]{1,0:T(8,128)(2,1)} %refs_4_.1, f32[128,1]{1,0:T(8,128)} %copy.49.refs_5_, ...), custom_call_target="tpu_custom_call" | custom-call | tf_op jit(solution)/shard_map/finish/pallas_call | solution.py:178
  (131 shorter events, 63.8 us)
Async XLA Ops:
  9.4 21.2 %all-to-all-start = ((bf16[8,8,9216]{2,1,0:T(8,128)(2,1)}), bf16[8,8,9216]{2,1,0:T(8,128)(2,1)}, u32[]{:S(2)}, u32[]{:S(2)}) async-start(bf16[8,8,9216]{2,1,0:T(8,128)(2,1)} %get-tuple-element.21), calls=%async_computation | async-start | bytes 2359296 | tf_op jit(solution)/shard_map/all_to_all | solution.py:446
  21.5 29.1 %copy-start.10 = (bf16[8,8,9216]{2,1,0:T(8,128)(2,1)S(1)}, bf16[8,8,9216]{2,1,0:T(8,128)(2,1)}, u32[]{:S(2)}) copy-start(bf16[8,8,9216]{2,1,0:T(8,128)(2,1)} %get-tuple-element.22) | copy-start | bytes 3538948
  50.6 111.8 %copy-start = (bf16[8,8,9216]{2,1,0:T(8,128)(2,1)}, bf16[8,8,9216]{2,1,0:T(8,128)(2,1)S(1)}, u32[]{:S(2)}) copy-start(bf16[8,8,9216]{2,1,0:T(8,128)(2,1)S(1)} %all_to_all.65.both_ref) | copy-start | bytes 3538948
  69.6 3.6 copy-start.2
  69.6 40.6 %all-to-all-start.5 = ((bf16[8,8,9216]{2,1,0:T(8,128)(2,1)}), bf16[8,8,9216]{2,1,0:T(8,128)(2,1)S(1)}, u32[]{:S(2)}, u32[]{:S(2)}) async-start(bf16[8,8,9216]{2,1,0:T(8,128)(2,1)} %get-tuple-element.23), calls=%async_computation.5 | async-start | bytes 2359296 | tf_op jit(solution)/shard_map/all_to_all | solution.py:446
  74.3 25.3 %collective-permute-start.2 = (bf16[8,4,9216]{2,1,0:T(4,128)(2,1)}, bf16[8,4,9216]{2,1,0:T(4,128)(2,1)S(1)}, u32[]{:S(2)}, u32[]{:S(2)}) collective-permute-start(bf16[8,4,9216]{2,1,0:T(4,128)(2,1)} %slice.130), channel_id=1, source_target_pairs={{0,8},{8,0},{1,9},{9,1},{2,10},{10,2},{3,11},{11,3},{4,12},{12,4},... | collective-permute-start | bytes 1769480 | tf_op jit(solution)/shard_map/ppermute | solution.py:450
  110.2 8.0 %copy-start.1 = (bf16[8,8,9216]{2,1,0:T(8,128)(2,1)}, bf16[8,8,9216]{2,1,0:T(8,128)(2,1)S(1)}, u32[]{:S(2)}) copy-start(bf16[8,8,9216]{2,1,0:T(8,128)(2,1)S(1)} %all-to-all-done.5.both_ref) | copy-start | bytes 3538948
  110.2 48.5 %all-to-all-start.4 = ((bf16[8,4,9216]{2,1,0:T(4,128)(2,1)}), bf16[8,4,9216]{2,1,0:T(4,128)(2,1)S(1)}, u32[]{:S(2)}, u32[]{:S(2)}) async-start(bf16[8,4,9216]{2,1,0:T(4,128)(2,1)} %mix_out.6), calls=%async_computation.4 | async-start | bytes 1179648 | tf_op jit(solution)/shard_map/all_to_all | solution.py:446
  118.1 30.0 %collective-permute-start.3 = (bf16[8,4,9216]{2,1,0:T(4,128)(2,1)S(1)}, bf16[8,4,9216]{2,1,0:T(4,128)(2,1)S(1)}, u32[]{:S(2)}, u32[]{:S(2)}) collective-permute-start(bf16[8,4,9216]{2,1,0:T(4,128)(2,1)S(1)} %slice.131), channel_id=1, source_target_pairs={{0,8},{8,0},{1,9},{9,1},{2,10},{10,2},{3,11},{11,3},{4,12},{12,4},... | collective-permute-start | bytes 1769480 | tf_op jit(solution)/shard_map/ppermute | solution.py:450
  158.7 4.1 copy-start.8
  158.7 69.9 %all-to-all-start.6 = ((bf16[8,4,9216]{2,1,0:T(4,128)(2,1)}), bf16[8,4,9216]{2,1,0:T(4,128)(2,1)S(1)}, u32[]{:S(2)}, u32[]{:S(2)}) async-start(bf16[8,4,9216]{2,1,0:T(4,128)(2,1)} %mix_out.7), calls=%async_computation.6 | async-start | bytes 1179648 | tf_op jit(solution)/shard_map/all_to_all | solution.py:446
  162.8 42.5 %collective-permute-start.1 = (bf16[8,4,9216]{2,1,0:T(4,128)(2,1)S(1)}, bf16[8,4,9216]{2,1,0:T(4,128)(2,1)S(1)}, u32[]{:S(2)}, u32[]{:S(2)}) collective-permute-start(bf16[8,4,9216]{2,1,0:T(4,128)(2,1)S(1)} %slice.129), channel_id=1, source_target_pairs={{0,8},{8,0},{1,9},{9,1},{2,10},{10,2},{3,11},{11,3},{4,12},{12,4},... | collective-permute-start | bytes 1769480 | tf_op jit(solution)/shard_map/ppermute | solution.py:450
  167.1 50.4 %collective-permute-start = (bf16[8,4,9216]{2,1,0:T(4,128)(2,1)S(1)}, bf16[8,4,9216]{2,1,0:T(4,128)(2,1)S(1)}, u32[]{:S(2)}, u32[]{:S(2)}) collective-permute-start(bf16[8,4,9216]{2,1,0:T(4,128)(2,1)S(1)} %slice.124), channel_id=1, source_target_pairs={{0,8},{8,0},{1,9},{9,1},{2,10},{10,2},{3,11},{11,3},{4,12},{12,4},... | collective-permute-start | bytes 1769480 | tf_op jit(solution)/shard_map/ppermute | solution.py:450
  228.7 4.4 copy-start.23
  228.7 5.7 %copy-start.21 = (bf16[128,128]{1,0:T(8,128)(2,1)S(1)}, bf16[128,128]{1,0:T(8,128)(2,1)}, u32[]{:S(2)}) copy-start(bf16[128,128]{1,0:T(8,128)(2,1)} %param.16) | copy-start | bytes 98308
  228.7 5.7 %copy-start.20 = (bf16[128,512]{1,0:T(8,128)(2,1)S(1)}, bf16[128,512]{1,0:T(8,128)(2,1)}, u32[]{:S(2)}) copy-start(bf16[128,512]{1,0:T(8,128)(2,1)} %param.18) | copy-start | bytes 393220
  229.5 19.4 %all-to-all-start.2 = ((bf16[8,8,9216]{2,1,0:T(8,128)(2,1)}), bf16[8,8,9216]{2,1,0:T(8,128)(2,1)S(1)}, u32[]{:S(2)}, u32[]{:S(2)}) async-start(bf16[8,8,9216]{2,1,0:T(8,128)(2,1)} %mix_out.5), calls=%async_computation.2 | async-start | bytes 2359296 | tf_op jit(solution)/shard_map/all_to_all | solution.py:446
  262.3 19.4 %all-to-all-start.7 = ((bf16[8,8,9216]{2,1,0:T(8,128)(2,1)}), bf16[8,8,9216]{2,1,0:T(8,128)(2,1)S(1)}, u32[]{:S(2)}, u32[]{:S(2)}) async-start(bf16[8,8,9216]{2,1,0:T(8,128)(2,1)} %get-tuple-element.24), calls=%async_computation.7 | async-start | bytes 2359296 | tf_op jit(solution)/shard_map/all_to_all | solution.py:446
  281.7 21.1 %copy-start.6 = (bf16[8,8,9216]{2,1,0:T(8,128)(2,1)}, bf16[8,8,9216]{2,1,0:T(8,128)(2,1)S(1)}, u32[]{:S(2)}) copy-start(bf16[8,8,9216]{2,1,0:T(8,128)(2,1)S(1)} %all-to-all-done.7.both_ref) | copy-start | bytes 3538948
  281.7 21.1 %copy-start.11 = (bf16[8,8,9216]{2,1,0:T(8,128)(2,1)S(1)}, bf16[8,8,9216]{2,1,0:T(8,128)(2,1)}, u32[]{:S(2)}) copy-start(bf16[8,8,9216]{2,1,0:T(8,128)(2,1)} %get-tuple-element.31) | copy-start | bytes 3538948
  322.4 73.0 %all-to-all-start.11 = ((bf16[8,8,9216]{2,1,0:T(8,128)(2,1)}), bf16[8,8,9216]{2,1,0:T(8,128)(2,1)S(1)}, u32[]{:S(2)}, u32[]{:S(2)}) async-start(bf16[8,8,9216]{2,1,0:T(8,128)(2,1)} %get-tuple-element.34), calls=%async_computation.11 | async-start | bytes 2359296 | tf_op jit(solution)/shard_map/all_to_all | solution.py:446
  335.8 42.6 %collective-permute-start.4 = (bf16[8,4,9216]{2,1,0:T(4,128)(2,1)}, bf16[8,4,9216]{2,1,0:T(4,128)(2,1)S(1)}, u32[]{:S(2)}, u32[]{:S(2)}) collective-permute-start(bf16[8,4,9216]{2,1,0:T(4,128)(2,1)} %get-tuple-element.26), channel_id=1, source_target_pairs={{0,8},{8,0},{1,9},{9,1},{2,10},{10,2},{3,11},{11,3},{4,12},{12,4},... | collective-permute-start | bytes 1769480 | tf_op jit(solution)/shard_map/ppermute | solution.py:450
  348.3 42.3 %collective-permute-start.5 = (bf16[8,4,9216]{2,1,0:T(4,128)(2,1)}, bf16[8,4,9216]{2,1,0:T(4,128)(2,1)S(1)}, u32[]{:S(2)}, u32[]{:S(2)}) collective-permute-start(bf16[8,4,9216]{2,1,0:T(4,128)(2,1)} %get-tuple-element.30), channel_id=1, source_target_pairs={{0,8},{8,0},{1,9},{9,1},{2,10},{10,2},{3,11},{11,3},{4,12},{12,4},... | collective-permute-start | bytes 1769480 | tf_op jit(solution)/shard_map/ppermute | solution.py:450
  378.4 12.1 %copy-start.13 = (bf16[8,4,9216]{2,1,0:T(4,128)(2,1)}, bf16[8,4,9216]{2,1,0:T(4,128)(2,1)S(1)}, u32[]{:S(2)}) copy-start(bf16[8,4,9216]{2,1,0:T(4,128)(2,1)S(1)} %collective-permute-done.4.refs_1_) | copy-start | bytes 1769476
  396.5 73.0 %all-to-all-start.9 = ((bf16[8,8,9216]{2,1,0:T(8,128)(2,1)}), bf16[8,8,9216]{2,1,0:T(8,128)(2,1)S(1)}, u32[]{:S(2)}, u32[]{:S(2)}) async-start(bf16[8,8,9216]{2,1,0:T(8,128)(2,1)} %add.10), calls=%async_computation.9 | async-start | bytes 2359296 | tf_op jit(solution)/shard_map/all_to_all | solution.py:446
  409.6 42.6 %collective-permute-start.6 = (bf16[8,4,9216]{2,1,0:T(4,128)(2,1)}, bf16[8,4,9216]{2,1,0:T(4,128)(2,1)S(1)}, u32[]{:S(2)}, u32[]{:S(2)}) collective-permute-start(bf16[8,4,9216]{2,1,0:T(4,128)(2,1)} %get-tuple-element.33), channel_id=1, source_target_pairs={{0,8},{8,0},{1,9},{9,1},{2,10},{10,2},{3,11},{11,3},{4,12},{12,4},... | collective-permute-start | bytes 1769480 | tf_op jit(solution)/shard_map/ppermute | solution.py:450
  422.1 42.6 %collective-permute-start.7 = (bf16[8,4,9216]{2,1,0:T(4,128)(2,1)}, bf16[8,4,9216]{2,1,0:T(4,128)(2,1)S(1)}, u32[]{:S(2)}, u32[]{:S(2)}) collective-permute-start(bf16[8,4,9216]{2,1,0:T(4,128)(2,1)} %get-tuple-element.36), channel_id=1, source_target_pairs={{0,8},{8,0},{1,9},{9,1},{2,10},{10,2},{3,11},{11,3},{4,12},{12,4},... | collective-permute-start | bytes 1769480 | tf_op jit(solution)/shard_map/ppermute | solution.py:450
  452.3 12.4 %copy-start.12 = (bf16[8,4,9216]{2,1,0:T(4,128)(2,1)}, bf16[8,4,9216]{2,1,0:T(4,128)(2,1)S(1)}, u32[]{:S(2)}) copy-start(bf16[8,4,9216]{2,1,0:T(4,128)(2,1)S(1)} %collective-permute-done.6.refs_1_) | copy-start | bytes 1769476
  469.4 4.6 copy-start.24
  469.5 5.8 %copy-start.22 = (bf16[128,128]{1,0:T(8,128)(2,1)S(1)}, bf16[128,128]{1,0:T(8,128)(2,1)}, u32[]{:S(2)}) copy-start(bf16[128,128]{1,0:T(8,128)(2,1)} %param.21) | copy-start | bytes 98308
  470.5 19.4 %all-to-all-start.12 = ((bf16[8,8,9216]{2,1,0:T(8,128)(2,1)}), bf16[8,8,9216]{2,1,0:T(8,128)(2,1)S(1)}, u32[]{:S(2)}, u32[]{:S(2)}) async-start(bf16[8,8,9216]{2,1,0:T(8,128)(2,1)} %add.11), calls=%async_computation.12 | async-start | bytes 2359296 | tf_op jit(solution)/shard_map/all_to_all | solution.py:446
  489.9 1.1 copy-start.4
  (10 other events, 8.9 us)

commit v8 on v6

--- a/solution.py
+++ b/solution.py
@@ -171,7 +171,7 @@
         out_shape=out_shape,
         compiler_params=pltpu.CompilerParams(vmem_limit_bytes=BUDGET),
         name="finish",
-    )(*mixes, state, *weights)
+    )(*(pltpu.with_memory_space_constraint(m, pltpu.HBM) for m in mixes), state, *weights)
 
 
 class Folds:
@@ -218,28 +218,29 @@
         return out
 
 
-def stage(source_ref, staged, shift=0, width=None):
-    parts, held, positions = source_ref.shape
-    width = width or held
+def stage(source_ref, staged):
+    parts, width, positions = source_ref.shape
     rows = parts * width
-    for part in range(parts):
-        values = source_ref[part].astype(jnp.float32)[shift : shift + width, :]
-        for tile in range(positions // LANES):
-            at = tile * rows + part * width
-            staged[at : at + width, :] = values[:, tile * LANES : (tile + 1) * LANES]
-
-
-def unstage(staged, target_ref, earlier_ref=None):
+
+    @pl.loop(0, positions // LANES, unroll=8)
+    def _(tile):
+        lanes = pl.ds(pl.multiple_of(tile * LANES, LANES), LANES)
+        for part in range(parts):
+            staged[pl.ds(tile * rows + part * width, width), :] = source_ref[part, :, lanes].astype(jnp.float32)
+
+
+def unstage(staged, target_ref, earlier_refs=()):
     parts, height, positions = target_ref.shape
-    width = height if earlier_ref is None else height // 2
+    width = height - sum(ref.shape[1] for ref in earlier_refs)
     rows = parts * width
-    for tile in range(positions // LANES):
-        lanes = slice(tile * LANES, (tile + 1) * LANES)
+
+    @pl.loop(0, positions // LANES, unroll=8)
+    def _(tile):
+        lanes = pl.ds(pl.multiple_of(tile * LANES, LANES), LANES)
         for part in range(parts):
-            at = tile * rows + part * width
-            values = staged[at : at + width, :]
-            if earlier_ref is not None:
-                values = jnp.concatenate([earlier_ref[part, :, lanes].astype(jnp.float32), values], axis=0)
+            values = [ref[part, :, lanes].astype(jnp.float32) for ref in earlier_refs]
+            values.append(staged[pl.ds(tile * rows + part * width, width), :])
+            values = values[0] if len(values) == 1 else jnp.concatenate(values, axis=0)
             target_ref[part, :, lanes] = values.astype(target_ref.dtype)
 
 
@@ -248,7 +249,7 @@
 
 
 def mix_out_kernel(folds, near, cols, width, half_ref, both_ref, there_ref, *refs):
-    earlier_ref, (mix_ref, staged, left, right) = (refs[0] if len(refs) == 5 else None), refs[-4:]
+    earlier_refs, (mix_ref, staged, left, right) = refs[:-4], refs[-4:]
     parts = near * cols
     rows = parts * width
     block = folds.rows
@@ -301,10 +302,7 @@
                 for at, value in zip(lane_rows_of(folds, rows, out_row), lane_rows):
                     staged[at, :] = value
 
-    if earlier_ref is None:
-        unstage(staged, mix_ref)
-    else:
-        unstage(staged, mix_ref, earlier_ref)
+    unstage(staged, mix_ref, earlier_refs)
 
 
 def mix_in_kernel(folds, near, cols, width, half_ref, both_ref, keep_ref, send_ref, staged, left, right, turned, mixed):
@@ -361,7 +359,7 @@
         functools.partial(mix_out_kernel, folds, near, cols, width),
         in_specs=[SMEM_SPEC] + [VMEM_SPEC] * (2 + len(earlier)),
         out_specs=VMEM_SPEC,
-        out_shape=jax.ShapeDtypeStruct((parts, width * (1 + len(earlier)), positions), jnp.bfloat16),
+        out_shape=jax.ShapeDtypeStruct((parts, width + sum(e.shape[1] for e in earlier), positions), jnp.bfloat16),
         scratch_shapes=[
             pltpu.VMEM((2 * rows * folds.lane_rows, LANES), jnp.float32),
             pltpu.VMEM((width * cols * near * block, LANES), jnp.bfloat16),
@@ -381,13 +379,13 @@
 
 
 def run_add(*arrays):
-    parts, width, positions = arrays[0].shape
+    parts, _, positions = arrays[0].shape
     step = row_step(positions)
-    height = width * len(arrays) // 2
+    height = sum(array.shape[1] for array in arrays) // 2
     return pl.pallas_call(
         add_kernel,
         grid=(positions // step,),
-        in_specs=[pl.BlockSpec((parts, width, step), lambda i: (0, 0, i))] * len(arrays),
+        in_specs=[pl.BlockSpec((*array.shape[:2], step), lambda i: (0, 0, i)) for array in arrays],
         out_specs=pl.BlockSpec((parts, height, step), lambda i: (0, 0, i)),
         out_shape=jax.ShapeDtypeStruct((parts, height, positions), jnp.bfloat16),
         compiler_params=pltpu.CompilerParams(vmem_limit_bytes=BUDGET),
@@ -419,7 +417,9 @@
     )(halves, both)
 
 
-PIECES = 4
+SHARES = (1, 2, 2, 2, 1)
+GROUPS = ((1, 2), (0, 3, 4))
+PIECES = len(SHARES)
 
 
 def exchange(array):
@@ -435,51 +435,60 @@
     row_count, col_count, features = pair_input.shape
     parts = near * cols
     width = features // parts
-    pieces = PIECES
-    piece_width = width // pieces
+    ends = [sum(SHARES[: at + 1]) * width // sum(SHARES) for at in range(PIECES)]
+    begins = [0] + ends[:-1]
     folds = Folds(row_count, col_count)
     half = lax.axis_index("far")
     halves = jnp.stack([half, 1 - half]).astype(jnp.int32)
 
-    def by_piece(rows):
-        return rows.reshape(parts, pieces, width // pieces, -1).transpose(1, 0, 2, 3)
-
-    def rows_of(project, order):
-        ga, va, gb, vb = (by_piece(rows) for rows in jnp.split(project.T, 4, axis=0))
-        return jnp.concatenate([order(ga, gb).reshape(-1, features), order(va, vb).reshape(-1, features)])
-
-    def side_by_side(left, right):
-        return jnp.concatenate([left, right], axis=2)
-
-    def unordered(array):
-        rows = array.reshape(parts, pieces // 2, 2 * piece_width, -1)
-        return rows.transpose(1, 0, 2, 3).reshape(array.shape)
+    def rows_of(project, *chosen):
+        ga, va, gb, vb = (rows.reshape(parts, width, features) for rows in jnp.split(project.T, 4, axis=0))
+
+        def ordered(left, right):
+            rows = [array[:, begins[piece] : ends[piece]] for piece in chosen for array in (left, right)]
+            pairs = [jnp.concatenate(rows[at : at + 2], axis=1).reshape(-1, features) for at in range(0, len(rows), 2)]
+            return pairs
+
+        return jnp.concatenate(ordered(ga, gb) + ordered(va, vb))
+
+    def in_groups(array):
+        rows = array.reshape(parts, width, -1)
+        ordered = [
+            jnp.concatenate([rows[:, begins[piece] : ends[piece]] for piece in group], axis=1).reshape(-1, rows.shape[-1])
+            for group in GROUPS
+        ]
+        return jnp.concatenate(ordered).reshape(array.shape)
 
     gain_1, project_1, gate_1, norm_1, final_1, gain_2, project_2, gate_2, norm_2, final_2 = weights
     state = pair_input.reshape(-1, features)
 
-    shapes = ((parts, 2 * piece_width),) * pieces
-    both, mixes = [], []
-    out = run_projections(state, gain_1, rows_of(project_1, side_by_side), shapes)
-    for piece in range(pieces):
+    shapes = [(parts, 2 * (end - begin)) for begin, end in zip(begins, ends)]
+    rest = range(1, PIECES)
+    both, mixed, mixes = [], [None] * PIECES, []
+    out = run_projections(state, gain_1, rows_of(project_1, 0), shapes[:1])
+    out += run_projections(state, gain_1, rows_of(project_1, *rest), shapes[1:])
+    for piece in range(PIECES):
         both.append(exchange(out[piece]))
-    for piece in range(pieces):
-        there = across(both[piece][:, piece_width:, :])
-        mixed = run_mix_out(folds, near, cols, halves, both[piece], there, (mixed,) if piece % 2 else ())
-        if piece % 2:
-            mixes.append(exchange(mixed))
-    onward = (gain_2, rows_of(project_2, side_by_side), shapes)
-    out = run_finish(mixes, state, gain_1, gate_1, unordered(norm_1), unordered(final_1), onward)
-    middle, both, parted, mixes = out[0], [], [], []
-    for piece in range(pieces):
-        both.append(exchange(out[1 + piece]))
-    for piece in range(pieces):
+    for piece in range(PIECES):
+        group = next(group for group in GROUPS if piece in group)
+        there = across(both[piece][:, both[piece].shape[1] // 2 :, :])
+        earlier = [mixed[other] for other in group[:-1]] if piece == group[-1] else ()
+        mixed[piece] = run_mix_out(folds, near, cols, halves, both[piece], there, earlier)
+        if piece == group[-1]:
+            mixes.append(exchange(mixed[piece]))
+    onward = (gain_2, rows_of(project_2, 0), shapes[:1])
+    middle, *out = run_finish(mixes, state, gain_1, gate_1, in_groups(norm_1), in_groups(final_1), onward)
+    out += run_projections(middle, gain_2, rows_of(project_2, *rest), shapes[1:])
+    both, parted, mixes = [], [], []
+    for piece in range(PIECES):
+        both.append(exchange(out[piece]))
+    for piece in range(PIECES):
         kept, sent = run_mix_in(folds, near, cols, halves, both[piece])
         parted.append((kept, across(sent)))
-    for pair in range(pieces // 2):
-        mixed = run_add(*parted[2 * pair], *parted[2 * pair + 1])
-        mixes.append(exchange(mixed))
-    result = run_finish(mixes, middle, gain_2, gate_2, unordered(norm_2), unordered(final_2))[0]
+    for group in GROUPS:
+        summed = run_add(*(array for piece in group for array in parted[piece]))
+        mixes.append(exchange(summed))
+    result = run_finish(mixes, middle, gain_2, gate_2, in_groups(norm_2), in_groups(final_2))[0]
     return result.reshape(pair_input.shape)
 
 
@@ -496,7 +505,7 @@
             and block_rows == block_cols
             and Folds(block_rows, block_cols).fits()
             and features == LANES
-            and features % (row_parts // 2 * col_parts * PIECES) == 0
+            and features % (row_parts // 2 * col_parts * sum(SHARES)) == 0
         )
         if halved:
             far, near = 2, row_parts // 2

time: 482 us -> 516 us (1.071)
  Pallas kernels: 114 us -> 128 us
  starting transfers between devices: 33.7 us -> 44.5 us
  local copies, waits for them, and re-layouts: 15.4 us -> 25.2 us
  waiting for transfers between devices: 194 us -> 187 us
  other arithmetic: 2.08 us -> 8.02 us
    pallas_call x1 -> x3, Pallas kernels: 7.33 us -> 20 us  [run_projections(): pl.pallas_call(project_kernel, grid=(positions // step,), in_specs=[pl.Bl...]
    ppermute x8 -> x10, waiting for transfers between devices: 166 us -> 160 us  [across(): return lax.ppermute(array, 'far', ((0, 1), (1, 0)))]
    ppermute x8 -> x10, starting transfers between devices: 11.9 us -> 17.4 us  [across(): return lax.ppermute(array, 'far', ((0, 1), (1, 0)))]
    all_to_all x6 -> x7, starting transfers between devices: 21.8 us -> 27 us  [exchange(): return lax.all_to_all(array, EVERY, split_axis=0, concat_axis=0, tiled=True)]
    unnamed x52 -> x74, local copies, waits for them, and re-layouts: 10.4 us -> 14.7 us
    pallas_call x4 -> x5, Pallas kernels: 40.1 us -> 41.8 us  [run_mix_out(): pl.pallas_call(functools.partial(mix_out_kernel, folds, near, cols, width...]
    pallas_call x4 -> x5, Pallas kernels: 38.2 us -> 39.7 us  [run_mix_in(): pl.pallas_call(functools.partial(mix_in_kernel, folds, near, cols, width)...]
    all_to_all x6 -> x7, blocking collectives: 121 us -> 120 us  [exchange(): return lax.all_to_all(array, EVERY, split_axis=0, concat_axis=0, tiled=True)]
  transfers between devices with their start and end apart: 14 -> 17, of which waited for: 10 -> 10; matrix products, arithmetic and copies ran while one was open for 1% -> 4% of each run, Pallas kernels for 18% -> 19%
where the time goes in v8:
time: 516 us; the launch traced here: 514 us
  waiting for transfers between devices  187 us (36%)
  Pallas kernels  128 us (25%)
  blocking collectives  120 us (23%)
  starting transfers between devices  44.5 us (9%)
  local copies, waits for them, and re-layouts  25.2 us (5%)
  other arithmetic  8.02 us (2%)
    ppermute x10, waiting for transfers between devices, across(): return lax.ppermute(array, 'far', ((0, 1), (1, 0)))  160 us
    all_to_all x7, blocking collectives, exchange(): return lax.all_to_all(array, EVERY, split_axis=0, concat_axis=0, tiled=True)  120 us
    pallas_call x5, Pallas kernels, run_mix_out(): pl.pallas_call(functools.partial(mix_out_kernel, folds, near, cols, width...  41.8 us
    pallas_call x5, Pallas kernels, run_mix_in(): pl.pallas_call(functools.partial(mix_in_kernel, folds, near, cols, width)...  39.7 us
    all_to_all x7, waiting for transfers between devices, exchange(): return lax.all_to_all(array, EVERY, split_axis=0, concat_axis=0, tiled=True)  27.2 us
    all_to_all x7, starting transfers between devices, exchange(): return lax.all_to_all(array, EVERY, split_axis=0, concat_axis=0, tiled=True)  27 us
    pallas_call x3, Pallas kernels, run_projections(): pl.pallas_call(project_kernel, grid=(positions // step,), in_specs=[pl.Bl...  20 us
    pallas_call x2, Pallas kernels, run_finish(): pl.pallas_call(functools.partial(finish_kernel, len(mixes), onward is not...  18.4 us
  transfers between devices with their start and end apart: 17, of which 10 were waited for; matrix products, arithmetic and copies ran while one was open for 4% of the time, Pallas kernels for 19%

profile of v8, /device:TPU:0, one launch (start us, length us, event | category | flops | bytes accessed | tf_op | source)
XLA Modules:
  0.0 513.7 jit_solution(14855298255584207284)
XLA Ops:
  2.1 7.2 %project.3 = (bf16[8,8,9216]{2,1,0:T(8,128)(2,1)}, bf16[8,8,9216]{2,1,0:T(8,128)(2,1)}, bf16[8,8,9216]{2,1,0:T(8,128)(2,1)}, bf16[8,4,9216]{2,1,0:T(4,128)(2,1)}) custom-call(bf16[9216,128]{1,0:T(8,128)(2,1)} %bitcast.92, f32[1,128]{1,0:T(1,128)} %bitcast.129, bf16[448,128]{1,0:T(8,128)(2,1)} %copy-done.25), custom_call_target="tpu_custom_call" | custom-call | tf_op jit(solution)/shard_map/project/pallas_call | solution.py:142
  9.3 5.3 %all-to-all-start.3 = ((bf16[8,4,9216]{2,1,0:T(4,128)(2,1)}), bf16[8,4,9216]{2,1,0:T(4,128)(2,1)S(1)}, u32[]{:S(2)}, u32[]{:S(2)}) async-start(bf16[8,4,9216]{2,1,0:T(4,128)(2,1)} %get-tuple-element.27), calls=%async_computation.3 | async-start | bytes 1179648 | tf_op jit(solution)/shard_map/all_to_all | solution.py:426
  15.1 5.6 %project.4 = bf16[8,4,9216]{2,1,0:T(4,128)(2,1)} custom-call(bf16[9216,128]{1,0:T(8,128)(2,1)} %bitcast.93, f32[1,128]{1,0:T(1,128)} %bitcast.130, bf16[64,128]{1,0:T(8,128)(2,1)} %pad_maximum_fusion.2.rows_ref), custom_call_target="tpu_custom_call" | custom-call | tf_op jit(solution)/shard_map/project/pallas_call | solution.py:142
  24.1 14.6 %all_to_all.70.both_ref = bf16[8,4,9216]{2,1,0:T(4,128)(2,1)} all-to-all(bf16[8,4,9216]{2,1,0:T(4,128)(2,1)} %project.4), channel_id=1, replica_groups=mesh['groups'=2,'far'=2,'near'=2,'chan'=2,'sub'=2] {'near','chan','sub'}, dimensions={0} | all-to-all | bytes 1179648 | tf_op jit(solution)/shard_map/all_to_all | solution.py:426
  38.7 19.1 %all_to_all.71.both_ref = bf16[8,8,9216]{2,1,0:T(8,128)(2,1)S(1)} all-to-all(bf16[8,8,9216]{2,1,0:T(8,128)(2,1)S(1)} %copy-done.12), channel_id=1, replica_groups=mesh['groups'=2,'far'=2,'near'=2,'chan'=2,'sub'=2] {'near','chan','sub'}, dimensions={0} | all-to-all | bytes 2359296 | tf_op jit(solution)/shard_map/all_to_all | solution.py:426
  57.8 19.0 %all_to_all.72.both_ref = bf16[8,8,9216]{2,1,0:T(8,128)(2,1)S(1)} all-to-all(bf16[8,8,9216]{2,1,0:T(8,128)(2,1)S(1)} %copy-done.11), channel_id=1, replica_groups=mesh['groups'=2,'far'=2,'near'=2,'chan'=2,'sub'=2] {'near','chan','sub'}, dimensions={0} | all-to-all | bytes 2359296 | tf_op jit(solution)/shard_map/all_to_all | solution.py:426
  89.1 41.5 %collective-permute-done.3.there_ref = bf16[8,2,9216]{2,1,0:T(2,128)(2,1)} collective-permute-done((bf16[8,2,9216]{2,1,0:T(2,128)(2,1)}, bf16[8,2,9216]{2,1,0:T(2,128)(2,1)}, u32[]{:S(2)}, u32[]{:S(2)}) %collective-permute-start.3) | collective-permute-done | bytes 294944 | tf_op jit(solution)/shard_map/ppermute | solution.py:430
  130.6 5.4 %mix_out.7.refs_0_ = bf16[8,2,9216]{2,1,0:T(2,128)(2,1)} custom-call(s32[2]{0:T(128)} %pad_add_fusion.half_ref, bf16[8,4,9216]{2,1,0:T(4,128)(2,1)} %all_to_all.70.both_ref, bf16[8,2,9216]{2,1,0:T(2,128)(2,1)} %collective-permute-done.3.there_ref), custom_call_target="tpu_custom_call" | custom-call | tf_op jit(solution)/shard_map/mix_out/pallas_call | solution.py:358
  136.8 9.8 %mix_out.8.refs_1_ = bf16[8,4,9216]{2,1,0:T(4,128)(2,1)} custom-call(s32[2]{0:T(128)} %pad_add_fusion.half_ref, bf16[8,8,9216]{2,1,0:T(8,128)(2,1)} %copy-done.1, bf16[8,4,9216]{2,1,0:T(4,128)(2,1)} %copy-done.18), custom_call_target="tpu_custom_call" | custom-call | tf_op jit(solution)/shard_map/mix_out/pallas_call | solution.py:358
  147.3 6.4 %mix_out.9 = bf16[8,8,9216]{2,1,0:T(8,128)(2,1)} custom-call(s32[2]{0:T(128)} %pad_add_fusion.half_ref, bf16[8,4,9216]{2,1,0:T(4,128)(2,1)} %copy-done.8, bf16[8,2,9216]{2,1,0:T(2,128)(2,1)} %copy-done.22, bf16[8,2,9216]{2,1,0:T(2,128)(2,1)} %mix_out.7.refs_0_, bf16[8,4,9216]{2,1,0:T(4,128)(2,1)} %mix_out.8.refs_1_), custom_call_target="tpu_custom_call" | custom-call | tf_op jit(solution)/shard_map/mix_out/pallas_call | solution.py:358
  170.2 36.2 %collective-permute-done.1.there_ref = bf16[8,4,9216]{2,1,0:T(4,128)(2,1)S(1)} collective-permute-done((bf16[8,4,9216]{2,1,0:T(4,128)(2,1)}, bf16[8,4,9216]{2,1,0:T(4,128)(2,1)S(1)}, u32[]{:S(2)}, u32[]{:S(2)}) %collective-permute-start.1) | collective-permute-done | bytes 589856 | tf_op jit(solution)/shard_map/ppermute | solution.py:430
  207.2 9.8 %mix_out.5.refs_0_ = bf16[8,4,9216]{2,1,0:T(4,128)(2,1)} custom-call(s32[2]{0:T(128)} %pad_add_fusion.half_ref, bf16[8,8,9216]{2,1,0:T(8,128)(2,1)} %copy-done, bf16[8,4,9216]{2,1,0:T(4,128)(2,1)} %copy-done.19), custom_call_target="tpu_custom_call" | custom-call | tf_op jit(solution)/shard_map/mix_out/pallas_call | solution.py:358
  219.7 10.4 %mix_out.6 = bf16[8,8,9216]{2,1,0:T(8,128)(2,1)} custom-call(s32[2]{0:T(128)} %pad_add_fusion.half_ref, bf16[8,8,9216]{2,1,0:T(8,128)(2,1)} %copy-done.2, bf16[8,4,9216]{2,1,0:T(4,128)(2,1)} %copy-done.21, bf16[8,4,9216]{2,1,0:T(4,128)(2,1)} %mix_out.5.refs_0_), custom_call_target="tpu_custom_call" | custom-call | tf_op jit(solution)/shard_map/mix_out/pallas_call | solution.py:358
  240.6 9.9 %all-to-all-done.2.refs_0_ = bf16[8,8,9216]{2,1,0:T(8,128)(2,1)S(1)} async-done(((bf16[8,8,9216]{2,1,0:T(8,128)(2,1)}), bf16[8,8,9216]{2,1,0:T(8,128)(2,1)S(1)}, u32[]{:S(2)}, u32[]{:S(2)}) %all-to-all-start.2) | async-done | bytes 1179680 | tf_op jit(solution)/shard_map/all_to_all | solution.py:426
  251.5 10.5 %finish.2 = (bf16[9216,128]{1,0:T(8,128)(2,1)}, bf16[8,4,9216]{2,1,0:T(4,128)(2,1)}) custom-call(bf16[8,8,9216]{2,1,0:T(8,128)(2,1)} %copy-done.7, bf16[8,8,9216]{2,1,0:T(8,128)(2,1)} %copy-done.6, bf16[9216,128]{1,0:T(8,128)(2,1)} %bitcast.94, f32[1,128]{1,0:T(1,128)} %bitcast.131, bf16[128,128]{1,0:T(8,128)(2,1)} %refs_4_.2, f32[128,1]{1,0:T(8,128)} %copy.64.refs_5_, ...), custom_call_target="tpu_custom_call" | custom-call | tf_op jit(solution)/shard_map/finish/pallas_call | solution.py:164
  262.0 7.2 %project.5 = (bf16[8,8,9216]{2,1,0:T(8,128)(2,1)}, bf16[8,8,9216]{2,1,0:T(8,128)(2,1)}, bf16[8,8,9216]{2,1,0:T(8,128)(2,1)}, bf16[8,4,9216]{2,1,0:T(4,128)(2,1)}) custom-call(bf16[9216,128]{1,0:T(8,128)(2,1)} %get-tuple-element.29.state_ref.refs_2_, f32[1,128]{1,0:T(1,128)} %bitcast.133, bf16[448,128]{1,0:T(8,128)(2,1)} %constant_dynamic-update-slice_fusion.8.rows_ref), custom_call_target="tpu_custom_call" | custom-call | tf_op jit(solution)/shard_map/project/pallas_call | solution.py:142
  269.3 14.7 %all_to_all.73.both_ref = bf16[8,4,9216]{2,1,0:T(4,128)(2,1)} all-to-all(bf16[8,4,9216]{2,1,0:T(4,128)(2,1)} %get-tuple-element.42), channel_id=1, replica_groups=mesh['groups'=2,'far'=2,'near'=2,'chan'=2,'sub'=2] {'near','chan','sub'}, dimensions={0} | all-to-all | bytes 1179648 | tf_op jit(solution)/shard_map/all_to_all | solution.py:426
  283.9 13.4 %all_to_all.74.both_ref = bf16[8,4,9216]{2,1,0:T(4,128)(2,1)} all-to-all(bf16[8,4,9216]{2,1,0:T(4,128)(2,1)S(1)} %copy-done.20), channel_id=1, replica_groups=mesh['groups'=2,'far'=2,'near'=2,'chan'=2,'sub'=2] {'near','chan','sub'}, dimensions={0} | all-to-all | bytes 1179648 | tf_op jit(solution)/shard_map/all_to_all | solution.py:426
  297.3 19.8 %all_to_all.75.both_ref = bf16[8,8,9216]{2,1,0:T(8,128)(2,1)} all-to-all(bf16[8,8,9216]{2,1,0:T(8,128)(2,1)S(1)} %copy-done.14), channel_id=1, replica_groups=mesh['groups'=2,'far'=2,'near'=2,'chan'=2,'sub'=2] {'near','chan','sub'}, dimensions={0} | all-to-all | bytes 2359296 | tf_op jit(solution)/shard_map/all_to_all | solution.py:426
  317.1 19.7 %all_to_all.76.both_ref = bf16[8,8,9216]{2,1,0:T(8,128)(2,1)} all-to-all(bf16[8,8,9216]{2,1,0:T(8,128)(2,1)S(1)} %copy-done.13), channel_id=1, replica_groups=mesh['groups'=2,'far'=2,'near'=2,'chan'=2,'sub'=2] {'near','chan','sub'}, dimensions={0} | all-to-all | bytes 2359296 | tf_op jit(solution)/shard_map/all_to_all | solution.py:426
  340.6 9.7 %mix_in.8 = (f32[8,4,9216]{2,1,0:T(4,128)}, bf16[8,4,9216]{2,1,0:T(4,128)(2,1)}) custom-call(s32[2]{0:T(128)} %pad_add_fusion.half_ref, bf16[8,8,9216]{2,1,0:T(8,128)(2,1)} %all_to_all.75.both_ref), custom_call_target="tpu_custom_call" | custom-call | tf_op jit(solution)/shard_map/mix_in/pallas_call | solution.py:400
  353.2 5.4 %mix_in.9 = (f32[8,2,9216]{2,1,0:T(2,128)}, bf16[8,2,9216]{2,1,0:T(2,128)(2,1)}) custom-call(s32[2]{0:T(128)} %pad_add_fusion.half_ref, bf16[8,4,9216]{2,1,0:T(4,128)(2,1)} %all_to_all.73.both_ref), custom_call_target="tpu_custom_call" | custom-call | tf_op jit(solution)/shard_map/mix_in/pallas_call | solution.py:400
  358.6 5.3 %mix_in.7 = (f32[8,2,9216]{2,1,0:T(2,128)}, bf16[8,2,9216]{2,1,0:T(2,128)(2,1)}) custom-call(s32[2]{0:T(128)} %pad_add_fusion.half_ref, bf16[8,4,9216]{2,1,0:T(4,128)(2,1)} %all_to_all.74.both_ref), custom_call_target="tpu_custom_call" | custom-call | tf_op jit(solution)/shard_map/mix_in/pallas_call | solution.py:400
  366.8 32.4 %collective-permute-done.9.refs_5_ = bf16[8,2,9216]{2,1,0:T(2,128)(2,1)S(1)} collective-permute-done((bf16[8,2,9216]{2,1,0:T(2,128)(2,1)}, bf16[8,2,9216]{2,1,0:T(2,128)(2,1)S(1)}, u32[]{:S(2)}, u32[]{:S(2)}) %collective-permute-start.9) | collective-permute-done | bytes 294944 | tf_op jit(solution)/shard_map/ppermute | solution.py:430
  399.3 5.8 %collective-permute-done.7.refs_1_ = bf16[8,2,9216]{2,1,0:T(2,128)(2,1)S(1)} collective-permute-done((bf16[8,2,9216]{2,1,0:T(2,128)(2,1)}, bf16[8,2,9216]{2,1,0:T(2,128)(2,1)S(1)}, u32[]{:S(2)}, u32[]{:S(2)}) %collective-permute-start.7) | collective-permute-done | bytes 294944 | tf_op jit(solution)/shard_map/ppermute | solution.py:430
  406.1 4.2 add.5
  414.9 9.6 %mix_in.6 = (f32[8,4,9216]{2,1,0:T(4,128)}, bf16[8,4,9216]{2,1,0:T(4,128)(2,1)}) custom-call(s32[2]{0:T(128)} %pad_add_fusion.half_ref, bf16[8,8,9216]{2,1,0:T(8,128)(2,1)} %all_to_all.76.both_ref), custom_call_target="tpu_custom_call" | custom-call | tf_op jit(solution)/shard_map/mix_in/pallas_call | solution.py:400
  427.4 9.7 %mix_in.5 = (f32[8,4,9216]{2,1,0:T(4,128)}, bf16[8,4,9216]{2,1,0:T(4,128)(2,1)}) custom-call(s32[2]{0:T(128)} %pad_add_fusion.half_ref, bf16[8,8,9216]{2,1,0:T(8,128)(2,1)} %copy-done.5), custom_call_target="tpu_custom_call" | custom-call | tf_op jit(solution)/shard_map/mix_in/pallas_call | solution.py:400
  437.1 30.0 %collective-permute-done.6.refs_3_ = bf16[8,4,9216]{2,1,0:T(4,128)(2,1)S(1)} collective-permute-done((bf16[8,4,9216]{2,1,0:T(4,128)(2,1)}, bf16[8,4,9216]{2,1,0:T(4,128)(2,1)S(1)}, u32[]{:S(2)}, u32[]{:S(2)}) %collective-permute-start.6) | collective-permute-done | bytes 589856 | tf_op jit(solution)/shard_map/ppermute | solution.py:430
  467.1 12.4 %collective-permute-done.5.refs_1_ = bf16[8,4,9216]{2,1,0:T(4,128)(2,1)S(1)} collective-permute-done((bf16[8,4,9216]{2,1,0:T(4,128)(2,1)}, bf16[8,4,9216]{2,1,0:T(4,128)(2,1)S(1)}, u32[]{:S(2)}, u32[]{:S(2)}) %collective-permute-start.5) | collective-permute-done | bytes 589856 | tf_op jit(solution)/shard_map/ppermute | solution.py:430
  490.9 13.8 %all-to-all-done.9.refs_0_ = bf16[8,8,9216]{2,1,0:T(8,128)(2,1)S(1)} async-done(((bf16[8,8,9216]{2,1,0:T(8,128)(2,1)}), bf16[8,8,9216]{2,1,0:T(8,128)(2,1)S(1)}, u32[]{:S(2)}, u32[]{:S(2)}) %all-to-all-start.9) | async-done | bytes 1179680 | tf_op jit(solution)/shard_map/all_to_all | solution.py:426
  505.8 7.9 %finish.3 = bf16[9216,128]{1,0:T(8,128)(2,1)} custom-call(bf16[8,8,9216]{2,1,0:T(8,128)(2,1)} %copy-done.4, bf16[8,8,9216]{2,1,0:T(8,128)(2,1)} %copy-done.3, bf16[9216,128]{1,0:T(8,128)(2,1)} %get-tuple-element.29.state_ref.refs_2_, f32[1,128]{1,0:T(1,128)} %bitcast.134, bf16[128,128]{1,0:T(8,128)(2,1)} %refs_4_.3, f32[128,1]{1,0:T(8,128)} %copy.65.refs_5_, ...), custom_call_target="tpu_custom_call" | custom-call | tf_op jit(solution)/shard_map/finish/pallas_call | solution.py:164
  (164 shorter events, 81.7 us)
Async XLA Ops:
  9.3 14.8 %all-to-all-start.3 = ((bf16[8,4,9216]{2,1,0:T(4,128)(2,1)}), bf16[8,4,9216]{2,1,0:T(4,128)(2,1)S(1)}, u32[]{:S(2)}, u32[]{:S(2)}) async-start(bf16[8,4,9216]{2,1,0:T(4,128)(2,1)} %get-tuple-element.27), calls=%async_computation.3 | async-start | bytes 1179648 | tf_op jit(solution)/shard_map/all_to_all | solution.py:426
  24.1 33.7 %copy-start.8 = (bf16[8,4,9216]{2,1,0:T(4,128)(2,1)}, bf16[8,4,9216]{2,1,0:T(4,128)(2,1)S(1)}, u32[]{:S(2)}) copy-start(bf16[8,4,9216]{2,1,0:T(4,128)(2,1)S(1)} %all-to-all-done.3.both_ref) | copy-start | bytes 1769476
  24.1 14.6 %copy-start.12 = (bf16[8,8,9216]{2,1,0:T(8,128)(2,1)S(1)}, bf16[8,8,9216]{2,1,0:T(8,128)(2,1)}, u32[]{:S(2)}) copy-start(bf16[8,8,9216]{2,1,0:T(8,128)(2,1)} %get-tuple-element.28) | copy-start | bytes 3538948
  38.7 19.1 %copy-start.11 = (bf16[8,8,9216]{2,1,0:T(8,128)(2,1)S(1)}, bf16[8,8,9216]{2,1,0:T(8,128)(2,1)}, u32[]{:S(2)}) copy-start(bf16[8,8,9216]{2,1,0:T(8,128)(2,1)} %get-tuple-element.26) | copy-start | bytes 3538948
  57.8 22.5 %copy-start.1 = (bf16[8,8,9216]{2,1,0:T(8,128)(2,1)}, bf16[8,8,9216]{2,1,0:T(8,128)(2,1)S(1)}, u32[]{:S(2)}) copy-start(bf16[8,8,9216]{2,1,0:T(8,128)(2,1)S(1)} %all_to_all.71.both_ref) | copy-start | bytes 3538948
  76.8 85.8 %copy-start = (bf16[8,8,9216]{2,1,0:T(8,128)(2,1)}, bf16[8,8,9216]{2,1,0:T(8,128)(2,1)S(1)}, u32[]{:S(2)}) copy-start(bf16[8,8,9216]{2,1,0:T(8,128)(2,1)S(1)} %all_to_all.72.both_ref) | copy-start | bytes 3538948
  76.8 77.0 %all-to-all-start = ((bf16[8,8,9216]{2,1,0:T(8,128)(2,1)}), bf16[8,8,9216]{2,1,0:T(8,128)(2,1)S(1)}, u32[]{:S(2)}, u32[]{:S(2)}) async-start(bf16[8,8,9216]{2,1,0:T(8,128)(2,1)} %get-tuple-element.25), calls=%async_computation | async-start | bytes 2359296 | tf_op jit(solution)/shard_map/all_to_all | solution.py:426
  81.5 54.5 %collective-permute-start.4 = (bf16[8,4,9216]{2,1,0:T(4,128)(2,1)}, bf16[8,4,9216]{2,1,0:T(4,128)(2,1)S(1)}, u32[]{:S(2)}, u32[]{:S(2)}) collective-permute-start(bf16[8,4,9216]{2,1,0:T(4,128)(2,1)} %slice.256), channel_id=1, source_target_pairs={{0,8},{8,0},{1,9},{9,1},{2,10},{10,2},{3,11},{11,3},{4,12},{12,4},... | collective-permute-start | bytes 1769480 | tf_op jit(solution)/shard_map/ppermute | solution.py:430
  85.1 45.4 %collective-permute-start.3 = (bf16[8,2,9216]{2,1,0:T(2,128)(2,1)}, bf16[8,2,9216]{2,1,0:T(2,128)(2,1)}, u32[]{:S(2)}, u32[]{:S(2)}) collective-permute-start(bf16[8,2,9216]{2,1,0:T(2,128)(2,1)} %slice.255), channel_id=1, source_target_pairs={{0,8},{8,0},{1,9},{9,1},{2,10},{10,2},{3,11},{11,3},{4,12},{12,4},... | collective-permute-start | bytes 884744 | tf_op jit(solution)/shard_map/ppermute | solution.py:430
  85.8 60.8 %collective-permute-start.2 = (bf16[8,2,9216]{2,1,0:T(2,128)(2,1)S(1)}, bf16[8,2,9216]{2,1,0:T(2,128)(2,1)S(1)}, u32[]{:S(2)}, u32[]{:S(2)}) collective-permute-start(bf16[8,2,9216]{2,1,0:T(2,128)(2,1)S(1)} %slice.250), channel_id=1, source_target_pairs={{0,8},{8,0},{1,9},{9,1},{2,10},{10,2},{3,11},{11,3},{4,12},{12,4},... | collective-permute-start | bytes 884744 | tf_op jit(solution)/shard_map/ppermute | solution.py:430
  153.7 5.4 %copy-start.33 = (f32[128]{0:T(128)S(1)}, f32[128]{0:T(128)}, u32[]{:S(2)}) copy-start(f32[128]{0:T(128)} %param.15) | copy-start | bytes 1540
  153.8 13.0 %copy-start.2 = (bf16[8,8,9216]{2,1,0:T(8,128)(2,1)}, bf16[8,8,9216]{2,1,0:T(8,128)(2,1)S(1)}, u32[]{:S(2)}) copy-start(bf16[8,8,9216]{2,1,0:T(8,128)(2,1)S(1)} %all-to-all-done.both_ref) | copy-start | bytes 3538948
  153.8 76.4 %all-to-all-start.6 = ((bf16[8,8,9216]{2,1,0:T(8,128)(2,1)}), bf16[8,8,9216]{2,1,0:T(8,128)(2,1)S(1)}, u32[]{:S(2)}, u32[]{:S(2)}) async-start(bf16[8,8,9216]{2,1,0:T(8,128)(2,1)} %mix_out.9), calls=%async_computation.6 | async-start | bytes 2359296 | tf_op jit(solution)/shard_map/all_to_all | solution.py:426
  163.8 42.7 %collective-permute-start.1 = (bf16[8,4,9216]{2,1,0:T(4,128)(2,1)}, bf16[8,4,9216]{2,1,0:T(4,128)(2,1)S(1)}, u32[]{:S(2)}, u32[]{:S(2)}) collective-permute-start(bf16[8,4,9216]{2,1,0:T(4,128)(2,1)} %slice.249), channel_id=1, source_target_pairs={{0,8},{8,0},{1,9},{9,1},{2,10},{10,2},{3,11},{11,3},{4,12},{12,4},... | collective-permute-start | bytes 1769480 | tf_op jit(solution)/shard_map/ppermute | solution.py:430
  167.0 51.9 %collective-permute-start = (bf16[8,4,9216]{2,1,0:T(4,128)(2,1)S(1)}, bf16[8,4,9216]{2,1,0:T(4,128)(2,1)S(1)}, u32[]{:S(2)}, u32[]{:S(2)}) collective-permute-start(bf16[8,4,9216]{2,1,0:T(4,128)(2,1)S(1)} %slice.248), channel_id=1, source_target_pairs={{0,8},{8,0},{1,9},{9,1},{2,10},{10,2},{3,11},{11,3},{4,12},{12,4},... | collective-permute-start | bytes 1769480 | tf_op jit(solution)/shard_map/ppermute | solution.py:430
  230.1 5.5 %copy-start.32 = (bf16[8,4,128]{2,1,0:T(4,128)(2,1)S(1)}, bf16[8,4,128]{2,1,0:T(4,128)(2,1)}, u32[]{:S(2)}) copy-start(bf16[8,4,128]{2,1,0:T(4,128)(2,1)} %get-tuple-element.111) | copy-start | bytes 24580
  230.1 6.7 %copy-start.26 = (bf16[128,128]{1,0:T(8,128)(2,1)S(1)}, bf16[128,128]{1,0:T(8,128)(2,1)}, u32[]{:S(2)}) copy-start(bf16[128,128]{1,0:T(8,128)(2,1)} %get-tuple-element.46) | copy-start | bytes 98308
  230.1 6.7 %copy-start.27 = (bf16[128,128]{1,0:T(8,128)(2,1)S(1)}, bf16[128,128]{1,0:T(8,128)(2,1)}, u32[]{:S(2)}) copy-start(bf16[128,128]{1,0:T(8,128)(2,1)} %get-tuple-element.47) | copy-start | bytes 98308
  231.1 19.4 %all-to-all-start.2 = ((bf16[8,8,9216]{2,1,0:T(8,128)(2,1)}), bf16[8,8,9216]{2,1,0:T(8,128)(2,1)S(1)}, u32[]{:S(2)}, u32[]{:S(2)}) async-start(bf16[8,8,9216]{2,1,0:T(8,128)(2,1)} %mix_out.6), calls=%async_computation.2 | async-start | bytes 2359296 | tf_op jit(solution)/shard_map/all_to_all | solution.py:426
  269.3 14.7 %copy-start.20 = (bf16[8,4,9216]{2,1,0:T(4,128)(2,1)S(1)}, bf16[8,4,9216]{2,1,0:T(4,128)(2,1)}, u32[]{:S(2)}) copy-start(bf16[8,4,9216]{2,1,0:T(4,128)(2,1)} %get-tuple-element.36) | copy-start | bytes 1769476
  269.3 28.1 %copy-start.14 = (bf16[8,8,9216]{2,1,0:T(8,128)(2,1)S(1)}, bf16[8,8,9216]{2,1,0:T(8,128)(2,1)}, u32[]{:S(2)}) copy-start(bf16[8,8,9216]{2,1,0:T(8,128)(2,1)} %get-tuple-element.39) | copy-start | bytes 3538948
  297.3 19.8 %copy-start.13 = (bf16[8,8,9216]{2,1,0:T(8,128)(2,1)S(1)}, bf16[8,8,9216]{2,1,0:T(8,128)(2,1)}, u32[]{:S(2)}) copy-start(bf16[8,8,9216]{2,1,0:T(8,128)(2,1)} %get-tuple-element.33) | copy-start | bytes 3538948
  336.8 73.5 %all-to-all-start.7 = ((bf16[8,8,9216]{2,1,0:T(8,128)(2,1)}), bf16[8,8,9216]{2,1,0:T(8,128)(2,1)S(1)}, u32[]{:S(2)}, u32[]{:S(2)}) async-start(bf16[8,8,9216]{2,1,0:T(8,128)(2,1)} %get-tuple-element.30), calls=%async_computation.7 | async-start | bytes 2359296 | tf_op jit(solution)/shard_map/all_to_all | solution.py:426
  350.3 54.8 %collective-permute-start.8 = (bf16[8,4,9216]{2,1,0:T(4,128)(2,1)}, bf16[8,4,9216]{2,1,0:T(4,128)(2,1)S(1)}, u32[]{:S(2)}, u32[]{:S(2)}) collective-permute-start(bf16[8,4,9216]{2,1,0:T(4,128)(2,1)} %get-tuple-element.41), channel_id=1, source_target_pairs={{0,8},{8,0},{1,9},{9,1},{2,10},{10,2},{3,11},{11,3},{4,12},{12,4},... | collective-permute-start | bytes 1769480 | tf_op jit(solution)/shard_map/ppermute | solution.py:430
  358.6 40.7 %collective-permute-start.9 = (bf16[8,2,9216]{2,1,0:T(2,128)(2,1)}, bf16[8,2,9216]{2,1,0:T(2,128)(2,1)S(1)}, u32[]{:S(2)}, u32[]{:S(2)}) collective-permute-start(bf16[8,2,9216]{2,1,0:T(2,128)(2,1)} %get-tuple-element.44), channel_id=1, source_target_pairs={{0,8},{8,0},{1,9},{9,1},{2,10},{10,2},{3,11},{11,3},{4,12},{12,4},... | collective-permute-start | bytes 884744 | tf_op jit(solution)/shard_map/ppermute | solution.py:430
  363.9 41.2 %collective-permute-start.7 = (bf16[8,2,9216]{2,1,0:T(2,128)(2,1)}, bf16[8,2,9216]{2,1,0:T(2,128)(2,1)S(1)}, u32[]{:S(2)}, u32[]{:S(2)}) collective-permute-start(bf16[8,2,9216]{2,1,0:T(2,128)(2,1)} %get-tuple-element.38), channel_id=1, source_target_pairs={{0,8},{8,0},{1,9},{9,1},{2,10},{10,2},{3,11},{11,3},{4,12},{12,4},... | collective-permute-start | bytes 884744 | tf_op jit(solution)/shard_map/ppermute | solution.py:430
  399.3 5.8 %copy-start.23 = (bf16[8,2,9216]{2,1,0:T(2,128)(2,1)}, bf16[8,2,9216]{2,1,0:T(2,128)(2,1)S(1)}, u32[]{:S(2)}) copy-start(bf16[8,2,9216]{2,1,0:T(2,128)(2,1)S(1)} %collective-permute-done.9.refs_5_) | copy-start | bytes 884740
  411.3 73.1 %all-to-all-start.13 = ((bf16[8,8,9216]{2,1,0:T(8,128)(2,1)}), bf16[8,8,9216]{2,1,0:T(8,128)(2,1)S(1)}, u32[]{:S(2)}, u32[]{:S(2)}) async-start(bf16[8,8,9216]{2,1,0:T(8,128)(2,1)} %add.5), calls=%async_computation.13 | async-start | bytes 2359296 | tf_op jit(solution)/shard_map/all_to_all | solution.py:426
  424.5 42.6 %collective-permute-start.6 = (bf16[8,4,9216]{2,1,0:T(4,128)(2,1)}, bf16[8,4,9216]{2,1,0:T(4,128)(2,1)S(1)}, u32[]{:S(2)}, u32[]{:S(2)}) collective-permute-start(bf16[8,4,9216]{2,1,0:T(4,128)(2,1)} %get-tuple-element.35), channel_id=1, source_target_pairs={{0,8},{8,0},{1,9},{9,1},{2,10},{10,2},{3,11},{11,3},{4,12},{12,4},... | collective-permute-start | bytes 1769480 | tf_op jit(solution)/shard_map/ppermute | solution.py:430
  437.1 42.5 %collective-permute-start.5 = (bf16[8,4,9216]{2,1,0:T(4,128)(2,1)}, bf16[8,4,9216]{2,1,0:T(4,128)(2,1)S(1)}, u32[]{:S(2)}, u32[]{:S(2)}) collective-permute-start(bf16[8,4,9216]{2,1,0:T(4,128)(2,1)} %get-tuple-element.32), channel_id=1, source_target_pairs={{0,8},{8,0},{1,9},{9,1},{2,10},{10,2},{3,11},{11,3},{4,12},{12,4},... | collective-permute-start | bytes 1769480 | tf_op jit(solution)/shard_map/ppermute | solution.py:430
  467.1 12.4 %copy-start.16 = (bf16[8,4,9216]{2,1,0:T(4,128)(2,1)}, bf16[8,4,9216]{2,1,0:T(4,128)(2,1)S(1)}, u32[]{:S(2)}) copy-start(bf16[8,4,9216]{2,1,0:T(4,128)(2,1)S(1)} %collective-permute-done.6.refs_3_) | copy-start | bytes 1769476
  485.4 19.4 %all-to-all-start.9 = ((bf16[8,8,9216]{2,1,0:T(8,128)(2,1)}), bf16[8,8,9216]{2,1,0:T(8,128)(2,1)S(1)}, u32[]{:S(2)}, u32[]{:S(2)}) async-start(bf16[8,8,9216]{2,1,0:T(8,128)(2,1)} %add.4), calls=%async_computation.9 | async-start | bytes 2359296 | tf_op jit(solution)/shard_map/all_to_all | solution.py:426
  (20 other events, 36.2 us)

commit v9 on v8

--- a/solution.py
+++ b/solution.py
@@ -248,36 +248,39 @@
     return [pl.ds(row + tile * rows, folds.groups, stride=folds.tiles * rows) for tile in range(folds.tiles)]
 
 
-def mix_out_kernel(folds, near, cols, width, half_ref, both_ref, there_ref, *refs):
+def mix_out_kernel(folds, near, cols, width, half_ref, left_ref, right_ref, there_ref, *refs):
     earlier_refs, (mix_ref, staged, left, right) = refs[:-4], refs[-4:]
     parts = near * cols
     rows = parts * width
     block = folds.rows
     far = cols // near
 
-    stage(both_ref, staged)
-
-    @pl.loop(0, rows, unroll=8)
-    def _(step):
-        source, channel = step // width, step % width
-        row = source * 2 * width + channel
-        pieces = folds.split([staged[at, :] for at in lane_rows_of(folds, 2 * rows, row)], clear=True)
-        at = (channel * cols + source % cols) * near * block + (source // cols) * block
-        left[pl.ds(pl.multiple_of(at, block), block), :] = jnp.concatenate(pieces, axis=0).astype(jnp.bfloat16)
-
-    def place(half, total, shift, height):
+    def unfold(ref, shift, store):
+        height = ref.shape[1]
+        stage(ref, staged)
+
         @pl.loop(0, rows, unroll=8)
         def _(step):
             source, channel = step // width, step % width
             row = source * height + shift + channel
-            pieces = folds.split([staged[at, :] for at in lane_rows_of(folds, total, row)])
+            store(source, channel, [staged[at, :] for at in lane_rows_of(folds, parts * height, row)])
+
+    def store_left(source, channel, lane_rows):
+        pieces = folds.split(lane_rows, clear=True)
+        at = (channel * cols + source % cols) * near * block + (source // cols) * block
+        left[pl.ds(pl.multiple_of(at, block), block), :] = jnp.concatenate(pieces, axis=0).astype(jnp.bfloat16)
+
+    def store_right(half):
+        def store(source, channel, lane_rows):
             at = ((channel * cols + source % cols) * far + half) * near * block + (source // cols) * block
-            for phase, piece in enumerate(pieces):
+            for phase, piece in enumerate(folds.split(lane_rows)):
                 right[pl.ds(at + phase, folds.groups, stride=folds.turn), :] = piece
 
-    place(half_ref[0], 2 * rows, width, 2 * width)
-    stage(there_ref, staged)
-    place(half_ref[1], rows, 0, width)
+        return store
+
+    unfold(left_ref, 0, store_left)
+    unfold(right_ref, right_ref.shape[1] - width, store_right(half_ref[0]))
+    unfold(there_ref, 0, store_right(half_ref[1]))
 
     @pl.loop(0, width, unroll=1)
     def _(channel):
@@ -351,13 +354,13 @@
 VMEM_SPEC = pl.BlockSpec(memory_space=pltpu.VMEM)
 
 
-def run_mix_out(folds, near, cols, halves, both, there, earlier=()):
+def run_mix_out(folds, near, cols, halves, left, right, there, earlier=()):
     parts, width, positions = there.shape
     rows = parts * width
     block = folds.rows
     return pl.pallas_call(
         functools.partial(mix_out_kernel, folds, near, cols, width),
-        in_specs=[SMEM_SPEC] + [VMEM_SPEC] * (2 + len(earlier)),
+        in_specs=[SMEM_SPEC] + [VMEM_SPEC] * (3 + len(earlier)),
         out_specs=VMEM_SPEC,
         out_shape=jax.ShapeDtypeStruct((parts, width + sum(e.shape[1] for e in earlier), positions), jnp.bfloat16),
         scratch_shapes=[
@@ -367,7 +370,7 @@
         ],
         compiler_params=pltpu.CompilerParams(vmem_limit_bytes=BUDGET),
         name="mix_out",
-    )(halves, both, there, *earlier)
+    )(halves, left, right, there, *earlier)
 
 
 def add_kernel(*refs):
@@ -417,8 +420,8 @@
     )(halves, both)
 
 
-SHARES = (1, 2, 2, 2, 1)
-GROUPS = ((1, 2), (0, 3, 4))
+SHARES = (1, 1, 1, 1)
+GROUPS = ((0, 1), (2, 3))
 PIECES = len(SHARES)
 
 
@@ -441,15 +444,24 @@
     half = lax.axis_index("far")
     halves = jnp.stack([half, 1 - half]).astype(jnp.int32)
 
-    def rows_of(project, *chosen):
+    def rows_of(project, *arrays):
         ga, va, gb, vb = (rows.reshape(parts, width, features) for rows in jnp.split(project.T, 4, axis=0))
 
         def ordered(left, right):
-            rows = [array[:, begins[piece] : ends[piece]] for piece in chosen for array in (left, right)]
-            pairs = [jnp.concatenate(rows[at : at + 2], axis=1).reshape(-1, features) for at in range(0, len(rows), 2)]
-            return pairs
+            return [
+                jnp.concatenate(
+                    [rows[:, begins[piece] : ends[piece]] for rows, piece in zip((left, right), pair) if piece is not None],
+                    axis=1,
+                ).reshape(-1, features)
+                for pair in arrays
+            ]
 
         return jnp.concatenate(ordered(ga, gb) + ordered(va, vb))
+
+    def shapes_of(*arrays):
+        return [
+            (parts, sum(ends[piece] - begins[piece] for piece in pair if piece is not None)) for pair in arrays
+        ]
 
     def in_groups(array):
         rows = array.reshape(parts, width, -1)
@@ -462,23 +474,24 @@
     gain_1, project_1, gate_1, norm_1, final_1, gain_2, project_2, gate_2, norm_2, final_2 = weights
     state = pair_input.reshape(-1, features)
 
-    shapes = [(parts, 2 * (end - begin)) for begin, end in zip(begins, ends)]
-    rest = range(1, PIECES)
-    both, mixed, mixes = [], [None] * PIECES, []
-    out = run_projections(state, gain_1, rows_of(project_1, 0), shapes[:1])
-    out += run_projections(state, gain_1, rows_of(project_1, *rest), shapes[1:])
-    for piece in range(PIECES):
-        both.append(exchange(out[piece]))
+    ahead = [(None, 0)] + [(piece, piece + 1) for piece in range(PIECES - 1)] + [(PIECES - 1, None)]
+    level = [(piece, piece) for piece in range(PIECES)]
+    sent, mixed, mixes = [], [None] * PIECES, []
+    out = run_projections(state, gain_1, rows_of(project_1, *ahead[:1]), shapes_of(*ahead[:1]))
+    out += run_projections(state, gain_1, rows_of(project_1, *ahead[1:]), shapes_of(*ahead[1:]))
+    for array in out:
+        sent.append(exchange(array))
     for piece in range(PIECES):
         group = next(group for group in GROUPS if piece in group)
-        there = across(both[piece][:, both[piece].shape[1] // 2 :, :])
+        right, left = sent[piece], sent[piece + 1]
+        there = across(right[:, right.shape[1] - (ends[piece] - begins[piece]) :, :])
         earlier = [mixed[other] for other in group[:-1]] if piece == group[-1] else ()
-        mixed[piece] = run_mix_out(folds, near, cols, halves, both[piece], there, earlier)
+        mixed[piece] = run_mix_out(folds, near, cols, halves, left, right, there, earlier)
         if piece == group[-1]:
             mixes.append(exchange(mixed[piece]))
-    onward = (gain_2, rows_of(project_2, 0), shapes[:1])
+    onward = (gain_2, rows_of(project_2, *level[:1]), shapes_of(*level[:1]))
     middle, *out = run_finish(mixes, state, gain_1, gate_1, in_groups(norm_1), in_groups(final_1), onward)
-    out += run_projections(middle, gain_2, rows_of(project_2, *rest), shapes[1:])
+    out += run_projections(middle, gain_2, rows_of(project_2, *level[1:]), shapes_of(*level[1:]))
     both, parted, mixes = [], [], []
     for piece in range(PIECES):
         both.append(exchange(out[piece]))

time: 516 us -> 487 us (0.944)
  blocking collectives: 120 us -> 94 us
  waiting for transfers between devices: 187 us -> 202 us
  local copies, waits for them, and re-layouts: 25.2 us -> 15 us
    all_to_all x7 -> x5, blocking collectives: 120 us -> 94 us  [exchange(): return lax.all_to_all(array, EVERY, split_axis=0, concat_axis=0, tiled=True)]
    all_to_all x7 -> x8, waiting for transfers between devices: 27.2 us -> 36.7 us  [exchange(): return lax.all_to_all(array, EVERY, split_axis=0, concat_axis=0, tiled=True)]
    ppermute x10 -> x8, starting transfers between devices: 17.4 us -> 12 us  [across(): return lax.ppermute(array, 'far', ((0, 1), (1, 0)))]
    slice x23 -> x7, local copies, waits for them, and re-layouts: 6.39 us -> 1.04 us  [the longest x3 0.92 us: in_halves(): there = across(right[:, right.shape[1] - (ends[piece] - begins[piece]):, :])]
    ppermute x10 -> x8, waiting for transfers between devices: 160 us -> 165 us  [across(): return lax.ppermute(array, 'far', ((0, 1), (1, 0)))]
    all_to_all x7 -> x8, starting transfers between devices: 27 us -> 30.5 us  [exchange(): return lax.all_to_all(array, EVERY, split_axis=0, concat_axis=0, tiled=True)]
    unnamed x74 -> x57, local copies, waits for them, and re-layouts: 14.7 us -> 11.9 us
    pallas_call x5 -> x4, Pallas kernels: 39.7 us -> 38.8 us  [run_mix_in(): pl.pallas_call(functools.partial(mix_in_kernel, folds, near, cols, width)...]
  transfers between devices with their start and end apart: 17 -> 16, of which waited for: 10 -> 12; matrix products, arithmetic and copies ran while one was open for 4% -> 1% of each run, Pallas kernels for 19% -> 21%
where the time goes in v9:
time: 487 us; the launch traced here: 485 us
  waiting for transfers between devices  202 us (41%)
  Pallas kernels  128 us (26%)
  blocking collectives  94 us (19%)
  starting transfers between devices  42.6 us (9%)
  local copies, waits for them, and re-layouts  15 us (3%)
    ppermute x8, waiting for transfers between devices, across(): return lax.ppermute(array, 'far', ((0, 1), (1, 0)))  165 us
    all_to_all x5, blocking collectives, exchange(): return lax.all_to_all(array, EVERY, split_axis=0, concat_axis=0, tiled=True)  94 us
    pallas_call x4, Pallas kernels, run_mix_out(): pl.pallas_call(functools.partial(mix_out_kernel, folds, near, cols, width...  42.5 us
    pallas_call x4, Pallas kernels, run_mix_in(): pl.pallas_call(functools.partial(mix_in_kernel, folds, near, cols, width)...  38.8 us
    all_to_all x8, waiting for transfers between devices, exchange(): return lax.all_to_all(array, EVERY, split_axis=0, concat_axis=0, tiled=True)  36.7 us
    all_to_all x8, starting transfers between devices, exchange(): return lax.all_to_all(array, EVERY, split_axis=0, concat_axis=0, tiled=True)  30.5 us
    pallas_call x3, Pallas kernels, run_projections(): pl.pallas_call(project_kernel, grid=(positions // step,), in_specs=[pl.Bl...  19.7 us
    pallas_call x2, Pallas kernels, run_finish(): pl.pallas_call(functools.partial(finish_kernel, len(mixes), onward is not...  18.7 us
  transfers between devices with their start and end apart: 16, of which 12 were waited for; matrix products, arithmetic and copies ran while one was open for 1% of the time, Pallas kernels for 21%

profile of v9, /device:TPU:0, one launch (start us, length us, event | category | flops | bytes accessed | tf_op | source)
XLA Modules:
  0.0 485.0 jit_solution(12020744939004741663)
XLA Ops:
  1.7 5.6 %project.4 = bf16[8,4,9216]{2,1,0:T(4,128)(2,1)} custom-call(bf16[9216,128]{1,0:T(8,128)(2,1)} %bitcast.90, f32[1,128]{1,0:T(1,128)} %bitcast.109, bf16[64,128]{1,0:T(8,128)(2,1)} %pad_maximum_fusion.3.rows_ref), custom_call_target="tpu_custom_call" | custom-call | tf_op jit(solution)/shard_map/project/pallas_call | solution.py:142
  7.3 5.3 %all-to-all-start.2 = ((bf16[8,4,9216]{2,1,0:T(4,128)(2,1)}), bf16[8,4,9216]{2,1,0:T(4,128)(2,1)S(1)}, u32[]{:S(2)}, u32[]{:S(2)}) async-start(bf16[8,4,9216]{2,1,0:T(4,128)(2,1)} %project.4), calls=%async_computation.2 | async-start | bytes 1179648 | tf_op jit(solution)/shard_map/all_to_all | solution.py:429
  13.4 7.2 %project.3 = (bf16[8,8,9216]{2,1,0:T(8,128)(2,1)}, bf16[8,8,9216]{2,1,0:T(8,128)(2,1)}, bf16[8,8,9216]{2,1,0:T(8,128)(2,1)}, bf16[8,4,9216]{2,1,0:T(4,128)(2,1)}) custom-call(bf16[9216,128]{1,0:T(8,128)(2,1)} %bitcast.91, f32[1,128]{1,0:T(1,128)} %bitcast.110, bf16[448,128]{1,0:T(8,128)(2,1)} %copy-done.20), custom_call_target="tpu_custom_call" | custom-call | tf_op jit(solution)/shard_map/project/pallas_call | solution.py:142
  22.1 14.5 %all_to_all.65.left_ref = bf16[8,4,9216]{2,1,0:T(4,128)(2,1)} all-to-all(bf16[8,4,9216]{2,1,0:T(4,128)(2,1)} %get-tuple-element.24), channel_id=1, replica_groups=mesh['groups'=2,'far'=2,'near'=2,'chan'=2,'sub'=2] {'near','chan','sub'}, dimensions={0} | all-to-all | bytes 1179648 | tf_op jit(solution)/shard_map/all_to_all | solution.py:429
  36.6 19.8 %all_to_all.66.left_ref.right_ref = bf16[8,8,9216]{2,1,0:T(8,128)(2,1)} all-to-all(bf16[8,8,9216]{2,1,0:T(8,128)(2,1)S(1)} %copy-done.11), channel_id=1, replica_groups=mesh['groups'=2,'far'=2,'near'=2,'chan'=2,'sub'=2] {'near','chan','sub'}, dimensions={0} | all-to-all | bytes 2359296 | tf_op jit(solution)/shard_map/all_to_all | solution.py:429
  56.4 18.9 %all_to_all.67.left_ref.right_ref = bf16[8,8,9216]{2,1,0:T(8,128)(2,1)S(1)} all-to-all(bf16[8,8,9216]{2,1,0:T(8,128)(2,1)S(1)} %copy-done.10), channel_id=1, replica_groups=mesh['groups'=2,'far'=2,'near'=2,'chan'=2,'sub'=2] {'near','chan','sub'}, dimensions={0} | all-to-all | bytes 2359296 | tf_op jit(solution)/shard_map/all_to_all | solution.py:429
  83.0 22.6 %collective-permute-done.1.there_ref = bf16[8,4,9216]{2,1,0:T(4,128)(2,1)} collective-permute-done((bf16[8,4,9216]{2,1,0:T(4,128)(2,1)S(1)}, bf16[8,4,9216]{2,1,0:T(4,128)(2,1)}, u32[]{:S(2)}, u32[]{:S(2)}) %collective-permute-start.1) | collective-permute-done | bytes 589856 | tf_op jit(solution)/shard_map/ppermute | solution.py:433
  105.6 10.2 %mix_out.4.refs_0_ = bf16[8,4,9216]{2,1,0:T(4,128)(2,1)} custom-call(s32[2]{0:T(128)} %pad_add_fusion.half_ref, bf16[8,8,9216]{2,1,0:T(8,128)(2,1)} %copy-done, bf16[8,4,9216]{2,1,0:T(4,128)(2,1)} %copy-done.9, bf16[8,4,9216]{2,1,0:T(4,128)(2,1)} %collective-permute-done.1.there_ref), custom_call_target="tpu_custom_call" | custom-call | tf_op jit(solution)/shard_map/mix_out/pallas_call | solution.py:361
  115.7 17.7 %collective-permute-done.there_ref = bf16[8,4,9216]{2,1,0:T(4,128)(2,1)S(1)} collective-permute-done((bf16[8,4,9216]{2,1,0:T(4,128)(2,1)S(1)}, bf16[8,4,9216]{2,1,0:T(4,128)(2,1)S(1)}, u32[]{:S(2)}, u32[]{:S(2)}) %collective-permute-start) | collective-permute-done | bytes 589856 | tf_op jit(solution)/shard_map/ppermute | solution.py:433
  134.3 11.1 %mix_out.5 = bf16[8,8,9216]{2,1,0:T(8,128)(2,1)} custom-call(s32[2]{0:T(128)} %pad_add_fusion.half_ref, bf16[8,8,9216]{2,1,0:T(8,128)(2,1)} %all_to_all.66.left_ref.right_ref, bf16[8,8,9216]{2,1,0:T(8,128)(2,1)} %copy-done, bf16[8,4,9216]{2,1,0:T(4,128)(2,1)} %copy-done.13, bf16[8,4,9216]{2,1,0:T(4,128)(2,1)} %mix_out.4.refs_0_), custom_call_target="tpu_custom_call" | custom-call | tf_op jit(solution)/shard_map/mix_out/pallas_call | solution.py:361
  152.8 22.9 %collective-permute-done.3.there_ref = bf16[8,4,9216]{2,1,0:T(4,128)(2,1)S(1)} collective-permute-done((bf16[8,4,9216]{2,1,0:T(4,128)(2,1)S(1)}, bf16[8,4,9216]{2,1,0:T(4,128)(2,1)S(1)}, u32[]{:S(2)}, u32[]{:S(2)}) %collective-permute-start.3) | collective-permute-done | bytes 589856 | tf_op jit(solution)/shard_map/ppermute | solution.py:433
  176.5 10.5 %mix_out.6.refs_0_ = bf16[8,4,9216]{2,1,0:T(4,128)(2,1)} custom-call(s32[2]{0:T(128)} %pad_add_fusion.half_ref, bf16[8,8,9216]{2,1,0:T(8,128)(2,1)} %copy-done.2, bf16[8,8,9216]{2,1,0:T(8,128)(2,1)} %all_to_all.66.left_ref.right_ref, bf16[8,4,9216]{2,1,0:T(4,128)(2,1)} %copy-done.19), custom_call_target="tpu_custom_call" | custom-call | tf_op jit(solution)/shard_map/mix_out/pallas_call | solution.py:361
  187.0 17.3 %collective-permute-done.2.there_ref = bf16[8,4,9216]{2,1,0:T(4,128)(2,1)S(1)} collective-permute-done((bf16[8,4,9216]{2,1,0:T(4,128)(2,1)S(1)}, bf16[8,4,9216]{2,1,0:T(4,128)(2,1)S(1)}, u32[]{:S(2)}, u32[]{:S(2)}) %collective-permute-start.2) | collective-permute-done | bytes 589856 | tf_op jit(solution)/shard_map/ppermute | solution.py:433
  205.1 10.8 %mix_out.7 = bf16[8,8,9216]{2,1,0:T(8,128)(2,1)} custom-call(s32[2]{0:T(128)} %pad_add_fusion.half_ref, bf16[8,4,9216]{2,1,0:T(4,128)(2,1)} %all_to_all.65.left_ref, bf16[8,8,9216]{2,1,0:T(8,128)(2,1)} %copy-done.2, bf16[8,4,9216]{2,1,0:T(4,128)(2,1)} %copy-done.16, bf16[8,4,9216]{2,1,0:T(4,128)(2,1)} %mix_out.6.refs_0_), custom_call_target="tpu_custom_call" | custom-call | tf_op jit(solution)/shard_map/mix_out/pallas_call | solution.py:361
  223.4 13.0 %all-to-all-done.6.refs_1_ = bf16[8,8,9216]{2,1,0:T(8,128)(2,1)S(1)} async-done(((bf16[8,8,9216]{2,1,0:T(8,128)(2,1)}), bf16[8,8,9216]{2,1,0:T(8,128)(2,1)S(1)}, u32[]{:S(2)}, u32[]{:S(2)}) %all-to-all-start.6) | async-done | bytes 1179680 | tf_op jit(solution)/shard_map/all_to_all | solution.py:429
  237.4 10.8 %finish.2 = (bf16[9216,128]{1,0:T(8,128)(2,1)}, bf16[8,8,9216]{2,1,0:T(8,128)(2,1)}) custom-call(bf16[8,8,9216]{2,1,0:T(8,128)(2,1)} %copy-done.7, bf16[8,8,9216]{2,1,0:T(8,128)(2,1)} %copy-done.8, bf16[9216,128]{1,0:T(8,128)(2,1)} %bitcast.92, f32[1,128]{1,0:T(1,128)} %bitcast.111, bf16[128,128]{1,0:T(8,128)(2,1)} %refs_4_.2, f32[128,1]{1,0:T(8,128)} %copy.56.refs_5_, ...), custom_call_target="tpu_custom_call" | custom-call | tf_op jit(solution)/shard_map/finish/pallas_call | solution.py:164
  252.6 6.9 %project.5 = (bf16[8,8,9216]{2,1,0:T(8,128)(2,1)}, bf16[8,8,9216]{2,1,0:T(8,128)(2,1)}, bf16[8,8,9216]{2,1,0:T(8,128)(2,1)}) custom-call(bf16[9216,128]{1,0:T(8,128)(2,1)} %get-tuple-element.29.state_ref.refs_2_, f32[1,128]{1,0:T(1,128)} %bitcast.113, bf16[384,128]{1,0:T(8,128)(2,1)} %copy-done.21), custom_call_target="tpu_custom_call" | custom-call | tf_op jit(solution)/shard_map/project/pallas_call | solution.py:142
  259.5 8.1 %all-to-all-done.7.both_ref = bf16[8,8,9216]{2,1,0:T(8,128)(2,1)S(1)} async-done(((bf16[8,8,9216]{2,1,0:T(8,128)(2,1)}), bf16[8,8,9216]{2,1,0:T(8,128)(2,1)S(1)}, u32[]{:S(2)}, u32[]{:S(2)}) %all-to-all-start.7) | async-done | bytes 1179680 | tf_op jit(solution)/shard_map/all_to_all | solution.py:429
  267.6 21.0 %all_to_all.68.both_ref = bf16[8,8,9216]{2,1,0:T(8,128)(2,1)} all-to-all(bf16[8,8,9216]{2,1,0:T(8,128)(2,1)} %get-tuple-element.30), channel_id=1, replica_groups=mesh['groups'=2,'far'=2,'near'=2,'chan'=2,'sub'=2] {'near','chan','sub'}, dimensions={0} | all-to-all | bytes 2359296 | tf_op jit(solution)/shard_map/all_to_all | solution.py:429
  288.6 19.7 %all_to_all.69.both_ref = bf16[8,8,9216]{2,1,0:T(8,128)(2,1)} all-to-all(bf16[8,8,9216]{2,1,0:T(8,128)(2,1)S(1)} %copy-done.12), channel_id=1, replica_groups=mesh['groups'=2,'far'=2,'near'=2,'chan'=2,'sub'=2] {'near','chan','sub'}, dimensions={0} | all-to-all | bytes 2359296 | tf_op jit(solution)/shard_map/all_to_all | solution.py:429
  311.9 9.7 %mix_in.4 = (f32[8,4,9216]{2,1,0:T(4,128)}, bf16[8,4,9216]{2,1,0:T(4,128)(2,1)}) custom-call(s32[2]{0:T(128)} %pad_add_fusion.half_ref, bf16[8,8,9216]{2,1,0:T(8,128)(2,1)} %copy-done.6), custom_call_target="tpu_custom_call" | custom-call | tf_op jit(solution)/shard_map/mix_in/pallas_call | solution.py:403
  324.5 9.7 %mix_in.5 = (f32[8,4,9216]{2,1,0:T(4,128)}, bf16[8,4,9216]{2,1,0:T(4,128)(2,1)}) custom-call(s32[2]{0:T(128)} %pad_add_fusion.half_ref, bf16[8,8,9216]{2,1,0:T(8,128)(2,1)} %all_to_all.68.both_ref), custom_call_target="tpu_custom_call" | custom-call | tf_op jit(solution)/shard_map/mix_in/pallas_call | solution.py:403
  334.3 30.0 %collective-permute-done.4.refs_1_ = bf16[8,4,9216]{2,1,0:T(4,128)(2,1)S(1)} collective-permute-done((bf16[8,4,9216]{2,1,0:T(4,128)(2,1)}, bf16[8,4,9216]{2,1,0:T(4,128)(2,1)S(1)}, u32[]{:S(2)}, u32[]{:S(2)}) %collective-permute-start.4) | collective-permute-done | bytes 589856 | tf_op jit(solution)/shard_map/ppermute | solution.py:433
  364.3 12.4 %collective-permute-done.5.refs_3_ = bf16[8,4,9216]{2,1,0:T(4,128)(2,1)S(1)} collective-permute-done((bf16[8,4,9216]{2,1,0:T(4,128)(2,1)}, bf16[8,4,9216]{2,1,0:T(4,128)(2,1)S(1)}, u32[]{:S(2)}, u32[]{:S(2)}) %collective-permute-start.5) | collective-permute-done | bytes 589856 | tf_op jit(solution)/shard_map/ppermute | solution.py:433
  377.5 4.0 add.4
  386.1 9.7 %mix_in.6 = (f32[8,4,9216]{2,1,0:T(4,128)}, bf16[8,4,9216]{2,1,0:T(4,128)(2,1)}) custom-call(s32[2]{0:T(128)} %pad_add_fusion.half_ref, bf16[8,8,9216]{2,1,0:T(8,128)(2,1)} %all_to_all.69.both_ref), custom_call_target="tpu_custom_call" | custom-call | tf_op jit(solution)/shard_map/mix_in/pallas_call | solution.py:403
  398.6 9.7 %mix_in.7 = (f32[8,4,9216]{2,1,0:T(4,128)}, bf16[8,4,9216]{2,1,0:T(4,128)(2,1)}) custom-call(s32[2]{0:T(128)} %pad_add_fusion.half_ref, bf16[8,8,9216]{2,1,0:T(8,128)(2,1)} %copy-done.5), custom_call_target="tpu_custom_call" | custom-call | tf_op jit(solution)/shard_map/mix_in/pallas_call | solution.py:403
  408.4 30.0 %collective-permute-done.6.refs_1_ = bf16[8,4,9216]{2,1,0:T(4,128)(2,1)S(1)} collective-permute-done((bf16[8,4,9216]{2,1,0:T(4,128)(2,1)}, bf16[8,4,9216]{2,1,0:T(4,128)(2,1)S(1)}, u32[]{:S(2)}, u32[]{:S(2)}) %collective-permute-start.6) | collective-permute-done | bytes 589856 | tf_op jit(solution)/shard_map/ppermute | solution.py:433
  438.4 12.4 %collective-permute-done.7.refs_3_ = bf16[8,4,9216]{2,1,0:T(4,128)(2,1)S(1)} collective-permute-done((bf16[8,4,9216]{2,1,0:T(4,128)(2,1)}, bf16[8,4,9216]{2,1,0:T(4,128)(2,1)S(1)}, u32[]{:S(2)}, u32[]{:S(2)}) %collective-permute-start.7) | collective-permute-done | bytes 589856 | tf_op jit(solution)/shard_map/ppermute | solution.py:433
  451.6 4.0 add.5
  462.0 14.0 %all-to-all-done.12.refs_1_ = bf16[8,8,9216]{2,1,0:T(8,128)(2,1)S(1)} async-done(((bf16[8,8,9216]{2,1,0:T(8,128)(2,1)}), bf16[8,8,9216]{2,1,0:T(8,128)(2,1)S(1)}, u32[]{:S(2)}, u32[]{:S(2)}) %all-to-all-start.12) | async-done | bytes 1179680 | tf_op jit(solution)/shard_map/all_to_all | solution.py:429
  477.1 7.9 %finish.3 = bf16[9216,128]{1,0:T(8,128)(2,1)} custom-call(bf16[8,8,9216]{2,1,0:T(8,128)(2,1)} %copy-done.3, bf16[8,8,9216]{2,1,0:T(8,128)(2,1)} %copy-done.4, bf16[9216,128]{1,0:T(8,128)(2,1)} %get-tuple-element.29.state_ref.refs_2_, f32[1,128]{1,0:T(1,128)} %bitcast.114, bf16[128,128]{1,0:T(8,128)(2,1)} %refs_4_.3, f32[128,1]{1,0:T(8,128)} %copy.57.refs_5_, ...), custom_call_target="tpu_custom_call" | custom-call | tf_op jit(solution)/shard_map/finish/pallas_call | solution.py:164
  (120 shorter events, 57.4 us)
Async XLA Ops:
  7.3 14.8 %all-to-all-start.2 = ((bf16[8,4,9216]{2,1,0:T(4,128)(2,1)}), bf16[8,4,9216]{2,1,0:T(4,128)(2,1)S(1)}, u32[]{:S(2)}, u32[]{:S(2)}) async-start(bf16[8,4,9216]{2,1,0:T(4,128)(2,1)} %project.4), calls=%async_computation.2 | async-start | bytes 1179648 | tf_op jit(solution)/shard_map/all_to_all | solution.py:429
  20.6 16.1 %copy-start.11 = (bf16[8,8,9216]{2,1,0:T(8,128)(2,1)S(1)}, bf16[8,8,9216]{2,1,0:T(8,128)(2,1)}, u32[]{:S(2)}) copy-start(bf16[8,8,9216]{2,1,0:T(8,128)(2,1)} %get-tuple-element.22) | copy-start | bytes 3538948
  22.1 56.8 %copy-start.9 = (bf16[8,4,9216]{2,1,0:T(4,128)(2,1)}, bf16[8,4,9216]{2,1,0:T(4,128)(2,1)S(1)}, u32[]{:S(2)}) copy-start(bf16[8,4,9216]{2,1,0:T(4,128)(2,1)S(1)} %all-to-all-done.2.right_ref) | copy-start | bytes 1769476
  36.6 19.8 %copy-start.10 = (bf16[8,8,9216]{2,1,0:T(8,128)(2,1)S(1)}, bf16[8,8,9216]{2,1,0:T(8,128)(2,1)}, u32[]{:S(2)}) copy-start(bf16[8,8,9216]{2,1,0:T(8,128)(2,1)} %get-tuple-element.23) | copy-start | bytes 3538948
  75.4 6.2 %copy-start = (bf16[8,8,9216]{2,1,0:T(8,128)(2,1)}, bf16[8,8,9216]{2,1,0:T(8,128)(2,1)S(1)}, u32[]{:S(2)}) copy-start(bf16[8,8,9216]{2,1,0:T(8,128)(2,1)S(1)} %all_to_all.67.left_ref.right_ref) | copy-start | bytes 3538948
  75.4 70.0 %all-to-all-start.5 = ((bf16[8,8,9216]{2,1,0:T(8,128)(2,1)}), bf16[8,8,9216]{2,1,0:T(8,128)(2,1)S(1)}, u32[]{:S(2)}, u32[]{:S(2)}) async-start(bf16[8,8,9216]{2,1,0:T(8,128)(2,1)} %get-tuple-element.25), calls=%async_computation.5 | async-start | bytes 2359296 | tf_op jit(solution)/shard_map/all_to_all | solution.py:429
  79.0 26.6 %collective-permute-start.1 = (bf16[8,4,9216]{2,1,0:T(4,128)(2,1)S(1)}, bf16[8,4,9216]{2,1,0:T(4,128)(2,1)}, u32[]{:S(2)}, u32[]{:S(2)}) collective-permute-start(bf16[8,4,9216]{2,1,0:T(4,128)(2,1)S(1)} %all-to-all-done.2.right_ref), channel_id=1, source_target_pairs={{0,8},{8,0},{1,9},{9,1},{2,10},{10,2},{3,11},{11,3},{4,12},{12,4},... | collective-permute-start | bytes 1769480 | tf_op jit(solution)/shard_map/ppermute | solution.py:433
  81.9 51.5 %collective-permute-start = (bf16[8,4,9216]{2,1,0:T(4,128)(2,1)S(1)}, bf16[8,4,9216]{2,1,0:T(4,128)(2,1)S(1)}, u32[]{:S(2)}, u32[]{:S(2)}) collective-permute-start(bf16[8,4,9216]{2,1,0:T(4,128)(2,1)S(1)} %slice.178), channel_id=1, source_target_pairs={{0,8},{8,0},{1,9},{9,1},{2,10},{10,2},{3,11},{11,3},{4,12},{12,4},... | collective-permute-start | bytes 1769480 | tf_op jit(solution)/shard_map/ppermute | solution.py:433
  145.4 3.7 copy-start.1
  145.4 7.0 %copy-start.2 = (bf16[8,8,9216]{2,1,0:T(8,128)(2,1)}, bf16[8,8,9216]{2,1,0:T(8,128)(2,1)S(1)}, u32[]{:S(2)}) copy-start(bf16[8,8,9216]{2,1,0:T(8,128)(2,1)S(1)} %all-to-all-done.5.left_ref.right_ref) | copy-start | bytes 3538948
  145.4 70.6 %all-to-all-start.3 = ((bf16[8,8,9216]{2,1,0:T(8,128)(2,1)}), bf16[8,8,9216]{2,1,0:T(8,128)(2,1)S(1)}, u32[]{:S(2)}, u32[]{:S(2)}) async-start(bf16[8,8,9216]{2,1,0:T(8,128)(2,1)} %mix_out.5), calls=%async_computation.3 | async-start | bytes 2359296 | tf_op jit(solution)/shard_map/all_to_all | solution.py:429
  149.4 26.3 %collective-permute-start.3 = (bf16[8,4,9216]{2,1,0:T(4,128)(2,1)S(1)}, bf16[8,4,9216]{2,1,0:T(4,128)(2,1)S(1)}, u32[]{:S(2)}, u32[]{:S(2)}) collective-permute-start(bf16[8,4,9216]{2,1,0:T(4,128)(2,1)S(1)} %slice.182), channel_id=1, source_target_pairs={{0,8},{8,0},{1,9},{9,1},{2,10},{10,2},{3,11},{11,3},{4,12},{12,4},... | collective-permute-start | bytes 1769480 | tf_op jit(solution)/shard_map/ppermute | solution.py:433
  152.7 51.6 %collective-permute-start.2 = (bf16[8,4,9216]{2,1,0:T(4,128)(2,1)S(1)}, bf16[8,4,9216]{2,1,0:T(4,128)(2,1)S(1)}, u32[]{:S(2)}, u32[]{:S(2)}) collective-permute-start(bf16[8,4,9216]{2,1,0:T(4,128)(2,1)S(1)} %slice.181), channel_id=1, source_target_pairs={{0,8},{8,0},{1,9},{9,1},{2,10},{10,2},{3,11},{11,3},{4,12},{12,4},... | collective-permute-start | bytes 1769480 | tf_op jit(solution)/shard_map/ppermute | solution.py:433
  215.9 4.8 copy-start.25
  215.9 5.9 %copy-start.22 = (bf16[128,512]{1,0:T(8,128)(2,1)S(1)}, bf16[128,512]{1,0:T(8,128)(2,1)}, u32[]{:S(2)}) copy-start(bf16[128,512]{1,0:T(8,128)(2,1)} %param.18) | copy-start | bytes 393220
  215.9 6.2 %copy-start.23 = (bf16[128,128]{1,0:T(8,128)(2,1)S(1)}, bf16[128,128]{1,0:T(8,128)(2,1)}, u32[]{:S(2)}) copy-start(bf16[128,128]{1,0:T(8,128)(2,1)} %param.16) | copy-start | bytes 98308
  217.0 19.4 %all-to-all-start.6 = ((bf16[8,8,9216]{2,1,0:T(8,128)(2,1)}), bf16[8,8,9216]{2,1,0:T(8,128)(2,1)S(1)}, u32[]{:S(2)}, u32[]{:S(2)}) async-start(bf16[8,8,9216]{2,1,0:T(8,128)(2,1)} %mix_out.7), calls=%async_computation.6 | async-start | bytes 2359296 | tf_op jit(solution)/shard_map/all_to_all | solution.py:429
  236.3 1.1 copy-start.8
  248.2 19.4 %all-to-all-start.7 = ((bf16[8,8,9216]{2,1,0:T(8,128)(2,1)}), bf16[8,8,9216]{2,1,0:T(8,128)(2,1)S(1)}, u32[]{:S(2)}, u32[]{:S(2)}) async-start(bf16[8,8,9216]{2,1,0:T(8,128)(2,1)} %get-tuple-element.26), calls=%async_computation.7 | async-start | bytes 2359296 | tf_op jit(solution)/shard_map/all_to_all | solution.py:429
  267.6 21.1 %copy-start.6 = (bf16[8,8,9216]{2,1,0:T(8,128)(2,1)}, bf16[8,8,9216]{2,1,0:T(8,128)(2,1)S(1)}, u32[]{:S(2)}) copy-start(bf16[8,8,9216]{2,1,0:T(8,128)(2,1)S(1)} %all-to-all-done.7.both_ref) | copy-start | bytes 3538948
  267.6 21.1 %copy-start.12 = (bf16[8,8,9216]{2,1,0:T(8,128)(2,1)S(1)}, bf16[8,8,9216]{2,1,0:T(8,128)(2,1)}, u32[]{:S(2)}) copy-start(bf16[8,8,9216]{2,1,0:T(8,128)(2,1)} %get-tuple-element.33) | copy-start | bytes 3538948
  308.3 73.2 %all-to-all-start.11 = ((bf16[8,8,9216]{2,1,0:T(8,128)(2,1)}), bf16[8,8,9216]{2,1,0:T(8,128)(2,1)S(1)}, u32[]{:S(2)}, u32[]{:S(2)}) async-start(bf16[8,8,9216]{2,1,0:T(8,128)(2,1)} %get-tuple-element.36), calls=%async_computation.11 | async-start | bytes 2359296 | tf_op jit(solution)/shard_map/all_to_all | solution.py:429
  321.6 42.7 %collective-permute-start.4 = (bf16[8,4,9216]{2,1,0:T(4,128)(2,1)}, bf16[8,4,9216]{2,1,0:T(4,128)(2,1)S(1)}, u32[]{:S(2)}, u32[]{:S(2)}) collective-permute-start(bf16[8,4,9216]{2,1,0:T(4,128)(2,1)} %get-tuple-element.28), channel_id=1, source_target_pairs={{0,8},{8,0},{1,9},{9,1},{2,10},{10,2},{3,11},{11,3},{4,12},{12,4},... | collective-permute-start | bytes 1769480 | tf_op jit(solution)/shard_map/ppermute | solution.py:433
  334.3 42.3 %collective-permute-start.5 = (bf16[8,4,9216]{2,1,0:T(4,128)(2,1)}, bf16[8,4,9216]{2,1,0:T(4,128)(2,1)S(1)}, u32[]{:S(2)}, u32[]{:S(2)}) collective-permute-start(bf16[8,4,9216]{2,1,0:T(4,128)(2,1)} %get-tuple-element.32), channel_id=1, source_target_pairs={{0,8},{8,0},{1,9},{9,1},{2,10},{10,2},{3,11},{11,3},{4,12},{12,4},... | collective-permute-start | bytes 1769480 | tf_op jit(solution)/shard_map/ppermute | solution.py:433
  364.3 12.4 %copy-start.15 = (bf16[8,4,9216]{2,1,0:T(4,128)(2,1)}, bf16[8,4,9216]{2,1,0:T(4,128)(2,1)S(1)}, u32[]{:S(2)}) copy-start(bf16[8,4,9216]{2,1,0:T(4,128)(2,1)S(1)} %collective-permute-done.4.refs_1_) | copy-start | bytes 1769476
  382.5 73.1 %all-to-all-start.9 = ((bf16[8,8,9216]{2,1,0:T(8,128)(2,1)}), bf16[8,8,9216]{2,1,0:T(8,128)(2,1)S(1)}, u32[]{:S(2)}, u32[]{:S(2)}) async-start(bf16[8,8,9216]{2,1,0:T(8,128)(2,1)} %add.4), calls=%async_computation.9 | async-start | bytes 2359296 | tf_op jit(solution)/shard_map/all_to_all | solution.py:429
  395.8 42.6 %collective-permute-start.6 = (bf16[8,4,9216]{2,1,0:T(4,128)(2,1)}, bf16[8,4,9216]{2,1,0:T(4,128)(2,1)S(1)}, u32[]{:S(2)}, u32[]{:S(2)}) collective-permute-start(bf16[8,4,9216]{2,1,0:T(4,128)(2,1)} %get-tuple-element.35), channel_id=1, source_target_pairs={{0,8},{8,0},{1,9},{9,1},{2,10},{10,2},{3,11},{11,3},{4,12},{12,4},... | collective-permute-start | bytes 1769480 | tf_op jit(solution)/shard_map/ppermute | solution.py:433
  408.3 42.5 %collective-permute-start.7 = (bf16[8,4,9216]{2,1,0:T(4,128)(2,1)}, bf16[8,4,9216]{2,1,0:T(4,128)(2,1)S(1)}, u32[]{:S(2)}, u32[]{:S(2)}) collective-permute-start(bf16[8,4,9216]{2,1,0:T(4,128)(2,1)} %get-tuple-element.38), channel_id=1, source_target_pairs={{0,8},{8,0},{1,9},{9,1},{2,10},{10,2},{3,11},{11,3},{4,12},{12,4},... | collective-permute-start | bytes 1769480 | tf_op jit(solution)/shard_map/ppermute | solution.py:433
  438.4 12.4 %copy-start.14 = (bf16[8,4,9216]{2,1,0:T(4,128)(2,1)}, bf16[8,4,9216]{2,1,0:T(4,128)(2,1)S(1)}, u32[]{:S(2)}) copy-start(bf16[8,4,9216]{2,1,0:T(4,128)(2,1)S(1)} %collective-permute-done.6.refs_1_) | copy-start | bytes 1769476
  455.6 4.6 copy-start.26
  455.6 5.7 %copy-start.24 = (bf16[128,128]{1,0:T(8,128)(2,1)S(1)}, bf16[128,128]{1,0:T(8,128)(2,1)}, u32[]{:S(2)}) copy-start(bf16[128,128]{1,0:T(8,128)(2,1)} %param.21) | copy-start | bytes 98308
  456.7 19.4 %all-to-all-start.12 = ((bf16[8,8,9216]{2,1,0:T(8,128)(2,1)}), bf16[8,8,9216]{2,1,0:T(8,128)(2,1)S(1)}, u32[]{:S(2)}, u32[]{:S(2)}) async-start(bf16[8,8,9216]{2,1,0:T(8,128)(2,1)} %add.5), calls=%async_computation.12 | async-start | bytes 2359296 | tf_op jit(solution)/shard_map/all_to_all | solution.py:429
  (11 other events, 9.6 us)

commit v10 on v9

--- a/solution.py
+++ b/solution.py
@@ -248,12 +248,18 @@
     return [pl.ds(row + tile * rows, folds.groups, stride=folds.tiles * rows) for tile in range(folds.tiles)]
 
 
-def mix_out_kernel(folds, near, cols, width, half_ref, left_ref, right_ref, there_ref, *refs):
-    earlier_refs, (mix_ref, staged, left, right) = refs[:-4], refs[-4:]
+def mix_out_kernel(folds, near, cols, width, stages, half_ref, *refs):
     parts = near * cols
     rows = parts * width
     block = folds.rows
-    far = cols // near
+    tall = near * block
+    earlier_refs, near_ref = (), None
+    if stages == (0, 1):
+        left_ref, right_ref, there_ref, *earlier_refs, mix_ref, staged, right, folded, left = refs
+    elif stages == (0,):
+        left_ref, right_ref, mix_ref, left, staged, right, folded = refs
+    else:
+        left, near_ref, there_ref, *earlier_refs, mix_ref, staged, right, folded = refs
 
     def unfold(ref, shift, store):
         height = ref.shape[1]
@@ -267,45 +273,54 @@
 
     def store_left(source, channel, lane_rows):
         pieces = folds.split(lane_rows, clear=True)
-        at = (channel * cols + source % cols) * near * block + (source // cols) * block
+        at = (channel * cols + source % cols) * tall + (source // cols) * block
         left[pl.ds(pl.multiple_of(at, block), block), :] = jnp.concatenate(pieces, axis=0).astype(jnp.bfloat16)
 
-    def store_right(half):
-        def store(source, channel, lane_rows):
-            at = ((channel * cols + source % cols) * far + half) * near * block + (source // cols) * block
-            for phase, piece in enumerate(folds.split(lane_rows)):
-                right[pl.ds(at + phase, folds.groups, stride=folds.turn), :] = piece
-
-        return store
-
-    unfold(left_ref, 0, store_left)
-    unfold(right_ref, right_ref.shape[1] - width, store_right(half_ref[0]))
-    unfold(there_ref, 0, store_right(half_ref[1]))
-
-    @pl.loop(0, width, unroll=1)
-    def _(channel):
-        tall = near * block
-        lhs = jnp.concatenate(
-            [left[pl.ds(pl.multiple_of((channel * cols + col) * tall, block), tall), :] for col in range(cols)], axis=1
-        )
-        for target in range(cols):
-            starts = [((channel * cols + col) * far * near + target) * block for col in range(cols)]
-            rhs = jnp.concatenate([right[pl.ds(pl.multiple_of(at, block), block), :] for at in starts], axis=1)
-            total = lax.dot_general(
-                lhs, rhs.astype(jnp.bfloat16), (((1,), (1,)), ((), ())), preferred_element_type=jnp.float32
-            )
-            total = jnp.concatenate([total, jnp.zeros((near * block, LANES - block), jnp.float32)], axis=1)
-            for piece in range(near):
-                groups = folds.groups
-                base = piece * block
-                lane_rows = folds.join(
-                    [total[base + phase * groups : base + (phase + 1) * groups, :] for phase in range(folds.turn)]
-                )
-                out_row = (piece * cols + target) * width + channel
-                for at, value in zip(lane_rows_of(folds, rows, out_row), lane_rows):
-                    staged[at, :] = value
-
-    unstage(staged, mix_ref, earlier_refs)
+    def store_right(source, channel, lane_rows):
+        at = (channel * cols + source % cols) * tall + (source // cols) * block
+        for phase, piece in enumerate(folds.split(lane_rows)):
+            right[pl.ds(at + phase, folds.groups, stride=folds.turn), :] = piece
+
+    def products(half):
+        @pl.loop(0, width)
+        def _(channel):
+            starts = [(channel * cols + col) * tall for col in range(cols)]
+            lhs = jnp.concatenate([left[pl.ds(pl.multiple_of(at, block), tall), :] for at in starts], axis=1)
+            for offset in range(near):
+                at = [pl.multiple_of(start + offset * block, block) for start in starts]
+                rhs = jnp.concatenate([right[pl.ds(begin, block), :] for begin in at], axis=1).astype(jnp.bfloat16)
+                total = lax.dot_general(lhs, rhs, (((1,), (1,)), ((), ())), preferred_element_type=jnp.float32)
+                total = jnp.concatenate([total, jnp.zeros((tall, LANES - block), jnp.float32)], axis=1)
+                for piece in range(near):
+                    lane_rows = folds.join(
+                        [
+                            total[piece * block + phase * folds.groups : piece * block + (phase + 1) * folds.groups, :]
+                            for phase in range(folds.turn)
+                        ]
+                    )
+                    out_row = (piece * cols + half * near + offset) * width + channel
+                    for lanes, value in zip(lane_rows_of(folds, rows, out_row), lane_rows):
+                        folded[lanes, :] = value
+
+    if 0 in stages:
+        unfold(left_ref, 0, store_left)
+        unfold(right_ref, right_ref.shape[1] - width, store_right)
+        products(half_ref[0])
+    if 1 in stages:
+        unfold(there_ref, 0, store_right)
+        products(half_ref[1])
+
+    @pl.loop(0, mix_ref.shape[2] // LANES, unroll=8)
+    def _(tile):
+        lanes = pl.ds(pl.multiple_of(tile * LANES, LANES), LANES)
+        for part in range(parts):
+            value = folded[pl.ds(tile * rows + part * width, width), :]
+            if near_ref is not None:
+                mine = half_ref[0] == part % cols // near
+                value = jnp.where(mine, near_ref[part, :, lanes].astype(jnp.float32), value)
+            values = [ref[part, :, lanes].astype(jnp.float32) for ref in earlier_refs] + [value]
+            values = values[0] if len(values) == 1 else jnp.concatenate(values, axis=0)
+            mix_ref[part, :, lanes] = values.astype(mix_ref.dtype)
 
 
 def mix_in_kernel(folds, near, cols, width, half_ref, both_ref, keep_ref, send_ref, staged, left, right, turned, mixed):
@@ -354,23 +369,29 @@
 VMEM_SPEC = pl.BlockSpec(memory_space=pltpu.VMEM)
 
 
-def run_mix_out(folds, near, cols, halves, left, right, there, earlier=()):
-    parts, width, positions = there.shape
+def run_mix_out(folds, near, cols, width, stages, halves, *arrays, earlier=()):
+    parts, _, positions = arrays[-1].shape
     rows = parts * width
-    block = folds.rows
+    tall = width * cols * near * folds.rows
+    out_shape = [jax.ShapeDtypeStruct((parts, width + sum(e.shape[1] for e in earlier), positions), jnp.bfloat16)]
+    scratch = [
+        pltpu.VMEM((2 * rows * folds.lane_rows, LANES), jnp.float32),
+        pltpu.VMEM((tall, LANES), jnp.float32),
+        pltpu.VMEM((rows * folds.lane_rows, LANES), jnp.float32),
+    ]
+    if stages == (0,):
+        out_shape.append(jax.ShapeDtypeStruct((tall, LANES), jnp.bfloat16))
+    elif stages == (0, 1):
+        scratch.append(pltpu.VMEM((tall, LANES), jnp.bfloat16))
     return pl.pallas_call(
-        functools.partial(mix_out_kernel, folds, near, cols, width),
-        in_specs=[SMEM_SPEC] + [VMEM_SPEC] * (3 + len(earlier)),
-        out_specs=VMEM_SPEC,
-        out_shape=jax.ShapeDtypeStruct((parts, width + sum(e.shape[1] for e in earlier), positions), jnp.bfloat16),
-        scratch_shapes=[
-            pltpu.VMEM((2 * rows * folds.lane_rows, LANES), jnp.float32),
-            pltpu.VMEM((width * cols * near * block, LANES), jnp.bfloat16),
-            pltpu.VMEM((width * cols * cols * block, LANES), jnp.float32),
-        ],
+        functools.partial(mix_out_kernel, folds, near, cols, width, stages),
+        in_specs=[SMEM_SPEC] + [VMEM_SPEC] * (len(arrays) + len(earlier)),
+        out_specs=[VMEM_SPEC] * len(out_shape),
+        out_shape=out_shape,
+        scratch_shapes=scratch,
         compiler_params=pltpu.CompilerParams(vmem_limit_bytes=BUDGET),
         name="mix_out",
-    )(halves, left, right, there, *earlier)
+    )(halves, *arrays, *earlier)
 
 
 def add_kernel(*refs):
@@ -486,7 +507,12 @@
         right, left = sent[piece], sent[piece + 1]
         there = across(right[:, right.shape[1] - (ends[piece] - begins[piece]) :, :])
         earlier = [mixed[other] for other in group[:-1]] if piece == group[-1] else ()
-        mixed[piece] = run_mix_out(folds, near, cols, halves, left, right, there, earlier)
+        mix = functools.partial(run_mix_out, folds, near, cols, ends[piece] - begins[piece])
+        if piece < PIECES - 1:
+            mixed[piece] = mix((0, 1), halves, left, right, there, earlier=earlier)[0]
+        else:
+            mine, unfolded = mix((0,), halves, left, right)
+            mixed[piece] = mix((1,), halves, unfolded, mine, there, earlier=earlier)[0]
         if piece == group[-1]:
             mixes.append(exchange(mixed[piece]))
     onward = (gain_2, rows_of(project_2, *level[:1]), shapes_of(*level[:1]))

time: 487 us -> 484 us (level)
  waiting for transfers between devices: 202 us -> 192 us
  Pallas kernels: 128 us -> 134 us
    ppermute x8, waiting for transfers between devices: 165 us -> 155 us  [across(): return lax.ppermute(array, 'far', ((0, 1), (1, 0)))]
    pallas_call x4 -> x5, Pallas kernels: 42.5 us -> 49.3 us  [run_mix_out(): pl.pallas_call(functools.partial(mix_out_kernel, folds, near, cols, width...]
  transfers between devices with their start and end apart: 16 -> 16, of which waited for: 12 -> 12; matrix products, arithmetic and copies ran while one was open for 1% -> 1% of each run, Pallas kernels for 21% -> 23%
where the time goes in v10:
time: 484 us; the launch traced here: 482 us
  waiting for transfers between devices  192 us (40%)
  Pallas kernels  134 us (28%)
  blocking collectives  94 us (19%)
  starting transfers between devices  42.9 us (9%)
  local copies, waits for them, and re-layouts  15.1 us (3%)
    ppermute x8, waiting for transfers between devices, across(): return lax.ppermute(array, 'far', ((0, 1), (1, 0)))  155 us
    all_to_all x5, blocking collectives, exchange(): return lax.all_to_all(array, EVERY, split_axis=0, concat_axis=0, tiled=True)  94 us
    pallas_call x5, Pallas kernels, run_mix_out(): pl.pallas_call(functools.partial(mix_out_kernel, folds, near, cols, width...  49.3 us
    pallas_call x4, Pallas kernels, run_mix_in(): pl.pallas_call(functools.partial(mix_in_kernel, folds, near, cols, width)...  38.8 us
    all_to_all x8, waiting for transfers between devices, exchange(): return lax.all_to_all(array, EVERY, split_axis=0, concat_axis=0, tiled=True)  36.7 us
    all_to_all x8, starting transfers between devices, exchange(): return lax.all_to_all(array, EVERY, split_axis=0, concat_axis=0, tiled=True)  30.5 us
    pallas_call x3, Pallas kernels, run_projections(): pl.pallas_call(project_kernel, grid=(positions // step,), in_specs=[pl.Bl...  19.7 us
    pallas_call x2, Pallas kernels, run_finish(): pl.pallas_call(functools.partial(finish_kernel, len(mixes), onward is not...  18.7 us
  transfers between devices with their start and end apart: 16, of which 12 were waited for; matrix products, arithmetic and copies ran while one was open for 1% of the time, Pallas kernels for 23%

profile of v10, /device:TPU:0, one launch (start us, length us, event | category | flops | bytes accessed | tf_op | source)
XLA Modules:
  0.0 482.4 jit_solution(14926157270782501334)
XLA Ops:
  1.7 5.6 %project.4 = bf16[8,4,9216]{2,1,0:T(4,128)(2,1)} custom-call(bf16[9216,128]{1,0:T(8,128)(2,1)} %bitcast.90, f32[1,128]{1,0:T(1,128)} %bitcast.109, bf16[64,128]{1,0:T(8,128)(2,1)} %pad_maximum_fusion.3.rows_ref), custom_call_target="tpu_custom_call" | custom-call | tf_op jit(solution)/shard_map/project/pallas_call | solution.py:142
  7.3 5.3 %all-to-all-start.2 = ((bf16[8,4,9216]{2,1,0:T(4,128)(2,1)}), bf16[8,4,9216]{2,1,0:T(4,128)(2,1)S(1)}, u32[]{:S(2)}, u32[]{:S(2)}) async-start(bf16[8,4,9216]{2,1,0:T(4,128)(2,1)} %project.4), calls=%async_computation.2 | async-start | bytes 1179648 | tf_op jit(solution)/shard_map/all_to_all | solution.py:450
  13.4 7.2 %project.3 = (bf16[8,8,9216]{2,1,0:T(8,128)(2,1)}, bf16[8,8,9216]{2,1,0:T(8,128)(2,1)}, bf16[8,8,9216]{2,1,0:T(8,128)(2,1)}, bf16[8,4,9216]{2,1,0:T(4,128)(2,1)}) custom-call(bf16[9216,128]{1,0:T(8,128)(2,1)} %bitcast.91, f32[1,128]{1,0:T(1,128)} %bitcast.110, bf16[448,128]{1,0:T(8,128)(2,1)} %copy-done.20), custom_call_target="tpu_custom_call" | custom-call | tf_op jit(solution)/shard_map/project/pallas_call | solution.py:142
  22.1 14.5 %all_to_all.65.refs_0_ = bf16[8,4,9216]{2,1,0:T(4,128)(2,1)} all-to-all(bf16[8,4,9216]{2,1,0:T(4,128)(2,1)} %get-tuple-element.26), channel_id=1, replica_groups=mesh['groups'=2,'far'=2,'near'=2,'chan'=2,'sub'=2] {'near','chan','sub'}, dimensions={0} | all-to-all | bytes 1179648 | tf_op jit(solution)/shard_map/all_to_all | solution.py:450
  36.6 19.8 %all_to_all.66.refs_0_.refs_1_ = bf16[8,8,9216]{2,1,0:T(8,128)(2,1)} all-to-all(bf16[8,8,9216]{2,1,0:T(8,128)(2,1)S(1)} %copy-done.11), channel_id=1, replica_groups=mesh['groups'=2,'far'=2,'near'=2,'chan'=2,'sub'=2] {'near','chan','sub'}, dimensions={0} | all-to-all | bytes 2359296 | tf_op jit(solution)/shard_map/all_to_all | solution.py:450
  56.4 18.9 %all_to_all.67.refs_0_.refs_1_ = bf16[8,8,9216]{2,1,0:T(8,128)(2,1)S(1)} all-to-all(bf16[8,8,9216]{2,1,0:T(8,128)(2,1)S(1)} %copy-done.10), channel_id=1, replica_groups=mesh['groups'=2,'far'=2,'near'=2,'chan'=2,'sub'=2] {'near','chan','sub'}, dimensions={0} | all-to-all | bytes 2359296 | tf_op jit(solution)/shard_map/all_to_all | solution.py:450
  83.0 22.6 %collective-permute-done.1.refs_2_ = bf16[8,4,9216]{2,1,0:T(4,128)(2,1)} collective-permute-done((bf16[8,4,9216]{2,1,0:T(4,128)(2,1)S(1)}, bf16[8,4,9216]{2,1,0:T(4,128)(2,1)}, u32[]{:S(2)}, u32[]{:S(2)}) %collective-permute-start.1) | collective-permute-done | bytes 589856 | tf_op jit(solution)/shard_map/ppermute | solution.py:454
  105.6 11.1 %mix_out.5.refs_3_ = bf16[8,4,9216]{2,1,0:T(4,128)(2,1)} custom-call(s32[2]{0:T(128)} %pad_add_fusion.half_ref, bf16[8,8,9216]{2,1,0:T(8,128)(2,1)} %copy-done, bf16[8,4,9216]{2,1,0:T(4,128)(2,1)} %copy-done.9, bf16[8,4,9216]{2,1,0:T(4,128)(2,1)} %collective-permute-done.1.refs_2_), custom_call_target="tpu_custom_call" | custom-call | tf_op jit(solution)/shard_map/mix_out/pallas_call | solution.py:386
  116.7 16.8 %collective-permute-done.refs_2_ = bf16[8,4,9216]{2,1,0:T(4,128)(2,1)S(1)} collective-permute-done((bf16[8,4,9216]{2,1,0:T(4,128)(2,1)S(1)}, bf16[8,4,9216]{2,1,0:T(4,128)(2,1)S(1)}, u32[]{:S(2)}, u32[]{:S(2)}) %collective-permute-start) | collective-permute-done | bytes 589856 | tf_op jit(solution)/shard_map/ppermute | solution.py:454
  134.3 12.1 %mix_out.6 = bf16[8,8,9216]{2,1,0:T(8,128)(2,1)} custom-call(s32[2]{0:T(128)} %pad_add_fusion.half_ref, bf16[8,8,9216]{2,1,0:T(8,128)(2,1)} %all_to_all.66.refs_0_.refs_1_, bf16[8,8,9216]{2,1,0:T(8,128)(2,1)} %copy-done, bf16[8,4,9216]{2,1,0:T(4,128)(2,1)} %copy-done.13, bf16[8,4,9216]{2,1,0:T(4,128)(2,1)} %mix_out.5.refs_3_), custom_call_target="tpu_custom_call" | custom-call | tf_op jit(solution)/shard_map/mix_out/pallas_call | solution.py:386
  153.8 7.9 %mix_out.7 = (bf16[8,4,9216]{2,1,0:T(4,128)(2,1)}, bf16[3072,128]{1,0:T(8,128)(2,1)}) custom-call(s32[2]{0:T(128)} %pad_add_fusion.half_ref, bf16[8,4,9216]{2,1,0:T(4,128)(2,1)} %all_to_all.65.refs_0_, bf16[8,8,9216]{2,1,0:T(8,128)(2,1)} %copy-done.2), custom_call_target="tpu_custom_call" | custom-call | tf_op jit(solution)/shard_map/mix_out/pallas_call | solution.py:386
  161.7 15.0 %collective-permute-done.3.refs_2_ = bf16[8,4,9216]{2,1,0:T(4,128)(2,1)S(1)} collective-permute-done((bf16[8,4,9216]{2,1,0:T(4,128)(2,1)S(1)}, bf16[8,4,9216]{2,1,0:T(4,128)(2,1)S(1)}, u32[]{:S(2)}, u32[]{:S(2)}) %collective-permute-start.3) | collective-permute-done | bytes 589856 | tf_op jit(solution)/shard_map/ppermute | solution.py:454
  177.5 11.5 %mix_out.8.refs_3_ = bf16[8,4,9216]{2,1,0:T(4,128)(2,1)} custom-call(s32[2]{0:T(128)} %pad_add_fusion.half_ref, bf16[8,8,9216]{2,1,0:T(8,128)(2,1)} %copy-done.2, bf16[8,8,9216]{2,1,0:T(8,128)(2,1)} %all_to_all.66.refs_0_.refs_1_, bf16[8,4,9216]{2,1,0:T(4,128)(2,1)} %copy-done.19), custom_call_target="tpu_custom_call" | custom-call | tf_op jit(solution)/shard_map/mix_out/pallas_call | solution.py:386
  189.0 16.3 %collective-permute-done.2.refs_2_ = bf16[8,4,9216]{2,1,0:T(4,128)(2,1)S(1)} collective-permute-done((bf16[8,4,9216]{2,1,0:T(4,128)(2,1)S(1)}, bf16[8,4,9216]{2,1,0:T(4,128)(2,1)S(1)}, u32[]{:S(2)}, u32[]{:S(2)}) %collective-permute-start.2) | collective-permute-done | bytes 589856 | tf_op jit(solution)/shard_map/ppermute | solution.py:454
  206.1 6.7 %mix_out.9 = bf16[8,8,9216]{2,1,0:T(8,128)(2,1)} custom-call(s32[2]{0:T(128)} %pad_add_fusion.half_ref, bf16[3072,128]{1,0:T(8,128)(2,1)} %get-tuple-element.28.refs_0_, bf16[8,4,9216]{2,1,0:T(4,128)(2,1)} %get-tuple-element.29.refs_1_, bf16[8,4,9216]{2,1,0:T(4,128)(2,1)} %copy-done.18, bf16[8,4,9216]{2,1,0:T(4,128)(2,1)} %mix_out.8.refs_3_), custom_call_target="tpu_custom_call" | custom-call | tf_op jit(solution)/shard_map/mix_out/pallas_call | solution.py:386
  220.2 13.0 %all-to-all-done.6.refs_1_ = bf16[8,8,9216]{2,1,0:T(8,128)(2,1)S(1)} async-done(((bf16[8,8,9216]{2,1,0:T(8,128)(2,1)}), bf16[8,8,9216]{2,1,0:T(8,128)(2,1)S(1)}, u32[]{:S(2)}, u32[]{:S(2)}) %all-to-all-start.6) | async-done | bytes 1179680 | tf_op jit(solution)/shard_map/all_to_all | solution.py:450
  234.3 10.8 %finish.2 = (bf16[9216,128]{1,0:T(8,128)(2,1)}, bf16[8,8,9216]{2,1,0:T(8,128)(2,1)}) custom-call(bf16[8,8,9216]{2,1,0:T(8,128)(2,1)} %copy-done.7, bf16[8,8,9216]{2,1,0:T(8,128)(2,1)} %copy-done.8, bf16[9216,128]{1,0:T(8,128)(2,1)} %bitcast.92, f32[1,128]{1,0:T(1,128)} %bitcast.111, bf16[128,128]{1,0:T(8,128)(2,1)} %refs_4_.2, f32[128,1]{1,0:T(8,128)} %copy.56.refs_5_, ...), custom_call_target="tpu_custom_call" | custom-call | tf_op jit(solution)/shard_map/finish/pallas_call | solution.py:164
  249.5 6.9 %project.5 = (bf16[8,8,9216]{2,1,0:T(8,128)(2,1)}, bf16[8,8,9216]{2,1,0:T(8,128)(2,1)}, bf16[8,8,9216]{2,1,0:T(8,128)(2,1)}) custom-call(bf16[9216,128]{1,0:T(8,128)(2,1)} %get-tuple-element.33.state_ref.refs_2_, f32[1,128]{1,0:T(1,128)} %bitcast.113, bf16[384,128]{1,0:T(8,128)(2,1)} %copy-done.21), custom_call_target="tpu_custom_call" | custom-call | tf_op jit(solution)/shard_map/project/pallas_call | solution.py:142
  256.4 8.1 %all-to-all-done.7.both_ref = bf16[8,8,9216]{2,1,0:T(8,128)(2,1)S(1)} async-done(((bf16[8,8,9216]{2,1,0:T(8,128)(2,1)}), bf16[8,8,9216]{2,1,0:T(8,128)(2,1)S(1)}, u32[]{:S(2)}, u32[]{:S(2)}) %all-to-all-start.7) | async-done | bytes 1179680 | tf_op jit(solution)/shard_map/all_to_all | solution.py:450
  264.5 21.0 %all_to_all.68.both_ref = bf16[8,8,9216]{2,1,0:T(8,128)(2,1)} all-to-all(bf16[8,8,9216]{2,1,0:T(8,128)(2,1)} %get-tuple-element.34), channel_id=1, replica_groups=mesh['groups'=2,'far'=2,'near'=2,'chan'=2,'sub'=2] {'near','chan','sub'}, dimensions={0} | all-to-all | bytes 2359296 | tf_op jit(solution)/shard_map/all_to_all | solution.py:450
  285.6 19.7 %all_to_all.69.both_ref = bf16[8,8,9216]{2,1,0:T(8,128)(2,1)} all-to-all(bf16[8,8,9216]{2,1,0:T(8,128)(2,1)S(1)} %copy-done.12), channel_id=1, replica_groups=mesh['groups'=2,'far'=2,'near'=2,'chan'=2,'sub'=2] {'near','chan','sub'}, dimensions={0} | all-to-all | bytes 2359296 | tf_op jit(solution)/shard_map/all_to_all | solution.py:450
  308.8 9.7 %mix_in.4 = (f32[8,4,9216]{2,1,0:T(4,128)}, bf16[8,4,9216]{2,1,0:T(4,128)(2,1)}) custom-call(s32[2]{0:T(128)} %pad_add_fusion.half_ref, bf16[8,8,9216]{2,1,0:T(8,128)(2,1)} %copy-done.6), custom_call_target="tpu_custom_call" | custom-call | tf_op jit(solution)/shard_map/mix_in/pallas_call | solution.py:424
  321.9 9.7 %mix_in.5 = (f32[8,4,9216]{2,1,0:T(4,128)}, bf16[8,4,9216]{2,1,0:T(4,128)(2,1)}) custom-call(s32[2]{0:T(128)} %pad_add_fusion.half_ref, bf16[8,8,9216]{2,1,0:T(8,128)(2,1)} %all_to_all.68.both_ref), custom_call_target="tpu_custom_call" | custom-call | tf_op jit(solution)/shard_map/mix_in/pallas_call | solution.py:424
  331.6 30.0 %collective-permute-done.4.refs_1_ = bf16[8,4,9216]{2,1,0:T(4,128)(2,1)S(1)} collective-permute-done((bf16[8,4,9216]{2,1,0:T(4,128)(2,1)}, bf16[8,4,9216]{2,1,0:T(4,128)(2,1)S(1)}, u32[]{:S(2)}, u32[]{:S(2)}) %collective-permute-start.4) | collective-permute-done | bytes 589856 | tf_op jit(solution)/shard_map/ppermute | solution.py:454
  361.6 12.4 %collective-permute-done.5.refs_3_ = bf16[8,4,9216]{2,1,0:T(4,128)(2,1)S(1)} collective-permute-done((bf16[8,4,9216]{2,1,0:T(4,128)(2,1)}, bf16[8,4,9216]{2,1,0:T(4,128)(2,1)S(1)}, u32[]{:S(2)}, u32[]{:S(2)}) %collective-permute-start.5) | collective-permute-done | bytes 589856 | tf_op jit(solution)/shard_map/ppermute | solution.py:454
  374.8 4.0 add.4
  383.4 9.7 %mix_in.6 = (f32[8,4,9216]{2,1,0:T(4,128)}, bf16[8,4,9216]{2,1,0:T(4,128)(2,1)}) custom-call(s32[2]{0:T(128)} %pad_add_fusion.half_ref, bf16[8,8,9216]{2,1,0:T(8,128)(2,1)} %all_to_all.69.both_ref), custom_call_target="tpu_custom_call" | custom-call | tf_op jit(solution)/shard_map/mix_in/pallas_call | solution.py:424
  396.0 9.7 %mix_in.7 = (f32[8,4,9216]{2,1,0:T(4,128)}, bf16[8,4,9216]{2,1,0:T(4,128)(2,1)}) custom-call(s32[2]{0:T(128)} %pad_add_fusion.half_ref, bf16[8,8,9216]{2,1,0:T(8,128)(2,1)} %copy-done.5), custom_call_target="tpu_custom_call" | custom-call | tf_op jit(solution)/shard_map/mix_in/pallas_call | solution.py:424
  405.7 30.1 %collective-permute-done.6.refs_1_ = bf16[8,4,9216]{2,1,0:T(4,128)(2,1)S(1)} collective-permute-done((bf16[8,4,9216]{2,1,0:T(4,128)(2,1)}, bf16[8,4,9216]{2,1,0:T(4,128)(2,1)S(1)}, u32[]{:S(2)}, u32[]{:S(2)}) %collective-permute-start.6) | collective-permute-done | bytes 589856 | tf_op jit(solution)/shard_map/ppermute | solution.py:454
  435.8 12.4 %collective-permute-done.7.refs_3_ = bf16[8,4,9216]{2,1,0:T(4,128)(2,1)S(1)} collective-permute-done((bf16[8,4,9216]{2,1,0:T(4,128)(2,1)}, bf16[8,4,9216]{2,1,0:T(4,128)(2,1)S(1)}, u32[]{:S(2)}, u32[]{:S(2)}) %collective-permute-start.7) | collective-permute-done | bytes 589856 | tf_op jit(solution)/shard_map/ppermute | solution.py:454
  459.4 14.0 %all-to-all-done.12.refs_1_ = bf16[8,8,9216]{2,1,0:T(8,128)(2,1)S(1)} async-done(((bf16[8,8,9216]{2,1,0:T(8,128)(2,1)}), bf16[8,8,9216]{2,1,0:T(8,128)(2,1)S(1)}, u32[]{:S(2)}, u32[]{:S(2)}) %all-to-all-start.12) | async-done | bytes 1179680 | tf_op jit(solution)/shard_map/all_to_all | solution.py:450
  474.5 7.9 %finish.3 = bf16[9216,128]{1,0:T(8,128)(2,1)} custom-call(bf16[8,8,9216]{2,1,0:T(8,128)(2,1)} %copy-done.3, bf16[8,8,9216]{2,1,0:T(8,128)(2,1)} %copy-done.4, bf16[9216,128]{1,0:T(8,128)(2,1)} %get-tuple-element.33.state_ref.refs_2_, f32[1,128]{1,0:T(1,128)} %bitcast.114, bf16[128,128]{1,0:T(8,128)(2,1)} %refs_4_.3, f32[128,1]{1,0:T(8,128)} %copy.57.refs_5_, ...), custom_call_target="tpu_custom_call" | custom-call | tf_op jit(solution)/shard_map/finish/pallas_call | solution.py:164
  (121 shorter events, 61.8 us)
Async XLA Ops:
  7.3 14.8 %all-to-all-start.2 = ((bf16[8,4,9216]{2,1,0:T(4,128)(2,1)}), bf16[8,4,9216]{2,1,0:T(4,128)(2,1)S(1)}, u32[]{:S(2)}, u32[]{:S(2)}) async-start(bf16[8,4,9216]{2,1,0:T(4,128)(2,1)} %project.4), calls=%async_computation.2 | async-start | bytes 1179648 | tf_op jit(solution)/shard_map/all_to_all | solution.py:450
  20.6 16.0 %copy-start.11 = (bf16[8,8,9216]{2,1,0:T(8,128)(2,1)S(1)}, bf16[8,8,9216]{2,1,0:T(8,128)(2,1)}, u32[]{:S(2)}) copy-start(bf16[8,8,9216]{2,1,0:T(8,128)(2,1)} %get-tuple-element.24) | copy-start | bytes 3538948
  22.1 56.8 %copy-start.9 = (bf16[8,4,9216]{2,1,0:T(4,128)(2,1)}, bf16[8,4,9216]{2,1,0:T(4,128)(2,1)S(1)}, u32[]{:S(2)}) copy-start(bf16[8,4,9216]{2,1,0:T(4,128)(2,1)S(1)} %all-to-all-done.2.refs_1_) | copy-start | bytes 1769476
  36.6 19.8 %copy-start.10 = (bf16[8,8,9216]{2,1,0:T(8,128)(2,1)S(1)}, bf16[8,8,9216]{2,1,0:T(8,128)(2,1)}, u32[]{:S(2)}) copy-start(bf16[8,8,9216]{2,1,0:T(8,128)(2,1)} %get-tuple-element.25) | copy-start | bytes 3538948
  75.4 6.2 %copy-start = (bf16[8,8,9216]{2,1,0:T(8,128)(2,1)}, bf16[8,8,9216]{2,1,0:T(8,128)(2,1)S(1)}, u32[]{:S(2)}) copy-start(bf16[8,8,9216]{2,1,0:T(8,128)(2,1)S(1)} %all_to_all.67.refs_0_.refs_1_) | copy-start | bytes 3538948
  75.4 71.0 %all-to-all-start.5 = ((bf16[8,8,9216]{2,1,0:T(8,128)(2,1)}), bf16[8,8,9216]{2,1,0:T(8,128)(2,1)S(1)}, u32[]{:S(2)}, u32[]{:S(2)}) async-start(bf16[8,8,9216]{2,1,0:T(8,128)(2,1)} %get-tuple-element.27), calls=%async_computation.5 | async-start | bytes 2359296 | tf_op jit(solution)/shard_map/all_to_all | solution.py:450
  79.0 26.6 %collective-permute-start.1 = (bf16[8,4,9216]{2,1,0:T(4,128)(2,1)S(1)}, bf16[8,4,9216]{2,1,0:T(4,128)(2,1)}, u32[]{:S(2)}, u32[]{:S(2)}) collective-permute-start(bf16[8,4,9216]{2,1,0:T(4,128)(2,1)S(1)} %all-to-all-done.2.refs_1_), channel_id=1, source_target_pairs={{0,8},{8,0},{1,9},{9,1},{2,10},{10,2},{3,11},{11,3},{4,12},{12,4},... | collective-permute-start | bytes 1769480 | tf_op jit(solution)/shard_map/ppermute | solution.py:454
  81.9 51.5 %collective-permute-start = (bf16[8,4,9216]{2,1,0:T(4,128)(2,1)S(1)}, bf16[8,4,9216]{2,1,0:T(4,128)(2,1)S(1)}, u32[]{:S(2)}, u32[]{:S(2)}) collective-permute-start(bf16[8,4,9216]{2,1,0:T(4,128)(2,1)S(1)} %slice.178), channel_id=1, source_target_pairs={{0,8},{8,0},{1,9},{9,1},{2,10},{10,2},{3,11},{11,3},{4,12},{12,4},... | collective-permute-start | bytes 1769480 | tf_op jit(solution)/shard_map/ppermute | solution.py:454
  146.4 3.7 copy-start.1
  146.4 7.0 %copy-start.2 = (bf16[8,8,9216]{2,1,0:T(8,128)(2,1)}, bf16[8,8,9216]{2,1,0:T(8,128)(2,1)S(1)}, u32[]{:S(2)}) copy-start(bf16[8,8,9216]{2,1,0:T(8,128)(2,1)S(1)} %all-to-all-done.5.refs_1_.refs_0_) | copy-start | bytes 3538948
  146.4 66.4 %all-to-all-start.3 = ((bf16[8,8,9216]{2,1,0:T(8,128)(2,1)}), bf16[8,8,9216]{2,1,0:T(8,128)(2,1)S(1)}, u32[]{:S(2)}, u32[]{:S(2)}) async-start(bf16[8,8,9216]{2,1,0:T(8,128)(2,1)} %mix_out.6), calls=%async_computation.3 | async-start | bytes 2359296 | tf_op jit(solution)/shard_map/all_to_all | solution.py:450
  150.4 26.3 %collective-permute-start.3 = (bf16[8,4,9216]{2,1,0:T(4,128)(2,1)S(1)}, bf16[8,4,9216]{2,1,0:T(4,128)(2,1)S(1)}, u32[]{:S(2)}, u32[]{:S(2)}) collective-permute-start(bf16[8,4,9216]{2,1,0:T(4,128)(2,1)S(1)} %slice.182), channel_id=1, source_target_pairs={{0,8},{8,0},{1,9},{9,1},{2,10},{10,2},{3,11},{11,3},{4,12},{12,4},... | collective-permute-start | bytes 1769480 | tf_op jit(solution)/shard_map/ppermute | solution.py:454
  153.6 51.6 %collective-permute-start.2 = (bf16[8,4,9216]{2,1,0:T(4,128)(2,1)S(1)}, bf16[8,4,9216]{2,1,0:T(4,128)(2,1)S(1)}, u32[]{:S(2)}, u32[]{:S(2)}) collective-permute-start(bf16[8,4,9216]{2,1,0:T(4,128)(2,1)S(1)} %slice.181), channel_id=1, source_target_pairs={{0,8},{8,0},{1,9},{9,1},{2,10},{10,2},{3,11},{11,3},{4,12},{12,4},... | collective-permute-start | bytes 1769480 | tf_op jit(solution)/shard_map/ppermute | solution.py:454
  212.8 4.8 copy-start.25
  212.8 5.9 %copy-start.22 = (bf16[128,512]{1,0:T(8,128)(2,1)S(1)}, bf16[128,512]{1,0:T(8,128)(2,1)}, u32[]{:S(2)}) copy-start(bf16[128,512]{1,0:T(8,128)(2,1)} %param.18) | copy-start | bytes 393220
  212.8 6.2 %copy-start.23 = (bf16[128,128]{1,0:T(8,128)(2,1)S(1)}, bf16[128,128]{1,0:T(8,128)(2,1)}, u32[]{:S(2)}) copy-start(bf16[128,128]{1,0:T(8,128)(2,1)} %param.16) | copy-start | bytes 98308
  213.8 19.5 %all-to-all-start.6 = ((bf16[8,8,9216]{2,1,0:T(8,128)(2,1)}), bf16[8,8,9216]{2,1,0:T(8,128)(2,1)S(1)}, u32[]{:S(2)}, u32[]{:S(2)}) async-start(bf16[8,8,9216]{2,1,0:T(8,128)(2,1)} %mix_out.9), calls=%async_computation.6 | async-start | bytes 2359296 | tf_op jit(solution)/shard_map/all_to_all | solution.py:450
  233.3 1.1 copy-start.8
  245.1 19.4 %all-to-all-start.7 = ((bf16[8,8,9216]{2,1,0:T(8,128)(2,1)}), bf16[8,8,9216]{2,1,0:T(8,128)(2,1)S(1)}, u32[]{:S(2)}, u32[]{:S(2)}) async-start(bf16[8,8,9216]{2,1,0:T(8,128)(2,1)} %get-tuple-element.30), calls=%async_computation.7 | async-start | bytes 2359296 | tf_op jit(solution)/shard_map/all_to_all | solution.py:450
  264.5 21.1 %copy-start.6 = (bf16[8,8,9216]{2,1,0:T(8,128)(2,1)}, bf16[8,8,9216]{2,1,0:T(8,128)(2,1)S(1)}, u32[]{:S(2)}) copy-start(bf16[8,8,9216]{2,1,0:T(8,128)(2,1)S(1)} %all-to-all-done.7.both_ref) | copy-start | bytes 3538948
  264.5 21.1 %copy-start.12 = (bf16[8,8,9216]{2,1,0:T(8,128)(2,1)S(1)}, bf16[8,8,9216]{2,1,0:T(8,128)(2,1)}, u32[]{:S(2)}) copy-start(bf16[8,8,9216]{2,1,0:T(8,128)(2,1)} %get-tuple-element.37) | copy-start | bytes 3538948
  305.2 73.6 %all-to-all-start.11 = ((bf16[8,8,9216]{2,1,0:T(8,128)(2,1)}), bf16[8,8,9216]{2,1,0:T(8,128)(2,1)S(1)}, u32[]{:S(2)}, u32[]{:S(2)}) async-start(bf16[8,8,9216]{2,1,0:T(8,128)(2,1)} %get-tuple-element.40), calls=%async_computation.11 | async-start | bytes 2359296 | tf_op jit(solution)/shard_map/all_to_all | solution.py:450
  318.5 43.1 %collective-permute-start.4 = (bf16[8,4,9216]{2,1,0:T(4,128)(2,1)}, bf16[8,4,9216]{2,1,0:T(4,128)(2,1)S(1)}, u32[]{:S(2)}, u32[]{:S(2)}) collective-permute-start(bf16[8,4,9216]{2,1,0:T(4,128)(2,1)} %get-tuple-element.32), channel_id=1, source_target_pairs={{0,8},{8,0},{1,9},{9,1},{2,10},{10,2},{3,11},{11,3},{4,12},{12,4},... | collective-permute-start | bytes 1769480 | tf_op jit(solution)/shard_map/ppermute | solution.py:454
  331.6 42.4 %collective-permute-start.5 = (bf16[8,4,9216]{2,1,0:T(4,128)(2,1)}, bf16[8,4,9216]{2,1,0:T(4,128)(2,1)S(1)}, u32[]{:S(2)}, u32[]{:S(2)}) collective-permute-start(bf16[8,4,9216]{2,1,0:T(4,128)(2,1)} %get-tuple-element.36), channel_id=1, source_target_pairs={{0,8},{8,0},{1,9},{9,1},{2,10},{10,2},{3,11},{11,3},{4,12},{12,4},... | collective-permute-start | bytes 1769480 | tf_op jit(solution)/shard_map/ppermute | solution.py:454
  361.6 12.4 %copy-start.15 = (bf16[8,4,9216]{2,1,0:T(4,128)(2,1)}, bf16[8,4,9216]{2,1,0:T(4,128)(2,1)S(1)}, u32[]{:S(2)}) copy-start(bf16[8,4,9216]{2,1,0:T(4,128)(2,1)S(1)} %collective-permute-done.4.refs_1_) | copy-start | bytes 1769476
  379.9 73.1 %all-to-all-start.9 = ((bf16[8,8,9216]{2,1,0:T(8,128)(2,1)}), bf16[8,8,9216]{2,1,0:T(8,128)(2,1)S(1)}, u32[]{:S(2)}, u32[]{:S(2)}) async-start(bf16[8,8,9216]{2,1,0:T(8,128)(2,1)} %add.4), calls=%async_computation.9 | async-start | bytes 2359296 | tf_op jit(solution)/shard_map/all_to_all | solution.py:450
  393.1 42.6 %collective-permute-start.6 = (bf16[8,4,9216]{2,1,0:T(4,128)(2,1)}, bf16[8,4,9216]{2,1,0:T(4,128)(2,1)S(1)}, u32[]{:S(2)}, u32[]{:S(2)}) collective-permute-start(bf16[8,4,9216]{2,1,0:T(4,128)(2,1)} %get-tuple-element.39), channel_id=1, source_target_pairs={{0,8},{8,0},{1,9},{9,1},{2,10},{10,2},{3,11},{11,3},{4,12},{12,4},... | collective-permute-start | bytes 1769480 | tf_op jit(solution)/shard_map/ppermute | solution.py:454
  405.6 42.5 %collective-permute-start.7 = (bf16[8,4,9216]{2,1,0:T(4,128)(2,1)}, bf16[8,4,9216]{2,1,0:T(4,128)(2,1)S(1)}, u32[]{:S(2)}, u32[]{:S(2)}) collective-permute-start(bf16[8,4,9216]{2,1,0:T(4,128)(2,1)} %get-tuple-element.42), channel_id=1, source_target_pairs={{0,8},{8,0},{1,9},{9,1},{2,10},{10,2},{3,11},{11,3},{4,12},{12,4},... | collective-permute-start | bytes 1769480 | tf_op jit(solution)/shard_map/ppermute | solution.py:454
  435.8 12.4 %copy-start.14 = (bf16[8,4,9216]{2,1,0:T(4,128)(2,1)}, bf16[8,4,9216]{2,1,0:T(4,128)(2,1)S(1)}, u32[]{:S(2)}) copy-start(bf16[8,4,9216]{2,1,0:T(4,128)(2,1)S(1)} %collective-permute-done.6.refs_1_) | copy-start | bytes 1769476
  453.0 4.6 copy-start.26
  453.0 5.8 %copy-start.24 = (bf16[128,128]{1,0:T(8,128)(2,1)S(1)}, bf16[128,128]{1,0:T(8,128)(2,1)}, u32[]{:S(2)}) copy-start(bf16[128,128]{1,0:T(8,128)(2,1)} %param.21) | copy-start | bytes 98308
  454.0 19.4 %all-to-all-start.12 = ((bf16[8,8,9216]{2,1,0:T(8,128)(2,1)}), bf16[8,8,9216]{2,1,0:T(8,128)(2,1)S(1)}, u32[]{:S(2)}, u32[]{:S(2)}) async-start(bf16[8,8,9216]{2,1,0:T(8,128)(2,1)} %add.5), calls=%async_computation.12 | async-start | bytes 2359296 | tf_op jit(solution)/shard_map/all_to_all | solution.py:450
  (11 other events, 9.6 us)

commit v11 on v10

--- a/solution.py
+++ b/solution.py
@@ -78,6 +78,18 @@
     return row_parts // near, near
 
 
+SMEM_SPEC = pl.BlockSpec(memory_space=pltpu.SMEM)
+VMEM_SPEC = pl.BlockSpec(memory_space=pltpu.VMEM)
+
+
+def near_core(array):
+    return pltpu.with_memory_space_constraint(array, pltpu.VMEM)
+
+
+def step_lanes(span):
+    return pl.ds(pl.multiple_of(pl.program_id(0) * span, span), span)
+
+
 def emit_projections(normed, rows_ref, out_refs):
     step = normed.shape[0]
     half = rows_ref.shape[0] // 2
@@ -106,8 +118,9 @@
     state = state_ref[...].astype(jnp.float32)
     normed = layer_norm(state, gain_ref[...], 1).astype(jnp.bfloat16)
     gating = sigmoid(jnp.dot(normed, gate_ref[...], preferred_element_type=jnp.float32))
+    lanes = step_lanes(state.shape[0])
     mixed = jnp.concatenate(
-        [ref[part].astype(jnp.float32) for ref in mix_refs for part in range(ref.shape[0])], axis=0
+        [ref[part, :, lanes].astype(jnp.float32) for ref in mix_refs for part in range(ref.shape[0])], axis=0
     )
     mixed = layer_norm(mixed, out_gain_ref[...], 0).astype(jnp.bfloat16)
     change = lax.dot_general(
@@ -164,14 +177,14 @@
     return pl.pallas_call(
         functools.partial(finish_kernel, len(mixes), onward is not None),
         grid=(positions // step,),
-        in_specs=[pl.BlockSpec((*m.shape[:2], step), lambda i: (0, 0, i)) for m in mixes]
+        in_specs=[VMEM_SPEC] * len(mixes)
         + [pl.BlockSpec((step, features), lambda i: (i, 0))]
         + [whole_spec(w) for w in weights],
         out_specs=out_specs,
         out_shape=out_shape,
         compiler_params=pltpu.CompilerParams(vmem_limit_bytes=BUDGET),
         name="finish",
-    )(*(pltpu.with_memory_space_constraint(m, pltpu.HBM) for m in mixes), state, *weights)
+    )(*map(near_core, mixes), state, *weights)
 
 
 class Folds:
@@ -365,11 +378,7 @@
     unstage(mixed.at[half_ref[1]], send_ref)
 
 
-SMEM_SPEC = pl.BlockSpec(memory_space=pltpu.SMEM)
-VMEM_SPEC = pl.BlockSpec(memory_space=pltpu.VMEM)
-
-
-def run_mix_out(folds, near, cols, width, stages, halves, *arrays, earlier=()):
+def run_mix_out(folds, near, cols, width, stages, halves, *arrays, mine=None, earlier=()):
     parts, _, positions = arrays[-1].shape
     rows = parts * width
     tall = width * cols * near * folds.rows
@@ -391,14 +400,15 @@
         scratch_shapes=scratch,
         compiler_params=pltpu.CompilerParams(vmem_limit_bytes=BUDGET),
         name="mix_out",
-    )(halves, *arrays, *earlier)
+    )(halves, *(array if array.ndim < 3 or array is mine else near_core(array) for array in arrays), *earlier)
 
 
 def add_kernel(*refs):
     target_ref = refs[-1]
     parts = target_ref.shape[0]
+    lanes = step_lanes(target_ref.shape[2])
     for part in range(parts):
-        sums = [kept[part] + got[part].astype(jnp.float32) for kept, got in zip(refs[:-1:2], refs[1:-1:2])]
+        sums = [kept[part] + got[part, :, lanes].astype(jnp.float32) for kept, got in zip(refs[:-1:2], refs[1:-1:2])]
         target_ref[part] = jnp.concatenate(sums, axis=0).astype(target_ref.dtype)
 
 
@@ -409,12 +419,12 @@
     return pl.pallas_call(
         add_kernel,
         grid=(positions // step,),
-        in_specs=[pl.BlockSpec((*array.shape[:2], step), lambda i: (0, 0, i)) for array in arrays],
+        in_specs=[pl.BlockSpec((*array.shape[:2], step), lambda i: (0, 0, i)) if at % 2 == 0 else VMEM_SPEC for at, array in enumerate(arrays)],
         out_specs=pl.BlockSpec((parts, height, step), lambda i: (0, 0, i)),
         out_shape=jax.ShapeDtypeStruct((parts, height, positions), jnp.bfloat16),
         compiler_params=pltpu.CompilerParams(vmem_limit_bytes=BUDGET),
         name="add",
-    )(*arrays)
+    )(*(near_core(array) if at % 2 else array for at, array in enumerate(arrays)))
 
 
 def run_mix_in(folds, near, cols, halves, both):
@@ -438,7 +448,7 @@
         ],
         compiler_params=pltpu.CompilerParams(vmem_limit_bytes=BUDGET),
         name="mix_in",
-    )(halves, both)
+    )(halves, near_core(both))
 
 
 SHARES = (1, 1, 1, 1)
@@ -512,7 +522,7 @@
             mixed[piece] = mix((0, 1), halves, left, right, there, earlier=earlier)[0]
         else:
             mine, unfolded = mix((0,), halves, left, right)
-            mixed[piece] = mix((1,), halves, unfolded, mine, there, earlier=earlier)[0]
+            mixed[piece] = mix((1,), halves, unfolded, mine, there, mine=mine, earlier=earlier)[0]
         if piece == group[-1]:
             mixes.append(exchange(mixed[piece]))
     onward = (gain_2, rows_of(project_2, *level[:1]), shapes_of(*level[:1]))

time: 484 us -> 471 us (0.973)
  local copies, waits for them, and re-layouts: 15.1 us -> 7.53 us
  Pallas kernels: 134 us -> 128 us
    unnamed x57 -> x31, local copies, waits for them, and re-layouts: 11.8 us -> 3.52 us
  transfers between devices with their start and end apart: 16 -> 16, of which waited for: 12 -> 12; matrix products, arithmetic and copies ran while one was open for 1% -> 1% of each run, Pallas kernels for 23% -> 22%
where the time goes in v11:
time: 471 us; the launch traced here: 469 us
  waiting for transfers between devices  195 us (41%)
  Pallas kernels  128 us (27%)
  blocking collectives  92.4 us (20%)
  starting transfers between devices  42.6 us (9%)
  local copies, waits for them, and re-layouts  7.53 us (2%)
    ppermute x8, waiting for transfers between devices, across(): return lax.ppermute(array, 'far', ((0, 1), (1, 0)))  159 us
    all_to_all x5, blocking collectives, exchange(): return lax.all_to_all(array, EVERY, split_axis=0, concat_axis=0, tiled=True)  92.4 us
    pallas_call x5, Pallas kernels, run_mix_out(): pl.pallas_call(functools.partial(mix_out_kernel, folds, near, cols, width...  45.9 us
    all_to_all x8, waiting for transfers between devices, exchange(): return lax.all_to_all(array, EVERY, split_axis=0, concat_axis=0, tiled=True)  36.6 us
    pallas_call x4, Pallas kernels, run_mix_in(): pl.pallas_call(functools.partial(mix_in_kernel, folds, near, cols, width)...  36.3 us
    all_to_all x8, starting transfers between devices, exchange(): return lax.all_to_all(array, EVERY, split_axis=0, concat_axis=0, tiled=True)  30.7 us
    pallas_call x3, Pallas kernels, run_projections(): pl.pallas_call(project_kernel, grid=(positions // step,), in_specs=[pl.Bl...  19.7 us
    pallas_call x2, Pallas kernels, run_finish(): pl.pallas_call(functools.partial(finish_kernel, len(mixes), onward is not...  18.2 us
  transfers between devices with their start and end apart: 16, of which 12 were waited for; matrix products, arithmetic and copies ran while one was open for 1% of the time, Pallas kernels for 22%

profile of v11, /device:TPU:0, one launch (start us, length us, event | category | flops | bytes accessed | tf_op | source)
XLA Modules:
  0.0 469.2 jit_solution(16029194471537525909)
XLA Ops:
  1.7 5.6 %project.4 = bf16[8,4,9216]{2,1,0:T(4,128)(2,1)} custom-call(bf16[9216,128]{1,0:T(8,128)(2,1)} %bitcast.90, f32[1,128]{1,0:T(1,128)} %bitcast.109, bf16[64,128]{1,0:T(8,128)(2,1)} %pad_maximum_fusion.3.rows_ref), custom_call_target="tpu_custom_call" | custom-call | tf_op jit(solution)/shard_map/project/pallas_call | solution.py:155
  7.3 5.3 %all-to-all-start.2 = ((bf16[8,4,9216]{2,1,0:T(4,128)(2,1)}), bf16[8,4,9216]{2,1,0:T(4,128)(2,1)S(1)}, u32[]{:S(2)}, u32[]{:S(2)}) async-start(bf16[8,4,9216]{2,1,0:T(4,128)(2,1)} %project.4), calls=%async_computation.2 | async-start | bytes 1179648 | tf_op jit(solution)/shard_map/all_to_all | solution.py:460
  13.4 7.2 %project.3 = (bf16[8,8,9216]{2,1,0:T(8,128)(2,1)}, bf16[8,8,9216]{2,1,0:T(8,128)(2,1)}, bf16[8,8,9216]{2,1,0:T(8,128)(2,1)}, bf16[8,4,9216]{2,1,0:T(4,128)(2,1)}) custom-call(bf16[9216,128]{1,0:T(8,128)(2,1)} %bitcast.91, f32[1,128]{1,0:T(1,128)} %bitcast.110, bf16[448,128]{1,0:T(8,128)(2,1)} %copy-done.7), custom_call_target="tpu_custom_call" | custom-call | tf_op jit(solution)/shard_map/project/pallas_call | solution.py:155
  22.1 14.5 %all_to_all.65.refs_0_ = bf16[8,4,9216]{2,1,0:T(4,128)(2,1)} all-to-all(bf16[8,4,9216]{2,1,0:T(4,128)(2,1)} %get-tuple-element.26), channel_id=1, replica_groups=mesh['groups'=2,'far'=2,'near'=2,'chan'=2,'sub'=2] {'near','chan','sub'}, dimensions={0} | all-to-all | bytes 1179648 | tf_op jit(solution)/shard_map/all_to_all | solution.py:460
  36.6 19.1 %all_to_all.66.refs_0_.refs_1_ = bf16[8,8,9216]{2,1,0:T(8,128)(2,1)S(1)} all-to-all(bf16[8,8,9216]{2,1,0:T(8,128)(2,1)S(1)} %copy-done.5), channel_id=1, replica_groups=mesh['groups'=2,'far'=2,'near'=2,'chan'=2,'sub'=2] {'near','chan','sub'}, dimensions={0} | all-to-all | bytes 2359296 | tf_op jit(solution)/shard_map/all_to_all | solution.py:460
  55.7 18.9 %all_to_all.67.refs_0_.refs_1_ = bf16[8,8,9216]{2,1,0:T(8,128)(2,1)S(1)} all-to-all(bf16[8,8,9216]{2,1,0:T(8,128)(2,1)S(1)} %copy-done.4), channel_id=1, replica_groups=mesh['groups'=2,'far'=2,'near'=2,'chan'=2,'sub'=2] {'near','chan','sub'}, dimensions={0} | all-to-all | bytes 2359296 | tf_op jit(solution)/shard_map/all_to_all | solution.py:460
  82.9 22.0 %collective-permute-done.1.refs_2_ = bf16[8,4,9216]{2,1,0:T(4,128)(2,1)} collective-permute-done((bf16[8,4,9216]{2,1,0:T(4,128)(2,1)}, bf16[8,4,9216]{2,1,0:T(4,128)(2,1)}, u32[]{:S(2)}, u32[]{:S(2)}) %collective-permute-start.1) | collective-permute-done | bytes 589856 | tf_op jit(solution)/shard_map/ppermute | solution.py:464
  106.0 10.6 %mix_out.5.refs_3_ = bf16[8,4,9216]{2,1,0:T(4,128)(2,1)} custom-call(s32[2]{0:T(128)} %pad_add_fusion.half_ref, bf16[8,8,9216]{2,1,0:T(8,128)(2,1)S(1)} %all_to_all.67.refs_0_.refs_1_, bf16[8,4,9216]{2,1,0:T(4,128)(2,1)S(1)} %copy-done.2, bf16[8,4,9216]{2,1,0:T(4,128)(2,1)} %collective-permute-done.1.refs_2_), custom_call_target="tpu_custom_call" | custom-call | tf_op jit(solution)/shard_map/mix_out/pallas_call | solution.py:395
  116.6 16.5 %collective-permute-done.refs_2_ = bf16[8,4,9216]{2,1,0:T(4,128)(2,1)} collective-permute-done((bf16[8,4,9216]{2,1,0:T(4,128)(2,1)}, bf16[8,4,9216]{2,1,0:T(4,128)(2,1)}, u32[]{:S(2)}, u32[]{:S(2)}) %collective-permute-start) | collective-permute-done | bytes 589856 | tf_op jit(solution)/shard_map/ppermute | solution.py:464
  133.1 11.4 %mix_out.6 = bf16[8,8,9216]{2,1,0:T(8,128)(2,1)} custom-call(s32[2]{0:T(128)} %pad_add_fusion.half_ref, bf16[8,8,9216]{2,1,0:T(8,128)(2,1)S(1)} %all_to_all.66.refs_0_.refs_1_, bf16[8,8,9216]{2,1,0:T(8,128)(2,1)S(1)} %all_to_all.67.refs_0_.refs_1_, bf16[8,4,9216]{2,1,0:T(4,128)(2,1)} %collective-permute-done.refs_2_, bf16[8,4,9216]{2,1,0:T(4,128)(2,1)} %mix_out.5.refs_3_), custom_call_target="tpu_custom_call" | custom-call | tf_op jit(solution)/shard_map/mix_out/pallas_call | solution.py:395
  151.7 7.2 %mix_out.7 = (bf16[8,4,9216]{2,1,0:T(4,128)(2,1)}, bf16[3072,128]{1,0:T(8,128)(2,1)}) custom-call(s32[2]{0:T(128)} %pad_add_fusion.half_ref, bf16[8,4,9216]{2,1,0:T(4,128)(2,1)S(1)} %copy-done.3, bf16[8,8,9216]{2,1,0:T(8,128)(2,1)S(1)} %all-to-all-done.5.refs_1_.refs_0_), custom_call_target="tpu_custom_call" | custom-call | tf_op jit(solution)/shard_map/mix_out/pallas_call | solution.py:395
  158.8 15.8 %collective-permute-done.3.refs_2_ = bf16[8,4,9216]{2,1,0:T(4,128)(2,1)S(1)} collective-permute-done((bf16[8,4,9216]{2,1,0:T(4,128)(2,1)S(1)}, bf16[8,4,9216]{2,1,0:T(4,128)(2,1)S(1)}, u32[]{:S(2)}, u32[]{:S(2)}) %collective-permute-start.3) | collective-permute-done | bytes 589856 | tf_op jit(solution)/shard_map/ppermute | solution.py:464
  174.6 10.3 %mix_out.8.refs_3_ = bf16[8,4,9216]{2,1,0:T(4,128)(2,1)} custom-call(s32[2]{0:T(128)} %pad_add_fusion.half_ref, bf16[8,8,9216]{2,1,0:T(8,128)(2,1)S(1)} %all-to-all-done.5.refs_1_.refs_0_, bf16[8,8,9216]{2,1,0:T(8,128)(2,1)S(1)} %all_to_all.66.refs_0_.refs_1_, bf16[8,4,9216]{2,1,0:T(4,128)(2,1)S(1)} %collective-permute-done.3.refs_2_), custom_call_target="tpu_custom_call" | custom-call | tf_op jit(solution)/shard_map/mix_out/pallas_call | solution.py:395
  184.9 18.3 %collective-permute-done.2.refs_2_ = bf16[8,4,9216]{2,1,0:T(4,128)(2,1)S(1)} collective-permute-done((bf16[8,4,9216]{2,1,0:T(4,128)(2,1)S(1)}, bf16[8,4,9216]{2,1,0:T(4,128)(2,1)S(1)}, u32[]{:S(2)}, u32[]{:S(2)}) %collective-permute-start.2) | collective-permute-done | bytes 589856 | tf_op jit(solution)/shard_map/ppermute | solution.py:464
  203.2 6.5 %mix_out.9 = bf16[8,8,9216]{2,1,0:T(8,128)(2,1)} custom-call(s32[2]{0:T(128)} %pad_add_fusion.half_ref, bf16[3072,128]{1,0:T(8,128)(2,1)} %get-tuple-element.28.refs_0_, bf16[8,4,9216]{2,1,0:T(4,128)(2,1)} %get-tuple-element.29.refs_1_, bf16[8,4,9216]{2,1,0:T(4,128)(2,1)S(1)} %collective-permute-done.2.refs_2_, bf16[8,4,9216]{2,1,0:T(4,128)(2,1)} %mix_out.8.refs_3_), custom_call_target="tpu_custom_call" | custom-call | tf_op jit(solution)/shard_map/mix_out/pallas_call | solution.py:395
  209.7 3.9 all-to-all-start.6
  216.3 13.0 %all-to-all-done.6.refs_1_ = bf16[8,8,9216]{2,1,0:T(8,128)(2,1)S(1)} async-done(((bf16[8,8,9216]{2,1,0:T(8,128)(2,1)}), bf16[8,8,9216]{2,1,0:T(8,128)(2,1)S(1)}, u32[]{:S(2)}, u32[]{:S(2)}) %all-to-all-start.6) | async-done | bytes 1179680 | tf_op jit(solution)/shard_map/all_to_all | solution.py:460
  229.2 10.5 %finish.2 = (bf16[9216,128]{1,0:T(8,128)(2,1)}, bf16[8,8,9216]{2,1,0:T(8,128)(2,1)}) custom-call(bf16[8,8,9216]{2,1,0:T(8,128)(2,1)S(1)} %all-to-all-done.3.refs_0_, bf16[8,8,9216]{2,1,0:T(8,128)(2,1)S(1)} %all-to-all-done.6.refs_1_, bf16[9216,128]{1,0:T(8,128)(2,1)} %bitcast.92, f32[1,128]{1,0:T(1,128)} %bitcast.111, bf16[128,128]{1,0:T(8,128)(2,1)} %refs_4_.2, ...), custom_call_target="tpu_custom_call" | custom-call | tf_op jit(solution)/shard_map/finish/pallas_call | solution.py:177
  244.1 6.9 %project.5 = (bf16[8,8,9216]{2,1,0:T(8,128)(2,1)}, bf16[8,8,9216]{2,1,0:T(8,128)(2,1)}, bf16[8,8,9216]{2,1,0:T(8,128)(2,1)}) custom-call(bf16[9216,128]{1,0:T(8,128)(2,1)} %get-tuple-element.33.state_ref.refs_2_, f32[1,128]{1,0:T(1,128)} %bitcast.113, bf16[384,128]{1,0:T(8,128)(2,1)} %copy-done.8), custom_call_target="tpu_custom_call" | custom-call | tf_op jit(solution)/shard_map/project/pallas_call | solution.py:155
  251.0 8.1 %all-to-all-done.7.both_ref = bf16[8,8,9216]{2,1,0:T(8,128)(2,1)S(1)} async-done(((bf16[8,8,9216]{2,1,0:T(8,128)(2,1)}), bf16[8,8,9216]{2,1,0:T(8,128)(2,1)S(1)}, u32[]{:S(2)}, u32[]{:S(2)}) %all-to-all-start.7) | async-done | bytes 1179680 | tf_op jit(solution)/shard_map/all_to_all | solution.py:460
  259.1 20.9 %all_to_all.68.both_ref = bf16[8,8,9216]{2,1,0:T(8,128)(2,1)} all-to-all(bf16[8,8,9216]{2,1,0:T(8,128)(2,1)} %get-tuple-element.34), channel_id=1, replica_groups=mesh['groups'=2,'far'=2,'near'=2,'chan'=2,'sub'=2] {'near','chan','sub'}, dimensions={0} | all-to-all | bytes 2359296 | tf_op jit(solution)/shard_map/all_to_all | solution.py:460
  280.0 18.9 %all_to_all.69.both_ref = bf16[8,8,9216]{2,1,0:T(8,128)(2,1)S(1)} all-to-all(bf16[8,8,9216]{2,1,0:T(8,128)(2,1)S(1)} %copy-done.6), channel_id=1, replica_groups=mesh['groups'=2,'far'=2,'near'=2,'chan'=2,'sub'=2] {'near','chan','sub'}, dimensions={0} | all-to-all | bytes 2359296 | tf_op jit(solution)/shard_map/all_to_all | solution.py:460
  302.6 9.1 %mix_in.4 = (f32[8,4,9216]{2,1,0:T(4,128)}, bf16[8,4,9216]{2,1,0:T(4,128)(2,1)}) custom-call(s32[2]{0:T(128)} %pad_add_fusion.half_ref, bf16[8,8,9216]{2,1,0:T(8,128)(2,1)S(1)} %all-to-all-done.7.both_ref), custom_call_target="tpu_custom_call" | custom-call | tf_op jit(solution)/shard_map/mix_in/pallas_call | solution.py:434
  314.6 9.1 %mix_in.5 = (f32[8,4,9216]{2,1,0:T(4,128)}, bf16[8,4,9216]{2,1,0:T(4,128)(2,1)}) custom-call(s32[2]{0:T(128)} %pad_add_fusion.half_ref, bf16[8,8,9216]{2,1,0:T(8,128)(2,1)S(1)} %copy-done), custom_call_target="tpu_custom_call" | custom-call | tf_op jit(solution)/shard_map/mix_in/pallas_call | solution.py:434
  323.7 30.6 %collective-permute-done.4.refs_1_ = bf16[8,4,9216]{2,1,0:T(4,128)(2,1)S(1)} collective-permute-done((bf16[8,4,9216]{2,1,0:T(4,128)(2,1)}, bf16[8,4,9216]{2,1,0:T(4,128)(2,1)S(1)}, u32[]{:S(2)}, u32[]{:S(2)}) %collective-permute-start.4) | collective-permute-done | bytes 589856 | tf_op jit(solution)/shard_map/ppermute | solution.py:464
  354.4 12.4 %collective-permute-done.5.refs_3_ = bf16[8,4,9216]{2,1,0:T(4,128)(2,1)S(1)} collective-permute-done((bf16[8,4,9216]{2,1,0:T(4,128)(2,1)}, bf16[8,4,9216]{2,1,0:T(4,128)(2,1)S(1)}, u32[]{:S(2)}, u32[]{:S(2)}) %collective-permute-start.5) | collective-permute-done | bytes 589856 | tf_op jit(solution)/shard_map/ppermute | solution.py:464
  374.0 9.0 %mix_in.6 = (f32[8,4,9216]{2,1,0:T(4,128)}, bf16[8,4,9216]{2,1,0:T(4,128)(2,1)}) custom-call(s32[2]{0:T(128)} %pad_add_fusion.half_ref, bf16[8,8,9216]{2,1,0:T(8,128)(2,1)S(1)} %all_to_all.69.both_ref), custom_call_target="tpu_custom_call" | custom-call | tf_op jit(solution)/shard_map/mix_in/pallas_call | solution.py:434
  386.0 9.0 %mix_in.7 = (f32[8,4,9216]{2,1,0:T(4,128)}, bf16[8,4,9216]{2,1,0:T(4,128)(2,1)}) custom-call(s32[2]{0:T(128)} %pad_add_fusion.half_ref, bf16[8,8,9216]{2,1,0:T(8,128)(2,1)S(1)} %all-to-all-done.11.both_ref), custom_call_target="tpu_custom_call" | custom-call | tf_op jit(solution)/shard_map/mix_in/pallas_call | solution.py:434
  395.0 30.7 %collective-permute-done.6.refs_1_ = bf16[8,4,9216]{2,1,0:T(4,128)(2,1)S(1)} collective-permute-done((bf16[8,4,9216]{2,1,0:T(4,128)(2,1)}, bf16[8,4,9216]{2,1,0:T(4,128)(2,1)S(1)}, u32[]{:S(2)}, u32[]{:S(2)}) %collective-permute-start.6) | collective-permute-done | bytes 589856 | tf_op jit(solution)/shard_map/ppermute | solution.py:464
  425.7 12.4 %collective-permute-done.7.refs_3_ = bf16[8,4,9216]{2,1,0:T(4,128)(2,1)S(1)} collective-permute-done((bf16[8,4,9216]{2,1,0:T(4,128)(2,1)}, bf16[8,4,9216]{2,1,0:T(4,128)(2,1)S(1)}, u32[]{:S(2)}, u32[]{:S(2)}) %collective-permute-start.7) | collective-permute-done | bytes 589856 | tf_op jit(solution)/shard_map/ppermute | solution.py:464
  447.4 14.0 %all-to-all-done.12.refs_1_ = bf16[8,8,9216]{2,1,0:T(8,128)(2,1)S(1)} async-done(((bf16[8,8,9216]{2,1,0:T(8,128)(2,1)}), bf16[8,8,9216]{2,1,0:T(8,128)(2,1)S(1)}, u32[]{:S(2)}, u32[]{:S(2)}) %all-to-all-start.12) | async-done | bytes 1179680 | tf_op jit(solution)/shard_map/all_to_all | solution.py:460
  461.5 7.7 %finish.3 = bf16[9216,128]{1,0:T(8,128)(2,1)} custom-call(bf16[8,8,9216]{2,1,0:T(8,128)(2,1)S(1)} %all-to-all-done.9.refs_0_, bf16[8,8,9216]{2,1,0:T(8,128)(2,1)S(1)} %all-to-all-done.12.refs_1_, bf16[9216,128]{1,0:T(8,128)(2,1)} %get-tuple-element.33.state_ref.refs_2_, f32[1,128]{1,0:T(1,128)} %bitcast.114, bf16[128,128]{1,0:T(8,128)(2,1)} %refs_4_.3, ...), custom_call_target="tpu_custom_call" | custom-call | tf_op jit(solution)/shard_map/finish/pallas_call | solution.py:177
  (95 shorter events, 53.5 us)
Async XLA Ops:
  7.3 14.8 %all-to-all-start.2 = ((bf16[8,4,9216]{2,1,0:T(4,128)(2,1)}), bf16[8,4,9216]{2,1,0:T(4,128)(2,1)S(1)}, u32[]{:S(2)}, u32[]{:S(2)}) async-start(bf16[8,4,9216]{2,1,0:T(4,128)(2,1)} %project.4), calls=%async_computation.2 | async-start | bytes 1179648 | tf_op jit(solution)/shard_map/all_to_all | solution.py:460
  12.7 0.7 copy-start.7
  20.6 16.0 %copy-start.5 = (bf16[8,8,9216]{2,1,0:T(8,128)(2,1)S(1)}, bf16[8,8,9216]{2,1,0:T(8,128)(2,1)}, u32[]{:S(2)}) copy-start(bf16[8,8,9216]{2,1,0:T(8,128)(2,1)} %get-tuple-element.24) | copy-start | bytes 3538948
  22.1 33.6 %copy-start.1 = (bf16[8,4,9216]{2,1,0:T(4,128)(2,1)}, bf16[8,4,9216]{2,1,0:T(4,128)(2,1)S(1)}, u32[]{:S(2)}) copy-start(bf16[8,4,9216]{2,1,0:T(4,128)(2,1)S(1)} %all-to-all-done.2.refs_1_) | copy-start | bytes 1769476
  36.6 19.1 %copy-start.4 = (bf16[8,8,9216]{2,1,0:T(8,128)(2,1)S(1)}, bf16[8,8,9216]{2,1,0:T(8,128)(2,1)}, u32[]{:S(2)}) copy-start(bf16[8,8,9216]{2,1,0:T(8,128)(2,1)} %get-tuple-element.25) | copy-start | bytes 3538948
  74.7 69.7 %all-to-all-start.5 = ((bf16[8,8,9216]{2,1,0:T(8,128)(2,1)}), bf16[8,8,9216]{2,1,0:T(8,128)(2,1)S(1)}, u32[]{:S(2)}, u32[]{:S(2)}) async-start(bf16[8,8,9216]{2,1,0:T(8,128)(2,1)} %get-tuple-element.27), calls=%async_computation.5 | async-start | bytes 2359296 | tf_op jit(solution)/shard_map/all_to_all | solution.py:460
  78.2 26.7 %collective-permute-start.1 = (bf16[8,4,9216]{2,1,0:T(4,128)(2,1)}, bf16[8,4,9216]{2,1,0:T(4,128)(2,1)}, u32[]{:S(2)}, u32[]{:S(2)}) collective-permute-start(bf16[8,4,9216]{2,1,0:T(4,128)(2,1)} %copy-done.1), channel_id=1, source_target_pairs={{0,8},{8,0},{1,9},{9,1},{2,10},{10,2},{3,11},{11,3},{4,12},{12,4},... | collective-permute-start | bytes 1769480 | tf_op jit(solution)/shard_map/ppermute | solution.py:464
  82.0 51.0 %collective-permute-start = (bf16[8,4,9216]{2,1,0:T(4,128)(2,1)}, bf16[8,4,9216]{2,1,0:T(4,128)(2,1)}, u32[]{:S(2)}, u32[]{:S(2)}) collective-permute-start(bf16[8,4,9216]{2,1,0:T(4,128)(2,1)} %slice.178), channel_id=1, source_target_pairs={{0,8},{8,0},{1,9},{9,1},{2,10},{10,2},{3,11},{11,3},{4,12},{12,4},... | collective-permute-start | bytes 1769480 | tf_op jit(solution)/shard_map/ppermute | solution.py:464
  105.0 1.1 copy-start.2
  144.4 65.3 %all-to-all-start.3 = ((bf16[8,8,9216]{2,1,0:T(8,128)(2,1)}), bf16[8,8,9216]{2,1,0:T(8,128)(2,1)S(1)}, u32[]{:S(2)}, u32[]{:S(2)}) async-start(bf16[8,8,9216]{2,1,0:T(8,128)(2,1)} %mix_out.6), calls=%async_computation.3 | async-start | bytes 2359296 | tf_op jit(solution)/shard_map/all_to_all | solution.py:460
  148.0 3.7 copy-start.3
  148.3 26.3 %collective-permute-start.3 = (bf16[8,4,9216]{2,1,0:T(4,128)(2,1)S(1)}, bf16[8,4,9216]{2,1,0:T(4,128)(2,1)S(1)}, u32[]{:S(2)}, u32[]{:S(2)}) collective-permute-start(bf16[8,4,9216]{2,1,0:T(4,128)(2,1)S(1)} %slice.182), channel_id=1, source_target_pairs={{0,8},{8,0},{1,9},{9,1},{2,10},{10,2},{3,11},{11,3},{4,12},{12,4},... | collective-permute-start | bytes 1769480 | tf_op jit(solution)/shard_map/ppermute | solution.py:464
  151.5 51.6 %collective-permute-start.2 = (bf16[8,4,9216]{2,1,0:T(4,128)(2,1)S(1)}, bf16[8,4,9216]{2,1,0:T(4,128)(2,1)S(1)}, u32[]{:S(2)}, u32[]{:S(2)}) collective-permute-start(bf16[8,4,9216]{2,1,0:T(4,128)(2,1)S(1)} %slice.181), channel_id=1, source_target_pairs={{0,8},{8,0},{1,9},{9,1},{2,10},{10,2},{3,11},{11,3},{4,12},{12,4},... | collective-permute-start | bytes 1769480 | tf_op jit(solution)/shard_map/ppermute | solution.py:464
  209.7 3.9 copy-start.12
  209.7 5.1 %copy-start.9 = (bf16[128,512]{1,0:T(8,128)(2,1)S(1)}, bf16[128,512]{1,0:T(8,128)(2,1)}, u32[]{:S(2)}) copy-start(bf16[128,512]{1,0:T(8,128)(2,1)} %param.18) | copy-start | bytes 393220
  209.7 5.3 %copy-start.10 = (bf16[128,128]{1,0:T(8,128)(2,1)S(1)}, bf16[128,128]{1,0:T(8,128)(2,1)}, u32[]{:S(2)}) copy-start(bf16[128,128]{1,0:T(8,128)(2,1)} %param.16) | copy-start | bytes 98308
  209.7 19.5 %all-to-all-start.6 = ((bf16[8,8,9216]{2,1,0:T(8,128)(2,1)}), bf16[8,8,9216]{2,1,0:T(8,128)(2,1)S(1)}, u32[]{:S(2)}, u32[]{:S(2)}) async-start(bf16[8,8,9216]{2,1,0:T(8,128)(2,1)} %mix_out.9), calls=%async_computation.6 | async-start | bytes 2359296 | tf_op jit(solution)/shard_map/all_to_all | solution.py:460
  239.7 19.4 %all-to-all-start.7 = ((bf16[8,8,9216]{2,1,0:T(8,128)(2,1)}), bf16[8,8,9216]{2,1,0:T(8,128)(2,1)S(1)}, u32[]{:S(2)}, u32[]{:S(2)}) async-start(bf16[8,8,9216]{2,1,0:T(8,128)(2,1)} %get-tuple-element.30), calls=%async_computation.7 | async-start | bytes 2359296 | tf_op jit(solution)/shard_map/all_to_all | solution.py:460
  243.4 0.6 copy-start.8
  259.1 20.9 %copy-start.6 = (bf16[8,8,9216]{2,1,0:T(8,128)(2,1)S(1)}, bf16[8,8,9216]{2,1,0:T(8,128)(2,1)}, u32[]{:S(2)}) copy-start(bf16[8,8,9216]{2,1,0:T(8,128)(2,1)} %get-tuple-element.37) | copy-start | bytes 3538948
  299.0 71.5 %all-to-all-start.11 = ((bf16[8,8,9216]{2,1,0:T(8,128)(2,1)}), bf16[8,8,9216]{2,1,0:T(8,128)(2,1)S(1)}, u32[]{:S(2)}, u32[]{:S(2)}) async-start(bf16[8,8,9216]{2,1,0:T(8,128)(2,1)} %get-tuple-element.40), calls=%async_computation.11 | async-start | bytes 2359296 | tf_op jit(solution)/shard_map/all_to_all | solution.py:460
  302.6 12.1 %copy-start = (bf16[8,8,9216]{2,1,0:T(8,128)(2,1)S(1)}, bf16[8,8,9216]{2,1,0:T(8,128)(2,1)}, u32[]{:S(2)}) copy-start(bf16[8,8,9216]{2,1,0:T(8,128)(2,1)} %all_to_all.68.both_ref) | copy-start | bytes 3538948
  311.7 42.6 %collective-permute-start.4 = (bf16[8,4,9216]{2,1,0:T(4,128)(2,1)}, bf16[8,4,9216]{2,1,0:T(4,128)(2,1)S(1)}, u32[]{:S(2)}, u32[]{:S(2)}) collective-permute-start(bf16[8,4,9216]{2,1,0:T(4,128)(2,1)} %get-tuple-element.32), channel_id=1, source_target_pairs={{0,8},{8,0},{1,9},{9,1},{2,10},{10,2},{3,11},{11,3},{4,12},{12,4},... | collective-permute-start | bytes 1769480 | tf_op jit(solution)/shard_map/ppermute | solution.py:464
  323.7 43.0 %collective-permute-start.5 = (bf16[8,4,9216]{2,1,0:T(4,128)(2,1)}, bf16[8,4,9216]{2,1,0:T(4,128)(2,1)S(1)}, u32[]{:S(2)}, u32[]{:S(2)}) collective-permute-start(bf16[8,4,9216]{2,1,0:T(4,128)(2,1)} %get-tuple-element.36), channel_id=1, source_target_pairs={{0,8},{8,0},{1,9},{9,1},{2,10},{10,2},{3,11},{11,3},{4,12},{12,4},... | collective-permute-start | bytes 1769480 | tf_op jit(solution)/shard_map/ppermute | solution.py:464
  370.5 71.5 %all-to-all-start.9 = ((bf16[8,8,9216]{2,1,0:T(8,128)(2,1)}), bf16[8,8,9216]{2,1,0:T(8,128)(2,1)S(1)}, u32[]{:S(2)}, u32[]{:S(2)}) async-start(bf16[8,8,9216]{2,1,0:T(8,128)(2,1)} %add.4), calls=%async_computation.9 | async-start | bytes 2359296 | tf_op jit(solution)/shard_map/all_to_all | solution.py:460
  383.1 42.6 %collective-permute-start.6 = (bf16[8,4,9216]{2,1,0:T(4,128)(2,1)}, bf16[8,4,9216]{2,1,0:T(4,128)(2,1)S(1)}, u32[]{:S(2)}, u32[]{:S(2)}) collective-permute-start(bf16[8,4,9216]{2,1,0:T(4,128)(2,1)} %get-tuple-element.39), channel_id=1, source_target_pairs={{0,8},{8,0},{1,9},{9,1},{2,10},{10,2},{3,11},{11,3},{4,12},{12,4},... | collective-permute-start | bytes 1769480 | tf_op jit(solution)/shard_map/ppermute | solution.py:464
  395.0 43.1 %collective-permute-start.7 = (bf16[8,4,9216]{2,1,0:T(4,128)(2,1)}, bf16[8,4,9216]{2,1,0:T(4,128)(2,1)S(1)}, u32[]{:S(2)}, u32[]{:S(2)}) collective-permute-start(bf16[8,4,9216]{2,1,0:T(4,128)(2,1)} %get-tuple-element.42), channel_id=1, source_target_pairs={{0,8},{8,0},{1,9},{9,1},{2,10},{10,2},{3,11},{11,3},{4,12},{12,4},... | collective-permute-start | bytes 1769480 | tf_op jit(solution)/shard_map/ppermute | solution.py:464
  441.9 3.7 copy-start.13
  442.0 4.9 %copy-start.11 = (bf16[128,128]{1,0:T(8,128)(2,1)S(1)}, bf16[128,128]{1,0:T(8,128)(2,1)}, u32[]{:S(2)}) copy-start(bf16[128,128]{1,0:T(8,128)(2,1)} %param.21) | copy-start | bytes 98308
  442.0 19.5 %all-to-all-start.12 = ((bf16[8,8,9216]{2,1,0:T(8,128)(2,1)}), bf16[8,8,9216]{2,1,0:T(8,128)(2,1)S(1)}, u32[]{:S(2)}, u32[]{:S(2)}) async-start(bf16[8,8,9216]{2,1,0:T(8,128)(2,1)} %add.5), calls=%async_computation.12 | async-start | bytes 2359296 | tf_op jit(solution)/shard_map/all_to_all | solution.py:460
